TPU v7x, 256 devices: a whole 4x4x8 slice. The times are simulated.
256 devices in a mesh: tmpl: 2 (over core), row: 128 (over x, y, z).
Axes of the slice: x: 4, y: 4, z: 8, core: 2. Of those that a mesh axis runs over, the one named last changes fastest.
Arguments:
- pair_maps: bfloat16 [2, 2048, 2048, 64], P('tmpl', 'row'), may hold values from -6 to 6
- crop_tiles: int32 [2, 8], P('tmpl'), may hold values from 0 to 15, as said below
- full_length: int32 [1], replicated, may hold values from 1536 to 2048
- proj_weight: bfloat16 [2, 64, 320], replicated, may hold values from -0.75 to 0.75
- out_weight: bfloat16 [2, 64, 64], replicated, may hold values from -0.75 to 0.75
- final_weight: bfloat16 [64, 128], replicated, may hold values from -0.75 to 0.75
Outputs:
- embedding: bfloat16 [128, 1024, 1024], P(None, 'row')
Inputs may be any that keep to these rules, and one draw needn't show every extreme that they name: Each row of crop_tiles names 8 different tiles of the 16, in increasing order; its last 4 entries are the tiles 16 - 8 // 2 to 15.
All inputs are finite; a program needn't handle non-finite values.
Results may differ from a plain program's by a relative error of at most 0.014.
Values may be sent and summed in bfloat16 or wider, within the bound.
No kernel may reach another device: no remote copies, remote signals or barrier semaphores. Data moves between devices by JAX's collectives and lax.ppermute only.
A program may use at most 64 MiB of HBM per device.

v0:
```python
import jax
import jax.numpy as jnp
from jax import lax
from jax.sharding import PartitionSpec as P

CH = 64
CROP = 1024
TILE = 128
NLAYER = 2
FULL = 2048


EPSILON = 1e-05


def from_partner(value, axis, bit):
    mask = 2**bit
    pairs = [(source, source ^ mask) for source in range(lax.axis_size(axis))]
    return lax.ppermute(value, axis, pairs)


def channel_norm(values):
    center = values - jnp.mean(values, axis=0, keepdims=True)
    spread = jnp.mean(center * center, axis=0, keepdims=True)
    return center * lax.rsqrt(spread + EPSILON)


def on_device(pair_maps, crop_tiles, full_length, proj_weight, out_weight, final_weight):
    row_count = lax.axis_size("row")
    my_index = lax.axis_index("row")
    pair_local = pair_maps[0]
    crop_ids = crop_tiles[0]
    local_rows = pair_local.shape[0]
    col_width = CROP // row_count
    parts_count = max(1, row_count // CH)
    per_group = CH * parts_count // row_count
    groups = CH // per_group
    part_rows = CROP // parts_count
    steps_crop = jnp.arange(CROP, dtype=jnp.int32)
    position = crop_ids[steps_crop // TILE] * TILE + steps_crop % TILE
    usable = (position < full_length[0]).astype(jnp.float32)
    col_usable = lax.dynamic_slice_in_dim(usable, my_index * col_width, col_width)
    pair_mask = col_usable[:, None] * usable[None, :]
    columns = pair_local.reshape(local_rows, FULL // TILE, TILE, CH)[:, crop_ids]
    columns = columns.reshape(local_rows, CROP * CH)
    received = lax.all_to_all(columns, "row", split_axis=1, concat_axis=0, tiled=True)
    cropped = received.reshape(FULL // TILE, TILE, col_width * CH)[crop_ids]
    current = jnp.transpose(cropped.reshape(CROP, col_width, CH), (2, 1, 0))
    for layer_idx in range(NLAYER):
        normed_in = channel_norm(current.astype(jnp.float32)).astype(jnp.bfloat16)
        projected = jnp.einsum(
            "cd,cwi->dwi", proj_weight[layer_idx], normed_in, preferred_element_type=jnp.float32
        )
        left_proj = (jax.nn.sigmoid(projected[:CH]) * projected[CH : 2 * CH] * pair_mask).astype(
            jnp.bfloat16
        )
        right_proj = (
            jax.nn.sigmoid(projected[2 * CH : 3 * CH]) * projected[3 * CH : 4 * CH] * pair_mask
        ).astype(jnp.bfloat16)
        gate_vals = jax.nn.sigmoid(projected[4 * CH :])
        left_send = left_proj.reshape(groups, per_group, col_width, parts_count, part_rows)
        left_send = jnp.transpose(left_send, (0, 3, 1, 2, 4)).reshape(
            row_count, per_group, col_width, part_rows
        )
        right_send = right_proj.reshape(groups, per_group, col_width, parts_count, part_rows)
        right_send = jnp.transpose(right_send, (0, 3, 1, 2, 4)).reshape(
            row_count, per_group, col_width, part_rows
        )
        left_got, right_got = (
            lax.all_to_all(left_send, "row", split_axis=0, concat_axis=2, tiled=True),
            lax.all_to_all(right_send, "row", split_axis=0, concat_axis=2, tiled=True),
        )
        right_whole = right_got[0]
        partner = from_partner(right_whole, "row", 0)
        lower_side = my_index // (1 << 0) % 2 == 0
        right_whole = jnp.where(
            lower_side,
            jnp.concatenate([right_whole, partner], axis=2),
            jnp.concatenate([partner, right_whole], axis=2),
        )
        products = jnp.einsum(
            "cki,ckj->cij", left_got[0], right_whole, preferred_element_type=jnp.float32
        ).astype(jnp.bfloat16)
        back_send = jnp.transpose(
            products.reshape(per_group, part_rows, row_count, col_width), (2, 0, 3, 1)
        )
        back_got = lax.all_to_all(back_send, "row", split_axis=0, concat_axis=0, tiled=True)
        merged = back_got.reshape(groups, parts_count, per_group, col_width, part_rows)
        merged = jnp.transpose(merged, (0, 2, 3, 1, 4)).reshape(CH, col_width, CROP)
        normed_out = channel_norm(merged.astype(jnp.float32)).astype(jnp.bfloat16)
        update = jnp.einsum(
            "cd,cwi->dwi", out_weight[layer_idx], normed_out, preferred_element_type=jnp.float32
        )
        current = (current.astype(jnp.float32) + gate_vals * update).astype(jnp.bfloat16)
    normed_final = channel_norm(current.astype(jnp.float32))
    template_count = lax.axis_size("tmpl")
    summed = lax.psum(normed_final.astype(jnp.bfloat16), "tmpl").astype(jnp.float32)
    hidden = jnp.maximum(summed / template_count, 0.0).astype(jnp.bfloat16)
    result = jnp.einsum(
        "cz,cwi->zwi", final_weight, hidden, preferred_element_type=jnp.float32
    ).astype(jnp.bfloat16)
    return result


def solution(mesh):
    placed = (P("tmpl", "row", None, None), P("tmpl", None), P(), P(), P(), P())
    return jax.shard_map(
        on_device, mesh=mesh, in_specs=placed, out_specs=P(None, "row", None), check_vma=False
    )
```

profile of v0, /device:TPU:1, one launch (start us, length us, event | category | flops | bytes accessed | tf_op | source)
XLA Modules:
  0.0 438.6 jit_solution(15340569308380098732)
XLA Ops:
  7.2 3.6 copy.60
  17.0 3.2 copy.42
  20.2 5.4 %all_to_all.19 = bf16[16,128,512]{2,1,0:T(8,128)(2,1)S(1)} reshape(bf16[16,8,128,64]{3,2,1,0:T(8,128)(2,1)} %copy.42) | data formatting | bytes 4194304 | tf_op jit(solution)/shard_map/all_to_all | solution.py:46
  28.1 16.6 %all-to-all-start = ((bf16[16,128,512]{2,0,1:T(8,128)(2,1)}), bf16[16,128,512]{2,0,1:T(8,128)(2,1)S(1)}, u32[]{:S(2)}, u32[]{:S(2)}) async-start(bf16[16,128,512]{2,0,1:T(8,128)(2,1)} %copy.43), calls=%async_computation | async-start | bytes 4194304 | tf_op jit(solution)/shard_map/all_to_all | solution.py:46
  46.1 4.3 compare_select_fusion.1
  51.1 46.3 %all-to-all-done = bf16[16,128,512]{2,0,1:T(8,128)(2,1)S(1)} async-done(((bf16[16,128,512]{2,0,1:T(8,128)(2,1)}), bf16[16,128,512]{2,0,1:T(8,128)(2,1)S(1)}, u32[]{:S(2)}, u32[]{:S(2)}) %all-to-all-start) | async-done | bytes 2097184 | tf_op jit(solution)/shard_map/all_to_all | solution.py:46
  110.8 3.3 copy.46
  114.2 7.3 %all-to-all-start.2 = ((bf16[128,1,8,512]{3,2,1,0:T(8,128)(2,1)}), bf16[128,1,8,512]{3,2,1,0:T(8,128)(2,1)}, u32[]{:S(2)}, u32[]{:S(2)}) async-start(bf16[128,1,8,512]{3,2,1,0:T(8,128)(2,1)} %bitcast.164), calls=%async_computation.2 | async-start | bytes 2097152 | tf_op jit(solution)/shard_map/all_to_all | solution.py:71
  123.1 3.4 copy.45
  126.5 23.1 %all-to-all-done.2 = bf16[128,1,8,512]{3,2,1,0:T(8,128)(2,1)} async-done(((bf16[128,1,8,512]{3,2,1,0:T(8,128)(2,1)}), bf16[128,1,8,512]{3,2,1,0:T(8,128)(2,1)}, u32[]{:S(2)}, u32[]{:S(2)}) %all-to-all-start.2) | async-done | bytes 1048608 | tf_op jit(solution)/shard_map/all_to_all | solution.py:71
  149.5 6.2 %all-to-all-start.1 = ((bf16[128,1,8,512]{3,2,1,0:T(8,128)(2,1)}), bf16[128,1,8,512]{3,2,1,0:T(8,128)(2,1)S(1)}, u32[]{:S(2)}, u32[]{:S(2)}) async-start(bf16[128,1,8,512]{3,2,1,0:T(8,128)(2,1)} %bitcast.20), calls=%async_computation.1 | async-start | bytes 2097152 | tf_op jit(solution)/shard_map/all_to_all | solution.py:70
  156.5 25.8 %all-to-all-done.1 = bf16[128,1,8,512]{3,2,1,0:T(8,128)(2,1)S(1)} async-done(((bf16[128,1,8,512]{3,2,1,0:T(8,128)(2,1)}), bf16[128,1,8,512]{3,2,1,0:T(8,128)(2,1)S(1)}, u32[]{:S(2)}, u32[]{:S(2)}) %all-to-all-start.1) | async-done | bytes 1048608 | tf_op jit(solution)/shard_map/all_to_all | solution.py:70
  182.3 17.1 %collective-permute-done = bf16[1,1024,512]{2,1,0:T(8,128)(2,1)} collective-permute-done((bf16[1,1024,512]{2,1,0:T(8,128)(2,1)}, bf16[1,1024,512]{2,1,0:T(8,128)(2,1)}, u32[]{:S(2)}, u32[]{:S(2)}) %collective-permute-start) | collective-permute-done | bytes 1048608 | tf_op jit(solution)/shard_map/ppermute | solution.py:19
  199.3 4.5 %fusion.66 = bf16[512,1024]{1,0:T(8,128)(2,1)} fusion(bf16[1024,512]{1,0:T(8,128)(2,1)} %bitcast.26, bf16[1024,512]{1,0:T(8,128)(2,1)} %bitcast.24, pred[]{:T(512)S(6)} %eq.9, bf16[128,1,8,512]{3,2,1,0:T(8,128)(2,1)S(1)} %all-to-all-done.1), kind=kOutput, calls=%fused_computation.95 | convolution fusion | flops 1083703296 | bytes 4194305 | tf_op jit(solution)/shard_map/cki,ckj->cij/dot_general | solution.py:81
  205.3 40.8 %all_to_all.62 = bf16[128,1,8,512]{3,2,1,0:T(8,128)(2,1)S(1)} all-to-all(bf16[128,1,8,512]{3,2,1,0:T(8,128)(2,1)S(1)} %bitcast.167), channel_id=1, replica_groups=mesh['tmpl'=2,'row'=128] {'row'}, dimensions={0} | all-to-all | bytes 2097152 | tf_op jit(solution)/shard_map/all_to_all | solution.py:87
  259.8 3.3 copy.52
  263.1 7.7 %all-to-all-start.5 = ((bf16[128,1,8,512]{3,2,1,0:T(8,128)(2,1)}), bf16[128,1,8,512]{3,2,1,0:T(8,128)(2,1)}, u32[]{:S(2)}, u32[]{:S(2)}) async-start(bf16[128,1,8,512]{3,2,1,0:T(8,128)(2,1)} %bitcast.43), calls=%async_computation.5 | async-start | bytes 2097152 | tf_op jit(solution)/shard_map/all_to_all | solution.py:71
  273.7 23.3 %all-to-all-done.5 = bf16[128,1,8,512]{3,2,1,0:T(8,128)(2,1)} async-done(((bf16[128,1,8,512]{3,2,1,0:T(8,128)(2,1)}), bf16[128,1,8,512]{3,2,1,0:T(8,128)(2,1)}, u32[]{:S(2)}, u32[]{:S(2)}) %all-to-all-start.5) | async-done | bytes 1048608 | tf_op jit(solution)/shard_map/all_to_all | solution.py:71
  297.0 6.2 %all-to-all-start.4 = ((bf16[128,1,8,512]{3,2,1,0:T(8,128)(2,1)}), bf16[128,1,8,512]{3,2,1,0:T(8,128)(2,1)S(1)}, u32[]{:S(2)}, u32[]{:S(2)}) async-start(bf16[128,1,8,512]{3,2,1,0:T(8,128)(2,1)} %bitcast.40), calls=%async_computation.4 | async-start | bytes 2097152 | tf_op jit(solution)/shard_map/all_to_all | solution.py:70
  303.8 24.5 %all-to-all-done.4 = bf16[128,1,8,512]{3,2,1,0:T(8,128)(2,1)S(1)} async-done(((bf16[128,1,8,512]{3,2,1,0:T(8,128)(2,1)}), bf16[128,1,8,512]{3,2,1,0:T(8,128)(2,1)S(1)}, u32[]{:S(2)}, u32[]{:S(2)}) %all-to-all-start.4) | async-done | bytes 1048608 | tf_op jit(solution)/shard_map/all_to_all | solution.py:70
  328.3 17.5 %collective-permute-done.1 = bf16[1,1024,512]{2,1,0:T(8,128)(2,1)S(1)} collective-permute-done((bf16[1,1024,512]{2,1,0:T(8,128)(2,1)}, bf16[1,1024,512]{2,1,0:T(8,128)(2,1)S(1)}, u32[]{:S(2)}, u32[]{:S(2)}) %collective-permute-start.1) | collective-permute-done | bytes 1048608 | tf_op jit(solution)/shard_map/ppermute | solution.py:19
  346.8 3.5 fusion.65
  350.9 39.5 %all_to_all.63 = bf16[128,1,8,512]{3,2,1,0:T(8,128)(2,1)S(1)} all-to-all(bf16[128,1,8,512]{3,2,1,0:T(8,128)(2,1)S(1)} %bitcast.170), channel_id=1, replica_groups=mesh['tmpl'=2,'row'=128] {'row'}, dimensions={0} | all-to-all | bytes 2097152 | tf_op jit(solution)/shard_map/all_to_all | solution.py:87
  397.0 29.6 %all-reduce.2.cloned.1.call-done = bf16[64,8,1024]{2,0,1:T(8,128)(2,1)} async-done(((bf16[64,8,1024]{2,0,1:T(8,128)(2,1)}), bf16[64,8,1024]{2,0,1:T(8,128)(2,1)}) %all-reduce.2.cloned.1.call-update) | async-done | bytes 1048592 | tf_op jit(solution)/shard_map/psum | solution.py:97
  (71 shorter events, 58.1 us)
Async XLA Ops:
  6.5 420.1 %copy-start = (bf16[64,128]{1,0:T(8,128)(2,1)S(1)}, bf16[64,128]{1,0:T(8,128)(2,1)}, u32[]{:S(2)}) copy-start(bf16[64,128]{1,0:T(8,128)(2,1)} %param.11) | copy-start | bytes 49156
  28.1 17.3 %copy-start.4 = (s32[1,8]{1,0:T(1,128)S(1)}, s32[1,8]{1,0:T(1,128)}, u32[]{:S(2)}) copy-start(s32[1,8]{1,0:T(1,128)} %param.7) | copy-start | bytes 100
  28.1 69.3 %all-to-all-start = ((bf16[16,128,512]{2,0,1:T(8,128)(2,1)}), bf16[16,128,512]{2,0,1:T(8,128)(2,1)S(1)}, u32[]{:S(2)}, u32[]{:S(2)}) async-start(bf16[16,128,512]{2,0,1:T(8,128)(2,1)} %copy.43), calls=%async_computation | async-start | bytes 4194304 | tf_op jit(solution)/shard_map/all_to_all | solution.py:46
  101.4 0.9 copy-start.3
  103.9 4.3 copy-start.1
  114.2 35.4 %all-to-all-start.2 = ((bf16[128,1,8,512]{3,2,1,0:T(8,128)(2,1)}), bf16[128,1,8,512]{3,2,1,0:T(8,128)(2,1)}, u32[]{:S(2)}, u32[]{:S(2)}) async-start(bf16[128,1,8,512]{3,2,1,0:T(8,128)(2,1)} %bitcast.164), calls=%async_computation.2 | async-start | bytes 2097152 | tf_op jit(solution)/shard_map/all_to_all | solution.py:71
  149.5 32.7 %all-to-all-start.1 = ((bf16[128,1,8,512]{3,2,1,0:T(8,128)(2,1)}), bf16[128,1,8,512]{3,2,1,0:T(8,128)(2,1)S(1)}, u32[]{:S(2)}, u32[]{:S(2)}) async-start(bf16[128,1,8,512]{3,2,1,0:T(8,128)(2,1)} %bitcast.20), calls=%async_computation.1 | async-start | bytes 2097152 | tf_op jit(solution)/shard_map/all_to_all | solution.py:70
  155.7 43.6 %collective-permute-start = (bf16[1,1024,512]{2,1,0:T(8,128)(2,1)}, bf16[1,1024,512]{2,1,0:T(8,128)(2,1)}, u32[]{:S(2)}, u32[]{:S(2)}) collective-permute-start(bf16[1,1024,512]{2,1,0:T(8,128)(2,1)} %bitcast.25), channel_id=1, source_target_pairs={{0,1},{1,0},{2,3},{3,2},{4,5},{5,4},{6,7},{7,6},{8,9},{9,8},{10,11... | collective-permute-start | bytes 3145736 | tf_op jit(solution)/shard_map/ppermute | solution.py:19
  247.0 2.4 copy-start.6
  254.3 4.0 copy-start.2
  263.1 33.9 %all-to-all-start.5 = ((bf16[128,1,8,512]{3,2,1,0:T(8,128)(2,1)}), bf16[128,1,8,512]{3,2,1,0:T(8,128)(2,1)}, u32[]{:S(2)}, u32[]{:S(2)}) async-start(bf16[128,1,8,512]{3,2,1,0:T(8,128)(2,1)} %bitcast.43), calls=%async_computation.5 | async-start | bytes 2097152 | tf_op jit(solution)/shard_map/all_to_all | solution.py:71
  297.0 31.3 %all-to-all-start.4 = ((bf16[128,1,8,512]{3,2,1,0:T(8,128)(2,1)}), bf16[128,1,8,512]{3,2,1,0:T(8,128)(2,1)S(1)}, u32[]{:S(2)}, u32[]{:S(2)}) async-start(bf16[128,1,8,512]{3,2,1,0:T(8,128)(2,1)} %bitcast.40), calls=%async_computation.4 | async-start | bytes 2097152 | tf_op jit(solution)/shard_map/all_to_all | solution.py:70
  303.2 123.4 %all-reduce.2.cloned.1.call-start = ((), (), s32[]{:S(2)}) async-start(), calls=%async_computation.7 | async-start | bytes 2097152 | tf_op jit(solution)/shard_map/psum | solution.py:97
  303.3 42.6 %collective-permute-start.1 = (bf16[1,1024,512]{2,1,0:T(8,128)(2,1)}, bf16[1,1024,512]{2,1,0:T(8,128)(2,1)S(1)}, u32[]{:S(2)}, u32[]{:S(2)}) collective-permute-start(bf16[1,1024,512]{2,1,0:T(8,128)(2,1)} %bitcast.45), channel_id=1, source_target_pairs={{0,1},{1,0},{2,3},{3,2},{4,5},{5,4},{6,7},{7,6},{8,9},{9,8},{10,11... | collective-permute-start | bytes 3145736 | tf_op jit(solution)/shard_map/ppermute | solution.py:19
  345.8 1.0 copy-start.5
Sparse Core Ops, SparseCore 0:
  397.1 29.4 all-reduce.1
where the time goes:
time: 445 us; the launch traced here: 439 us
  waiting for transfers between devices  207 us (47%)
  blocking collectives  80.3 us (18%)
  local copies, waits for them, and re-layouts  58.5 us (13%)
  starting transfers between devices  45.4 us (10%)
  matrix products  18.7 us (4%)
  between operations  14.6 us (3%)
  other arithmetic  13.9 us (3%)
    all_to_all x2, blocking collectives, on_device(): lax.all_to_all(back_send, 'row', split_axis=0, concat_axis=0, tiled=True)  80.3 us
    all_to_all x2, waiting for transfers between devices, on_device(): lax.all_to_all(left_send, 'row', split_axis=0, concat_axis=2, tiled=True)  50.3 us
    all_to_all x2, waiting for transfers between devices, on_device(): lax.all_to_all(right_send, 'row', split_axis=0, concat_axis=2, tiled=True)  46.3 us
    all_to_all x1, waiting for transfers between devices, on_device(): lax.all_to_all(columns, 'row', split_axis=1, concat_axis=0, tiled=True)  46.3 us
    ppermute x2, waiting for transfers between devices, from_partner(): return lax.ppermute(value, axis, pairs)  34.6 us
    psum x1, waiting for transfers between devices, on_device(): lax.psum(normed_final.astype(jnp.bfloat16), 'tmpl').astype(jnp.float32)  29.6 us
    all_to_all x1, starting transfers between devices, on_device(): lax.all_to_all(columns, 'row', split_axis=1, concat_axis=0, tiled=True)  16.6 us
    all_to_all x2, starting transfers between devices, on_device(): lax.all_to_all(right_send, 'row', split_axis=0, concat_axis=2, tiled=True)  15 us
  transfers between devices with their start and end apart: 8, of which 8 were waited for; matrix products, arithmetic and copies ran while one was open for 3% of the time, Pallas kernels for 0%

commit v1 on v0

v1 whole, which is shorter than its diff:
```python
import jax
import jax.numpy as jnp
from jax import lax
from jax.experimental import pallas as pl
from jax.experimental.pallas import tpu as pltpu
from jax.sharding import PartitionSpec as P

CH = 64
CZ = 128
CROP = 1024
TILE = 128
NLAYER = 2
FULL = 2048
ROWS = 8
EPSILON = 1e-05
BF = jnp.bfloat16
F32 = jnp.float32

PLANE = [[s * 8 + z for s in range(16)] for z in range(8)]
SAME_X0 = [
    [(x1 * 2 + x0) * 32 + y * 8 + z for x1 in range(2) for y in range(4) for z in range(8)]
    for x0 in range(2)
]
BY_Z = [[s * 8 + z for z in range(8) for s in range(16)]]
X0_PAIRS = [(r, r ^ 32) for r in range(128)]
CORES = [(0, 1), (1, 0)]
VMEM_LIMIT = 56 * 1024 * 1024


def iota(shape, dim):
    return lax.broadcasted_iota(jnp.int32, shape, dim)


def onehot(mask):
    return jnp.where(mask, 1.0, 0.0).astype(BF)


def dot(a, b):
    return jnp.dot(a, b, preferred_element_type=F32)


def dot_nt(a, b):
    return lax.dot_general(a, b, (((1,), (1,)), ((), ())), preferred_element_type=F32)


def dot_tn(a, b):
    return lax.dot_general(a, b, (((0,), (0,)), ((), ())), preferred_element_type=F32)


def lane_token(lane):
    return (
        (lane % 8) * 128
        + ((lane // 8) % 8) * 16
        + ((lane // 256) % 2) * 8
        + (lane // 512) * 4
        + ((lane // 64) % 4)
    )


def weights_kernel(proj_ref, out_ref, final_ref, wp_ref, wo_ref, wf_ref, prow_ref, q_ref, pj_ref, sel_ref):
    core = lax.axis_index("tmpl")
    spread = onehot(iota((CH, 512), 0) == iota((CH, 512), 1) // 8)
    repeat = onehot(iota((512, CH), 0) // 8 == iota((512, CH), 1))
    diag = iota((512, 512), 0) % 8 == iota((512, 512), 1) % 8
    for layer in range(NLAYER):
        for group in range(5):
            w = proj_ref[layer, :, group * CH : (group + 1) * CH]
            wide = dot_tn(w, spread).astype(BF)
            big = dot(repeat, wide)
            wp_ref[layer, group * 512 : (group + 1) * 512, :] = jnp.where(diag, big, 0.0).astype(BF)
        wide = dot_tn(out_ref[layer], spread).astype(BF)
        wo_ref[layer] = jnp.where(diag, dot(repeat, wide), 0.0).astype(BF)
    down = onehot(iota((512, CZ), 0) % CZ == iota((512, CZ), 1))
    across = onehot(iota((CH, 256), 0) == iota((CH, 256), 1) % CH)
    tall = dot_nt(down, final_ref[...]).astype(BF)
    block = iota((512, 256), 0) // CZ == iota((512, 256), 1) // CH
    wf_ref[...] = jnp.where(block, dot(tall, across), 0.0).astype(BF)
    r0, c0 = iota((512, 512), 0), iota((512, 512), 1)
    prow_ref[...] = onehot((r0 // 8 == c0 % CH) & (r0 % 8 == c0 // CH))
    half = (r0 // 256) ^ core
    sel_ref[...] = onehot((r0 % CH == c0 // 8) & (half * 4 + (r0 // CH) % 4 == c0 % 8))
    r1, c1 = iota((CROP, CROP), 0), iota((CROP, CROP), 1)
    token = lane_token(c1)
    q_ref[...] = onehot(r1 == token)
    dest = r1 // 8
    pj_ref[...] = onehot(((dest % 16) * 8 + dest // 16) * 8 + r1 % 8 == token)


def make_weights(proj_weight, out_weight, final_weight):
    shapes = [
        (NLAYER, 2560, 512), (NLAYER, 512, 512), (512, 256), (512, 512),
        (CROP, CROP), (CROP, CROP), (512, 512),
    ]
    return pl.pallas_call(
        weights_kernel,
        out_shape=[jax.ShapeDtypeStruct(shape, BF) for shape in shapes],
        compiler_params=pltpu.CompilerParams(vmem_limit_bytes=VMEM_LIMIT),
        cost_estimate=pl.CostEstimate(flops=2 * 10**9, bytes_accessed=12 * 2**20, transcendentals=0),
        name="weights",
    )(proj_weight, out_weight, final_weight)


def crop_kernel(crop_ref, x_ref, o_ref):
    del crop_ref
    o_ref[...] = x_ref[...]


def crop_columns(crop_tiles, pair):
    return pl.pallas_call(
        crop_kernel,
        grid_spec=pltpu.PrefetchScalarGridSpec(
            num_scalar_prefetch=1,
            grid=(8,),
            in_specs=[pl.BlockSpec((16, CH, TILE), lambda a, crop: (0, 0, crop[0, a]))],
            out_specs=pl.BlockSpec((16, CH, TILE), lambda a, crop: (0, 0, a)),
        ),
        out_shape=jax.ShapeDtypeStruct((16, CH, CROP), BF),
        name="crop",
    )(crop_tiles, pair)


def norm_channels(values):
    rows, lanes = values.shape
    cube = values.reshape(CH, ROWS, lanes)
    center = cube - (jnp.sum(cube, axis=0, keepdims=True) * (1.0 / CH))
    spread = jnp.sum(center * center, axis=0, keepdims=True) * (1.0 / CH)
    return (center * lax.rsqrt(spread + EPSILON)).reshape(rows, lanes)


def sigmoid(values):
    return 0.5 * jnp.tanh(0.5 * values) + 0.5


def pair_mask(crop_ref, length_ref, lanes, start):
    chip = lax.axis_index("row")
    inside = (chip % 8) * 16 + chip // 8
    length = length_ref[0]
    lane = iota((ROWS, lanes), 1) + start
    row = iota((ROWS, lanes), 0)
    token = lane_token(lane)
    col_pos = jnp.zeros((ROWS, lanes), jnp.int32)
    row_pos = jnp.zeros((ROWS, lanes), jnp.int32)
    for a in range(8):
        base = crop_ref[0, a] * TILE
        col_pos = jnp.where(lane % 8 == a, base, col_pos)
        row_pos = jnp.where(row == a, base, row_pos)
    col_pos = col_pos + token % TILE
    row_pos = row_pos + inside
    return jnp.where((col_pos < length) & (row_pos < length), 1.0, 0.0)


def project(current, wp, mask, left_ref, right_ref, gate_ref):
    lanes = current.shape[1]
    normed = norm_channels(current).astype(BF)
    wide = jnp.broadcast_to(mask[None], (CH, ROWS, lanes)).reshape(512, lanes)
    gate_a = dot(wp[0:512], normed)
    value_a = dot(wp[512:1024], normed)
    left_ref[...] = (sigmoid(gate_a) * value_a * wide).astype(BF)
    gate_b = dot(wp[1024:1536], normed)
    value_b = dot(wp[1536:2048], normed)
    right_ref[...] = (sigmoid(gate_b) * value_b * wide).astype(BF)
    gate_ref[...] = sigmoid(dot(wp[2048:2560], normed))


BLOCK = 256
STEPS = CROP // BLOCK


def first_kernel(crop_ref, length_ref, got_ref, prow_ref, q_ref, wp_ref, cur_ref, left_ref, right_ref, gate_ref, rows_ref):
    step = pl.program_id(0)

    @pl.when(step == 0)
    def _():
        parts = jnp.concatenate([got_ref[crop_ref[0, a]] for a in range(8)], axis=0)
        rows_ref[...] = dot(prow_ref[...], parts).astype(BF)

    current = dot(rows_ref[...], q_ref[...])
    cur_ref[...] = current.astype(BF)
    mask = pair_mask(crop_ref, length_ref, BLOCK, step * BLOCK)
    project(current, wp_ref[0], mask, left_ref, right_ref, gate_ref)


def full(shape):
    return pl.BlockSpec(shape, lambda step, crop, length: (0,) * len(shape), pipeline_mode=pl.Buffered(1))


def lanes_of(rows):
    return pl.BlockSpec((rows, BLOCK), lambda step, crop, length: (0, step))


def layer_weight(rows, layer):
    return pl.BlockSpec((1, rows, 512), lambda step, crop, length: (layer, 0, 0), pipeline_mode=pl.Buffered(1))


STATE = [
    jax.ShapeDtypeStruct((512, CROP), BF), jax.ShapeDtypeStruct((512, CROP), BF),
    jax.ShapeDtypeStruct((512, CROP), BF), jax.ShapeDtypeStruct((512, CROP), F32),
]


def first_projection(crop_tiles, full_length, got, prow, q, wp):
    return pl.pallas_call(
        first_kernel,
        grid_spec=pltpu.PrefetchScalarGridSpec(
            num_scalar_prefetch=2,
            grid=(STEPS,),
            in_specs=[full((16, CH, CROP)), full((512, 512)), lanes_of(CROP), layer_weight(2560, 0)],
            out_specs=[lanes_of(512)] * 4,
            scratch_shapes=[pltpu.VMEM((512, CROP), BF)],
        ),
        out_shape=STATE,
        compiler_params=pltpu.CompilerParams(vmem_limit_bytes=VMEM_LIMIT),
        name="first",
    )(crop_tiles, full_length, got, prow, q, wp)


def update(back_ref, cur_ref, gate_ref, wo):
    normed = norm_channels(back_ref[...].astype(F32)).astype(BF)
    change = dot(wo, normed)
    return (cur_ref[...].astype(F32) + gate_ref[...] * change).astype(BF)


def middle_kernel(crop_ref, length_ref, back_ref, cur_ref, gate_ref, wo_ref, wp_ref, next_ref, left_ref, right_ref, gate_out_ref):
    step = pl.program_id(0)
    current = update(back_ref, cur_ref, gate_ref, wo_ref[0])
    next_ref[...] = current
    mask = pair_mask(crop_ref, length_ref, BLOCK, step * BLOCK)
    project(current.astype(F32), wp_ref[0], mask, left_ref, right_ref, gate_out_ref)


def middle_layer(crop_tiles, full_length, back, current, gate, wo, wp, layer):
    return pl.pallas_call(
        middle_kernel,
        grid_spec=pltpu.PrefetchScalarGridSpec(
            num_scalar_prefetch=2,
            grid=(STEPS,),
            in_specs=[lanes_of(512)] * 3 + [layer_weight(512, layer), layer_weight(2560, layer + 1)],
            out_specs=[lanes_of(512)] * 4,
        ),
        out_shape=STATE,
        compiler_params=pltpu.CompilerParams(vmem_limit_bytes=VMEM_LIMIT),
        name="middle",
    )(crop_tiles, full_length, back, current, gate, wo, wp)


def last_kernel(back_ref, cur_ref, gate_ref, wo_ref, sel_ref, pj_ref, mine_ref, other_ref, total_ref):
    step = pl.program_id(0)
    current = update(back_ref, cur_ref, gate_ref, wo_ref[0])
    normed = norm_channels(current.astype(F32)).astype(BF)
    chosen = dot(sel_ref[...], normed).astype(BF)
    part = dot_nt(pj_ref[...], chosen)

    @pl.when(step == 0)
    def _():
        total_ref[...] = part

    @pl.when(step > 0)
    def _():
        total_ref[...] += part

    @pl.when(step == STEPS - 1)
    def _():
        mine_ref[...] = total_ref[:, :256].astype(BF)
        other_ref[...] = total_ref[:, 256:].astype(BF)


def last_layer(back, current, gate, wo, sel, pj, layer):
    lanes = pl.BlockSpec((512, BLOCK), lambda step: (0, step))
    half = pl.BlockSpec((CROP, 256), lambda step: (0, 0))
    return pl.pallas_call(
        last_kernel,
        grid=(STEPS,),
        in_specs=[lanes] * 3
        + [
            pl.BlockSpec((1, 512, 512), lambda step: (layer, 0, 0)),
            pl.BlockSpec((512, 512), lambda step: (0, 0)),
            pl.BlockSpec((CROP, BLOCK), lambda step: (0, step)),
        ],
        out_specs=[half, half],
        out_shape=[jax.ShapeDtypeStruct((CROP, 256), BF)] * 2,
        scratch_shapes=[pltpu.VMEM((CROP, 512), F32)],
        compiler_params=pltpu.CompilerParams(vmem_limit_bytes=VMEM_LIMIT),
        name="last",
    )(back, current, gate, wo, sel, pj)


def products_kernel(left_ref, own_ref, peer_ref, out_ref):
    x0 = (lax.axis_index("row") // 32) % 2
    left = left_ref[...]
    own = pl.multiple_of(x0 * 512, 512)
    peer = pl.multiple_of(512 - x0 * 512, 512)
    out_ref[:, pl.ds(own, 512)] = dot_nt(left, own_ref[...]).astype(BF)
    out_ref[:, pl.ds(peer, 512)] = dot_nt(left, peer_ref[...]).astype(BF)


def triangle_products(left, own, peer):
    return pl.pallas_call(
        products_kernel,
        out_shape=jax.ShapeDtypeStruct((512, CROP), BF),
        compiler_params=pltpu.CompilerParams(vmem_limit_bytes=VMEM_LIMIT),
        name="products",
    )(left, own, peer)


def hidden_kernel(mine_ref, peer_ref, out_ref):
    total = mine_ref[...].astype(F32) + peer_ref[...].astype(F32)
    out_ref[...] = jnp.maximum(total * 0.5, 0.0).astype(BF)


def hidden_features(mine, peer):
    return pl.pallas_call(
        hidden_kernel, out_shape=jax.ShapeDtypeStruct((CROP, 256), BF), name="hidden"
    )(mine, peer)


def final_kernel(mine_ref, peer_ref, wf_ref, out_ref, tall0_ref, tall1_ref, wide_ref):
    core = lax.axis_index("tmpl")
    wf = wf_ref[...]
    for source, ref in enumerate((mine_ref, peer_ref)):
        half = core if source == 0 else 1 - core
        tall0_ref[...] = ref[:, :128].astype(F32)
        tall1_ref[...] = ref[:, 128:].astype(F32)
        for j in range(8):
            rows = jnp.concatenate(
                [tall0_ref[pl.ds(j, 128, stride=8), :], tall1_ref[pl.ds(j, 128, stride=8), :]], axis=1
            ).astype(BF)
            result = dot_nt(wf, rows)
            for a in range(4):
                wide_ref[half * 4 + a, pl.ds(j, CZ, stride=8), :] = result[a * CZ : (a + 1) * CZ]
    for a in range(8):
        out_ref[:, a * TILE : (a + 1) * TILE] = wide_ref[a].astype(BF)


def final_projection(mine, peer, wf):
    return pl.pallas_call(
        final_kernel,
        out_shape=jax.ShapeDtypeStruct((CZ * 8, CROP), BF),
        scratch_shapes=[
            pltpu.VMEM((CROP, 128), F32), pltpu.VMEM((CROP, 128), F32), pltpu.VMEM((8, CZ * 8, TILE), F32)
        ],
        compiler_params=pltpu.CompilerParams(vmem_limit_bytes=VMEM_LIMIT),
        name="final",
    )(mine, peer, wf)


def exchange(values, groups, count):
    cube = values.reshape(count, -1, values.shape[-1])
    moved = lax.all_to_all(cube, "row", 0, 0, axis_index_groups=groups, tiled=True)
    return moved.reshape(values.shape)


def on_device(pair_maps, crop_tiles, full_length, proj_weight, out_weight, final_weight):
    wp, wo, wf, prow, q, pj, sel = make_weights(proj_weight, out_weight, final_weight)
    pair = jnp.transpose(pair_maps[0], (0, 2, 1))
    cropped = crop_columns(crop_tiles, pair)
    got = lax.all_to_all(cropped, "row", 0, 0, axis_index_groups=PLANE, tiled=True)
    current, left, right, gate = first_projection(crop_tiles, full_length, got, prow, q, wp)
    for layer in range(NLAYER):
        right_own = exchange(right, SAME_X0, CH)
        left_own = exchange(left, SAME_X0, CH)
        right_peer = lax.ppermute(right_own, "row", X0_PAIRS)
        products = triangle_products(left_own, right_own, right_peer)
        back = exchange(products, SAME_X0, CH)
        if layer + 1 < NLAYER:
            current, left, right, gate = middle_layer(
                crop_tiles, full_length, back, current, gate, wo, wp, layer
            )
    mine, other = last_layer(back, current, gate, wo, sel, pj, NLAYER - 1)
    hidden = hidden_features(mine, lax.ppermute(other, "tmpl", CORES))
    moved = exchange(hidden, BY_Z, 128)
    result = final_projection(moved, lax.ppermute(moved, "tmpl", CORES), wf)
    return result.reshape(CZ, 8, CROP)


def solution(mesh):
    placed = (P("tmpl", "row", None, None), P("tmpl", None), P(), P(), P(), P())
    return jax.shard_map(
        on_device, mesh=mesh, in_specs=placed, out_specs=P(None, "row", None), check_vma=False
    )
```

time: 445 us -> 363 us (0.82); the launches traced: 439 us -> 362 us
  waiting for transfers between devices: 207 us -> 88.4 us
  blocking collectives: 80.3 us -> 173 us
  Pallas kernels: 0 us -> 62.4 us
  local copies, waits for them, and re-layouts: 58.5 us -> 4.88 us
  matrix products: 18.7 us -> 0 us
  other arithmetic: 13.9 us -> 0 us
  between operations: 14.6 us -> 0.7 us
  starting transfers between devices: 45.4 us -> 32.3 us
    all_to_all x2 -> x5, blocking collectives: 80.3 us -> 173 us  [exchange(): lax.all_to_all(cube, 'row', 0, 0, axis_index_groups=groups, tiled=True)]
    all_to_all x5 -> x3, waiting for transfers between devices: 143 us -> 67.1 us  [the longest x2 48.9 us: exchange(): lax.all_to_all(cube, 'row', 0, 0, axis_index_groups=groups, tiled=True)]
    pallas_call x0 -> x9, Pallas kernels: none -> 62.4 us  [the longest x1 11.6 us: first_projection(): pl.pallas_call(first_kernel, grid_spec=pltpu.PrefetchScalarGridSpec(num_s...]
    psum x1 -> x0, waiting for transfers between devices: 29.6 us -> none  [on_device(): lax.psum(normed_final.astype(jnp.bfloat16), 'tmpl').astype(jnp.float32)]
    all_to_all x5 -> x3, starting transfers between devices: 44 us -> 24.2 us  [the longest x2 16.6 us: exchange(): lax.all_to_all(cube, 'row', 0, 0, axis_index_groups=groups, tiled=True)]
    dot_general x7 -> x0, matrix products: 18.7 us -> none  [the longest x2 8 us: on_device(): jnp.einsum('cki,ckj->cij', left_got[0], right_whole, preferred_element_ty...]
    ppermute x2 -> x4, waiting for transfers between devices: 34.6 us -> 21.3 us  [the longest x2 18 us: on_device(): right_peer = lax.ppermute(right_own, 'row', X0_PAIRS)]
    convert_element_type x9 -> x0, local copies, waits for them, and re-layouts: 12.2 us -> none  [the longest x4 3.93 us: on_device(): normed_out = channel_norm(merged.astype(jnp.float32)).astype(jnp.bfloat16)]
  transfers between devices with their start and end apart: 8 -> 7, of which waited for: 8 -> 7; matrix products, arithmetic and copies ran while one was open for 3% -> 0% of each run, Pallas kernels for 0% -> 2%
where the time goes in v1:
time: 363 us; the launch traced here: 362 us
  blocking collectives  173 us (48%)
  waiting for transfers between devices  88.4 us (24%)
  Pallas kernels  62.4 us (17%)
  starting transfers between devices  32.3 us (9%)
  local copies, waits for them, and re-layouts  4.88 us (1%)
    all_to_all x5, blocking collectives, exchange(): lax.all_to_all(cube, 'row', 0, 0, axis_index_groups=groups, tiled=True)  173 us
    all_to_all x2, waiting for transfers between devices, exchange(): lax.all_to_all(cube, 'row', 0, 0, axis_index_groups=groups, tiled=True)  48.9 us
    all_to_all x1, waiting for transfers between devices, on_device(): lax.all_to_all(cropped, 'row', 0, 0, axis_index_groups=PLANE, tiled=True)  18.2 us
    ppermute x2, waiting for transfers between devices, on_device(): right_peer = lax.ppermute(right_own, 'row', X0_PAIRS)  18 us
    all_to_all x2, starting transfers between devices, exchange(): lax.all_to_all(cube, 'row', 0, 0, axis_index_groups=groups, tiled=True)  16.6 us
    pallas_call x1, Pallas kernels, first_projection(): pl.pallas_call(first_kernel, grid_spec=pltpu.PrefetchScalarGridSpec(num_s...  11.6 us
    pallas_call x1, Pallas kernels, middle_layer(): pl.pallas_call(middle_kernel, grid_spec=pltpu.PrefetchScalarGridSpec(num_...  10.7 us
    pallas_call x1, Pallas kernels, last_layer(): pl.pallas_call(last_kernel, grid=(STEPS,), in_specs=[lanes] * 3 + [pl.Blo...  9.89 us
  transfers between devices with their start and end apart: 7, of which 7 were waited for; matrix products, arithmetic and copies ran while one was open for 0% of the time, Pallas kernels for 2%

profile of v1, /device:TPU:1, one launch (start us, length us, event | category | flops | bytes accessed | tf_op | source)
XLA Modules:
  0.0 362.1 jit_solution(9203615597546720303)
XLA Ops:
  0.0 6.3 %crop.1 = bf16[16,64,1024]{2,1,0:T(8,128)(2,1)} custom-call(s32[1,8]{1,0:T(1,128)} %crop_ref.5, bf16[16,64,2048]{2,1,0:T(8,128)(2,1)} %bitcast.19), custom_call_target="tpu_custom_call" | custom-call | tf_op jit(solution)/shard_map/crop/pallas_call | solution.py:109
  6.3 7.6 %all-to-all-start = ((bf16[16,64,1024]{2,1,0:T(8,128)(2,1)}), bf16[16,64,1024]{2,1,0:T(8,128)(2,1)S(1)}, u32[]{:S(2)}, u32[]{:S(2)}) async-start(bf16[16,64,1024]{2,1,0:T(8,128)(2,1)} %crop.1), calls=%async_computation | async-start | bytes 4194304 | tf_op jit(solution)/shard_map/all_to_all | solution.py:356
  14.6 9.0 %weights.1 = (bf16[2,2560,512]{2,1,0:T(8,128)(2,1)}, bf16[2,512,512]{2,1,0:T(8,128)(2,1)}, bf16[512,256]{1,0:T(8,128)(2,1)}, bf16[512,512]{1,0:T(8,128)(2,1)}, b...) custom-call(bf16[2,64,320]{2,1,0:T(8,128)(2,1)} %proj_ref.1, ...), custom_call_target="tpu_custom_call" | custom-call | flops 2000000000 | bytes 12582912 | tf_op jit(solution)/shard_map/weights/pallas_call | solution.py:94
  23.6 18.2 %all-to-all-done.got_ref = bf16[16,64,1024]{2,1,0:T(8,128)(2,1)S(1)} async-done(((bf16[16,64,1024]{2,1,0:T(8,128)(2,1)}), bf16[16,64,1024]{2,1,0:T(8,128)(2,1)S(1)}, u32[]{:S(2)}, u32[]{:S(2)}) %all-to-all-start) | async-done | bytes 2097184 | tf_op jit(solution)/shard_map/all_to_all | solution.py:356
  43.1 11.6 %first.1 = (bf16[512,1024]{1,0:T(8,128)(2,1)}, bf16[512,1024]{1,0:T(8,128)(2,1)}, bf16[512,1024]{1,0:T(8,128)(2,1)}, f32[512,1024]{1,0:T(8,128)}) custom-call(s32[1,8]{1,0:T(1,128)} %crop_ref.5, s32[1]{0:T(128)S(6)} %copy.7.length_ref, bf16[16,64,1024]{2,1,0:T(8,128)(2,1)} %copy-done, bf16[512,512]{1,0:T(8,128)(2,1)} %get-tuple-element.22.prow_ref, ...), custom_call_target="tpu_custom_call" | custom-call | tf_op jit(solution)/shard_map/first/pallas_call | solution.py:202
  54.7 37.0 %all_to_all.40 = bf16[64,8,1024]{2,1,0:T(8,128)(2,1)S(1)} all-to-all(bf16[64,8,1024]{2,1,0:T(8,128)(2,1)} %bitcast.33), channel_id=1, replica_groups={{0,1,2,3,4,5,6,7,8,9,10,11,12,13,14,15,16,17,18,19,20,21,22,23,24,25,26..., dimensions={0} | all-to-all | bytes 2097152 | tf_op jit(solution)/shard_map/all_to_all | solution.py:348
  91.7 8.3 %all-to-all-start.1 = ((bf16[64,8,1024]{2,1,0:T(8,128)(2,1)}), bf16[64,8,1024]{2,1,0:T(8,128)(2,1)S(1)}, u32[]{:S(2)}, u32[]{:S(2)}) async-start(bf16[64,8,1024]{2,1,0:T(8,128)(2,1)} %bitcast.2), calls=%async_computation.1 | async-start | bytes 2097152 | tf_op jit(solution)/shard_map/all_to_all | solution.py:348
  100.2 24.3 %all-to-all-done.1 = bf16[64,8,1024]{2,1,0:T(8,128)(2,1)S(1)} async-done(((bf16[64,8,1024]{2,1,0:T(8,128)(2,1)}), bf16[64,8,1024]{2,1,0:T(8,128)(2,1)S(1)}, u32[]{:S(2)}, u32[]{:S(2)}) %all-to-all-start.1) | async-done | bytes 1048608 | tf_op jit(solution)/shard_map/all_to_all | solution.py:348
  124.5 9.3 %collective-permute-done.peer_ref = bf16[512,1024]{1,0:T(8,128)(2,1)S(1)} collective-permute-done((bf16[512,1024]{1,0:T(8,128)(2,1)S(1)}, bf16[512,1024]{1,0:T(8,128)(2,1)S(1)}, u32[]{:S(2)}, u32[]{:S(2)}) %collective-permute-start) | collective-permute-done | bytes 1048608 | tf_op jit(solution)/shard_map/ppermute | solution.py:361
  134.7 4.1 %products.2 = bf16[512,1024]{1,0:T(8,128)(2,1)} custom-call(bf16[512,1024]{1,0:T(8,128)(2,1)} %bitcast.24, bf16[512,1024]{1,0:T(8,128)(2,1)} %bitcast.21, bf16[512,1024]{1,0:T(8,128)(2,1)} %copy-done.6), custom_call_target="tpu_custom_call" | custom-call | tf_op jit(solution)/shard_map/products/pallas_call | solution.py:297
  138.9 38.4 %all_to_all.41 = bf16[64,8,1024]{2,1,0:T(8,128)(2,1)} all-to-all(bf16[64,8,1024]{2,1,0:T(8,128)(2,1)} %bitcast.26), channel_id=1, replica_groups={{0,1,2,3,4,5,6,7,8,9,10,11,12,13,14,15,16,17,18,19,20,21,22,23,24,25,26..., dimensions={0} | all-to-all | bytes 2097152 | tf_op jit(solution)/shard_map/all_to_all | solution.py:348
  177.3 10.7 %middle.1 = (bf16[512,1024]{1,0:T(8,128)(2,1)}, bf16[512,1024]{1,0:T(8,128)(2,1)}, bf16[512,1024]{1,0:T(8,128)(2,1)}, f32[512,1024]{1,0:T(8,128)}) custom-call(s32[1,8]{1,0:T(1,128)} %crop_ref.5, s32[1]{0:T(128)S(6)} %copy.7.length_ref, bf16[512,1024]{1,0:T(8,128)(2,1)} %bitcast.28, bf16[512,1024]{1,0:T(8,128)(2,1)} %get-tuple-element.27.cur_ref, ...), custom_call_target="tpu_custom_call" | custom-call | tf_op jit(solution)/shard_map/middle/pallas_call | solution.py:232
  188.0 33.7 %all_to_all.42 = bf16[64,8,1024]{2,1,0:T(8,128)(2,1)S(1)} all-to-all(bf16[64,8,1024]{2,1,0:T(8,128)(2,1)} %bitcast.32), channel_id=1, replica_groups={{0,1,2,3,4,5,6,7,8,9,10,11,12,13,14,15,16,17,18,19,20,21,22,23,24,25,26..., dimensions={0} | all-to-all | bytes 2097152 | tf_op jit(solution)/shard_map/all_to_all | solution.py:348
  221.6 8.3 %all-to-all-start.4 = ((bf16[64,8,1024]{2,1,0:T(8,128)(2,1)}), bf16[64,8,1024]{2,1,0:T(8,128)(2,1)S(1)}, u32[]{:S(2)}, u32[]{:S(2)}) async-start(bf16[64,8,1024]{2,1,0:T(8,128)(2,1)} %bitcast.8), calls=%async_computation.4 | async-start | bytes 2097152 | tf_op jit(solution)/shard_map/all_to_all | solution.py:348
  230.0 24.6 %all-to-all-done.4 = bf16[64,8,1024]{2,1,0:T(8,128)(2,1)S(1)} async-done(((bf16[64,8,1024]{2,1,0:T(8,128)(2,1)}), bf16[64,8,1024]{2,1,0:T(8,128)(2,1)S(1)}, u32[]{:S(2)}, u32[]{:S(2)}) %all-to-all-start.4) | async-done | bytes 1048608 | tf_op jit(solution)/shard_map/all_to_all | solution.py:348
  254.6 8.7 %collective-permute-done.1.peer_ref = bf16[512,1024]{1,0:T(8,128)(2,1)S(1)} collective-permute-done((bf16[512,1024]{1,0:T(8,128)(2,1)S(1)}, bf16[512,1024]{1,0:T(8,128)(2,1)S(1)}, u32[]{:S(2)}, u32[]{:S(2)}) %collective-permute-start.1) | collective-permute-done | bytes 1048608 | tf_op jit(solution)/shard_map/ppermute | solution.py:361
  264.3 4.2 %products.3 = bf16[512,1024]{1,0:T(8,128)(2,1)} custom-call(bf16[512,1024]{1,0:T(8,128)(2,1)} %bitcast.25, bf16[512,1024]{1,0:T(8,128)(2,1)} %bitcast.23, bf16[512,1024]{1,0:T(8,128)(2,1)} %copy-done.7), custom_call_target="tpu_custom_call" | custom-call | tf_op jit(solution)/shard_map/products/pallas_call | solution.py:297
  268.5 38.3 %all_to_all.43 = bf16[64,8,1024]{2,1,0:T(8,128)(2,1)} all-to-all(bf16[64,8,1024]{2,1,0:T(8,128)(2,1)} %bitcast.27), channel_id=1, replica_groups={{0,1,2,3,4,5,6,7,8,9,10,11,12,13,14,15,16,17,18,19,20,21,22,23,24,25,26..., dimensions={0} | all-to-all | bytes 2097152 | tf_op jit(solution)/shard_map/all_to_all | solution.py:348
  306.8 9.9 %last.1 = (bf16[1024,256]{1,0:T(8,128)(2,1)}, bf16[1024,256]{1,0:T(8,128)(2,1)}) custom-call(bf16[512,1024]{1,0:T(8,128)(2,1)} %bitcast.18, bf16[512,1024]{1,0:T(8,128)(2,1)} %get-tuple-element.32.cur_ref, f32[512,1024]{1,0:T(8,128)} %get-tuple-element.33.gate_ref, bf16[2,512,512]{2,1,0:T(8,128)(2,1)} %get-tuple-element.29.wo_ref, ...), custom_call_target="tpu_custom_call" | custom-call | tf_op jit(solution)/shard_map/last/pallas_call | solution.py:270
  316.7 5.0 %collective-permute-start.2 = (bf16[1024,256]{1,0:T(8,128)(2,1)}, bf16[1024,256]{1,0:T(8,128)(2,1)S(1)}, u32[]{:S(2)}, u32[]{:S(2)}) collective-permute-start(bf16[1024,256]{1,0:T(8,128)(2,1)} %get-tuple-element.37), channel_id=1, source_target_pairs={{0,128},{128,0},{1,129},{129,1},{2,130},{130,2},{3,131},{131,3},{4... | collective-permute-start | bytes 1572872 | tf_op jit(solution)/shard_map/ppermute | solution.py:369
  324.3 2.2 hidden.1
  326.5 26.1 %all_to_all.44 = bf16[128,8,256]{2,1,0:T(8,128)(2,1)S(1)} all-to-all(bf16[128,8,256]{2,1,0:T(8,128)(2,1)} %bitcast.29), channel_id=1, replica_groups={{0,8,16,24,32,40,48,56,64,72,80,88,96,104,112,120,1,9,17,25,33,41,49,57..., dimensions={0} | all-to-all | bytes 1048576 | tf_op jit(solution)/shard_map/all_to_all | solution.py:348
  352.6 2.8 collective-permute-start.3
  357.8 4.3 %final.1 = bf16[1024,1024]{1,0:T(8,128)(2,1)} custom-call(bf16[1024,256]{1,0:T(8,128)(2,1)} %bitcast.31, bf16[1024,256]{1,0:T(8,128)(2,1)} %copy-done.9, bf16[512,256]{1,0:T(8,128)(2,1)} %get-tuple-element.38.wf_ref), custom_call_target="tpu_custom_call" | custom-call | tf_op jit(solution)/shard_map/final/pallas_call | solution.py:335
  (24 shorter events, 8.5 us)
Async XLA Ops:
  6.3 35.5 %all-to-all-start = ((bf16[16,64,1024]{2,1,0:T(8,128)(2,1)}), bf16[16,64,1024]{2,1,0:T(8,128)(2,1)S(1)}, u32[]{:S(2)}, u32[]{:S(2)}) async-start(bf16[16,64,1024]{2,1,0:T(8,128)(2,1)} %crop.1), calls=%async_computation | async-start | bytes 4194304 | tf_op jit(solution)/shard_map/all_to_all | solution.py:356
  41.8 1.3 copy-start
  91.7 42.1 %copy-start.1 = (bf16[64,8,1024]{2,1,0:T(8,128)(2,1)}, bf16[64,8,1024]{2,1,0:T(8,128)(2,1)S(1)}, u32[]{:S(2)}) copy-start(bf16[64,8,1024]{2,1,0:T(8,128)(2,1)S(1)} %all_to_all.40) | copy-start | bytes 3145732
  91.7 32.8 %all-to-all-start.1 = ((bf16[64,8,1024]{2,1,0:T(8,128)(2,1)}), bf16[64,8,1024]{2,1,0:T(8,128)(2,1)S(1)}, u32[]{:S(2)}, u32[]{:S(2)}) async-start(bf16[64,8,1024]{2,1,0:T(8,128)(2,1)} %bitcast.2), calls=%async_computation.1 | async-start | bytes 2097152 | tf_op jit(solution)/shard_map/all_to_all | solution.py:348
  100.0 33.8 %collective-permute-start = (bf16[512,1024]{1,0:T(8,128)(2,1)S(1)}, bf16[512,1024]{1,0:T(8,128)(2,1)S(1)}, u32[]{:S(2)}, u32[]{:S(2)}) collective-permute-start(bf16[512,1024]{1,0:T(8,128)(2,1)S(1)} %bitcast.20), channel_id=1, source_target_pairs={{0,32},{1,33},{2,34},{3,35},{4,36},{5,37},{6,38},{7,39},{8,40},{9,... | collective-permute-start | bytes 3145736 | tf_op jit(solution)/shard_map/ppermute | solution.py:361
  124.5 9.3 %copy-start.3 = (bf16[64,8,1024]{2,1,0:T(8,128)(2,1)}, bf16[64,8,1024]{2,1,0:T(8,128)(2,1)S(1)}, u32[]{:S(2)}) copy-start(bf16[64,8,1024]{2,1,0:T(8,128)(2,1)S(1)} %all-to-all-done.1) | copy-start | bytes 3145732
  133.8 1.0 copy-start.6
  221.6 41.7 %copy-start.2 = (bf16[64,8,1024]{2,1,0:T(8,128)(2,1)}, bf16[64,8,1024]{2,1,0:T(8,128)(2,1)S(1)}, u32[]{:S(2)}) copy-start(bf16[64,8,1024]{2,1,0:T(8,128)(2,1)S(1)} %all_to_all.42) | copy-start | bytes 3145732
  221.6 33.0 %all-to-all-start.4 = ((bf16[64,8,1024]{2,1,0:T(8,128)(2,1)}), bf16[64,8,1024]{2,1,0:T(8,128)(2,1)S(1)}, u32[]{:S(2)}, u32[]{:S(2)}) async-start(bf16[64,8,1024]{2,1,0:T(8,128)(2,1)} %bitcast.8), calls=%async_computation.4 | async-start | bytes 2097152 | tf_op jit(solution)/shard_map/all_to_all | solution.py:348
  229.9 33.4 %collective-permute-start.1 = (bf16[512,1024]{1,0:T(8,128)(2,1)S(1)}, bf16[512,1024]{1,0:T(8,128)(2,1)S(1)}, u32[]{:S(2)}, u32[]{:S(2)}) collective-permute-start(bf16[512,1024]{1,0:T(8,128)(2,1)S(1)} %bitcast.22), channel_id=1, source_target_pairs={{0,32},{1,33},{2,34},{3,35},{4,36},{5,37},{6,38},{7,39},{8,40},{9,... | collective-permute-start | bytes 3145736 | tf_op jit(solution)/shard_map/ppermute | solution.py:361
  254.6 8.7 %copy-start.4 = (bf16[64,8,1024]{2,1,0:T(8,128)(2,1)}, bf16[64,8,1024]{2,1,0:T(8,128)(2,1)S(1)}, u32[]{:S(2)}) copy-start(bf16[64,8,1024]{2,1,0:T(8,128)(2,1)S(1)} %all-to-all-done.4) | copy-start | bytes 3145732
  263.3 1.0 copy-start.7
  316.7 6.8 %collective-permute-start.2 = (bf16[1024,256]{1,0:T(8,128)(2,1)}, bf16[1024,256]{1,0:T(8,128)(2,1)S(1)}, u32[]{:S(2)}, u32[]{:S(2)}) collective-permute-start(bf16[1024,256]{1,0:T(8,128)(2,1)} %get-tuple-element.37), channel_id=1, source_target_pairs={{0,128},{128,0},{1,129},{129,1},{2,130},{130,2},{3,131},{131,3},{4... | collective-permute-start | bytes 1572872 | tf_op jit(solution)/shard_map/ppermute | solution.py:369
  323.5 0.8 copy-start.8
  352.6 4.3 %copy-start.5 = (bf16[128,8,256]{2,1,0:T(8,128)(2,1)}, bf16[128,8,256]{2,1,0:T(8,128)(2,1)S(1)}, u32[]{:S(2)}) copy-start(bf16[128,8,256]{2,1,0:T(8,128)(2,1)S(1)} %all_to_all.44) | copy-start | bytes 1572868
  352.6 4.3 %collective-permute-start.3 = (bf16[1024,256]{1,0:T(8,128)(2,1)S(1)}, bf16[1024,256]{1,0:T(8,128)(2,1)S(1)}, u32[]{:S(2)}, u32[]{:S(2)}) collective-permute-start(bf16[1024,256]{1,0:T(8,128)(2,1)S(1)} %bitcast.30), channel_id=1, source_target_pairs={{0,128},{128,0},{1,129},{129,1},{2,130},{130,2},{3,131},{131,3},{4... | collective-permute-start | bytes 1572872 | tf_op jit(solution)/shard_map/ppermute | solution.py:371
  357.0 0.8 copy-start.9

commit v2 on v1

--- a/solution.py
+++ b/solution.py
@@ -1,3 +1,5 @@
+import functools
+
 import jax
 import jax.numpy as jnp
 from jax import lax
@@ -48,11 +50,12 @@
 
 
 def lane_token(lane):
+    x0 = (lax.axis_index("row") // 32) % 2
     return (
         (lane % 8) * 128
         + ((lane // 8) % 8) * 16
         + ((lane // 256) % 2) * 8
-        + (lane // 512) * 4
+        + ((lane // 512) ^ x0) * 4
         + ((lane // 64) % 4)
     )
 
@@ -101,8 +104,9 @@
 
 
 def crop_kernel(crop_ref, x_ref, o_ref):
-    del crop_ref
-    o_ref[...] = x_ref[...]
+    for a in range(8):
+        start = pl.multiple_of(crop_ref[0, a] * TILE, TILE)
+        o_ref[:, :, a * TILE : (a + 1) * TILE] = x_ref[:, :, pl.ds(start, TILE)]
 
 
 def crop_columns(crop_tiles, pair):
@@ -111,8 +115,8 @@
         grid_spec=pltpu.PrefetchScalarGridSpec(
             num_scalar_prefetch=1,
             grid=(8,),
-            in_specs=[pl.BlockSpec((16, CH, TILE), lambda a, crop: (0, 0, crop[0, a]))],
-            out_specs=pl.BlockSpec((16, CH, TILE), lambda a, crop: (0, 0, a)),
+            in_specs=[pl.BlockSpec((2, CH, FULL), lambda m, crop: (m, 0, 0))],
+            out_specs=pl.BlockSpec((2, CH, CROP), lambda m, crop: (m, 0, 0)),
         ),
         out_shape=jax.ShapeDtypeStruct((16, CH, CROP), BF),
         name="crop",
@@ -149,24 +153,26 @@
     return jnp.where((col_pos < length) & (row_pos < length), 1.0, 0.0)
 
 
-def project(current, wp, mask, left_ref, right_ref, gate_ref):
+def project(current, wp, mask, both_ref, gate_ref):
     lanes = current.shape[1]
     normed = norm_channels(current).astype(BF)
     wide = jnp.broadcast_to(mask[None], (CH, ROWS, lanes)).reshape(512, lanes)
     gate_a = dot(wp[0:512], normed)
     value_a = dot(wp[512:1024], normed)
-    left_ref[...] = (sigmoid(gate_a) * value_a * wide).astype(BF)
+    both_ref[:, :lanes] = (sigmoid(gate_a) * value_a * wide).astype(BF)
     gate_b = dot(wp[1024:1536], normed)
     value_b = dot(wp[1536:2048], normed)
-    right_ref[...] = (sigmoid(gate_b) * value_b * wide).astype(BF)
+    both_ref[:, lanes:] = (sigmoid(gate_b) * value_b * wide).astype(BF)
     gate_ref[...] = sigmoid(dot(wp[2048:2560], normed))
 
 
 BLOCK = 256
 STEPS = CROP // BLOCK
-
-
-def first_kernel(crop_ref, length_ref, got_ref, prow_ref, q_ref, wp_ref, cur_ref, left_ref, right_ref, gate_ref, rows_ref):
+HALF_STEPS = STEPS // 2
+BOTH = jax.ShapeDtypeStruct((512, 2 * CROP), BF)
+
+
+def first_kernel(crop_ref, length_ref, got_ref, prow_ref, q_ref, wp_ref, cur_ref, both_ref, gate_ref, rows_ref):
     step = pl.program_id(0)
 
     @pl.when(step == 0)
@@ -177,25 +183,19 @@
     current = dot(rows_ref[...], q_ref[...])
     cur_ref[...] = current.astype(BF)
     mask = pair_mask(crop_ref, length_ref, BLOCK, step * BLOCK)
-    project(current, wp_ref[0], mask, left_ref, right_ref, gate_ref)
+    project(current, wp_ref[0], mask, both_ref, gate_ref)
 
 
 def full(shape):
-    return pl.BlockSpec(shape, lambda step, crop, length: (0,) * len(shape), pipeline_mode=pl.Buffered(1))
-
-
-def lanes_of(rows):
-    return pl.BlockSpec((rows, BLOCK), lambda step, crop, length: (0, step))
+    return pl.BlockSpec(shape, lambda step, *_: (0,) * len(shape), pipeline_mode=pl.Buffered(1))
+
+
+def lanes_of(rows, lanes=BLOCK, offset=0):
+    return pl.BlockSpec((rows, lanes), lambda step, *_: (0, step + offset))
 
 
 def layer_weight(rows, layer):
-    return pl.BlockSpec((1, rows, 512), lambda step, crop, length: (layer, 0, 0), pipeline_mode=pl.Buffered(1))
-
-
-STATE = [
-    jax.ShapeDtypeStruct((512, CROP), BF), jax.ShapeDtypeStruct((512, CROP), BF),
-    jax.ShapeDtypeStruct((512, CROP), BF), jax.ShapeDtypeStruct((512, CROP), F32),
-]
+    return pl.BlockSpec((1, rows, 512), lambda step, *_: (layer, 0, 0), pipeline_mode=pl.Buffered(1))
 
 
 def first_projection(crop_tiles, full_length, got, prow, q, wp):
@@ -205,10 +205,10 @@
             num_scalar_prefetch=2,
             grid=(STEPS,),
             in_specs=[full((16, CH, CROP)), full((512, 512)), lanes_of(CROP), layer_weight(2560, 0)],
-            out_specs=[lanes_of(512)] * 4,
+            out_specs=[lanes_of(512), lanes_of(512, 2 * BLOCK), lanes_of(512)],
             scratch_shapes=[pltpu.VMEM((512, CROP), BF)],
         ),
-        out_shape=STATE,
+        out_shape=[jax.ShapeDtypeStruct((512, CROP), BF), BOTH, jax.ShapeDtypeStruct((512, CROP), F32)],
         compiler_params=pltpu.CompilerParams(vmem_limit_bytes=VMEM_LIMIT),
         name="first",
     )(crop_tiles, full_length, got, prow, q, wp)
@@ -220,86 +220,119 @@
     return (cur_ref[...].astype(F32) + gate_ref[...] * change).astype(BF)
 
 
-def middle_kernel(crop_ref, length_ref, back_ref, cur_ref, gate_ref, wo_ref, wp_ref, next_ref, left_ref, right_ref, gate_out_ref):
-    step = pl.program_id(0)
+def middle_kernel(half, *refs):
+    crop_ref, length_ref, back_ref, cur_ref, gate_ref, wo_ref, wp_ref = refs[:7]
+    next_ref, both_ref, gate_out_ref = refs[-3:]
     current = update(back_ref, cur_ref, gate_ref, wo_ref[0])
     next_ref[...] = current
-    mask = pair_mask(crop_ref, length_ref, BLOCK, step * BLOCK)
-    project(current.astype(F32), wp_ref[0], mask, left_ref, right_ref, gate_out_ref)
-
-
-def middle_layer(crop_tiles, full_length, back, current, gate, wo, wp, layer):
-    return pl.pallas_call(
-        middle_kernel,
+    start = half * 512 + pl.program_id(0) * BLOCK
+    mask = pair_mask(crop_ref, length_ref, BLOCK, start)
+    project(current.astype(F32), wp_ref[0], mask, both_ref, gate_out_ref)
+
+
+def middle_half(half, crop_tiles, full_length, back, current, gate, wo, wp, layer, both):
+    offset = half * HALF_STEPS
+    aliased = [] if both is None else [both]
+    return pl.pallas_call(
+        functools.partial(middle_kernel, half),
         grid_spec=pltpu.PrefetchScalarGridSpec(
             num_scalar_prefetch=2,
-            grid=(STEPS,),
-            in_specs=[lanes_of(512)] * 3 + [layer_weight(512, layer), layer_weight(2560, layer + 1)],
-            out_specs=[lanes_of(512)] * 4,
+            grid=(HALF_STEPS,),
+            in_specs=[
+                lanes_of(512), lanes_of(512, offset=offset), lanes_of(512, offset=offset),
+                layer_weight(512, layer), layer_weight(2560, layer + 1),
+            ]
+            + [pl.BlockSpec(memory_space=pl.ANY)] * len(aliased),
+            out_specs=[lanes_of(512), lanes_of(512, 2 * BLOCK, offset), lanes_of(512)],
         ),
-        out_shape=STATE,
-        compiler_params=pltpu.CompilerParams(vmem_limit_bytes=VMEM_LIMIT),
-        name="middle",
-    )(crop_tiles, full_length, back, current, gate, wo, wp)
-
-
-def last_kernel(back_ref, cur_ref, gate_ref, wo_ref, sel_ref, pj_ref, mine_ref, other_ref, total_ref):
-    step = pl.program_id(0)
+        out_shape=[jax.ShapeDtypeStruct((512, 512), BF), BOTH, jax.ShapeDtypeStruct((512, 512), F32)],
+        input_output_aliases={7: 1} if aliased else {},
+        compiler_params=pltpu.CompilerParams(vmem_limit_bytes=VMEM_LIMIT),
+        name="middle" + str(half),
+    )(crop_tiles, full_length, back, current, gate, wo, wp, *aliased)
+
+
+def chosen_rows(back_ref, cur_ref, gate_ref, wo_ref, sel_ref):
     current = update(back_ref, cur_ref, gate_ref, wo_ref[0])
     normed = norm_channels(current.astype(F32)).astype(BF)
-    chosen = dot(sel_ref[...], normed).astype(BF)
-    part = dot_nt(pj_ref[...], chosen)
-
-    @pl.when(step == 0)
+    return dot(sel_ref[...], normed).astype(BF)
+
+
+def last_own_kernel(back_ref, cur_ref, gate_ref, wo_ref, sel_ref, chosen_ref):
+    chosen_ref[...] = chosen_rows(back_ref, cur_ref, gate_ref, wo_ref, sel_ref)
+
+
+def last_peer_kernel(back_ref, cur_ref, gate_ref, wo_ref, sel_ref, own_ref, pj_ref, mine_ref, other_ref, part_ref):
+    step = pl.program_id(0)
+    part_ref[step] = chosen_rows(back_ref, cur_ref, gate_ref, wo_ref, sel_ref)
+
+    @pl.when(step == HALF_STEPS - 1)
     def _():
-        total_ref[...] = part
-
-    @pl.when(step > 0)
-    def _():
-        total_ref[...] += part
-
-    @pl.when(step == STEPS - 1)
-    def _():
-        mine_ref[...] = total_ref[:, :256].astype(BF)
-        other_ref[...] = total_ref[:, 256:].astype(BF)
-
-
-def last_layer(back, current, gate, wo, sel, pj, layer):
-    lanes = pl.BlockSpec((512, BLOCK), lambda step: (0, step))
-    half = pl.BlockSpec((CROP, 256), lambda step: (0, 0))
-    return pl.pallas_call(
-        last_kernel,
-        grid=(STEPS,),
-        in_specs=[lanes] * 3
-        + [
-            pl.BlockSpec((1, 512, 512), lambda step: (layer, 0, 0)),
-            pl.BlockSpec((512, 512), lambda step: (0, 0)),
-            pl.BlockSpec((CROP, BLOCK), lambda step: (0, step)),
-        ],
-        out_specs=[half, half],
+        chosen = jnp.concatenate([own_ref[...]] + [part_ref[k] for k in range(HALF_STEPS)], axis=1)
+        mine_ref[...] = dot_nt(pj_ref[...], chosen[:256]).astype(BF)
+        other_ref[...] = dot_nt(pj_ref[...], chosen[256:]).astype(BF)
+
+
+def last_own(back, current, gate, wo, sel, layer):
+    return pl.pallas_call(
+        last_own_kernel,
+        grid=(HALF_STEPS,),
+        in_specs=[lanes_of(512)] * 3 + [layer_weight(512, layer), full((512, 512))],
+        out_specs=lanes_of(512),
+        out_shape=jax.ShapeDtypeStruct((512, 512), BF),
+        compiler_params=pltpu.CompilerParams(vmem_limit_bytes=VMEM_LIMIT),
+        name="last_own",
+    )(back, current, gate, wo, sel)
+
+
+def last_peer(back, current, gate, wo, sel, own, pj, layer):
+    return pl.pallas_call(
+        last_peer_kernel,
+        grid=(HALF_STEPS,),
+        in_specs=[lanes_of(512)] * 3
+        + [layer_weight(512, layer), full((512, 512)), full((512, 512)), full((CROP, CROP))],
+        out_specs=[full((CROP, 256))] * 2,
         out_shape=[jax.ShapeDtypeStruct((CROP, 256), BF)] * 2,
-        scratch_shapes=[pltpu.VMEM((CROP, 512), F32)],
-        compiler_params=pltpu.CompilerParams(vmem_limit_bytes=VMEM_LIMIT),
-        name="last",
-    )(back, current, gate, wo, sel, pj)
-
-
-def products_kernel(left_ref, own_ref, peer_ref, out_ref):
-    x0 = (lax.axis_index("row") // 32) % 2
-    left = left_ref[...]
-    own = pl.multiple_of(x0 * 512, 512)
-    peer = pl.multiple_of(512 - x0 * 512, 512)
-    out_ref[:, pl.ds(own, 512)] = dot_nt(left, own_ref[...]).astype(BF)
-    out_ref[:, pl.ds(peer, 512)] = dot_nt(left, peer_ref[...]).astype(BF)
-
-
-def triangle_products(left, own, peer):
-    return pl.pallas_call(
-        products_kernel,
-        out_shape=jax.ShapeDtypeStruct((512, CROP), BF),
-        compiler_params=pltpu.CompilerParams(vmem_limit_bytes=VMEM_LIMIT),
-        name="products",
-    )(left, own, peer)
+        scratch_shapes=[pltpu.VMEM((HALF_STEPS, 512, BLOCK), BF)],
+        compiler_params=pltpu.CompilerParams(vmem_limit_bytes=VMEM_LIMIT),
+        name="last_peer",
+    )(back, current, gate, wo, sel, own, pj)
+
+
+def lane_blocks(both_ref, which, order):
+    starts = [(2 * block + which) * BLOCK for block in order]
+    return jnp.concatenate([both_ref[:, start : start + BLOCK] for start in starts], axis=1)
+
+
+def own_products_kernel(both_ref, out_ref, right_ref):
+    right = lane_blocks(both_ref, 1, range(STEPS))
+    right_ref[...] = right
+    out_ref[...] = dot_nt(lane_blocks(both_ref, 0, range(STEPS)), right).astype(BF)
+
+
+def own_products(both):
+    return pl.pallas_call(
+        own_products_kernel,
+        out_shape=[jax.ShapeDtypeStruct((512, 512), BF), jax.ShapeDtypeStruct((512, CROP), BF)],
+        compiler_params=pltpu.CompilerParams(vmem_limit_bytes=VMEM_LIMIT),
+        cost_estimate=pl.CostEstimate(flops=2**29, bytes_accessed=4 * 2**20, transcendentals=0),
+        name="own_products",
+    )(both)
+
+
+def peer_products_kernel(both_ref, right_ref, out_ref):
+    left = lane_blocks(both_ref, 0, [2, 3, 0, 1])
+    out_ref[...] = dot_nt(left, right_ref[...]).astype(BF)
+
+
+def peer_products(both, right):
+    return pl.pallas_call(
+        peer_products_kernel,
+        out_shape=jax.ShapeDtypeStruct((512, 512), BF),
+        compiler_params=pltpu.CompilerParams(vmem_limit_bytes=VMEM_LIMIT),
+        cost_estimate=pl.CostEstimate(flops=2**29, bytes_accessed=4 * 2**20, transcendentals=0),
+        name="peer_products",
+    )(both, right)
 
 
 def hidden_kernel(mine_ref, peer_ref, out_ref):
@@ -354,18 +387,25 @@
     pair = jnp.transpose(pair_maps[0], (0, 2, 1))
     cropped = crop_columns(crop_tiles, pair)
     got = lax.all_to_all(cropped, "row", 0, 0, axis_index_groups=PLANE, tiled=True)
-    current, left, right, gate = first_projection(crop_tiles, full_length, got, prow, q, wp)
+    current, both, gate = first_projection(crop_tiles, full_length, got, prow, q, wp)
+    currents, gates = (current, current), (gate, gate)
     for layer in range(NLAYER):
-        right_own = exchange(right, SAME_X0, CH)
-        left_own = exchange(left, SAME_X0, CH)
-        right_peer = lax.ppermute(right_own, "row", X0_PAIRS)
-        products = triangle_products(left_own, right_own, right_peer)
-        back = exchange(products, SAME_X0, CH)
+        gathered = exchange(both, SAME_X0, CH)
+        products, right = own_products(gathered)
+        back_own = exchange(products, SAME_X0, CH)
+        right_peer = lax.ppermute(right, "row", X0_PAIRS)
+        back_peer = exchange(peer_products(gathered, right_peer), SAME_X0, CH)
         if layer + 1 < NLAYER:
-            current, left, right, gate = middle_layer(
-                crop_tiles, full_length, back, current, gate, wo, wp, layer
+            shared = (wo, wp, layer)
+            own, both, gate_own = middle_half(
+                0, crop_tiles, full_length, back_own, currents[0], gates[0], *shared, None
             )
-    mine, other = last_layer(back, current, gate, wo, sel, pj, NLAYER - 1)
+            peer, both, gate_peer = middle_half(
+                1, crop_tiles, full_length, back_peer, currents[1], gates[1], *shared, both
+            )
+            currents, gates = (own, peer), (gate_own, gate_peer)
+    chosen = last_own(back_own, currents[0], gates[0], wo, sel, NLAYER - 1)
+    mine, other = last_peer(back_peer, currents[1], gates[1], wo, sel, chosen, pj, NLAYER - 1)
     hidden = hidden_features(mine, lax.ppermute(other, "tmpl", CORES))
     moved = exchange(hidden, BY_Z, 128)
     result = final_projection(moved, lax.ppermute(moved, "tmpl", CORES), wf)

time: 363 us -> 345 us (0.950)
  blocking collectives: 173 us -> 133 us
  starting transfers between devices: 32.3 us -> 65.6 us
  waiting for transfers between devices: 88.4 us -> 64.1 us
  Pallas kernels: 62.4 us -> 73.8 us
    all_to_all x5 -> x3, blocking collectives: 173 us -> 133 us  [exchange(): lax.all_to_all(cube, 'row', 0, 0, axis_index_groups=groups, tiled=True)]
    all_to_all x2 -> x4, waiting for transfers between devices: 48.9 us -> 17.9 us  [exchange(): lax.all_to_all(cube, 'row', 0, 0, axis_index_groups=groups, tiled=True)]
    all_to_all x2 -> x4, starting transfers between devices: 16.6 us -> 42.3 us  [exchange(): lax.all_to_all(cube, 'row', 0, 0, axis_index_groups=groups, tiled=True)]
    pallas_call x4 -> x8, Pallas kernels: 28.9 us -> 39.5 us  [the longest x2 14.6 us: middle_half(): pl.pallas_call(functools.partial(middle_kernel, half), grid_spec=pltpu.Pr...]
    ppermute x2, waiting for transfers between devices: 18 us -> 24.8 us  [on_device(): right_peer = lax.ppermute(right, 'row', X0_PAIRS)]
    ppermute x2, starting transfers between devices: 0.29 us -> 5.05 us  [on_device(): right_peer = lax.ppermute(right, 'row', X0_PAIRS)]
  transfers between devices with their start and end apart: 7 -> 9, of which waited for: 7 -> 8; matrix products, arithmetic and copies ran while one was open for 0% -> 0% of each run, Pallas kernels for 2% -> 8%
where the time goes in v2:
time: 345 us; the launch traced here: 344 us
  blocking collectives  133 us (39%)
  Pallas kernels  73.8 us (21%)
  starting transfers between devices  65.6 us (19%)
  waiting for transfers between devices  64.1 us (19%)
  local copies, waits for them, and re-layouts  6.52 us (2%)
    all_to_all x3, blocking collectives, exchange(): lax.all_to_all(cube, 'row', 0, 0, axis_index_groups=groups, tiled=True)  133 us
    all_to_all x4, starting transfers between devices, exchange(): lax.all_to_all(cube, 'row', 0, 0, axis_index_groups=groups, tiled=True)  42.3 us
    ppermute x2, waiting for transfers between devices, on_device(): right_peer = lax.ppermute(right, 'row', X0_PAIRS)  24.8 us
    all_to_all x1, waiting for transfers between devices, on_device(): lax.all_to_all(cropped, 'row', 0, 0, axis_index_groups=PLANE, tiled=True)  18.2 us
    all_to_all x4, waiting for transfers between devices, exchange(): lax.all_to_all(cube, 'row', 0, 0, axis_index_groups=groups, tiled=True)  17.9 us
    pallas_call x2, Pallas kernels, middle_half(): pl.pallas_call(functools.partial(middle_kernel, half), grid_spec=pltpu.Pr...  14.6 us
    pallas_call x1, Pallas kernels, first_projection(): pl.pallas_call(first_kernel, grid_spec=pltpu.PrefetchScalarGridSpec(num_s...  11.9 us
    pallas_call x1, Pallas kernels, make_weights(): pl.pallas_call(weights_kernel, out_shape=[jax.ShapeDtypeStruct(shape, BF)...  8.97 us
  transfers between devices with their start and end apart: 9, of which 8 were waited for; matrix products, arithmetic and copies ran while one was open for 0% of the time, Pallas kernels for 8%

profile of v2, /device:TPU:1, one launch (start us, length us, event | category | flops | bytes accessed | tf_op | source)
XLA Modules:
  0.0 344.2 jit_solution(15255900760388861462)
XLA Ops:
  0.0 6.9 %crop.1 = bf16[16,64,1024]{2,1,0:T(8,128)(2,1)} custom-call(s32[1,8]{1,0:T(1,128)} %refs_0_.3, bf16[16,64,2048]{2,1,0:T(8,128)(2,1)} %bitcast.23), custom_call_target="tpu_custom_call" | custom-call | tf_op jit(solution)/shard_map/crop/pallas_call | solution.py:113
  6.9 7.6 %all-to-all-start = ((bf16[16,64,1024]{2,1,0:T(8,128)(2,1)}), bf16[16,64,1024]{2,1,0:T(8,128)(2,1)S(1)}, u32[]{:S(2)}, u32[]{:S(2)}) async-start(bf16[16,64,1024]{2,1,0:T(8,128)(2,1)} %crop.1), calls=%async_computation | async-start | bytes 4194304 | tf_op jit(solution)/shard_map/all_to_all | solution.py:389
  15.2 9.0 %weights.1 = (bf16[2,2560,512]{2,1,0:T(8,128)(2,1)}, bf16[2,512,512]{2,1,0:T(8,128)(2,1)}, bf16[512,256]{1,0:T(8,128)(2,1)}, bf16[512,512]{1,0:T(8,128)(2,1)}, b...) custom-call(bf16[2,64,320]{2,1,0:T(8,128)(2,1)} %proj_ref.1, ...), custom_call_target="tpu_custom_call" | custom-call | flops 2000000000 | bytes 12582912 | tf_op jit(solution)/shard_map/weights/pallas_call | solution.py:97
  24.1 18.2 %all-to-all-done.got_ref = bf16[16,64,1024]{2,1,0:T(8,128)(2,1)S(1)} async-done(((bf16[16,64,1024]{2,1,0:T(8,128)(2,1)}), bf16[16,64,1024]{2,1,0:T(8,128)(2,1)S(1)}, u32[]{:S(2)}, u32[]{:S(2)}) %all-to-all-start) | async-done | bytes 2097184 | tf_op jit(solution)/shard_map/all_to_all | solution.py:389
  43.7 11.9 %first.1 = (bf16[512,1024]{1,0:T(8,128)(2,1)}, bf16[512,2048]{1,0:T(8,128)(2,1)}, f32[512,1024]{1,0:T(8,128)}) custom-call(s32[1,8]{1,0:T(1,128)} %refs_0_.3, s32[1]{0:T(128)S(6)} %copy.9.length_ref.refs_1_, bf16[16,64,1024]{2,1,0:T(8,128)(2,1)} %copy-done, bf16[512,512]{1,0:T(8,128)(2,1)} %get-tuple-element.27.prow_ref, ...), custom_call_target="tpu_custom_call" | custom-call | tf_op jit(solution)/shard_map/first/pallas_call | solution.py:202
  55.5 59.0 %all_to_all.40 = bf16[64,8,2048]{2,1,0:T(8,128)(2,1)} all-to-all(bf16[64,8,2048]{2,1,0:T(8,128)(2,1)} %bitcast.30), channel_id=1, replica_groups={{0,1,2,3,4,5,6,7,8,9,10,11,12,13,14,15,16,17,18,19,20,21,22,23,24,25,26..., dimensions={0} | all-to-all | bytes 4194304 | tf_op jit(solution)/shard_map/all_to_all | solution.py:381
  117.7 9.6 %all-to-all-start.3 = ((bf16[64,8,512]{2,1,0:T(8,128)(2,1)}), bf16[64,8,512]{2,1,0:T(8,128)(2,1)S(1)}, u32[]{:S(2)}, u32[]{:S(2)}) async-start(bf16[64,8,512]{2,1,0:T(8,128)(2,1)} %bitcast.34), calls=%async_computation.3 | async-start | bytes 1048576 | tf_op jit(solution)/shard_map/all_to_all | solution.py:381
  127.2 14.9 %collective-permute-done.right_ref = bf16[512,1024]{1,0:T(8,128)(2,1)S(1)} collective-permute-done((bf16[512,1024]{1,0:T(8,128)(2,1)}, bf16[512,1024]{1,0:T(8,128)(2,1)S(1)}, u32[]{:S(2)}, u32[]{:S(2)}) %collective-permute-start) | collective-permute-done | bytes 1048608 | tf_op jit(solution)/shard_map/ppermute | solution.py:396
  143.1 3.4 peer_products.2
  146.5 10.7 %all-to-all-start.2 = ((bf16[64,8,512]{2,1,0:T(8,128)(2,1)}), bf16[64,8,512]{2,1,0:T(8,128)(2,1)S(1)}, u32[]{:S(2)}, u32[]{:S(2)}) async-start(bf16[64,8,512]{2,1,0:T(8,128)(2,1)} %bitcast.27), calls=%async_computation.2 | async-start | bytes 1048576 | tf_op jit(solution)/shard_map/all_to_all | solution.py:381
  157.2 7.3 %middle0.1 = (bf16[512,512]{1,0:T(8,128)(2,1)}, bf16[512,2048]{1,0:T(8,128)(2,1)}, f32[512,512]{1,0:T(8,128)}) custom-call(s32[1,8]{1,0:T(1,128)} %refs_0_.3, s32[1]{0:T(128)S(6)} %copy.9.length_ref.refs_1_, bf16[512,512]{1,0:T(8,128)(2,1)} %bitcast.24, bf16[512,1024]{1,0:T(8,128)(2,1)} %get-tuple-element.32.refs_3_, f32[512,1024]{1,0:T(8,128)} %get-tuple-element.33.refs_4_, ...), custom_call_target="tpu_custom_call" | custom-call | tf_op jit(solution)/shard_map/middle0/pallas_call | solution.py:236
  164.5 7.3 %all-to-all-done.2 = bf16[64,8,512]{2,1,0:T(8,128)(2,1)S(1)} async-done(((bf16[64,8,512]{2,1,0:T(8,128)(2,1)}), bf16[64,8,512]{2,1,0:T(8,128)(2,1)S(1)}, u32[]{:S(2)}, u32[]{:S(2)}) %all-to-all-start.2) | async-done | bytes 524320 | tf_op jit(solution)/shard_map/all_to_all | solution.py:381
  172.7 7.3 %middle1.1 = (bf16[512,512]{1,0:T(8,128)(2,1)}, bf16[512,2048]{1,0:T(8,128)(2,1)}, f32[512,512]{1,0:T(8,128)}) custom-call(s32[1,8]{1,0:T(1,128)} %refs_0_.3, s32[1]{0:T(128)S(6)} %copy.9.length_ref.refs_1_, bf16[512,512]{1,0:T(8,128)(2,1)} %bitcast.25, bf16[512,1024]{1,0:T(8,128)(2,1)} %get-tuple-element.32.refs_3_, ...), custom_call_target="tpu_custom_call", output_to_operand_aliasing={{1}: (7, {})} | custom-call | tf_op jit(solution)/shard_map/middle1/pallas_call | solution.py:236
  180.0 49.0 %all_to_all.41 = bf16[64,8,2048]{2,1,0:T(8,128)(2,1)} all-to-all(bf16[64,8,2048]{2,1,0:T(8,128)(2,1)} %bitcast.22), channel_id=1, replica_groups={{0,1,2,3,4,5,6,7,8,9,10,11,12,13,14,15,16,17,18,19,20,21,22,23,24,25,26..., dimensions={0} | all-to-all | bytes 4194304 | tf_op jit(solution)/shard_map/all_to_all | solution.py:381
  232.2 5.0 %collective-permute-start.1 = (bf16[512,1024]{1,0:T(8,128)(2,1)}, bf16[512,1024]{1,0:T(8,128)(2,1)S(1)}, u32[]{:S(2)}, u32[]{:S(2)}) collective-permute-start(bf16[512,1024]{1,0:T(8,128)(2,1)} %get-tuple-element.38), channel_id=1, source_target_pairs={{0,32},{1,33},{2,34},{3,35},{4,36},{5,37},{6,38},{7,39},{8,40},{9,... | collective-permute-start | bytes 3145736 | tf_op jit(solution)/shard_map/ppermute | solution.py:396
  237.2 9.5 %all-to-all-start.6 = ((bf16[64,8,512]{2,1,0:T(8,128)(2,1)}), bf16[64,8,512]{2,1,0:T(8,128)(2,1)S(1)}, u32[]{:S(2)}, u32[]{:S(2)}) async-start(bf16[64,8,512]{2,1,0:T(8,128)(2,1)} %bitcast.35), calls=%async_computation.6 | async-start | bytes 1048576 | tf_op jit(solution)/shard_map/all_to_all | solution.py:381
  246.7 9.9 %collective-permute-done.1.right_ref = bf16[512,1024]{1,0:T(8,128)(2,1)S(1)} collective-permute-done((bf16[512,1024]{1,0:T(8,128)(2,1)}, bf16[512,1024]{1,0:T(8,128)(2,1)S(1)}, u32[]{:S(2)}, u32[]{:S(2)}) %collective-permute-start.1) | collective-permute-done | bytes 1048608 | tf_op jit(solution)/shard_map/ppermute | solution.py:396
  261.5 12.6 %all-to-all-start.5 = ((bf16[64,8,512]{2,1,0:T(8,128)(2,1)}), bf16[64,8,512]{2,1,0:T(8,128)(2,1)S(1)}, u32[]{:S(2)}, u32[]{:S(2)}) async-start(bf16[64,8,512]{2,1,0:T(8,128)(2,1)} %bitcast.28), calls=%async_computation.5 | async-start | bytes 1048576 | tf_op jit(solution)/shard_map/all_to_all | solution.py:381
  274.1 4.7 %last_own.1.own_ref = bf16[512,512]{1,0:T(8,128)(2,1)} custom-call(bf16[512,512]{1,0:T(8,128)(2,1)} %bitcast.33, bf16[512,512]{1,0:T(8,128)(2,1)} %get-tuple-element.43.cur_ref, f32[512,512]{1,0:T(8,128)} %get-tuple-element.44.gate_ref, bf16[2,512,512]{2,1,0:T(8,128)(2,1)} %get-tuple-element.34.refs_5_.wo_ref, bf16[512,512]{1,0:T(8,128)(2,1)} %get-tuple-element.41.sel_ref), custom_call_target="tpu_custom_call" | custom-call | tf_op jit(solution)/shard_map/last_own/pallas_call | solution.py:277
  278.8 10.0 %all-to-all-done.5 = bf16[64,8,512]{2,1,0:T(8,128)(2,1)S(1)} async-done(((bf16[64,8,512]{2,1,0:T(8,128)(2,1)}), bf16[64,8,512]{2,1,0:T(8,128)(2,1)S(1)}, u32[]{:S(2)}, u32[]{:S(2)}) %all-to-all-start.5) | async-done | bytes 524320 | tf_op jit(solution)/shard_map/all_to_all | solution.py:381
  289.7 7.0 %last_peer.1 = (bf16[1024,256]{1,0:T(8,128)(2,1)}, bf16[1024,256]{1,0:T(8,128)(2,1)}) custom-call(bf16[512,512]{1,0:T(8,128)(2,1)} %bitcast.26, bf16[512,512]{1,0:T(8,128)(2,1)} %get-tuple-element.39.cur_ref, f32[512,512]{1,0:T(8,128)} %get-tuple-element.40.gate_ref, bf16[2,512,512]{2,1,0:T(8,128)(2,1)} %get-tuple-element.34.refs_5_.wo_ref, ...), custom_call_target="tpu_custom_call" | custom-call | tf_op jit(solution)/shard_map/last_peer/pallas_call | solution.py:289
  296.6 7.9 %collective-permute-start.2 = (bf16[1024,256]{1,0:T(8,128)(2,1)}, bf16[1024,256]{1,0:T(8,128)(2,1)S(1)}, u32[]{:S(2)}, u32[]{:S(2)}) collective-permute-start(bf16[1024,256]{1,0:T(8,128)(2,1)} %get-tuple-element.47), channel_id=1, source_target_pairs={{0,128},{128,0},{1,129},{129,1},{2,130},{130,2},{3,131},{131,3},{4... | collective-permute-start | bytes 1572872 | tf_op jit(solution)/shard_map/ppermute | solution.py:409
  309.3 25.5 %all_to_all.42 = bf16[128,8,256]{2,1,0:T(8,128)(2,1)S(1)} all-to-all(bf16[128,8,256]{2,1,0:T(8,128)(2,1)} %bitcast.29), channel_id=1, replica_groups={{0,8,16,24,32,40,48,56,64,72,80,88,96,104,112,120,1,9,17,25,33,41,49,57..., dimensions={0} | all-to-all | bytes 1048576 | tf_op jit(solution)/shard_map/all_to_all | solution.py:381
  339.9 4.3 %final.1 = bf16[1024,1024]{1,0:T(8,128)(2,1)} custom-call(bf16[1024,256]{1,0:T(8,128)(2,1)} %bitcast.32, bf16[1024,256]{1,0:T(8,128)(2,1)} %copy-done.9, bf16[512,256]{1,0:T(8,128)(2,1)} %get-tuple-element.48.wf_ref), custom_call_target="tpu_custom_call" | custom-call | tf_op jit(solution)/shard_map/final/pallas_call | solution.py:368
  (30 shorter events, 25.1 us)
Async XLA Ops:
  6.9 35.4 %all-to-all-start = ((bf16[16,64,1024]{2,1,0:T(8,128)(2,1)}), bf16[16,64,1024]{2,1,0:T(8,128)(2,1)S(1)}, u32[]{:S(2)}, u32[]{:S(2)}) async-start(bf16[16,64,1024]{2,1,0:T(8,128)(2,1)} %crop.1), calls=%async_computation | async-start | bytes 4194304 | tf_op jit(solution)/shard_map/all_to_all | solution.py:389
  42.3 1.3 copy-start
  117.7 24.5 %collective-permute-start = (bf16[512,1024]{1,0:T(8,128)(2,1)}, bf16[512,1024]{1,0:T(8,128)(2,1)S(1)}, u32[]{:S(2)}, u32[]{:S(2)}) collective-permute-start(bf16[512,1024]{1,0:T(8,128)(2,1)} %get-tuple-element.31), channel_id=1, source_target_pairs={{0,32},{1,33},{2,34},{3,35},{4,36},{5,37},{6,38},{7,39},{8,40},{9,... | collective-permute-start | bytes 3145736 | tf_op jit(solution)/shard_map/ppermute | solution.py:396
  117.7 28.8 %all-to-all-start.3 = ((bf16[64,8,512]{2,1,0:T(8,128)(2,1)}), bf16[64,8,512]{2,1,0:T(8,128)(2,1)S(1)}, u32[]{:S(2)}, u32[]{:S(2)}) async-start(bf16[64,8,512]{2,1,0:T(8,128)(2,1)} %bitcast.34), calls=%async_computation.3 | async-start | bytes 1048576 | tf_op jit(solution)/shard_map/all_to_all | solution.py:381
  142.1 1.0 copy-start.6
  146.5 10.7 %copy-start.1 = (bf16[64,8,512]{2,1,0:T(8,128)(2,1)}, bf16[64,8,512]{2,1,0:T(8,128)(2,1)S(1)}, u32[]{:S(2)}) copy-start(bf16[64,8,512]{2,1,0:T(8,128)(2,1)S(1)} %all-to-all-done.3) | copy-start | bytes 1572868
  146.5 25.3 %all-to-all-start.2 = ((bf16[64,8,512]{2,1,0:T(8,128)(2,1)}), bf16[64,8,512]{2,1,0:T(8,128)(2,1)S(1)}, u32[]{:S(2)}, u32[]{:S(2)}) async-start(bf16[64,8,512]{2,1,0:T(8,128)(2,1)} %bitcast.27), calls=%async_computation.2 | async-start | bytes 1048576 | tf_op jit(solution)/shard_map/all_to_all | solution.py:381
  171.8 0.9 copy-start.2
  232.2 24.4 %collective-permute-start.1 = (bf16[512,1024]{1,0:T(8,128)(2,1)}, bf16[512,1024]{1,0:T(8,128)(2,1)S(1)}, u32[]{:S(2)}, u32[]{:S(2)}) collective-permute-start(bf16[512,1024]{1,0:T(8,128)(2,1)} %get-tuple-element.38), channel_id=1, source_target_pairs={{0,32},{1,33},{2,34},{3,35},{4,36},{5,37},{6,38},{7,39},{8,40},{9,... | collective-permute-start | bytes 3145736 | tf_op jit(solution)/shard_map/ppermute | solution.py:396
  237.2 24.3 %all-to-all-start.6 = ((bf16[64,8,512]{2,1,0:T(8,128)(2,1)}), bf16[64,8,512]{2,1,0:T(8,128)(2,1)S(1)}, u32[]{:S(2)}, u32[]{:S(2)}) async-start(bf16[64,8,512]{2,1,0:T(8,128)(2,1)} %bitcast.35), calls=%async_computation.6 | async-start | bytes 1048576 | tf_op jit(solution)/shard_map/all_to_all | solution.py:381
  256.6 1.0 copy-start.7
  261.5 12.6 %copy-start.5 = (bf16[64,8,512]{2,1,0:T(8,128)(2,1)}, bf16[64,8,512]{2,1,0:T(8,128)(2,1)S(1)}, u32[]{:S(2)}) copy-start(bf16[64,8,512]{2,1,0:T(8,128)(2,1)S(1)} %all-to-all-done.6) | copy-start | bytes 1572868
  261.5 27.4 %all-to-all-start.5 = ((bf16[64,8,512]{2,1,0:T(8,128)(2,1)}), bf16[64,8,512]{2,1,0:T(8,128)(2,1)S(1)}, u32[]{:S(2)}, u32[]{:S(2)}) async-start(bf16[64,8,512]{2,1,0:T(8,128)(2,1)} %bitcast.28), calls=%async_computation.5 | async-start | bytes 1048576 | tf_op jit(solution)/shard_map/all_to_all | solution.py:381
  288.9 0.8 copy-start.3
  296.6 9.6 %collective-permute-start.2 = (bf16[1024,256]{1,0:T(8,128)(2,1)}, bf16[1024,256]{1,0:T(8,128)(2,1)S(1)}, u32[]{:S(2)}, u32[]{:S(2)}) collective-permute-start(bf16[1024,256]{1,0:T(8,128)(2,1)} %get-tuple-element.47), channel_id=1, source_target_pairs={{0,128},{128,0},{1,129},{129,1},{2,130},{130,2},{3,131},{131,3},{4... | collective-permute-start | bytes 1572872 | tf_op jit(solution)/shard_map/ppermute | solution.py:409
  306.2 0.8 copy-start.8
  334.7 4.3 %copy-start.4 = (bf16[128,8,256]{2,1,0:T(8,128)(2,1)}, bf16[128,8,256]{2,1,0:T(8,128)(2,1)S(1)}, u32[]{:S(2)}) copy-start(bf16[128,8,256]{2,1,0:T(8,128)(2,1)S(1)} %all_to_all.42) | copy-start | bytes 1572868
  334.7 4.3 %collective-permute-start.3 = (bf16[1024,256]{1,0:T(8,128)(2,1)S(1)}, bf16[1024,256]{1,0:T(8,128)(2,1)S(1)}, u32[]{:S(2)}, u32[]{:S(2)}) collective-permute-start(bf16[1024,256]{1,0:T(8,128)(2,1)S(1)} %bitcast.31), channel_id=1, source_target_pairs={{0,128},{128,0},{1,129},{129,1},{2,130},{130,2},{3,131},{131,3},{4... | collective-permute-start | bytes 1572872 | tf_op jit(solution)/shard_map/ppermute | solution.py:411
  339.1 0.8 copy-start.9

commit v3 on v2

--- a/solution.py
+++ b/solution.py
@@ -26,7 +26,7 @@
 BY_Z = [[s * 8 + z for z in range(8) for s in range(16)]]
 X0_PAIRS = [(r, r ^ 32) for r in range(128)]
 CORES = [(0, 1), (1, 0)]
-VMEM_LIMIT = 56 * 1024 * 1024
+VMEM_LIMIT = 20 * 1024 * 1024
 
 
 def iota(shape, dim):
@@ -97,7 +97,7 @@
     return pl.pallas_call(
         weights_kernel,
         out_shape=[jax.ShapeDtypeStruct(shape, BF) for shape in shapes],
-        compiler_params=pltpu.CompilerParams(vmem_limit_bytes=VMEM_LIMIT),
+        compiler_params=pltpu.CompilerParams(vmem_limit_bytes=48 * 1024 * 1024),
         cost_estimate=pl.CostEstimate(flops=2 * 10**9, bytes_accessed=12 * 2**20, transcendentals=0),
         name="weights",
     )(proj_weight, out_weight, final_weight)
@@ -114,11 +114,12 @@
         crop_kernel,
         grid_spec=pltpu.PrefetchScalarGridSpec(
             num_scalar_prefetch=1,
-            grid=(8,),
-            in_specs=[pl.BlockSpec((2, CH, FULL), lambda m, crop: (m, 0, 0))],
-            out_specs=pl.BlockSpec((2, CH, CROP), lambda m, crop: (m, 0, 0)),
+            grid=(4,),
+            in_specs=[pl.BlockSpec((4, CH, FULL), lambda m, crop: (m, 0, 0))],
+            out_specs=pl.BlockSpec((4, CH, CROP), lambda m, crop: (m, 0, 0)),
         ),
         out_shape=jax.ShapeDtypeStruct((16, CH, CROP), BF),
+        compiler_params=pltpu.CompilerParams(vmem_limit_bytes=VMEM_LIMIT),
         name="crop",
     )(crop_tiles, pair)
 

time: 345 us -> 347 us (level)
  local copies, waits for them, and re-layouts: 6.52 us -> 40.2 us
  Pallas kernels: 73.8 us -> 47.3 us
  waiting for transfers between devices: 64.1 us -> 53.6 us
  blocking collectives: 133 us -> 141 us
    unnamed x20 -> x84, local copies, waits for them, and re-layouts: 6.52 us -> 40.2 us
    all_to_all x4, waiting for transfers between devices: 17.9 us -> 8.93 us  [exchange(): lax.all_to_all(cube, 'row', 0, 0, axis_index_groups=groups, tiled=True)]
    all_to_all x3, blocking collectives: 133 us -> 141 us  [exchange(): lax.all_to_all(cube, 'row', 0, 0, axis_index_groups=groups, tiled=True)]
    pallas_call x1, Pallas kernels: 6.94 us -> 1.22 us  [crop_columns(): pl.pallas_call(crop_kernel, grid_spec=pltpu.PrefetchScalarGridSpec(num_sc...]
    ppermute x2, starting transfers between devices: 5.05 us -> 0.01 us  [on_device(): right_peer = lax.ppermute(right, 'row', X0_PAIRS)]
    pallas_call x2, Pallas kernels: 14.6 us -> 10.4 us  [middle_half(): pl.pallas_call(functools.partial(middle_kernel, half), grid_spec=pltpu.Pr...]
    pallas_call x2, Pallas kernels: 6.37 us -> 2.89 us  [own_products(): pl.pallas_call(own_products_kernel, out_shape=[jax.ShapeDtypeStruct((512,...]
  transfers between devices with their start and end apart: 9 -> 9, of which waited for: 8 -> 8; matrix products, arithmetic and copies ran while one was open for 0% -> 0% of each run, Pallas kernels for 8% -> 6%
where the time goes in v3:
time: 347 us; the launch traced here: 345 us
  blocking collectives  141 us (41%)
  starting transfers between devices  62.2 us (18%)
  waiting for transfers between devices  53.6 us (15%)
  Pallas kernels  47.3 us (14%)
  local copies, waits for them, and re-layouts  40.2 us (12%)
    all_to_all x3, blocking collectives, exchange(): lax.all_to_all(cube, 'row', 0, 0, axis_index_groups=groups, tiled=True)  141 us
    all_to_all x4, starting transfers between devices, exchange(): lax.all_to_all(cube, 'row', 0, 0, axis_index_groups=groups, tiled=True)  44 us
    unnamed x84, local copies, waits for them, and re-layouts  40.2 us
    ppermute x2, waiting for transfers between devices, on_device(): right_peer = lax.ppermute(right, 'row', X0_PAIRS)  25.3 us
    all_to_all x1, waiting for transfers between devices, on_device(): lax.all_to_all(cropped, 'row', 0, 0, axis_index_groups=PLANE, tiled=True)  16.3 us
    pallas_call x2, Pallas kernels, middle_half(): pl.pallas_call(functools.partial(middle_kernel, half), grid_spec=pltpu.Pr...  10.4 us
    all_to_all x4, waiting for transfers between devices, exchange(): lax.all_to_all(cube, 'row', 0, 0, axis_index_groups=groups, tiled=True)  8.93 us
    pallas_call x1, Pallas kernels, first_projection(): pl.pallas_call(first_kernel, grid_spec=pltpu.PrefetchScalarGridSpec(num_s...  8.62 us
  transfers between devices with their start and end apart: 9, of which 8 were waited for; matrix products, arithmetic and copies ran while one was open for 0% of the time, Pallas kernels for 6%

profile of v3, /device:TPU:1, one launch (start us, length us, event | category | flops | bytes accessed | tf_op | source)
XLA Modules:
  0.0 345.0 jit_solution(8137463375962898994)
XLA Ops:
  5.4 7.7 %all-to-all-start = ((bf16[16,64,1024]{2,1,0:T(8,128)(2,1)}), bf16[16,64,1024]{2,1,0:T(8,128)(2,1)S(1)}, u32[]{:S(2)}, u32[]{:S(2)}) async-start(bf16[16,64,1024]{2,1,0:T(8,128)(2,1)} %copy-done.3), calls=%async_computation | async-start | bytes 4194304 | tf_op jit(solution)/shard_map/all_to_all | solution.py:390
  14.5 7.1 %weights.1 = (bf16[2,2560,512]{2,1,0:T(8,128)(2,1)}, bf16[2,512,512]{2,1,0:T(8,128)(2,1)S(1)}, bf16[512,256]{1,0:T(8,128)(2,1)S(1)}, bf16[512,512]{1,0:T(8,128)(...) custom-call(bf16[2,64,320]{2,1,0:T(8,128)(2,1)S(1)} %copy-done.38, ...), custom_call_target="tpu_custom_call" | custom-call | flops 2000000000 | bytes 12582912 | tf_op jit(solution)/shard_map/weights/pallas_call | solution.py:97
  24.7 16.3 %all-to-all-done.got_ref = bf16[16,64,1024]{2,1,0:T(8,128)(2,1)S(1)} async-done(((bf16[16,64,1024]{2,1,0:T(8,128)(2,1)}), bf16[16,64,1024]{2,1,0:T(8,128)(2,1)S(1)}, u32[]{:S(2)}, u32[]{:S(2)}) %all-to-all-start) | async-done | bytes 2097184 | tf_op jit(solution)/shard_map/all_to_all | solution.py:390
  41.0 2.5 copy-done
  46.1 8.6 %first.1 = (bf16[512,1024]{1,0:T(8,128)(2,1)S(1)}, bf16[512,2048]{1,0:T(8,128)(2,1)S(1)}, f32[512,1024]{1,0:T(8,128)S(1)}) custom-call(s32[1,8]{1,0:T(1,128)S(1)} %copy-done.37, s32[1]{0:T(128)S(6)} %copy.9.length_ref.refs_1_, bf16[16,64,1024]{2,1,0:T(8,128)(2,1)S(1)} %all-to-all-done.got_ref, bf16[512,512]{1,0:T(8,128)(2,1)S(1)} %copy-done.30, ...), custom_call_target="tpu_custom_call" | custom-call | tf_op jit(solution)/shard_map/first/pallas_call | solution.py:203
  54.8 58.6 %all_to_all.40 = bf16[64,8,2048]{2,1,0:T(8,128)(2,1)S(1)} all-to-all(bf16[64,8,2048]{2,1,0:T(8,128)(2,1)S(1)} %bitcast.26), channel_id=1, replica_groups={{0,1,2,3,4,5,6,7,8,9,10,11,12,13,14,15,16,17,18,19,20,21,22,23,24,25,26..., dimensions={0} | all-to-all | bytes 4194304 | tf_op jit(solution)/shard_map/all_to_all | solution.py:382
  115.7 9.8 %all-to-all-start.3 = ((bf16[64,8,512]{2,1,0:T(8,128)(2,1)}), bf16[64,8,512]{2,1,0:T(8,128)(2,1)}, u32[]{:S(2)}, u32[]{:S(2)}) async-start(bf16[64,8,512]{2,1,0:T(8,128)(2,1)} %bitcast.29), calls=%async_computation.3 | async-start | bytes 1048576 | tf_op jit(solution)/shard_map/all_to_all | solution.py:382
  125.5 14.8 %collective-permute-done.right_ref = bf16[512,1024]{1,0:T(8,128)(2,1)} collective-permute-done((bf16[512,1024]{1,0:T(8,128)(2,1)}, bf16[512,1024]{1,0:T(8,128)(2,1)}, u32[]{:S(2)}, u32[]{:S(2)}) %collective-permute-start) | collective-permute-done | bytes 1048608 | tf_op jit(solution)/shard_map/ppermute | solution.py:397
  143.0 11.9 %all-to-all-start.2 = ((bf16[64,8,512]{2,1,0:T(8,128)(2,1)}), bf16[64,8,512]{2,1,0:T(8,128)(2,1)}, u32[]{:S(2)}, u32[]{:S(2)}) async-start(bf16[64,8,512]{2,1,0:T(8,128)(2,1)} %bitcast.24), calls=%async_computation.2 | async-start | bytes 1048576 | tf_op jit(solution)/shard_map/all_to_all | solution.py:382
  155.0 2.5 copy-done.1
  160.2 5.2 %middle0.1 = (bf16[512,512]{1,0:T(8,128)(2,1)S(1)}, bf16[512,2048]{1,0:T(8,128)(2,1)S(1)}, f32[512,512]{1,0:T(8,128)S(1)}) custom-call(s32[1,8]{1,0:T(1,128)S(1)} %copy-done.37, s32[1]{0:T(128)S(6)} %copy.9.length_ref.refs_1_, bf16[512,512]{1,0:T(8,128)(2,1)} %bitcast.7.refs_2_, bf16[512,1024]{1,0:T(8,128)(2,1)S(1)} %copy-done.10, ...), custom_call_target="tpu_custom_call" | custom-call | tf_op jit(solution)/shard_map/middle0/pallas_call | solution.py:237
  169.3 2.5 copy-done.2
  174.6 5.2 %middle1.1 = (bf16[512,512]{1,0:T(8,128)(2,1)S(1)}, bf16[512,2048]{1,0:T(8,128)(2,1)S(1)}, f32[512,512]{1,0:T(8,128)S(1)}) custom-call(s32[1,8]{1,0:T(1,128)S(1)} %copy-done.37, s32[1]{0:T(128)S(6)} %copy.9.length_ref.refs_1_, bf16[512,512]{1,0:T(8,128)(2,1)} %bitcast.5.refs_2_, bf16[512,1024]{1,0:T(8,128)(2,1)S(1)} %copy-done.11, ...), custom_call_target="tpu_custom_call", output_to_operand_aliasing={{1}: (7, {})} | custom-call | tf_op jit(solution)/shard_map/middle1/pallas_call | solution.py:237
  179.8 56.5 %all_to_all.41 = bf16[64,8,2048]{2,1,0:T(8,128)(2,1)S(1)} all-to-all(bf16[64,8,2048]{2,1,0:T(8,128)(2,1)S(1)} %bitcast.22), channel_id=1, replica_groups={{0,1,2,3,4,5,6,7,8,9,10,11,12,13,14,15,16,17,18,19,20,21,22,23,24,25,26..., dimensions={0} | all-to-all | bytes 4194304 | tf_op jit(solution)/shard_map/all_to_all | solution.py:382
  238.6 9.9 %all-to-all-start.6 = ((bf16[64,8,512]{2,1,0:T(8,128)(2,1)}), bf16[64,8,512]{2,1,0:T(8,128)(2,1)}, u32[]{:S(2)}, u32[]{:S(2)}) async-start(bf16[64,8,512]{2,1,0:T(8,128)(2,1)} %bitcast.30), calls=%async_computation.6 | async-start | bytes 1048576 | tf_op jit(solution)/shard_map/all_to_all | solution.py:382
  248.5 10.5 %collective-permute-done.1.right_ref = bf16[512,1024]{1,0:T(8,128)(2,1)} collective-permute-done((bf16[512,1024]{1,0:T(8,128)(2,1)}, bf16[512,1024]{1,0:T(8,128)(2,1)}, u32[]{:S(2)}, u32[]{:S(2)}) %collective-permute-start.1) | collective-permute-done | bytes 1048608 | tf_op jit(solution)/shard_map/ppermute | solution.py:397
  263.1 12.4 %all-to-all-start.5 = ((bf16[64,8,512]{2,1,0:T(8,128)(2,1)}), bf16[64,8,512]{2,1,0:T(8,128)(2,1)}, u32[]{:S(2)}, u32[]{:S(2)}) async-start(bf16[64,8,512]{2,1,0:T(8,128)(2,1)} %bitcast.25), calls=%async_computation.5 | async-start | bytes 1048576 | tf_op jit(solution)/shard_map/all_to_all | solution.py:382
  278.8 3.4 last_own.1.own_ref
  283.1 7.0 %all-to-all-done.5 = bf16[64,8,512]{2,1,0:T(8,128)(2,1)} async-done(((bf16[64,8,512]{2,1,0:T(8,128)(2,1)}), bf16[64,8,512]{2,1,0:T(8,128)(2,1)}, u32[]{:S(2)}, u32[]{:S(2)}) %all-to-all-start.5) | async-done | bytes 524320 | tf_op jit(solution)/shard_map/all_to_all | solution.py:382
  294.4 4.5 %last_peer.1 = (bf16[1024,256]{1,0:T(8,128)(2,1)S(1)}, bf16[1024,256]{1,0:T(8,128)(2,1)S(1)}) custom-call(bf16[512,512]{1,0:T(8,128)(2,1)} %bitcast.11.back_ref, bf16[512,512]{1,0:T(8,128)(2,1)S(1)} %copy-done.28, f32[512,512]{1,0:T(8,128)S(1)} %copy-done.24, bf16[2,512,512]{2,1,0:T(8,128)(2,1)S(1)} %get-tuple-element.34.refs_5_.wo_ref, ...), custom_call_target="tpu_custom_call" | custom-call | tf_op jit(solution)/shard_map/last_peer/pallas_call | solution.py:290
  299.7 7.7 %collective-permute-start.2 = (bf16[1024,256]{1,0:T(8,128)(2,1)S(1)}, bf16[1024,256]{1,0:T(8,128)(2,1)S(1)}, u32[]{:S(2)}, u32[]{:S(2)}) collective-permute-start(bf16[1024,256]{1,0:T(8,128)(2,1)S(1)} %get-tuple-element.47), channel_id=1, source_target_pairs={{0,128},{128,0},{1,129},{129,1},{2,130},{130,2},{3,131},{131,3},{4... | collective-permute-start | bytes 1572872 | tf_op jit(solution)/shard_map/ppermute | solution.py:410
  311.9 25.7 %all_to_all.42 = bf16[128,8,256]{2,1,0:T(8,128)(2,1)S(1)} all-to-all(bf16[128,8,256]{2,1,0:T(8,128)(2,1)} %bitcast.31), channel_id=1, replica_groups={{0,8,16,24,32,40,48,56,64,72,80,88,96,104,112,120,1,9,17,25,33,41,49,57..., dimensions={0} | all-to-all | bytes 1048576 | tf_op jit(solution)/shard_map/all_to_all | solution.py:382
  337.6 2.8 collective-permute-start.3
  341.9 3.1 final.1
  (94 shorter events, 48.0 us)
Async XLA Ops:
  0.0 2.2 copy-start.12
  5.4 8.4 %copy-start.38 = (bf16[2,64,320]{2,1,0:T(8,128)(2,1)S(1)}, bf16[2,64,320]{2,1,0:T(8,128)(2,1)}, u32[]{:S(2)}) copy-start(bf16[2,64,320]{2,1,0:T(8,128)(2,1)} %proj_ref.1) | copy-start | bytes 245764
  5.4 8.4 %copy-start.39 = (bf16[2,64,64]{2,1,0:T(8,128)(2,1)S(1)}, bf16[2,64,64]{2,1,0:T(8,128)(2,1)}, u32[]{:S(2)}) copy-start(bf16[2,64,64]{2,1,0:T(8,128)(2,1)} %out_ref.1) | copy-start | bytes 49156
  5.4 35.6 %all-to-all-start = ((bf16[16,64,1024]{2,1,0:T(8,128)(2,1)}), bf16[16,64,1024]{2,1,0:T(8,128)(2,1)S(1)}, u32[]{:S(2)}, u32[]{:S(2)}) async-start(bf16[16,64,1024]{2,1,0:T(8,128)(2,1)} %copy-done.3), calls=%async_computation | async-start | bytes 4194304 | tf_op jit(solution)/shard_map/all_to_all | solution.py:390
  14.5 26.5 %copy-start.37 = (s32[1,8]{1,0:T(1,128)S(1)}, s32[1,8]{1,0:T(1,128)}, u32[]{:S(2)}) copy-start(s32[1,8]{1,0:T(1,128)} %refs_0_.3) | copy-start | bytes 100
  41.0 2.5 copy-start
  43.5 1.6 copy-start.15
  54.8 58.7 %copy-start.4 = (f32[512,1024]{1,0:T(8,128)}, f32[512,1024]{1,0:T(8,128)S(1)}, u32[]{:S(2)}) copy-start(f32[512,1024]{1,0:T(8,128)S(1)} %get-tuple-element.33.refs_4_) | copy-start | bytes 6291460
  54.8 58.6 %copy-start.9 = (bf16[512,1024]{1,0:T(8,128)(2,1)}, bf16[512,1024]{1,0:T(8,128)(2,1)S(1)}, u32[]{:S(2)}) copy-start(bf16[512,1024]{1,0:T(8,128)(2,1)S(1)} %get-tuple-element.32.refs_3_) | copy-start | bytes 3145732
  115.7 24.6 %collective-permute-start = (bf16[512,1024]{1,0:T(8,128)(2,1)}, bf16[512,1024]{1,0:T(8,128)(2,1)}, u32[]{:S(2)}, u32[]{:S(2)}) collective-permute-start(bf16[512,1024]{1,0:T(8,128)(2,1)} %get-tuple-element.31), channel_id=1, source_target_pairs={{0,32},{1,33},{2,34},{3,35},{4,36},{5,37},{6,38},{7,39},{8,40},{9,... | collective-permute-start | bytes 3145736 | tf_op jit(solution)/shard_map/ppermute | solution.py:397
  115.7 27.3 %all-to-all-start.3 = ((bf16[64,8,512]{2,1,0:T(8,128)(2,1)}), bf16[64,8,512]{2,1,0:T(8,128)(2,1)}, u32[]{:S(2)}, u32[]{:S(2)}) async-start(bf16[64,8,512]{2,1,0:T(8,128)(2,1)} %bitcast.29), calls=%async_computation.3 | async-start | bytes 1048576 | tf_op jit(solution)/shard_map/all_to_all | solution.py:382
  143.0 26.3 %all-to-all-start.2 = ((bf16[64,8,512]{2,1,0:T(8,128)(2,1)}), bf16[64,8,512]{2,1,0:T(8,128)(2,1)}, u32[]{:S(2)}, u32[]{:S(2)}) async-start(bf16[64,8,512]{2,1,0:T(8,128)(2,1)} %bitcast.24), calls=%async_computation.2 | async-start | bytes 1048576 | tf_op jit(solution)/shard_map/all_to_all | solution.py:382
  154.9 2.5 copy-start.1
  157.4 1.6 copy-start.5
  160.2 9.1 %copy-start.6 = (f32[512,1024]{1,0:T(8,128)S(1)}, f32[512,1024]{1,0:T(8,128)}, u32[]{:S(2)}) copy-start(f32[512,1024]{1,0:T(8,128)} %copy-done.4) | copy-start | bytes 6291460
  169.3 2.5 copy-start.2
  179.8 56.5 %copy-start.23 = (f32[512,512]{1,0:T(8,128)}, f32[512,512]{1,0:T(8,128)S(1)}, u32[]{:S(2)}) copy-start(f32[512,512]{1,0:T(8,128)S(1)} %get-tuple-element.40.gate_ref) | copy-start | bytes 3145732
  179.8 56.5 %copy-start.27 = (bf16[512,512]{1,0:T(8,128)(2,1)}, bf16[512,512]{1,0:T(8,128)(2,1)S(1)}, u32[]{:S(2)}) copy-start(bf16[512,512]{1,0:T(8,128)(2,1)S(1)} %get-tuple-element.39.cur_ref) | copy-start | bytes 1572868
  238.6 20.4 %collective-permute-start.1 = (bf16[512,1024]{1,0:T(8,128)(2,1)}, bf16[512,1024]{1,0:T(8,128)(2,1)}, u32[]{:S(2)}, u32[]{:S(2)}) collective-permute-start(bf16[512,1024]{1,0:T(8,128)(2,1)} %get-tuple-element.38), channel_id=1, source_target_pairs={{0,32},{1,33},{2,34},{3,35},{4,36},{5,37},{6,38},{7,39},{8,40},{9,... | collective-permute-start | bytes 3145736 | tf_op jit(solution)/shard_map/ppermute | solution.py:397
  238.6 24.5 %all-to-all-start.6 = ((bf16[64,8,512]{2,1,0:T(8,128)(2,1)}), bf16[64,8,512]{2,1,0:T(8,128)(2,1)}, u32[]{:S(2)}, u32[]{:S(2)}) async-start(bf16[64,8,512]{2,1,0:T(8,128)(2,1)} %bitcast.30), calls=%async_computation.6 | async-start | bytes 1048576 | tf_op jit(solution)/shard_map/all_to_all | solution.py:382
  263.1 27.0 %all-to-all-start.5 = ((bf16[64,8,512]{2,1,0:T(8,128)(2,1)}), bf16[64,8,512]{2,1,0:T(8,128)(2,1)}, u32[]{:S(2)}, u32[]{:S(2)}) async-start(bf16[64,8,512]{2,1,0:T(8,128)(2,1)} %bitcast.25), calls=%async_computation.5 | async-start | bytes 1048576 | tf_op jit(solution)/shard_map/all_to_all | solution.py:382
  278.8 11.3 %copy-start.13 = (bf16[1024,1024]{1,0:T(8,128)(2,1)S(1)}, bf16[1024,1024]{1,0:T(8,128)(2,1)}, u32[]{:S(2)}) copy-start(bf16[1024,1024]{1,0:T(8,128)(2,1)} %get-tuple-element.45.pj_ref) | copy-start | bytes 6291460
  299.7 9.2 %collective-permute-start.2 = (bf16[1024,256]{1,0:T(8,128)(2,1)S(1)}, bf16[1024,256]{1,0:T(8,128)(2,1)S(1)}, u32[]{:S(2)}, u32[]{:S(2)}) collective-permute-start(bf16[1024,256]{1,0:T(8,128)(2,1)S(1)} %get-tuple-element.47), channel_id=1, source_target_pairs={{0,128},{128,0},{1,129},{129,1},{2,130},{130,2},{3,131},{131,3},{4... | collective-permute-start | bytes 1572872 | tf_op jit(solution)/shard_map/ppermute | solution.py:410
  337.6 4.3 %collective-permute-start.3 = (bf16[1024,256]{1,0:T(8,128)(2,1)S(1)}, bf16[1024,256]{1,0:T(8,128)(2,1)S(1)}, u32[]{:S(2)}, u32[]{:S(2)}) collective-permute-start(bf16[1024,256]{1,0:T(8,128)(2,1)S(1)} %bitcast.27), channel_id=1, source_target_pairs={{0,128},{128,0},{1,129},{129,1},{2,130},{130,2},{3,131},{131,3},{4... | collective-permute-start | bytes 1572872 | tf_op jit(solution)/shard_map/ppermute | solution.py:412
  (27 other events, 27.4 us)

commit v4 on v3

v4 whole, which is shorter than its diff:
```python
import functools

import jax
import jax.numpy as jnp
from jax import lax
from jax.experimental import pallas as pl
from jax.experimental.pallas import tpu as pltpu
from jax.sharding import PartitionSpec as P

CH = 64
CZ = 128
CROP = 1024
TILE = 128
NLAYER = 2
FULL = 2048
ROWS = 8
EPSILON = 1e-05
BF = jnp.bfloat16
F32 = jnp.float32

PLANE = [[s * 8 + z for s in range(16)] for z in range(8)]
SAME_X0 = [
    [(x1 * 2 + x0) * 32 + y * 8 + z for x1 in range(2) for y in range(4) for z in range(8)]
    for x0 in range(2)
]
BY_Z = [[s * 8 + z for z in range(8) for s in range(16)]]
X0_PAIRS = [(r, r ^ 32) for r in range(128)]
CORES = [(0, 1), (1, 0)]
VMEM_LIMIT = 20 * 1024 * 1024


def in_vmem(*arrays):
    return [pltpu.with_memory_space_constraint(array, pltpu.VMEM) for array in arrays]


def in_hbm(*arrays):
    return [pltpu.with_memory_space_constraint(array, pltpu.HBM) for array in arrays]


def iota(shape, dim):
    return lax.broadcasted_iota(jnp.int32, shape, dim)


def onehot(mask):
    return jnp.where(mask, 1.0, 0.0).astype(BF)


def dot(a, b):
    return jnp.dot(a, b, preferred_element_type=F32)


def dot_nt(a, b):
    return lax.dot_general(a, b, (((1,), (1,)), ((), ())), preferred_element_type=F32)


def dot_tn(a, b):
    return lax.dot_general(a, b, (((0,), (0,)), ((), ())), preferred_element_type=F32)


def lane_token(lane):
    x0 = (lax.axis_index("row") // 32) % 2
    return (
        (lane % 8) * 128
        + ((lane // 8) % 8) * 16
        + ((lane // 256) % 2) * 8
        + ((lane // 512) ^ x0) * 4
        + ((lane // 64) % 4)
    )


def weights_kernel(proj_ref, out_ref, final_ref, wp_ref, wu_ref, wf_ref, prow_ref, q_ref, pj_ref, sel_ref):
    core = lax.axis_index("tmpl")
    spread = onehot(iota((CH, 512), 0) == iota((CH, 512), 1) // 8)
    repeat = onehot(iota((512, CH), 0) // 8 == iota((512, CH), 1))
    diag = iota((512, 512), 0) % 8 == iota((512, 512), 1) % 8
    for layer in range(NLAYER):
        for group in range(5):
            w = proj_ref[layer, :, group * CH : (group + 1) * CH]
            wide = dot_tn(w, spread).astype(BF)
            big = dot(repeat, wide)
            big = jnp.where(diag, big, 0.0).astype(BF)
            if group < 4:
                wp_ref[layer, group * 512 : (group + 1) * 512, :] = big
            else:
                wu_ref[layer, :512, :] = big
        wide = dot_tn(out_ref[layer], spread).astype(BF)
        wu_ref[layer, 512:, :] = jnp.where(diag, dot(repeat, wide), 0.0).astype(BF)
    down = onehot(iota((512, CZ), 0) % CZ == iota((512, CZ), 1))
    across = onehot(iota((CH, 256), 0) == iota((CH, 256), 1) % CH)
    tall = dot_nt(down, final_ref[...]).astype(BF)
    block = iota((512, 256), 0) // CZ == iota((512, 256), 1) // CH
    wf_ref[...] = jnp.where(block, dot(tall, across), 0.0).astype(BF)
    r0, c0 = iota((512, 512), 0), iota((512, 512), 1)
    prow_ref[...] = onehot((r0 // 8 == c0 % CH) & (r0 % 8 == c0 // CH))
    half = (r0 // 256) ^ core
    sel_ref[...] = onehot((r0 % CH == c0 // 8) & (half * 4 + (r0 // CH) % 4 == c0 % 8))
    r1, c1 = iota((CROP, CROP), 0), iota((CROP, CROP), 1)
    token = lane_token(c1)
    q_ref[...] = onehot(r1 == token)
    dest = r1 // 8
    pj_ref[...] = onehot(((dest % 16) * 8 + dest // 16) * 8 + r1 % 8 == token)


def make_weights(proj_weight, out_weight, final_weight):
    shapes = [
        (NLAYER, 2048, 512), (NLAYER, 1024, 512), (512, 256), (512, 512),
        (CROP, CROP), (CROP, CROP), (512, 512),
    ]
    return pl.pallas_call(
        weights_kernel,
        out_shape=[pltpu.VMEM(shape, BF) if index in (1, 2, 6) else pltpu.HBM(shape, BF) for index, shape in enumerate(shapes)],
        compiler_params=pltpu.CompilerParams(vmem_limit_bytes=40 * 1024 * 1024),
        cost_estimate=pl.CostEstimate(flops=2 * 10**9, bytes_accessed=12 * 2**20, transcendentals=0),
        name="weights",
    )(proj_weight, out_weight, final_weight)


def crop_kernel(crop_ref, x_ref, o_ref):
    for a in range(8):
        start = pl.multiple_of(crop_ref[0, a] * TILE, TILE)
        o_ref[:, :, a * TILE : (a + 1) * TILE] = x_ref[:, :, pl.ds(start, TILE)]


def crop_columns(crop_tiles, pair):
    return pl.pallas_call(
        crop_kernel,
        grid_spec=pltpu.PrefetchScalarGridSpec(
            num_scalar_prefetch=1,
            grid=(4,),
            in_specs=[pl.BlockSpec((4, CH, FULL), lambda m, crop: (m, 0, 0))],
            out_specs=pl.BlockSpec((4, CH, CROP), lambda m, crop: (m, 0, 0)),
        ),
        out_shape=pltpu.HBM((16, CH, CROP), BF),
        compiler_params=pltpu.CompilerParams(vmem_limit_bytes=VMEM_LIMIT),
        name="crop",
    )(crop_tiles, *in_hbm(pair))


def norm_channels(values):
    rows, lanes = values.shape
    cube = values.reshape(CH, ROWS, lanes)
    center = cube - (jnp.sum(cube, axis=0, keepdims=True) * (1.0 / CH))
    spread = jnp.sum(center * center, axis=0, keepdims=True) * (1.0 / CH)
    return (center * lax.rsqrt(spread + EPSILON)).reshape(rows, lanes)


def sigmoid(values):
    return 0.5 * jnp.tanh(0.5 * values) + 0.5


def pair_mask(crop_ref, length_ref, lanes, start):
    chip = lax.axis_index("row")
    inside = (chip % 8) * 16 + chip // 8
    length = length_ref[0]
    lane = iota((ROWS, lanes), 1) + start
    row = iota((ROWS, lanes), 0)
    token = lane_token(lane)
    col_pos = jnp.zeros((ROWS, lanes), jnp.int32)
    row_pos = jnp.zeros((ROWS, lanes), jnp.int32)
    for a in range(8):
        base = crop_ref[0, a] * TILE
        col_pos = jnp.where(lane % 8 == a, base, col_pos)
        row_pos = jnp.where(row == a, base, row_pos)
    col_pos = col_pos + token % TILE
    row_pos = row_pos + inside
    return jnp.where((col_pos < length) & (row_pos < length), 1.0, 0.0)


def project(current, wp, mask, both_ref):
    lanes = current.shape[1]
    normed = norm_channels(current).astype(BF)
    wide = jnp.broadcast_to(mask[None], (CH, ROWS, lanes)).reshape(512, lanes)
    gate_a = dot(wp[0:512], normed)
    value_a = dot(wp[512:1024], normed)
    both_ref[:, :lanes] = (sigmoid(gate_a) * value_a * wide).astype(BF)
    gate_b = dot(wp[1024:1536], normed)
    value_b = dot(wp[1536:2048], normed)
    both_ref[:, lanes:] = (sigmoid(gate_b) * value_b * wide).astype(BF)


BLOCK = 256
ANYWHERE = pl.BlockSpec(memory_space=pl.ANY)
STEPS = CROP // BLOCK
HALF_STEPS = STEPS // 2
BOTH = pltpu.HBM((512, 2 * CROP), BF)


def when_first(step, action):
    @pl.when(step == 0)
    def _():
        action()


def first_kernel(crop_ref, length_ref, got_ref, prow_ref, q_ref, wp_hbm, cur_ref, both_ref, rows_ref, wp_ref, sem):
    step = pl.program_id(0)
    load = pltpu.make_async_copy(wp_hbm.at[0], wp_ref, sem)

    @pl.when(step == 0)
    def _():
        load.start()
        parts = jnp.concatenate([got_ref[crop_ref[0, a]] for a in range(8)], axis=0)
        rows_ref[...] = dot(prow_ref[...], parts).astype(BF)

    current = dot(rows_ref[...], q_ref[...])
    cur_ref[...] = current.astype(BF)
    mask = pair_mask(crop_ref, length_ref, BLOCK, step * BLOCK)
    when_first(step, load.wait)
    project(current, wp_ref, mask, both_ref)


def full(shape):
    return pl.BlockSpec(shape, lambda step, *_: (0,) * len(shape), pipeline_mode=pl.Buffered(1))


def lanes_of(rows, lanes=BLOCK, offset=0):
    return pl.BlockSpec((rows, lanes), lambda step, *_: (0, step + offset))


def layer_weight(rows, layer):
    return pl.BlockSpec((1, rows, 512), lambda step, *_: (layer, 0, 0), pipeline_mode=pl.Buffered(1))


def first_projection(crop_tiles, full_length, got, prow, q, wp):
    return pl.pallas_call(
        first_kernel,
        grid_spec=pltpu.PrefetchScalarGridSpec(
            num_scalar_prefetch=2,
            grid=(STEPS,),
            in_specs=[full((16, CH, CROP)), full((512, 512)), lanes_of(CROP), ANYWHERE],
            out_specs=[lanes_of(512), lanes_of(512, 2 * BLOCK)],
            scratch_shapes=[pltpu.VMEM((512, CROP), BF), pltpu.VMEM((2048, 512), BF), pltpu.SemaphoreType.DMA],
        ),
        out_shape=[pltpu.HBM((512, CROP), BF), BOTH],
        compiler_params=pltpu.CompilerParams(vmem_limit_bytes=VMEM_LIMIT),
        name="first",
    )(crop_tiles, full_length, *in_hbm(got, prow, q, wp))


def update(back_ref, cur_ref, wu):
    current = cur_ref[...].astype(F32)
    gate = sigmoid(dot(wu[:512], norm_channels(current).astype(BF)))
    normed = norm_channels(back_ref[...].astype(F32)).astype(BF)
    return (current + gate * dot(wu[512:], normed)).astype(BF)


def middle_kernel(half, layer, *refs):
    crop_ref, length_ref, back_ref, cur_ref, wu_ref, wp_hbm = refs[:6]
    next_ref, both_ref, wp_ref, sem = refs[-4:]
    step = pl.program_id(0)
    load = pltpu.make_async_copy(wp_hbm.at[layer + 1], wp_ref, sem)
    when_first(step, load.start)
    current = update(back_ref, cur_ref, wu_ref[0])
    next_ref[...] = current
    start = half * 512 + step * BLOCK
    mask = pair_mask(crop_ref, length_ref, BLOCK, start)
    when_first(step, load.wait)
    project(current.astype(F32), wp_ref, mask, both_ref)


def middle_half(half, crop_tiles, full_length, back, current, wu, wp, layer, both):
    offset = half * HALF_STEPS
    aliased = [] if both is None else [both]
    return pl.pallas_call(
        functools.partial(middle_kernel, half, layer),
        grid_spec=pltpu.PrefetchScalarGridSpec(
            num_scalar_prefetch=2,
            grid=(HALF_STEPS,),
            in_specs=[
                lanes_of(512), lanes_of(512, offset=offset),
                layer_weight(1024, layer), ANYWHERE,
            ]
            + [ANYWHERE] * len(aliased),
            out_specs=[lanes_of(512), lanes_of(512, 2 * BLOCK, offset)],
            scratch_shapes=[pltpu.VMEM((2048, 512), BF), pltpu.SemaphoreType.DMA],
        ),
        out_shape=[pltpu.HBM((512, 512), BF), BOTH],
        input_output_aliases={6: 1} if aliased else {},
        compiler_params=pltpu.CompilerParams(vmem_limit_bytes=VMEM_LIMIT),
        name="middle" + str(half),
    )(crop_tiles, full_length, *in_hbm(back, current), *in_vmem(wu), *in_hbm(wp), *aliased)


def chosen_rows(back_ref, cur_ref, wu_ref, sel_ref):
    current = update(back_ref, cur_ref, wu_ref[0])
    normed = norm_channels(current.astype(F32)).astype(BF)
    return dot(sel_ref[...], normed).astype(BF)


def last_own_kernel(back_ref, cur_ref, wu_ref, sel_ref, chosen_ref):
    chosen_ref[...] = chosen_rows(back_ref, cur_ref, wu_ref, sel_ref)


def last_peer_kernel(back_ref, cur_ref, wu_ref, sel_ref, own_ref, pj_hbm, mine_ref, other_ref, part_ref, pj_ref, sem):
    step = pl.program_id(0)
    load = pltpu.make_async_copy(pj_hbm, pj_ref, sem)
    when_first(step, load.start)
    part_ref[step] = chosen_rows(back_ref, cur_ref, wu_ref, sel_ref)

    @pl.when(step == HALF_STEPS - 1)
    def _():
        load.wait()
        chosen = jnp.concatenate([own_ref[...]] + [part_ref[k] for k in range(HALF_STEPS)], axis=1)
        mine_ref[...] = dot_nt(pj_ref[...], chosen[:256]).astype(BF)
        other_ref[...] = dot_nt(pj_ref[...], chosen[256:]).astype(BF)


def last_own(back, current, wu, sel, layer):
    return pl.pallas_call(
        last_own_kernel,
        grid=(HALF_STEPS,),
        in_specs=[lanes_of(512)] * 2 + [layer_weight(1024, layer), full((512, 512))],
        out_specs=lanes_of(512),
        out_shape=pltpu.HBM((512, 512), BF),
        compiler_params=pltpu.CompilerParams(vmem_limit_bytes=VMEM_LIMIT),
        name="last_own",
    )(*in_hbm(back, current), *in_vmem(wu, sel))


def last_peer(back, current, wu, sel, own, pj, layer):
    return pl.pallas_call(
        last_peer_kernel,
        grid=(HALF_STEPS,),
        in_specs=[lanes_of(512)] * 2
        + [layer_weight(1024, layer), full((512, 512)), full((512, 512)), ANYWHERE],
        out_specs=[full((CROP, 256))] * 2,
        out_shape=[jax.ShapeDtypeStruct((CROP, 256), BF)] * 2,
        scratch_shapes=[
            pltpu.VMEM((HALF_STEPS, 512, BLOCK), BF), pltpu.VMEM((CROP, CROP), BF), pltpu.SemaphoreType.DMA,
        ],
        compiler_params=pltpu.CompilerParams(vmem_limit_bytes=VMEM_LIMIT),
        name="last_peer",
    )(*in_hbm(back, current), *in_vmem(wu, sel), *in_hbm(own, pj))


def own_products_kernel(both_ref, out_ref, right_ref, sum_ref):
    step = pl.program_id(0)
    right = both_ref[:, BLOCK:]
    right_ref[...] = right
    part = dot_nt(both_ref[:, :BLOCK], right)
    add_products(step, part, out_ref, sum_ref)


def add_products(step, part, out_ref, sum_ref):
    @pl.when(step == 0)
    def _():
        sum_ref[...] = part

    @pl.when((step > 0) & (step < STEPS - 1))
    def _():
        sum_ref[...] += part

    @pl.when(step == STEPS - 1)
    def _():
        out_ref[...] = (sum_ref[...] + part).astype(BF)


def own_products(both):
    return pl.pallas_call(
        own_products_kernel,
        grid=(STEPS,),
        in_specs=[lanes_of(512, 2 * BLOCK)],
        out_specs=[full((512, 512)), lanes_of(512)],
        out_shape=[pltpu.HBM((512, 512), BF), pltpu.HBM((512, CROP), BF)],
        scratch_shapes=[pltpu.VMEM((512, 512), F32)],
        compiler_params=pltpu.CompilerParams(vmem_limit_bytes=VMEM_LIMIT),
        cost_estimate=pl.CostEstimate(flops=2**29, bytes_accessed=4 * 2**20, transcendentals=0),
        name="own_products",
    )(*in_hbm(both))


def peer_products_kernel(left_ref, right_ref, out_ref, sum_ref):
    add_products(pl.program_id(0), dot_nt(left_ref[...], right_ref[...]), out_ref, sum_ref)


def peer_products(both, right):
    return pl.pallas_call(
        peer_products_kernel,
        grid=(STEPS,),
        in_specs=[
            pl.BlockSpec((512, BLOCK), lambda step: (0, ((step + HALF_STEPS) % STEPS) * 2)),
            lanes_of(512),
        ],
        out_specs=full((512, 512)),
        out_shape=pltpu.HBM((512, 512), BF),
        scratch_shapes=[pltpu.VMEM((512, 512), F32)],
        compiler_params=pltpu.CompilerParams(vmem_limit_bytes=VMEM_LIMIT),
        cost_estimate=pl.CostEstimate(flops=2**29, bytes_accessed=4 * 2**20, transcendentals=0),
        name="peer_products",
    )(*in_hbm(both, right))


def hidden_features(mine, peer):
    total = mine.astype(F32) + peer.astype(F32)
    return jnp.maximum(total * 0.5, 0.0).astype(BF)


def final_kernel(mine_ref, peer_ref, wf_ref, out_ref, tall0_ref, tall1_ref, wide_ref):
    core = lax.axis_index("tmpl")
    wf = wf_ref[...]
    for source, ref in enumerate((mine_ref, peer_ref)):
        half = core if source == 0 else 1 - core
        tall0_ref[...] = ref[:, :128].astype(F32)
        tall1_ref[...] = ref[:, 128:].astype(F32)
        for j in range(8):
            rows = jnp.concatenate(
                [tall0_ref[pl.ds(j, 128, stride=8), :], tall1_ref[pl.ds(j, 128, stride=8), :]], axis=1
            ).astype(BF)
            result = dot_nt(wf, rows)
            for a in range(4):
                wide_ref[half * 4 + a, pl.ds(j, CZ, stride=8), :] = result[a * CZ : (a + 1) * CZ]
    for a in range(8):
        out_ref[:, a * TILE : (a + 1) * TILE] = wide_ref[a].astype(BF)


def final_projection(mine, peer, wf):
    return pl.pallas_call(
        final_kernel,
        out_shape=jax.ShapeDtypeStruct((CZ * 8, CROP), BF),
        scratch_shapes=[
            pltpu.VMEM((CROP, 128), F32), pltpu.VMEM((CROP, 128), F32), pltpu.VMEM((8, CZ * 8, TILE), F32)
        ],
        compiler_params=pltpu.CompilerParams(vmem_limit_bytes=VMEM_LIMIT),
        name="final",
    )(mine, peer, wf)


def exchange(values, groups, count):
    cube = values.reshape(count, -1, values.shape[-1])
    moved = lax.all_to_all(cube, "row", 0, 0, axis_index_groups=groups, tiled=True)
    return moved.reshape(values.shape)


def on_device(pair_maps, crop_tiles, full_length, proj_weight, out_weight, final_weight):
    wp, wu, wf, prow, q, pj, sel = make_weights(proj_weight, out_weight, final_weight)
    pair = jnp.transpose(pair_maps[0], (0, 2, 1))
    cropped = crop_columns(crop_tiles, pair)
    got = lax.all_to_all(cropped, "row", 0, 0, axis_index_groups=PLANE, tiled=True)
    current, both = first_projection(crop_tiles, full_length, got, prow, q, wp)
    currents = (current, current)
    for layer in range(NLAYER):
        gathered = exchange(both, SAME_X0, CH)
        products, right = own_products(gathered)
        back_own = exchange(products, SAME_X0, CH)
        right_peer = lax.ppermute(right, "row", X0_PAIRS)
        back_peer = exchange(peer_products(gathered, right_peer), SAME_X0, CH)
        if layer + 1 < NLAYER:
            scalars, weights = (crop_tiles, full_length), (wu, wp, layer)
            own, both = middle_half(0, *scalars, back_own, currents[0], *weights, None)
            peer, both = middle_half(1, *scalars, back_peer, currents[1], *weights, both)
            currents = (own, peer)
    chosen = last_own(back_own, currents[0], wu, sel, NLAYER - 1)
    mine, other = last_peer(back_peer, currents[1], wu, sel, chosen, pj, NLAYER - 1)
    hidden = hidden_features(mine, lax.ppermute(other, "tmpl", CORES))
    moved = exchange(hidden, BY_Z, 128)
    result = final_projection(moved, lax.ppermute(moved, "tmpl", CORES), wf)
    return result.reshape(CZ, 8, CROP)


def solution(mesh):
    placed = (P("tmpl", "row", None, None), P("tmpl", None), P(), P(), P(), P())
    return jax.shard_map(
        on_device, mesh=mesh, in_specs=placed, out_specs=P(None, "row", None), check_vma=False
    )
```

time: 347 us -> 338 us (0.974)
  local copies, waits for them, and re-layouts: 40.2 us -> 2.28 us
  Pallas kernels: 47.3 us -> 67.2 us
  waiting for transfers between devices: 53.6 us -> 66.7 us
  blocking collectives: 141 us -> 133 us
  starting transfers between devices: 62.2 us -> 66 us
    unnamed x84 -> x16, local copies, waits for them, and re-layouts: 40.2 us -> 2.28 us
    pallas_call x8 -> x7, Pallas kernels: 26.6 us -> 37.8 us  [the longest x2 13.2 us: middle_half(): pl.pallas_call(functools.partial(middle_kernel, half, layer), grid_spec=p...]
    all_to_all x4, waiting for transfers between devices: 8.93 us -> 18.8 us  [exchange(): lax.all_to_all(cube, 'row', 0, 0, axis_index_groups=groups, tiled=True)]
    all_to_all x3, blocking collectives: 141 us -> 133 us  [exchange(): lax.all_to_all(cube, 'row', 0, 0, axis_index_groups=groups, tiled=True)]
    ppermute x2, starting transfers between devices: 0.01 us -> 4.96 us  [on_device(): right_peer = lax.ppermute(right, 'row', X0_PAIRS)]
    pallas_call x1, Pallas kernels: 1.22 us -> 4.99 us  [crop_columns(): pl.pallas_call(crop_kernel, grid_spec=pltpu.PrefetchScalarGridSpec(num_sc...]
    all_to_all x1, waiting for transfers between devices: 16.3 us -> 19.9 us  [on_device(): lax.all_to_all(cropped, 'row', 0, 0, axis_index_groups=PLANE, tiled=True)]
  transfers between devices with their start and end apart: 9 -> 9, of which waited for: 8 -> 8; matrix products, arithmetic and copies ran while one was open for 0% -> 0% of each run, Pallas kernels for 6% -> 8%
where the time goes in v4:
time: 338 us; the launch traced here: 337 us
  blocking collectives  133 us (39%)
  Pallas kernels  67.2 us (20%)
  waiting for transfers between devices  66.7 us (20%)
  starting transfers between devices  66 us (20%)
    all_to_all x3, blocking collectives, exchange(): lax.all_to_all(cube, 'row', 0, 0, axis_index_groups=groups, tiled=True)  133 us
    all_to_all x4, starting transfers between devices, exchange(): lax.all_to_all(cube, 'row', 0, 0, axis_index_groups=groups, tiled=True)  42.6 us
    ppermute x2, waiting for transfers between devices, on_device(): right_peer = lax.ppermute(right, 'row', X0_PAIRS)  24.9 us
    all_to_all x1, waiting for transfers between devices, on_device(): lax.all_to_all(cropped, 'row', 0, 0, axis_index_groups=PLANE, tiled=True)  19.9 us
    all_to_all x4, waiting for transfers between devices, exchange(): lax.all_to_all(cube, 'row', 0, 0, axis_index_groups=groups, tiled=True)  18.8 us
    pallas_call x2, Pallas kernels, middle_half(): pl.pallas_call(functools.partial(middle_kernel, half, layer), grid_spec=p...  13.2 us
    pallas_call x1, Pallas kernels, first_projection(): pl.pallas_call(first_kernel, grid_spec=pltpu.PrefetchScalarGridSpec(num_s...  11.8 us
    pallas_call x2, Pallas kernels, own_products(): pl.pallas_call(own_products_kernel, grid=(STEPS,), in_specs=[lanes_of(512...  8.98 us
  transfers between devices with their start and end apart: 9, of which 8 were waited for; matrix products, arithmetic and copies ran while one was open for 0% of the time, Pallas kernels for 8%

profile of v4, /device:TPU:1, one launch (start us, length us, event | category | flops | bytes accessed | tf_op | source)
XLA Modules:
  0.0 336.5 jit_solution(10999275769012421015)
XLA Ops:
  0.7 5.0 %crop.1 = bf16[16,64,1024]{2,1,0:T(8,128)(2,1)} custom-call(s32[1,8]{1,0:T(1,128)S(1)} %copy-done, bf16[16,64,2048]{2,1,0:T(8,128)(2,1)} %bitcast.26), custom_call_target="tpu_custom_call" | custom-call | tf_op jit(solution)/shard_map/crop/pallas_call | solution.py:125
  5.7 7.8 %all-to-all-start = ((bf16[16,64,1024]{2,1,0:T(8,128)(2,1)}), bf16[16,64,1024]{2,1,0:T(8,128)(2,1)}, u32[]{:S(2)}, u32[]{:S(2)}) async-start(bf16[16,64,1024]{2,1,0:T(8,128)(2,1)} %crop.1), calls=%async_computation | async-start | bytes 4194304 | tf_op jit(solution)/shard_map/all_to_all | solution.py:437
  14.1 7.3 %weights.1 = (bf16[2,2048,512]{2,1,0:T(8,128)(2,1)}, bf16[2,1024,512]{2,1,0:T(8,128)(2,1)S(1)}, bf16[512,256]{1,0:T(8,128)(2,1)S(1)}, bf16[512,512]{1,0:T(8,128)...) custom-call(bf16[2,64,320]{2,1,0:T(8,128)(2,1)S(1)} %copy-done.2, ...), custom_call_target="tpu_custom_call" | custom-call | flops 2000000000 | bytes 12582912 | tf_op jit(solution)/shard_map/weights/pallas_call | solution.py:109
  21.4 19.9 %all-to-all-done.got_ref = bf16[16,64,1024]{2,1,0:T(8,128)(2,1)} async-done(((bf16[16,64,1024]{2,1,0:T(8,128)(2,1)}), bf16[16,64,1024]{2,1,0:T(8,128)(2,1)}, u32[]{:S(2)}, u32[]{:S(2)}) %all-to-all-start) | async-done | bytes 2097184 | tf_op jit(solution)/shard_map/all_to_all | solution.py:437
  41.3 11.8 %first.1 = (bf16[512,1024]{1,0:T(8,128)(2,1)}, bf16[512,2048]{1,0:T(8,128)(2,1)}) custom-call(s32[1,8]{1,0:T(1,128)S(1)} %copy-done.1, s32[1]{0:T(128)S(6)} %copy.9.length_ref.refs_1_, bf16[16,64,1024]{2,1,0:T(8,128)(2,1)} %all-to-all-done.got_ref, bf16[512,512]{1,0:T(8,128)(2,1)} %get-tuple-element.24.prow_ref, bf16[1024,1024]{1,0:T(8,128)(2,1)} %get-tuple-element.25.q_ref, ...), custom_call_target="tpu_custom_call" | custom-call | tf_op jit(solution)/shard_map/first/pallas_call | solution.py:224
  53.1 59.0 %all_to_all.40 = bf16[64,8,2048]{2,1,0:T(8,128)(2,1)} all-to-all(bf16[64,8,2048]{2,1,0:T(8,128)(2,1)} %bitcast.31), channel_id=1, replica_groups={{0,1,2,3,4,5,6,7,8,9,10,11,12,13,14,15,16,17,18,19,20,21,22,23,24,25,26..., dimensions={0} | all-to-all | bytes 4194304 | tf_op jit(solution)/shard_map/all_to_all | solution.py:429
  112.1 4.5 %own_products.2 = (bf16[512,512]{1,0:T(8,128)(2,1)}, bf16[512,1024]{1,0:T(8,128)(2,1)}) custom-call(bf16[512,2048]{1,0:T(8,128)(2,1)} %bitcast.21), custom_call_target="tpu_custom_call" | custom-call | flops 536870912 | bytes 4194304 | tf_op jit(solution)/shard_map/own_products/pallas_call | solution.py:358
  116.6 9.6 %all-to-all-start.3 = ((bf16[64,8,512]{2,1,0:T(8,128)(2,1)}), bf16[64,8,512]{2,1,0:T(8,128)(2,1)S(1)}, u32[]{:S(2)}, u32[]{:S(2)}) async-start(bf16[64,8,512]{2,1,0:T(8,128)(2,1)} %bitcast.33), calls=%async_computation.3 | async-start | bytes 1048576 | tf_op jit(solution)/shard_map/all_to_all | solution.py:429
  126.1 15.0 %collective-permute-done.right_ref = bf16[512,1024]{1,0:T(8,128)(2,1)} collective-permute-done((bf16[512,1024]{1,0:T(8,128)(2,1)}, bf16[512,1024]{1,0:T(8,128)(2,1)}, u32[]{:S(2)}, u32[]{:S(2)}) %collective-permute-start) | collective-permute-done | bytes 1048608 | tf_op jit(solution)/shard_map/ppermute | solution.py:444
  145.3 11.0 %all-to-all-start.2 = ((bf16[64,8,512]{2,1,0:T(8,128)(2,1)}), bf16[64,8,512]{2,1,0:T(8,128)(2,1)}, u32[]{:S(2)}, u32[]{:S(2)}) async-start(bf16[64,8,512]{2,1,0:T(8,128)(2,1)} %bitcast.29), calls=%async_computation.2 | async-start | bytes 1048576 | tf_op jit(solution)/shard_map/all_to_all | solution.py:429
  156.3 6.6 %middle0.1 = (bf16[512,512]{1,0:T(8,128)(2,1)}, bf16[512,2048]{1,0:T(8,128)(2,1)}) custom-call(s32[1,8]{1,0:T(1,128)S(1)} %copy-done.1, s32[1]{0:T(128)S(6)} %copy.9.length_ref.refs_1_, bf16[512,512]{1,0:T(8,128)(2,1)} %bitcast.27, bf16[512,1024]{1,0:T(8,128)(2,1)} %get-tuple-element.29.refs_3_, bf16[2,1024,512]{2,1,0:T(8,128)(2,1)S(1)} %get-tuple-element.30.refs_4_.wu_ref, ...), custom_call_target="tpu_custom_call" | custom-call | tf_op jit(solution)/shard_map/middle0/pallas_call | solution.py:263
  162.9 7.8 %all-to-all-done.2 = bf16[64,8,512]{2,1,0:T(8,128)(2,1)} async-done(((bf16[64,8,512]{2,1,0:T(8,128)(2,1)}), bf16[64,8,512]{2,1,0:T(8,128)(2,1)}, u32[]{:S(2)}, u32[]{:S(2)}) %all-to-all-start.2) | async-done | bytes 524320 | tf_op jit(solution)/shard_map/all_to_all | solution.py:429
  170.7 6.6 %middle1.1 = (bf16[512,512]{1,0:T(8,128)(2,1)}, bf16[512,2048]{1,0:T(8,128)(2,1)}) custom-call(s32[1,8]{1,0:T(1,128)S(1)} %copy-done.1, s32[1]{0:T(128)S(6)} %copy.9.length_ref.refs_1_, bf16[512,512]{1,0:T(8,128)(2,1)} %bitcast.5.refs_2_, bf16[512,1024]{1,0:T(8,128)(2,1)} %get-tuple-element.29.refs_3_, ...), custom_call_target="tpu_custom_call", output_to_operand_aliasing={{1}: (6, {})} | custom-call | tf_op jit(solution)/shard_map/middle1/pallas_call | solution.py:263
  177.3 49.1 %all_to_all.41 = bf16[64,8,2048]{2,1,0:T(8,128)(2,1)} all-to-all(bf16[64,8,2048]{2,1,0:T(8,128)(2,1)} %bitcast.25), channel_id=1, replica_groups={{0,1,2,3,4,5,6,7,8,9,10,11,12,13,14,15,16,17,18,19,20,21,22,23,24,25,26..., dimensions={0} | all-to-all | bytes 4194304 | tf_op jit(solution)/shard_map/all_to_all | solution.py:429
  226.3 4.5 %own_products.3 = (bf16[512,512]{1,0:T(8,128)(2,1)}, bf16[512,1024]{1,0:T(8,128)(2,1)}) custom-call(bf16[512,2048]{1,0:T(8,128)(2,1)} %bitcast.23), custom_call_target="tpu_custom_call" | custom-call | flops 536870912 | bytes 4194304 | tf_op jit(solution)/shard_map/own_products/pallas_call | solution.py:358
  230.8 5.0 %collective-permute-start.1 = (bf16[512,1024]{1,0:T(8,128)(2,1)}, bf16[512,1024]{1,0:T(8,128)(2,1)}, u32[]{:S(2)}, u32[]{:S(2)}) collective-permute-start(bf16[512,1024]{1,0:T(8,128)(2,1)} %get-tuple-element.34), channel_id=1, source_target_pairs={{0,32},{1,33},{2,34},{3,35},{4,36},{5,37},{6,38},{7,39},{8,40},{9,... | collective-permute-start | bytes 3145736 | tf_op jit(solution)/shard_map/ppermute | solution.py:444
  235.8 9.5 %all-to-all-start.6 = ((bf16[64,8,512]{2,1,0:T(8,128)(2,1)}), bf16[64,8,512]{2,1,0:T(8,128)(2,1)S(1)}, u32[]{:S(2)}, u32[]{:S(2)}) async-start(bf16[64,8,512]{2,1,0:T(8,128)(2,1)} %bitcast.34), calls=%async_computation.6 | async-start | bytes 1048576 | tf_op jit(solution)/shard_map/all_to_all | solution.py:429
  245.3 10.0 %collective-permute-done.1.right_ref = bf16[512,1024]{1,0:T(8,128)(2,1)} collective-permute-done((bf16[512,1024]{1,0:T(8,128)(2,1)}, bf16[512,1024]{1,0:T(8,128)(2,1)}, u32[]{:S(2)}, u32[]{:S(2)}) %collective-permute-start.1) | collective-permute-done | bytes 1048608 | tf_op jit(solution)/shard_map/ppermute | solution.py:444
  260.9 12.6 %all-to-all-start.5 = ((bf16[64,8,512]{2,1,0:T(8,128)(2,1)}), bf16[64,8,512]{2,1,0:T(8,128)(2,1)S(1)}, u32[]{:S(2)}, u32[]{:S(2)}) async-start(bf16[64,8,512]{2,1,0:T(8,128)(2,1)} %bitcast.30), calls=%async_computation.5 | async-start | bytes 1048576 | tf_op jit(solution)/shard_map/all_to_all | solution.py:429
  273.5 4.4 %last_own.1.own_ref = bf16[512,512]{1,0:T(8,128)(2,1)} custom-call(bf16[512,512]{1,0:T(8,128)(2,1)} %bitcast.32, bf16[512,512]{1,0:T(8,128)(2,1)} %get-tuple-element.38.cur_ref, bf16[2,1024,512]{2,1,0:T(8,128)(2,1)S(1)} %get-tuple-element.30.refs_4_.wu_ref, bf16[512,512]{1,0:T(8,128)(2,1)S(1)} %get-tuple-element.36.sel_ref), custom_call_target="tpu_custom_call" | custom-call | tf_op jit(solution)/shard_map/last_own/pallas_call | solution.py:308
  277.9 10.4 %all-to-all-done.5 = bf16[64,8,512]{2,1,0:T(8,128)(2,1)S(1)} async-done(((bf16[64,8,512]{2,1,0:T(8,128)(2,1)}), bf16[64,8,512]{2,1,0:T(8,128)(2,1)S(1)}, u32[]{:S(2)}, u32[]{:S(2)}) %all-to-all-start.5) | async-done | bytes 524320 | tf_op jit(solution)/shard_map/all_to_all | solution.py:429
  289.0 5.2 %last_peer.1 = (bf16[1024,256]{1,0:T(8,128)(2,1)S(1)}, bf16[1024,256]{1,0:T(8,128)(2,1)S(1)}) custom-call(bf16[512,512]{1,0:T(8,128)(2,1)} %bitcast.28, bf16[512,512]{1,0:T(8,128)(2,1)} %get-tuple-element.35.cur_ref, bf16[2,1024,512]{2,1,0:T(8,128)(2,1)S(1)} %get-tuple-element.30.refs_4_.wu_ref, bf16[512,512]{1,0:T(8,128)(2,1)S(1)} %get-tuple-element.36.sel_ref, ...), custom_call_target="tpu_custom_call" | custom-call | tf_op jit(solution)/shard_map/last_peer/pallas_call | solution.py:320
  294.2 7.9 %collective-permute-start.2 = (bf16[1024,256]{1,0:T(8,128)(2,1)S(1)}, bf16[1024,256]{1,0:T(8,128)(2,1)S(1)}, u32[]{:S(2)}, u32[]{:S(2)}) collective-permute-start(bf16[1024,256]{1,0:T(8,128)(2,1)S(1)} %get-tuple-element.41), channel_id=1, source_target_pairs={{0,128},{128,0},{1,129},{129,1},{2,130},{130,2},{3,131},{131,3},{4... | collective-permute-start | bytes 1572872 | tf_op jit(solution)/shard_map/ppermute | solution.py:453
  303.8 25.3 %all_to_all.42 = bf16[128,8,256]{2,1,0:T(8,128)(2,1)S(1)} all-to-all(bf16[128,8,256]{2,1,0:T(8,128)(2,1)S(1)} %fusion), channel_id=1, replica_groups={{0,8,16,24,32,40,48,56,64,72,80,88,96,104,112,120,1,9,17,25,33,41,49,57..., dimensions={0} | all-to-all | bytes 1048576 | tf_op jit(solution)/shard_map/all_to_all | solution.py:429
  (26 shorter events, 20.4 us)
Async XLA Ops:
  0.0 0.7 copy-start
  5.6 8.4 %copy-start.2 = (bf16[2,64,320]{2,1,0:T(8,128)(2,1)S(1)}, bf16[2,64,320]{2,1,0:T(8,128)(2,1)}, u32[]{:S(2)}) copy-start(bf16[2,64,320]{2,1,0:T(8,128)(2,1)} %proj_ref.1) | copy-start | bytes 245764
  5.6 8.4 %copy-start.3 = (bf16[2,64,64]{2,1,0:T(8,128)(2,1)S(1)}, bf16[2,64,64]{2,1,0:T(8,128)(2,1)}, u32[]{:S(2)}) copy-start(bf16[2,64,64]{2,1,0:T(8,128)(2,1)} %out_ref.1) | copy-start | bytes 49156
  5.6 8.5 %copy-start.4 = (bf16[64,128]{1,0:T(8,128)(2,1)S(1)}, bf16[64,128]{1,0:T(8,128)(2,1)}, u32[]{:S(2)}) copy-start(bf16[64,128]{1,0:T(8,128)(2,1)} %final_ref.1) | copy-start | bytes 49156
  5.7 35.6 %all-to-all-start = ((bf16[16,64,1024]{2,1,0:T(8,128)(2,1)}), bf16[16,64,1024]{2,1,0:T(8,128)(2,1)}, u32[]{:S(2)}, u32[]{:S(2)}) async-start(bf16[16,64,1024]{2,1,0:T(8,128)(2,1)} %crop.1), calls=%async_computation | async-start | bytes 4194304 | tf_op jit(solution)/shard_map/all_to_all | solution.py:437
  14.1 27.2 %copy-start.1 = (s32[1,8]{1,0:T(1,128)S(1)}, s32[1,8]{1,0:T(1,128)}, u32[]{:S(2)}) copy-start(s32[1,8]{1,0:T(1,128)} %refs_0_.3) | copy-start | bytes 100
  116.6 24.6 %collective-permute-start = (bf16[512,1024]{1,0:T(8,128)(2,1)}, bf16[512,1024]{1,0:T(8,128)(2,1)}, u32[]{:S(2)}, u32[]{:S(2)}) collective-permute-start(bf16[512,1024]{1,0:T(8,128)(2,1)} %get-tuple-element.28), channel_id=1, source_target_pairs={{0,32},{1,33},{2,34},{3,35},{4,36},{5,37},{6,38},{7,39},{8,40},{9,... | collective-permute-start | bytes 3145736 | tf_op jit(solution)/shard_map/ppermute | solution.py:444
  116.6 28.7 %all-to-all-start.3 = ((bf16[64,8,512]{2,1,0:T(8,128)(2,1)}), bf16[64,8,512]{2,1,0:T(8,128)(2,1)S(1)}, u32[]{:S(2)}, u32[]{:S(2)}) async-start(bf16[64,8,512]{2,1,0:T(8,128)(2,1)} %bitcast.33), calls=%async_computation.3 | async-start | bytes 1048576 | tf_op jit(solution)/shard_map/all_to_all | solution.py:429
  145.3 11.0 %copy-start.5 = (bf16[64,8,512]{2,1,0:T(8,128)(2,1)}, bf16[64,8,512]{2,1,0:T(8,128)(2,1)S(1)}, u32[]{:S(2)}) copy-start(bf16[64,8,512]{2,1,0:T(8,128)(2,1)S(1)} %all-to-all-done.3) | copy-start | bytes 1572868
  145.3 25.4 %all-to-all-start.2 = ((bf16[64,8,512]{2,1,0:T(8,128)(2,1)}), bf16[64,8,512]{2,1,0:T(8,128)(2,1)}, u32[]{:S(2)}, u32[]{:S(2)}) async-start(bf16[64,8,512]{2,1,0:T(8,128)(2,1)} %bitcast.29), calls=%async_computation.2 | async-start | bytes 1048576 | tf_op jit(solution)/shard_map/all_to_all | solution.py:429
  230.8 24.4 %collective-permute-start.1 = (bf16[512,1024]{1,0:T(8,128)(2,1)}, bf16[512,1024]{1,0:T(8,128)(2,1)}, u32[]{:S(2)}, u32[]{:S(2)}) collective-permute-start(bf16[512,1024]{1,0:T(8,128)(2,1)} %get-tuple-element.34), channel_id=1, source_target_pairs={{0,32},{1,33},{2,34},{3,35},{4,36},{5,37},{6,38},{7,39},{8,40},{9,... | collective-permute-start | bytes 3145736 | tf_op jit(solution)/shard_map/ppermute | solution.py:444
  235.8 24.3 %all-to-all-start.6 = ((bf16[64,8,512]{2,1,0:T(8,128)(2,1)}), bf16[64,8,512]{2,1,0:T(8,128)(2,1)S(1)}, u32[]{:S(2)}, u32[]{:S(2)}) async-start(bf16[64,8,512]{2,1,0:T(8,128)(2,1)} %bitcast.34), calls=%async_computation.6 | async-start | bytes 1048576 | tf_op jit(solution)/shard_map/all_to_all | solution.py:429
  260.1 0.8 copy-start.7
  260.9 27.4 %all-to-all-start.5 = ((bf16[64,8,512]{2,1,0:T(8,128)(2,1)}), bf16[64,8,512]{2,1,0:T(8,128)(2,1)S(1)}, u32[]{:S(2)}, u32[]{:S(2)}) async-start(bf16[64,8,512]{2,1,0:T(8,128)(2,1)} %bitcast.30), calls=%async_computation.5 | async-start | bytes 1048576 | tf_op jit(solution)/shard_map/all_to_all | solution.py:429
  288.2 0.8 copy-start.6
  294.2 9.4 %collective-permute-start.2 = (bf16[1024,256]{1,0:T(8,128)(2,1)S(1)}, bf16[1024,256]{1,0:T(8,128)(2,1)S(1)}, u32[]{:S(2)}, u32[]{:S(2)}) collective-permute-start(bf16[1024,256]{1,0:T(8,128)(2,1)S(1)} %get-tuple-element.41), channel_id=1, source_target_pairs={{0,128},{128,0},{1,129},{129,1},{2,130},{130,2},{3,131},{131,3},{4... | collective-permute-start | bytes 1572872 | tf_op jit(solution)/shard_map/ppermute | solution.py:453
  329.1 4.3 %collective-permute-start.3 = (bf16[1024,256]{1,0:T(8,128)(2,1)S(1)}, bf16[1024,256]{1,0:T(8,128)(2,1)S(1)}, u32[]{:S(2)}, u32[]{:S(2)}) collective-permute-start(bf16[1024,256]{1,0:T(8,128)(2,1)S(1)} %bitcast.19), channel_id=1, source_target_pairs={{0,128},{128,0},{1,129},{129,1},{2,130},{130,2},{3,131},{131,3},{4... | collective-permute-start | bytes 1572872 | tf_op jit(solution)/shard_map/ppermute | solution.py:455

commit v5 on v4

--- a/solution.py
+++ b/solution.py
@@ -68,8 +68,21 @@
     )
 
 
-def weights_kernel(proj_ref, out_ref, final_ref, wp_ref, wu_ref, wf_ref, prow_ref, q_ref, pj_ref, sel_ref):
-    core = lax.axis_index("tmpl")
+def weights_kernel(builder, *refs):
+    count = len(WEIGHT_SHAPES)
+    outs, scratch, sems = refs[-2 * count - 1 : -count - 1], refs[-count - 1 : -1], refs[-1]
+
+    @pl.when(lax.axis_index("tmpl") == builder)
+    def _():
+        build_weights(builder, *refs[:3], *scratch)
+        copies = [pltpu.make_async_copy(scratch[k], outs[k], sems.at[k]) for k in range(count)]
+        for copy in copies:
+            copy.start()
+        for copy in copies:
+            copy.wait()
+
+
+def build_weights(core, proj_ref, out_ref, final_ref, wp_ref, wu_ref, wf_ref, prow_ref, q_ref, pj_ref, sel_ref):
     spread = onehot(iota((CH, 512), 0) == iota((CH, 512), 1) // 8)
     repeat = onehot(iota((512, CH), 0) // 8 == iota((512, CH), 1))
     diag = iota((512, 512), 0) % 8 == iota((512, 512), 1) % 8
@@ -101,39 +114,48 @@
     pj_ref[...] = onehot(((dest % 16) * 8 + dest // 16) * 8 + r1 % 8 == token)
 
 
-def make_weights(proj_weight, out_weight, final_weight):
-    shapes = [
-        (NLAYER, 2048, 512), (NLAYER, 1024, 512), (512, 256), (512, 512),
-        (CROP, CROP), (CROP, CROP), (512, 512),
-    ]
-    return pl.pallas_call(
-        weights_kernel,
-        out_shape=[pltpu.VMEM(shape, BF) if index in (1, 2, 6) else pltpu.HBM(shape, BF) for index, shape in enumerate(shapes)],
-        compiler_params=pltpu.CompilerParams(vmem_limit_bytes=40 * 1024 * 1024),
+WEIGHT_SHAPES = [
+    (NLAYER, 2048, 512), (NLAYER, 1024, 512), (512, 256), (512, 512), (CROP, CROP), (CROP, CROP), (512, 512),
+]
+
+
+def make_weights(builder, params, earlier=()):
+    count = len(WEIGHT_SHAPES)
+    anywhere = pl.BlockSpec(memory_space=pl.ANY)
+    in_vmem_specs = [pl.BlockSpec(memory_space=pltpu.VMEM)] * 3
+    return pl.pallas_call(
+        functools.partial(weights_kernel, builder),
+        in_specs=in_vmem_specs + [anywhere] * len(earlier),
+        out_specs=[anywhere] * count,
+        out_shape=[pltpu.HBM(shape, BF) for shape in WEIGHT_SHAPES],
+        scratch_shapes=[pltpu.VMEM(shape, BF) for shape in WEIGHT_SHAPES] + [pltpu.SemaphoreType.DMA((count,))],
+        input_output_aliases={3 + k: k for k in range(len(earlier))},
+        compiler_params=pltpu.CompilerParams(vmem_limit_bytes=48 * 1024 * 1024),
         cost_estimate=pl.CostEstimate(flops=2 * 10**9, bytes_accessed=12 * 2**20, transcendentals=0),
-        name="weights",
-    )(proj_weight, out_weight, final_weight)
-
-
-def crop_kernel(crop_ref, x_ref, o_ref):
+        name="weights" + str(builder),
+    )(*params, *earlier)
+
+
+def crop_kernel(crop_ref, x_ref, after_ref, o_ref):
+    del after_ref
     for a in range(8):
         start = pl.multiple_of(crop_ref[0, a] * TILE, TILE)
         o_ref[:, :, a * TILE : (a + 1) * TILE] = x_ref[:, :, pl.ds(start, TILE)]
 
 
-def crop_columns(crop_tiles, pair):
+def crop_columns(crop_tiles, pair, after):
     return pl.pallas_call(
         crop_kernel,
         grid_spec=pltpu.PrefetchScalarGridSpec(
             num_scalar_prefetch=1,
             grid=(4,),
-            in_specs=[pl.BlockSpec((4, CH, FULL), lambda m, crop: (m, 0, 0))],
+            in_specs=[pl.BlockSpec((4, CH, FULL), lambda m, crop: (m, 0, 0)), pl.BlockSpec(memory_space=pl.ANY)],
             out_specs=pl.BlockSpec((4, CH, CROP), lambda m, crop: (m, 0, 0)),
         ),
         out_shape=pltpu.HBM((16, CH, CROP), BF),
         compiler_params=pltpu.CompilerParams(vmem_limit_bytes=VMEM_LIMIT),
         name="crop",
-    )(crop_tiles, *in_hbm(pair))
+    )(crop_tiles, *in_hbm(pair), after)
 
 
 def norm_channels(values):
@@ -233,7 +255,7 @@
         out_shape=[pltpu.HBM((512, CROP), BF), BOTH],
         compiler_params=pltpu.CompilerParams(vmem_limit_bytes=VMEM_LIMIT),
         name="first",
-    )(crop_tiles, full_length, *in_hbm(got, prow, q, wp))
+    )(crop_tiles, full_length, got, *in_hbm(prow, q, wp))
 
 
 def update(back_ref, cur_ref, wu):
@@ -277,7 +299,7 @@
         input_output_aliases={6: 1} if aliased else {},
         compiler_params=pltpu.CompilerParams(vmem_limit_bytes=VMEM_LIMIT),
         name="middle" + str(half),
-    )(crop_tiles, full_length, *in_hbm(back, current), *in_vmem(wu), *in_hbm(wp), *aliased)
+    )(crop_tiles, full_length, back, *in_hbm(current), *in_vmem(wu), *in_hbm(wp), *aliased)
 
 
 def chosen_rows(back_ref, cur_ref, wu_ref, sel_ref):
@@ -313,7 +335,7 @@
         out_shape=pltpu.HBM((512, 512), BF),
         compiler_params=pltpu.CompilerParams(vmem_limit_bytes=VMEM_LIMIT),
         name="last_own",
-    )(*in_hbm(back, current), *in_vmem(wu, sel))
+    )(back, *in_hbm(current), *in_vmem(wu, sel))
 
 
 def last_peer(back, current, wu, sel, own, pj, layer):
@@ -329,64 +351,43 @@
         ],
         compiler_params=pltpu.CompilerParams(vmem_limit_bytes=VMEM_LIMIT),
         name="last_peer",
-    )(*in_hbm(back, current), *in_vmem(wu, sel), *in_hbm(own, pj))
-
-
-def own_products_kernel(both_ref, out_ref, right_ref, sum_ref):
-    step = pl.program_id(0)
-    right = both_ref[:, BLOCK:]
+    )(back, *in_hbm(current), *in_vmem(wu, sel), *in_hbm(own, pj))
+
+
+def lane_blocks(both_ref, which, order):
+    starts = [(2 * block + which) * BLOCK for block in order]
+    return jnp.concatenate([both_ref[:, start : start + BLOCK] for start in starts], axis=1)
+
+
+def own_products_kernel(both_ref, out_ref, right_ref):
+    right = lane_blocks(both_ref, 1, range(STEPS))
     right_ref[...] = right
-    part = dot_nt(both_ref[:, :BLOCK], right)
-    add_products(step, part, out_ref, sum_ref)
-
-
-def add_products(step, part, out_ref, sum_ref):
-    @pl.when(step == 0)
-    def _():
-        sum_ref[...] = part
-
-    @pl.when((step > 0) & (step < STEPS - 1))
-    def _():
-        sum_ref[...] += part
-
-    @pl.when(step == STEPS - 1)
-    def _():
-        out_ref[...] = (sum_ref[...] + part).astype(BF)
+    out_ref[...] = dot_nt(lane_blocks(both_ref, 0, range(STEPS)), right).astype(BF)
 
 
 def own_products(both):
     return pl.pallas_call(
         own_products_kernel,
-        grid=(STEPS,),
-        in_specs=[lanes_of(512, 2 * BLOCK)],
-        out_specs=[full((512, 512)), lanes_of(512)],
         out_shape=[pltpu.HBM((512, 512), BF), pltpu.HBM((512, CROP), BF)],
-        scratch_shapes=[pltpu.VMEM((512, 512), F32)],
         compiler_params=pltpu.CompilerParams(vmem_limit_bytes=VMEM_LIMIT),
         cost_estimate=pl.CostEstimate(flops=2**29, bytes_accessed=4 * 2**20, transcendentals=0),
         name="own_products",
-    )(*in_hbm(both))
-
-
-def peer_products_kernel(left_ref, right_ref, out_ref, sum_ref):
-    add_products(pl.program_id(0), dot_nt(left_ref[...], right_ref[...]), out_ref, sum_ref)
+    )(both)
+
+
+def peer_products_kernel(both_ref, right_ref, out_ref):
+    left = lane_blocks(both_ref, 0, [2, 3, 0, 1])
+    out_ref[...] = dot_nt(left, right_ref[...]).astype(BF)
 
 
 def peer_products(both, right):
     return pl.pallas_call(
         peer_products_kernel,
-        grid=(STEPS,),
-        in_specs=[
-            pl.BlockSpec((512, BLOCK), lambda step: (0, ((step + HALF_STEPS) % STEPS) * 2)),
-            lanes_of(512),
-        ],
-        out_specs=full((512, 512)),
         out_shape=pltpu.HBM((512, 512), BF),
-        scratch_shapes=[pltpu.VMEM((512, 512), F32)],
         compiler_params=pltpu.CompilerParams(vmem_limit_bytes=VMEM_LIMIT),
         cost_estimate=pl.CostEstimate(flops=2**29, bytes_accessed=4 * 2**20, transcendentals=0),
         name="peer_products",
-    )(*in_hbm(both, right))
+    )(both, right)
 
 
 def hidden_features(mine, peer):
@@ -431,10 +432,12 @@
 
 
 def on_device(pair_maps, crop_tiles, full_length, proj_weight, out_weight, final_weight):
-    wp, wu, wf, prow, q, pj, sel = make_weights(proj_weight, out_weight, final_weight)
+    params = (proj_weight, out_weight, final_weight)
+    early = make_weights(1, params)
     pair = jnp.transpose(pair_maps[0], (0, 2, 1))
-    cropped = crop_columns(crop_tiles, pair)
+    cropped = crop_columns(crop_tiles, pair, early[2])
     got = lax.all_to_all(cropped, "row", 0, 0, axis_index_groups=PLANE, tiled=True)
+    wp, wu, wf, prow, q, pj, sel = make_weights(0, params, early)
     current, both = first_projection(crop_tiles, full_length, got, prow, q, wp)
     currents = (current, current)
     for layer in range(NLAYER):

time: 338 us -> 352 us (1.041)
  waiting for transfers between devices: 66.7 us -> 79.3 us
  local copies, waits for them, and re-layouts: 2.28 us -> 11 us
  Pallas kernels: 67.2 us -> 58.9 us
  blocking collectives: 133 us -> 139 us
  starting transfers between devices: 66 us -> 61.3 us
    unnamed x16 -> x34, local copies, waits for them, and re-layouts: 2.28 us -> 11 us
    ppermute x2, waiting for transfers between devices: 24.9 us -> 33.6 us  [on_device(): right_peer = lax.ppermute(right, 'row', X0_PAIRS)]
    pallas_call x5 -> x6, Pallas kernels: 24.6 us -> 17.2 us  [the longest x2 8.09 us: make_weights(): pl.pallas_call(functools.partial(weights_kernel, builder), in_specs=in_vm...]
    all_to_all x3, blocking collectives: 133 us -> 139 us  [exchange(): lax.all_to_all(cube, 'row', 0, 0, axis_index_groups=groups, tiled=True)]
  transfers between devices with their start and end apart: 9 -> 9, of which waited for: 8 -> 7; matrix products, arithmetic and copies ran while one was open for 0% -> 0% of each run, Pallas kernels for 8% -> 5%
where the time goes in v5:
time: 352 us; the launch traced here: 350 us
  blocking collectives  139 us (39%)
  waiting for transfers between devices  79.3 us (23%)
  starting transfers between devices  61.3 us (17%)
  Pallas kernels  58.9 us (17%)
  local copies, waits for them, and re-layouts  11 us (3%)
    all_to_all x3, blocking collectives, exchange(): lax.all_to_all(cube, 'row', 0, 0, axis_index_groups=groups, tiled=True)  139 us
    all_to_all x4, starting transfers between devices, exchange(): lax.all_to_all(cube, 'row', 0, 0, axis_index_groups=groups, tiled=True)  39.7 us
    ppermute x2, waiting for transfers between devices, on_device(): right_peer = lax.ppermute(right, 'row', X0_PAIRS)  33.6 us
    all_to_all x1, waiting for transfers between devices, on_device(): lax.all_to_all(cropped, 'row', 0, 0, axis_index_groups=PLANE, tiled=True)  22.8 us
    all_to_all x4, waiting for transfers between devices, exchange(): lax.all_to_all(cube, 'row', 0, 0, axis_index_groups=groups, tiled=True)  19.7 us
    pallas_call x2, Pallas kernels, middle_half(): pl.pallas_call(functools.partial(middle_kernel, half, layer), grid_spec=p...  13.1 us
    pallas_call x1, Pallas kernels, first_projection(): pl.pallas_call(first_kernel, grid_spec=pltpu.PrefetchScalarGridSpec(num_s...  11.1 us
    unnamed x34, local copies, waits for them, and re-layouts  11 us
  transfers between devices with their start and end apart: 9, of which 7 were waited for; matrix products, arithmetic and copies ran while one was open for 0% of the time, Pallas kernels for 5%

profile of v5, /device:TPU:1, one launch (start us, length us, event | category | flops | bytes accessed | tf_op | source)
XLA Modules:
  0.0 350.2 jit_solution(5196923977395560554)
XLA Ops:
  2.4 8.0 %weights1.1 = (bf16[2,2048,512]{2,1,0:T(8,128)(2,1)}, bf16[2,1024,512]{2,1,0:T(8,128)(2,1)}, bf16[512,256]{1,0:T(8,128)(2,1)}, bf16[512,512]{1,0:T(8,128)(2,1)},...) custom-call(bf16[2,64,320]{2,1,0:T(8,128)(2,1)S(1)} %copy-done.10, ...), custom_call_target="tpu_custom_call" | custom-call | flops 2000000000 | bytes 12582912 | tf_op jit(solution)/shard_map/weights1/pallas_call | solution.py:126
  11.4 5.1 %crop.1 = bf16[16,64,1024]{2,1,0:T(8,128)(2,1)} custom-call(s32[1,8]{1,0:T(1,128)S(1)} %copy-done.16, bf16[16,64,2048]{2,1,0:T(8,128)(2,1)} %bitcast.30, bf16[512,256]{1,0:T(8,128)(2,1)S(1)} %copy-done.6), custom_call_target="tpu_custom_call" | custom-call | tf_op jit(solution)/shard_map/crop/pallas_call | solution.py:147
  16.4 7.7 %all-to-all-start = ((bf16[16,64,1024]{2,1,0:T(8,128)(2,1)}), bf16[16,64,1024]{2,1,0:T(8,128)(2,1)S(1)}, u32[]{:S(2)}, u32[]{:S(2)}) async-start(bf16[16,64,1024]{2,1,0:T(8,128)(2,1)} %crop.1), calls=%async_computation | async-start | bytes 4194304 | tf_op jit(solution)/shard_map/all_to_all | solution.py:439
  24.9 22.8 %all-to-all-done.got_ref = bf16[16,64,1024]{2,1,0:T(8,128)(2,1)S(1)} async-done(((bf16[16,64,1024]{2,1,0:T(8,128)(2,1)}), bf16[16,64,1024]{2,1,0:T(8,128)(2,1)S(1)}, u32[]{:S(2)}, u32[]{:S(2)}) %all-to-all-start) | async-done | bytes 2097184 | tf_op jit(solution)/shard_map/all_to_all | solution.py:439
  47.7 11.1 %first.1 = (bf16[512,1024]{1,0:T(8,128)(2,1)}, bf16[512,2048]{1,0:T(8,128)(2,1)}) custom-call(s32[1,8]{1,0:T(1,128)S(1)} %copy-done.16, s32[1]{0:T(128)S(6)} %copy.23.length_ref.refs_1_, bf16[16,64,1024]{2,1,0:T(8,128)(2,1)S(1)} %all-to-all-done.got_ref, bf16[512,512]{1,0:T(8,128)(2,1)} %get-tuple-element.38.prow_ref, ...), custom_call_target="tpu_custom_call" | custom-call | tf_op jit(solution)/shard_map/first/pallas_call | solution.py:246
  58.8 59.0 %all_to_all.40 = bf16[64,8,2048]{2,1,0:T(8,128)(2,1)S(1)} all-to-all(bf16[64,8,2048]{2,1,0:T(8,128)(2,1)} %bitcast.33), channel_id=1, replica_groups={{0,1,2,3,4,5,6,7,8,9,10,11,12,13,14,15,16,17,18,19,20,21,22,23,24,25,26..., dimensions={0} | all-to-all | bytes 4194304 | tf_op jit(solution)/shard_map/all_to_all | solution.py:430
  121.0 3.7 %collective-permute-start = (bf16[512,1024]{1,0:T(8,128)(2,1)}, bf16[512,1024]{1,0:T(8,128)(2,1)}, u32[]{:S(2)}, u32[]{:S(2)}) collective-permute-start(bf16[512,1024]{1,0:T(8,128)(2,1)} %get-tuple-element.42), channel_id=1, source_target_pairs={{0,32},{1,33},{2,34},{3,35},{4,36},{5,37},{6,38},{7,39},{8,40},{9,... | collective-permute-start | bytes 3145736 | tf_op jit(solution)/shard_map/ppermute | solution.py:447
  124.6 9.0 %all-to-all-start.3 = ((bf16[64,8,512]{2,1,0:T(8,128)(2,1)}), bf16[64,8,512]{2,1,0:T(8,128)(2,1)S(1)}, u32[]{:S(2)}, u32[]{:S(2)}) async-start(bf16[64,8,512]{2,1,0:T(8,128)(2,1)} %bitcast.34), calls=%async_computation.3 | async-start | bytes 1048576 | tf_op jit(solution)/shard_map/all_to_all | solution.py:430
  133.6 19.3 %collective-permute-done.right_ref = bf16[512,1024]{1,0:T(8,128)(2,1)} collective-permute-done((bf16[512,1024]{1,0:T(8,128)(2,1)}, bf16[512,1024]{1,0:T(8,128)(2,1)}, u32[]{:S(2)}, u32[]{:S(2)}) %collective-permute-start) | collective-permute-done | bytes 1048608 | tf_op jit(solution)/shard_map/ppermute | solution.py:447
  157.3 9.1 %all-to-all-start.2 = ((bf16[64,8,512]{2,1,0:T(8,128)(2,1)}), bf16[64,8,512]{2,1,0:T(8,128)(2,1)S(1)}, u32[]{:S(2)}, u32[]{:S(2)}) async-start(bf16[64,8,512]{2,1,0:T(8,128)(2,1)} %bitcast.31), calls=%async_computation.2 | async-start | bytes 1048576 | tf_op jit(solution)/shard_map/all_to_all | solution.py:430
  166.4 6.5 %middle0.1 = (bf16[512,512]{1,0:T(8,128)(2,1)}, bf16[512,2048]{1,0:T(8,128)(2,1)}) custom-call(s32[1,8]{1,0:T(1,128)S(1)} %copy-done.16, s32[1]{0:T(128)S(6)} %copy.23.length_ref.refs_1_, bf16[512,512]{1,0:T(8,128)(2,1)S(1)} %bitcast.23, bf16[512,1024]{1,0:T(8,128)(2,1)} %get-tuple-element.43.refs_3_, bf16[2,1024,512]{2,1,0:T(8,128)(2,1)S(1)} %copy-done, ...), custom_call_target="tpu_custom_call" | custom-call | tf_op jit(solution)/shard_map/middle0/pallas_call | solution.py:285
  173.0 10.6 %all-to-all-done.2 = bf16[64,8,512]{2,1,0:T(8,128)(2,1)S(1)} async-done(((bf16[64,8,512]{2,1,0:T(8,128)(2,1)}), bf16[64,8,512]{2,1,0:T(8,128)(2,1)S(1)}, u32[]{:S(2)}, u32[]{:S(2)}) %all-to-all-start.2) | async-done | bytes 524320 | tf_op jit(solution)/shard_map/all_to_all | solution.py:430
  183.6 6.5 %middle1.1 = (bf16[512,512]{1,0:T(8,128)(2,1)}, bf16[512,2048]{1,0:T(8,128)(2,1)}) custom-call(s32[1,8]{1,0:T(1,128)S(1)} %copy-done.16, s32[1]{0:T(128)S(6)} %copy.23.length_ref.refs_1_, bf16[512,512]{1,0:T(8,128)(2,1)S(1)} %bitcast.25, bf16[512,1024]{1,0:T(8,128)(2,1)} %get-tuple-element.43.refs_3_, ...), custom_call_target="tpu_custom_call", output_to_operand_aliasing={{1}: (6, {})} | custom-call | tf_op jit(solution)/shard_map/middle1/pallas_call | solution.py:285
  190.2 54.3 %all_to_all.41 = bf16[64,8,2048]{2,1,0:T(8,128)(2,1)S(1)} all-to-all(bf16[64,8,2048]{2,1,0:T(8,128)(2,1)} %bitcast.29), channel_id=1, replica_groups={{0,1,2,3,4,5,6,7,8,9,10,11,12,13,14,15,16,17,18,19,20,21,22,23,24,25,26..., dimensions={0} | all-to-all | bytes 4194304 | tf_op jit(solution)/shard_map/all_to_all | solution.py:430
  248.6 9.5 %all-to-all-start.6 = ((bf16[64,8,512]{2,1,0:T(8,128)(2,1)}), bf16[64,8,512]{2,1,0:T(8,128)(2,1)S(1)}, u32[]{:S(2)}, u32[]{:S(2)}) async-start(bf16[64,8,512]{2,1,0:T(8,128)(2,1)} %bitcast.35), calls=%async_computation.6 | async-start | bytes 1048576 | tf_op jit(solution)/shard_map/all_to_all | solution.py:430
  258.0 14.3 %collective-permute-done.1.right_ref = bf16[512,1024]{1,0:T(8,128)(2,1)} collective-permute-done((bf16[512,1024]{1,0:T(8,128)(2,1)}, bf16[512,1024]{1,0:T(8,128)(2,1)}, u32[]{:S(2)}, u32[]{:S(2)}) %collective-permute-start.1) | collective-permute-done | bytes 1048608 | tf_op jit(solution)/shard_map/ppermute | solution.py:447
  274.0 2.8 peer_products.3
  277.6 12.2 %all-to-all-start.5 = ((bf16[64,8,512]{2,1,0:T(8,128)(2,1)}), bf16[64,8,512]{2,1,0:T(8,128)(2,1)S(1)}, u32[]{:S(2)}, u32[]{:S(2)}) async-start(bf16[64,8,512]{2,1,0:T(8,128)(2,1)} %bitcast.32), calls=%async_computation.5 | async-start | bytes 1048576 | tf_op jit(solution)/shard_map/all_to_all | solution.py:430
  290.8 4.4 %last_own.1.own_ref = bf16[512,512]{1,0:T(8,128)(2,1)} custom-call(bf16[512,512]{1,0:T(8,128)(2,1)S(1)} %bitcast.28, bf16[512,512]{1,0:T(8,128)(2,1)} %get-tuple-element.52.cur_ref, bf16[2,1024,512]{2,1,0:T(8,128)(2,1)S(1)} %copy-done, bf16[512,512]{1,0:T(8,128)(2,1)S(1)} %copy-done.5), custom_call_target="tpu_custom_call" | custom-call | tf_op jit(solution)/shard_map/last_own/pallas_call | solution.py:330
  295.2 9.1 %all-to-all-done.5 = bf16[64,8,512]{2,1,0:T(8,128)(2,1)S(1)} async-done(((bf16[64,8,512]{2,1,0:T(8,128)(2,1)}), bf16[64,8,512]{2,1,0:T(8,128)(2,1)S(1)}, u32[]{:S(2)}, u32[]{:S(2)}) %all-to-all-start.5) | async-done | bytes 524320 | tf_op jit(solution)/shard_map/all_to_all | solution.py:430
  304.3 5.1 %last_peer.1 = (bf16[1024,256]{1,0:T(8,128)(2,1)S(1)}, bf16[1024,256]{1,0:T(8,128)(2,1)S(1)}) custom-call(bf16[512,512]{1,0:T(8,128)(2,1)S(1)} %bitcast.24, bf16[512,512]{1,0:T(8,128)(2,1)} %get-tuple-element.49.cur_ref, bf16[2,1024,512]{2,1,0:T(8,128)(2,1)S(1)} %copy-done, bf16[512,512]{1,0:T(8,128)(2,1)S(1)} %copy-done.5, ...), custom_call_target="tpu_custom_call" | custom-call | tf_op jit(solution)/shard_map/last_peer/pallas_call | solution.py:342
  309.4 6.4 %collective-permute-start.2 = (bf16[1024,256]{1,0:T(8,128)(2,1)S(1)}, bf16[1024,256]{1,0:T(8,128)(2,1)S(1)}, u32[]{:S(2)}, u32[]{:S(2)}) collective-permute-start(bf16[1024,256]{1,0:T(8,128)(2,1)S(1)} %get-tuple-element.55), channel_id=1, source_target_pairs={{0,128},{128,0},{1,129},{129,1},{2,130},{130,2},{3,131},{131,3},{4... | collective-permute-start | bytes 1572872 | tf_op jit(solution)/shard_map/ppermute | solution.py:456
  317.6 25.3 %all_to_all.42 = bf16[128,8,256]{2,1,0:T(8,128)(2,1)S(1)} all-to-all(bf16[128,8,256]{2,1,0:T(8,128)(2,1)S(1)} %fusion), channel_id=1, replica_groups={{0,8,16,24,32,40,48,56,64,72,80,88,96,104,112,120,1,9,17,25,33,41,49,57..., dimensions={0} | all-to-all | bytes 1048576 | tf_op jit(solution)/shard_map/all_to_all | solution.py:430
  347.2 3.1 final.1
  (45 shorter events, 24.5 us)
Async XLA Ops:
  0.0 0.9 copy-start.10
  2.4 8.0 %copy-start.16 = (s32[1,8]{1,0:T(1,128)S(1)}, s32[1,8]{1,0:T(1,128)}, u32[]{:S(2)}) copy-start(s32[1,8]{1,0:T(1,128)} %refs_0_.7) | copy-start | bytes 100
  10.4 1.0 copy-start.6
  16.4 8.4 %copy-start.11 = (bf16[2,64,320]{2,1,0:T(8,128)(2,1)S(1)}, bf16[2,64,320]{2,1,0:T(8,128)(2,1)}, u32[]{:S(2)}) copy-start(bf16[2,64,320]{2,1,0:T(8,128)(2,1)} %refs_0_.5) | copy-start | bytes 245764
  16.4 8.4 %copy-start.13 = (bf16[2,64,64]{2,1,0:T(8,128)(2,1)S(1)}, bf16[2,64,64]{2,1,0:T(8,128)(2,1)}, u32[]{:S(2)}) copy-start(bf16[2,64,64]{2,1,0:T(8,128)(2,1)} %refs_1_.5) | copy-start | bytes 49156
  16.4 8.4 %copy-start.15 = (bf16[64,128]{1,0:T(8,128)(2,1)S(1)}, bf16[64,128]{1,0:T(8,128)(2,1)}, u32[]{:S(2)}) copy-start(bf16[64,128]{1,0:T(8,128)(2,1)} %refs_2_.3) | copy-start | bytes 49156
  16.4 31.3 %all-to-all-start = ((bf16[16,64,1024]{2,1,0:T(8,128)(2,1)}), bf16[16,64,1024]{2,1,0:T(8,128)(2,1)S(1)}, u32[]{:S(2)}, u32[]{:S(2)}) async-start(bf16[16,64,1024]{2,1,0:T(8,128)(2,1)} %crop.1), calls=%async_computation | async-start | bytes 4194304 | tf_op jit(solution)/shard_map/all_to_all | solution.py:439
  119.6 1.4 copy-start.1
  121.0 32.0 %collective-permute-start = (bf16[512,1024]{1,0:T(8,128)(2,1)}, bf16[512,1024]{1,0:T(8,128)(2,1)}, u32[]{:S(2)}, u32[]{:S(2)}) collective-permute-start(bf16[512,1024]{1,0:T(8,128)(2,1)} %get-tuple-element.42), channel_id=1, source_target_pairs={{0,32},{1,33},{2,34},{3,35},{4,36},{5,37},{6,38},{7,39},{8,40},{9,... | collective-permute-start | bytes 3145736 | tf_op jit(solution)/shard_map/ppermute | solution.py:447
  124.6 32.7 %all-to-all-start.3 = ((bf16[64,8,512]{2,1,0:T(8,128)(2,1)}), bf16[64,8,512]{2,1,0:T(8,128)(2,1)S(1)}, u32[]{:S(2)}, u32[]{:S(2)}) async-start(bf16[64,8,512]{2,1,0:T(8,128)(2,1)} %bitcast.34), calls=%async_computation.3 | async-start | bytes 1048576 | tf_op jit(solution)/shard_map/all_to_all | solution.py:430
  133.6 32.8 %copy-start = (bf16[2,1024,512]{2,1,0:T(8,128)(2,1)S(1)}, bf16[2,1024,512]{2,1,0:T(8,128)(2,1)}, u32[]{:S(2)}) copy-start(bf16[2,1024,512]{2,1,0:T(8,128)(2,1)} %get-tuple-element.44.refs_4_.wu_ref) | copy-start | bytes 6291460
  152.9 1.6 copy-start.2
  157.3 26.3 %all-to-all-start.2 = ((bf16[64,8,512]{2,1,0:T(8,128)(2,1)}), bf16[64,8,512]{2,1,0:T(8,128)(2,1)S(1)}, u32[]{:S(2)}, u32[]{:S(2)}) async-start(bf16[64,8,512]{2,1,0:T(8,128)(2,1)} %bitcast.31), calls=%async_computation.2 | async-start | bytes 1048576 | tf_op jit(solution)/shard_map/all_to_all | solution.py:430
  246.2 1.3 copy-start.3
  247.5 24.9 %collective-permute-start.1 = (bf16[512,1024]{1,0:T(8,128)(2,1)}, bf16[512,1024]{1,0:T(8,128)(2,1)}, u32[]{:S(2)}, u32[]{:S(2)}) collective-permute-start(bf16[512,1024]{1,0:T(8,128)(2,1)} %get-tuple-element.48), channel_id=1, source_target_pairs={{0,32},{1,33},{2,34},{3,35},{4,36},{5,37},{6,38},{7,39},{8,40},{9,... | collective-permute-start | bytes 3145736 | tf_op jit(solution)/shard_map/ppermute | solution.py:447
  248.6 28.2 %all-to-all-start.6 = ((bf16[64,8,512]{2,1,0:T(8,128)(2,1)}), bf16[64,8,512]{2,1,0:T(8,128)(2,1)S(1)}, u32[]{:S(2)}, u32[]{:S(2)}) async-start(bf16[64,8,512]{2,1,0:T(8,128)(2,1)} %bitcast.35), calls=%async_computation.6 | async-start | bytes 1048576 | tf_op jit(solution)/shard_map/all_to_all | solution.py:430
  272.4 1.6 copy-start.4
  274.0 15.8 %copy-start.5 = (bf16[512,512]{1,0:T(8,128)(2,1)S(1)}, bf16[512,512]{1,0:T(8,128)(2,1)}, u32[]{:S(2)}) copy-start(bf16[512,512]{1,0:T(8,128)(2,1)} %get-tuple-element.50.sel_ref) | copy-start | bytes 1572868
  276.8 0.8 copy-start.8
  277.6 26.7 %all-to-all-start.5 = ((bf16[64,8,512]{2,1,0:T(8,128)(2,1)}), bf16[64,8,512]{2,1,0:T(8,128)(2,1)S(1)}, u32[]{:S(2)}, u32[]{:S(2)}) async-start(bf16[64,8,512]{2,1,0:T(8,128)(2,1)} %bitcast.32), calls=%async_computation.5 | async-start | bytes 1048576 | tf_op jit(solution)/shard_map/all_to_all | solution.py:430
  289.8 1.0 copy-start.9
  309.4 37.8 %copy-start.7 = (bf16[512,256]{1,0:T(8,128)(2,1)S(1)}, bf16[512,256]{1,0:T(8,128)(2,1)}, u32[]{:S(2)}) copy-start(bf16[512,256]{1,0:T(8,128)(2,1)} %get-tuple-element.56.wf_ref) | copy-start | bytes 786436
  309.4 7.9 %collective-permute-start.2 = (bf16[1024,256]{1,0:T(8,128)(2,1)S(1)}, bf16[1024,256]{1,0:T(8,128)(2,1)S(1)}, u32[]{:S(2)}, u32[]{:S(2)}) collective-permute-start(bf16[1024,256]{1,0:T(8,128)(2,1)S(1)} %get-tuple-element.55), channel_id=1, source_target_pairs={{0,128},{128,0},{1,129},{129,1},{2,130},{130,2},{3,131},{131,3},{4... | collective-permute-start | bytes 1572872 | tf_op jit(solution)/shard_map/ppermute | solution.py:456
  342.8 4.3 %collective-permute-start.3 = (bf16[1024,256]{1,0:T(8,128)(2,1)S(1)}, bf16[1024,256]{1,0:T(8,128)(2,1)S(1)}, u32[]{:S(2)}, u32[]{:S(2)}) collective-permute-start(bf16[1024,256]{1,0:T(8,128)(2,1)S(1)} %bitcast.26), channel_id=1, source_target_pairs={{0,128},{128,0},{1,129},{129,1},{2,130},{130,2},{3,131},{131,3},{4... | collective-permute-start | bytes 1572872 | tf_op jit(solution)/shard_map/ppermute | solution.py:458
  (2 other events, 1.5 us)

commit v6 on v3

v6 whole, which is shorter than its diff:
```python
import functools

import jax
import jax.numpy as jnp
from jax import lax
from jax.experimental import pallas as pl
from jax.experimental.pallas import tpu as pltpu
from jax.sharding import PartitionSpec as P

CH = 64
CZ = 128
CROP = 1024
TILE = 128
NLAYER = 2
FULL = 2048
ROWS = 8
EPSILON = 1e-05
BF = jnp.bfloat16
F32 = jnp.float32

PLANE = [[s * 8 + z for s in range(16)] for z in range(8)]
SAME_X0 = [
    [(x1 * 2 + x0) * 32 + y * 8 + z for x1 in range(2) for y in range(4) for z in range(8)]
    for x0 in range(2)
]
BY_Z = [[s * 8 + z for z in range(8) for s in range(16)]]
X0_PAIRS = [(r, r ^ 32) for r in range(128)]
CORES = [(0, 1), (1, 0)]
VMEM_LIMIT = 20 * 1024 * 1024


def in_vmem(*arrays):
    return [pltpu.with_memory_space_constraint(array, pltpu.VMEM) for array in arrays]


def in_hbm(*arrays):
    return [pltpu.with_memory_space_constraint(array, pltpu.HBM) for array in arrays]


def iota(shape, dim):
    return lax.broadcasted_iota(jnp.int32, shape, dim)


def onehot(mask):
    return jnp.where(mask, 1.0, 0.0).astype(BF)


def dot(a, b):
    return jnp.dot(a, b, preferred_element_type=F32)


def dot_nt(a, b):
    return lax.dot_general(a, b, (((1,), (1,)), ((), ())), preferred_element_type=F32)


def dot_tn(a, b):
    return lax.dot_general(a, b, (((0,), (0,)), ((), ())), preferred_element_type=F32)


def lane_token(lane):
    x0 = (lax.axis_index("row") // 32) % 2
    return (
        (lane % 8) * 128
        + ((lane // 8) % 8) * 16
        + ((lane // 256) % 2) * 8
        + ((lane // 512) ^ x0) * 4
        + ((lane // 64) % 4)
    )


def tables_kernel(final_ref, wf_ref, prow_ref, q_ref, pj_ref):
    down = onehot(iota((512, CZ), 0) % CZ == iota((512, CZ), 1))
    across = onehot(iota((CH, 256), 0) == iota((CH, 256), 1) % CH)
    tall = dot_nt(down, final_ref[...]).astype(BF)
    block = iota((512, 256), 0) // CZ == iota((512, 256), 1) // CH
    wf_ref[...] = jnp.where(block, dot(tall, across), 0.0).astype(BF)
    r0, c0 = iota((512, 512), 0), iota((512, 512), 1)
    prow_ref[...] = onehot((r0 // 8 == c0 % CH) & (r0 % 8 == c0 // CH))
    r1, c1 = iota((CROP, CROP), 0), iota((CROP, CROP), 1)
    token = lane_token(c1)
    q_ref[...] = onehot(r1 == token)
    dest = r1 // 8
    pj_ref[...] = onehot(((dest % 16) * 8 + dest // 16) * 8 + r1 % 8 == token)


def make_tables(final_weight):
    return pl.pallas_call(
        tables_kernel,
        out_shape=[
            pltpu.VMEM((512, 256), BF), pltpu.VMEM((512, 512), BF),
            pltpu.HBM((CROP, CROP), BF), pltpu.HBM((CROP, CROP), BF),
        ],
        compiler_params=pltpu.CompilerParams(vmem_limit_bytes=40 * 1024 * 1024),
        cost_estimate=pl.CostEstimate(flops=10**9, bytes_accessed=6 * 2**20, transcendentals=0),
        name="tables",
    )(final_weight)


def crop_kernel(crop_ref, x_ref, o_ref):
    for a in range(8):
        start = pl.multiple_of(crop_ref[0, a] * TILE, TILE)
        o_ref[:, :, a * TILE : (a + 1) * TILE] = x_ref[:, :, pl.ds(start, TILE)]


def crop_columns(crop_tiles, pair):
    return pl.pallas_call(
        crop_kernel,
        grid_spec=pltpu.PrefetchScalarGridSpec(
            num_scalar_prefetch=1,
            grid=(4,),
            in_specs=[pl.BlockSpec((4, CH, FULL), lambda m, crop: (m, 0, 0))],
            out_specs=pl.BlockSpec((4, CH, CROP), lambda m, crop: (m, 0, 0)),
        ),
        out_shape=pltpu.HBM((16, CH, CROP), BF),
        compiler_params=pltpu.CompilerParams(vmem_limit_bytes=VMEM_LIMIT),
        name="crop",
    )(crop_tiles, *in_hbm(pair))


def norm_channels(values):
    center = values - jnp.sum(values, axis=0, keepdims=True) * (1.0 / CH)
    spread = jnp.sum(center * center, axis=0, keepdims=True) * (1.0 / CH)
    return center * lax.rsqrt(spread + EPSILON)


def sigmoid(values):
    return 0.5 * jnp.tanh(0.5 * values) + 0.5


def side_by_side(values):
    return jnp.concatenate([values[a * CH : (a + 1) * CH] for a in range(ROWS)], axis=1)


def stacked(values):
    lanes = values.shape[1] // ROWS
    return jnp.concatenate([values[:, a * lanes : (a + 1) * lanes] for a in range(ROWS)], axis=0)


def pair_mask(crop_ref, length_ref, lanes, start):
    chip = lax.axis_index("row")
    inside = (chip % 8) * 16 + chip // 8
    length = length_ref[0]
    lane = iota((1, lanes), 1) + start
    position = lane_token(lane) % TILE
    for a in range(ROWS):
        position = position + jnp.where(lane % 8 == a, crop_ref[0, a] * TILE, 0)
    parts = []
    for a in range(ROWS):
        row_position = crop_ref[0, a] * TILE + inside
        parts.append(jnp.where((position < length) & (row_position < length), 1.0, 0.0))
    return jnp.concatenate(parts, axis=1)


def project(current, w, prow, mask, both_ref):
    values = dot_tn(w[:, : 4 * CH], norm_channels(current).astype(BF))
    lanes = both_ref.shape[1] // 2
    for side in range(2):
        gate = values[side * 128 : side * 128 + CH]
        value = values[side * 128 + CH : side * 128 + 2 * CH]
        factor = (sigmoid(gate) * value * mask).astype(BF)
        both_ref[:, side * lanes : (side + 1) * lanes] = dot(prow, stacked(factor)).astype(BF)


BLOCK = 256
ANYWHERE = pl.BlockSpec(memory_space=pl.ANY)
STEPS = CROP // BLOCK
HALF_STEPS = STEPS // 2
BOTH = pltpu.HBM((512, 2 * CROP), BF)


def first_kernel(crop_ref, length_ref, got_ref, prow_ref, q_ref, w_ref, cur_ref, both_ref):
    step = pl.program_id(0)
    parts = jnp.concatenate([got_ref[crop_ref[0, a]] for a in range(ROWS)], axis=0)
    current = dot(parts, q_ref[...])
    cur_ref[...] = current.astype(BF)
    mask = pair_mask(crop_ref, length_ref, BLOCK, step * BLOCK)
    project(side_by_side(current), w_ref[0], prow_ref[...], mask, both_ref)


def full(shape):
    return pl.BlockSpec(shape, lambda step, *_: (0,) * len(shape), pipeline_mode=pl.Buffered(1))


def lanes_of(rows, lanes=BLOCK, offset=0):
    return pl.BlockSpec((rows, lanes), lambda step, *_: (0, step + offset))


def layer_weight(columns, layer):
    return pl.BlockSpec((1, CH, columns), lambda step, *_: (layer, 0, 0), pipeline_mode=pl.Buffered(1))


def first_projection(crop_tiles, full_length, got, prow, q, proj_weight):
    return pl.pallas_call(
        first_kernel,
        grid_spec=pltpu.PrefetchScalarGridSpec(
            num_scalar_prefetch=2,
            grid=(STEPS,),
            in_specs=[full((16, CH, CROP)), full((512, 512)), lanes_of(CROP), layer_weight(320, 0)],
            out_specs=[lanes_of(512), lanes_of(512, 2 * BLOCK)],
        ),
        out_shape=[pltpu.HBM((512, CROP), BF), BOTH],
        compiler_params=pltpu.CompilerParams(vmem_limit_bytes=VMEM_LIMIT),
        name="first",
    )(crop_tiles, full_length, got, *in_vmem(prow), *in_hbm(q), proj_weight)


def update(back_ref, cur_ref, prow, w_proj, w_out):
    current = side_by_side(cur_ref[...].astype(F32))
    gate = sigmoid(dot_tn(w_proj[:, 4 * CH :], norm_channels(current).astype(BF)))
    products = side_by_side(dot_tn(prow, back_ref[...]))
    change = dot_tn(w_out, norm_channels(products).astype(BF))
    return (current + gate * change).astype(BF)


def middle_kernel(half, *refs):
    crop_ref, length_ref, back_ref, cur_ref, prow_ref, w_ref, w_out_ref, w_next_ref = refs[:8]
    next_ref, both_ref = refs[-2:]
    current = update(back_ref, cur_ref, prow_ref[...], w_ref[0], w_out_ref[0])
    next_ref[...] = stacked(current)
    mask = pair_mask(crop_ref, length_ref, BLOCK, half * 512 + pl.program_id(0) * BLOCK)
    project(current.astype(F32), w_next_ref[0], prow_ref[...], mask, both_ref)


def middle_half(half, crop_tiles, full_length, back, current, prow, proj_weight, out_weight, layer, both):
    offset = half * HALF_STEPS
    aliased = [] if both is None else [both]
    return pl.pallas_call(
        functools.partial(middle_kernel, half),
        grid_spec=pltpu.PrefetchScalarGridSpec(
            num_scalar_prefetch=2,
            grid=(HALF_STEPS,),
            in_specs=[
                lanes_of(512), lanes_of(512, offset=offset), full((512, 512)),
                layer_weight(320, layer), layer_weight(CH, layer), layer_weight(320, layer + 1),
            ]
            + [ANYWHERE] * len(aliased),
            out_specs=[lanes_of(512), lanes_of(512, 2 * BLOCK, offset)],
        ),
        out_shape=[pltpu.HBM((512, 512), BF), BOTH],
        input_output_aliases={8: 1} if aliased else {},
        compiler_params=pltpu.CompilerParams(vmem_limit_bytes=VMEM_LIMIT),
        name="middle" + str(half),
    )(
        crop_tiles, full_length, back, *in_hbm(current), *in_vmem(prow), proj_weight, out_weight, proj_weight,
        *aliased,
    )


def last_rows(back_ref, cur_ref, prow_ref, w_ref, w_out_ref):
    current = update(back_ref, cur_ref, prow_ref[...], w_ref[0], w_out_ref[0])
    return stacked(norm_channels(current.astype(F32)).astype(BF))


def last_own_kernel(back_ref, cur_ref, prow_ref, w_ref, w_out_ref, rows_ref):
    rows_ref[...] = last_rows(back_ref, cur_ref, prow_ref, w_ref, w_out_ref)


def last_peer_kernel(
    back_ref, cur_ref, prow_ref, w_ref, w_out_ref, own_hbm, pj_hbm, mine_ref, other_ref, rows_ref, pj_ref, sems
):
    step = pl.program_id(0)
    loads = [
        pltpu.make_async_copy(own_hbm, rows_ref.at[:, pl.ds(0, 512)], sems.at[0]),
        pltpu.make_async_copy(pj_hbm, pj_ref, sems.at[1]),
    ]

    @pl.when(step == 0)
    def _():
        for load in loads:
            load.start()

    lanes = pl.ds(pl.multiple_of(512 + step * BLOCK, BLOCK), BLOCK)
    rows_ref[:, lanes] = last_rows(back_ref, cur_ref, prow_ref, w_ref, w_out_ref)

    @pl.when(step == HALF_STEPS - 1)
    def _():
        for load in loads:
            load.wait()
        core = lax.axis_index("tmpl")
        pj = pj_ref[...]
        mine_ref[...] = dot_nt(pj, rows_ref[pl.ds(pl.multiple_of(core * 256, 256), 256), :]).astype(BF)
        other_ref[...] = dot_nt(pj, rows_ref[pl.ds(pl.multiple_of(256 - core * 256, 256), 256), :]).astype(BF)


def last_specs(layer):
    return [lanes_of(512)] * 2 + [full((512, 512)), layer_weight(320, layer), layer_weight(CH, layer)]


def last_own(back, current, prow, proj_weight, out_weight, layer):
    return pl.pallas_call(
        last_own_kernel,
        grid=(HALF_STEPS,),
        in_specs=last_specs(layer),
        out_specs=lanes_of(512),
        out_shape=pltpu.HBM((512, 512), BF),
        compiler_params=pltpu.CompilerParams(vmem_limit_bytes=VMEM_LIMIT),
        name="last_own",
    )(back, *in_hbm(current), *in_vmem(prow), proj_weight, out_weight)


def last_peer(back, current, prow, proj_weight, out_weight, own, pj, layer):
    return pl.pallas_call(
        last_peer_kernel,
        grid=(HALF_STEPS,),
        in_specs=last_specs(layer) + [ANYWHERE, ANYWHERE],
        out_specs=[full((CROP, 256))] * 2,
        out_shape=[jax.ShapeDtypeStruct((CROP, 256), BF)] * 2,
        scratch_shapes=[
            pltpu.VMEM((512, CROP), BF), pltpu.VMEM((CROP, CROP), BF), pltpu.SemaphoreType.DMA((2,)),
        ],
        compiler_params=pltpu.CompilerParams(vmem_limit_bytes=VMEM_LIMIT),
        name="last_peer",
    )(back, *in_hbm(current), *in_vmem(prow), proj_weight, out_weight, *in_hbm(own, pj))


def own_products_kernel(both_ref, out_ref, left_hbm, right_hbm, sems):
    copies = []
    for block in range(STEPS):
        for side, target in enumerate((left_hbm, right_hbm)):
            source = both_ref.at[:, pl.ds((2 * block + side) * BLOCK, BLOCK)]
            place = target.at[:, pl.ds(block * BLOCK, BLOCK)]
            copies.append(pltpu.make_async_copy(source, place, sems.at[2 * block + side]))
    for copy in copies:
        copy.start()
    starts = [2 * block * BLOCK for block in range(STEPS)]
    left = jnp.concatenate([both_ref[:, start : start + BLOCK] for start in starts], axis=1)
    right = jnp.concatenate([both_ref[:, start + BLOCK : start + 2 * BLOCK] for start in starts], axis=1)
    out_ref[...] = dot_nt(left, right).astype(BF)
    for copy in copies:
        copy.wait()


def own_products(both):
    return pl.pallas_call(
        own_products_kernel,
        out_specs=[pl.BlockSpec(memory_space=pltpu.VMEM), ANYWHERE, ANYWHERE],
        out_shape=[jax.ShapeDtypeStruct((512, 512), BF), pltpu.HBM((512, CROP), BF), pltpu.HBM((512, CROP), BF)],
        scratch_shapes=[pltpu.SemaphoreType.DMA((2 * STEPS,))],
        compiler_params=pltpu.CompilerParams(vmem_limit_bytes=VMEM_LIMIT),
        cost_estimate=pl.CostEstimate(flops=2**29, bytes_accessed=4 * 2**20, transcendentals=0),
        name="own_products",
    )(both)


def peer_products_kernel(left_ref, right_ref, out_ref):
    left = jnp.concatenate([left_ref[:, 512:], left_ref[:, :512]], axis=1)
    out_ref[...] = dot_nt(left, right_ref[...]).astype(BF)


def peer_products(left, right):
    return pl.pallas_call(
        peer_products_kernel,
        out_shape=pltpu.HBM((512, 512), BF),
        compiler_params=pltpu.CompilerParams(vmem_limit_bytes=VMEM_LIMIT),
        cost_estimate=pl.CostEstimate(flops=2**29, bytes_accessed=4 * 2**20, transcendentals=0),
        name="peer_products",
    )(left, right)


def hidden_features(mine, peer):
    total = mine.astype(F32) + peer.astype(F32)
    return jnp.maximum(total * 0.5, 0.0).astype(BF)


def final_kernel(mine_ref, peer_ref, wf_ref, out_ref, tall0_ref, tall1_ref, wide_ref):
    core = lax.axis_index("tmpl")
    wf = wf_ref[...]
    for source, ref in enumerate((mine_ref, peer_ref)):
        half = core if source == 0 else 1 - core
        tall0_ref[...] = ref[:, :128].astype(F32)
        tall1_ref[...] = ref[:, 128:].astype(F32)
        for j in range(8):
            rows = jnp.concatenate(
                [tall0_ref[pl.ds(j, 128, stride=8), :], tall1_ref[pl.ds(j, 128, stride=8), :]], axis=1
            ).astype(BF)
            result = dot_nt(wf, rows)
            for a in range(4):
                wide_ref[half * 4 + a, pl.ds(j, CZ, stride=8), :] = result[a * CZ : (a + 1) * CZ]
    for a in range(8):
        out_ref[:, a * TILE : (a + 1) * TILE] = wide_ref[a].astype(BF)


def final_projection(mine, peer, wf):
    return pl.pallas_call(
        final_kernel,
        out_shape=jax.ShapeDtypeStruct((CZ * 8, CROP), BF),
        scratch_shapes=[
            pltpu.VMEM((CROP, 128), F32), pltpu.VMEM((CROP, 128), F32), pltpu.VMEM((8, CZ * 8, TILE), F32)
        ],
        compiler_params=pltpu.CompilerParams(vmem_limit_bytes=VMEM_LIMIT),
        name="final",
    )(mine, peer, wf)


def exchange(values, groups, count):
    cube = values.reshape(count, -1, values.shape[-1])
    moved = lax.all_to_all(cube, "row", 0, 0, axis_index_groups=groups, tiled=True)
    return moved.reshape(values.shape)


def on_device(pair_maps, crop_tiles, full_length, proj_weight, out_weight, final_weight):
    wf, prow, q, pj = make_tables(final_weight)
    pair = jnp.transpose(pair_maps[0], (0, 2, 1))
    cropped = crop_columns(crop_tiles, pair)
    got = lax.all_to_all(cropped, "row", 0, 0, axis_index_groups=PLANE, tiled=True)
    current, both = first_projection(crop_tiles, full_length, got, prow, q, proj_weight)
    currents = (current, current)
    weights = (prow, proj_weight, out_weight)
    for layer in range(NLAYER):
        products, left, right = own_products(exchange(both, SAME_X0, CH))
        back_own = exchange(products, SAME_X0, CH)
        right_peer = lax.ppermute(right, "row", X0_PAIRS)
        back_peer = exchange(peer_products(left, right_peer), SAME_X0, CH)
        if layer + 1 < NLAYER:
            scalars = (crop_tiles, full_length)
            own, both = middle_half(0, *scalars, back_own, currents[0], *weights, layer, None)
            peer, both = middle_half(1, *scalars, back_peer, currents[1], *weights, layer, both)
            currents = (own, peer)
    rows = last_own(back_own, currents[0], *weights, NLAYER - 1)
    mine, other = last_peer(back_peer, currents[1], *weights, rows, pj, NLAYER - 1)
    hidden = hidden_features(mine, lax.ppermute(other, "tmpl", CORES))
    moved = exchange(hidden, BY_Z, 128)
    result = final_projection(moved, lax.ppermute(moved, "tmpl", CORES), wf)
    return result.reshape(CZ, 8, CROP)


def solution(mesh):
    placed = (P("tmpl", "row", None, None), P("tmpl", None), P(), P(), P(), P())
    return jax.shard_map(
        on_device, mesh=mesh, in_specs=placed, out_specs=P(None, "row", None), check_vma=False
    )
```

time: 347 us -> 323 us (0.931)
  local copies, waits for them, and re-layouts: 40.2 us -> 3.13 us
  waiting for transfers between devices: 53.6 us -> 74.5 us
  blocking collectives: 141 us -> 136 us
    unnamed x84 -> x14, local copies, waits for them, and re-layouts: 40.2 us -> 3.13 us
    all_to_all x4, waiting for transfers between devices: 8.93 us -> 23 us  [exchange(): lax.all_to_all(cube, 'row', 0, 0, axis_index_groups=groups, tiled=True)]
    all_to_all x1, waiting for transfers between devices: 16.3 us -> 23.9 us  [on_device(): lax.all_to_all(cropped, 'row', 0, 0, axis_index_groups=PLANE, tiled=True)]
    pallas_call x8 -> x7, Pallas kernels: 24 us -> 18.5 us  [the longest x2 4.47 us: own_products(): pl.pallas_call(own_products_kernel, out_specs=[pl.BlockSpec(memory_space=...]
    all_to_all x3, blocking collectives: 141 us -> 136 us  [exchange(): lax.all_to_all(cube, 'row', 0, 0, axis_index_groups=groups, tiled=True)]
    pallas_call x1, Pallas kernels: 1.22 us -> 4.99 us  [crop_columns(): pl.pallas_call(crop_kernel, grid_spec=pltpu.PrefetchScalarGridSpec(num_sc...]
  transfers between devices with their start and end apart: 9 -> 9, of which waited for: 8 -> 8; matrix products, arithmetic and copies ran while one was open for 0% -> 0% of each run, Pallas kernels for 6% -> 5%
where the time goes in v6:
time: 323 us; the launch traced here: 322 us
  blocking collectives  136 us (42%)
  waiting for transfers between devices  74.5 us (23%)
  starting transfers between devices  61.5 us (19%)
  Pallas kernels  45.9 us (14%)
    all_to_all x3, blocking collectives, exchange(): lax.all_to_all(cube, 'row', 0, 0, axis_index_groups=groups, tiled=True)  136 us
    all_to_all x4, starting transfers between devices, exchange(): lax.all_to_all(cube, 'row', 0, 0, axis_index_groups=groups, tiled=True)  42.6 us
    ppermute x2, waiting for transfers between devices, on_device(): right_peer = lax.ppermute(right, 'row', X0_PAIRS)  24.6 us
    all_to_all x1, waiting for transfers between devices, on_device(): lax.all_to_all(cropped, 'row', 0, 0, axis_index_groups=PLANE, tiled=True)  23.9 us
    all_to_all x4, waiting for transfers between devices, exchange(): lax.all_to_all(cube, 'row', 0, 0, axis_index_groups=groups, tiled=True)  23 us
    pallas_call x2, Pallas kernels, middle_half(): pl.pallas_call(functools.partial(middle_kernel, half), grid_spec=pltpu.Pr...  10.5 us
    pallas_call x1, Pallas kernels, first_projection(): pl.pallas_call(first_kernel, grid_spec=pltpu.PrefetchScalarGridSpec(num_s...  8.74 us
    ppermute x1, starting transfers between devices, on_device(): hidden = hidden_features(mine, lax.ppermute(other, 'tmpl', CORES))  8.2 us
  transfers between devices with their start and end apart: 9, of which 8 were waited for; matrix products, arithmetic and copies ran while one was open for 0% of the time, Pallas kernels for 5%

profile of v6, /device:TPU:1, one launch (start us, length us, event | category | flops | bytes accessed | tf_op | source)
XLA Modules:
  0.0 322.0 jit_solution(18000813144446220071)
XLA Ops:
  0.7 5.0 %crop.1 = bf16[16,64,1024]{2,1,0:T(8,128)(2,1)} custom-call(s32[1,8]{1,0:T(1,128)S(1)} %copy-done.4, bf16[16,64,2048]{2,1,0:T(8,128)(2,1)} %bitcast.28), custom_call_target="tpu_custom_call" | custom-call | tf_op jit(solution)/shard_map/crop/pallas_call | solution.py:106
  5.6 7.7 %all-to-all-start = ((bf16[16,64,1024]{2,1,0:T(8,128)(2,1)}), bf16[16,64,1024]{2,1,0:T(8,128)(2,1)S(1)}, u32[]{:S(2)}, u32[]{:S(2)}) async-start(bf16[16,64,1024]{2,1,0:T(8,128)(2,1)} %crop.1), calls=%async_computation | async-start | bytes 4194304 | tf_op jit(solution)/shard_map/all_to_all | solution.py:405
  14.1 3.3 %tables.1 = (bf16[512,256]{1,0:T(8,128)(2,1)S(1)}, bf16[512,512]{1,0:T(8,128)(2,1)S(1)}, bf16[1024,1024]{1,0:T(8,128)(2,1)}, bf16[1024,1024]{1,0:T(8,128)(2,1)}) custom-call(bf16[64,128]{1,0:T(8,128)(2,1)S(1)} %copy-done.6), custom_call_target="tpu_custom_call" | custom-call | flops 1000000000 | bytes 6291456 | tf_op jit(solution)/shard_map/tables/pallas_call | solution.py:87
  17.4 23.9 %all-to-all-done.got_ref = bf16[16,64,1024]{2,1,0:T(8,128)(2,1)S(1)} async-done(((bf16[16,64,1024]{2,1,0:T(8,128)(2,1)}), bf16[16,64,1024]{2,1,0:T(8,128)(2,1)S(1)}, u32[]{:S(2)}, u32[]{:S(2)}) %all-to-all-start) | async-done | bytes 2097184 | tf_op jit(solution)/shard_map/all_to_all | solution.py:405
  41.3 8.7 %first.1 = (bf16[512,1024]{1,0:T(8,128)(2,1)}, bf16[512,2048]{1,0:T(8,128)(2,1)}) custom-call(s32[1,8]{1,0:T(1,128)S(1)} %copy-done.5, s32[1]{0:T(128)S(6)} %copy.9.length_ref.refs_1_, bf16[16,64,1024]{2,1,0:T(8,128)(2,1)S(1)} %all-to-all-done.got_ref, bf16[512,512]{1,0:T(8,128)(2,1)S(1)} %get-tuple-element.23.prow_ref.refs_4_, ...), custom_call_target="tpu_custom_call" | custom-call | tf_op jit(solution)/shard_map/first/pallas_call | solution.py:193
  50.0 58.8 %all_to_all.40 = bf16[64,8,2048]{2,1,0:T(8,128)(2,1)S(1)} all-to-all(bf16[64,8,2048]{2,1,0:T(8,128)(2,1)} %bitcast.31), channel_id=1, replica_groups={{0,1,2,3,4,5,6,7,8,9,10,11,12,13,14,15,16,17,18,19,20,21,22,23,24,25,26..., dimensions={0} | all-to-all | bytes 4194304 | tf_op jit(solution)/shard_map/all_to_all | solution.py:397
  111.2 9.7 %all-to-all-start.3 = ((bf16[64,8,512]{2,1,0:T(8,128)(2,1)}), bf16[64,8,512]{2,1,0:T(8,128)(2,1)S(1)}, u32[]{:S(2)}, u32[]{:S(2)}) async-start(bf16[64,8,512]{2,1,0:T(8,128)(2,1)} %bitcast.6), calls=%async_computation.3 | async-start | bytes 1048576 | tf_op jit(solution)/shard_map/all_to_all | solution.py:397
  120.8 14.7 %collective-permute-done.right_ref = bf16[512,1024]{1,0:T(8,128)(2,1)S(1)} collective-permute-done((bf16[512,1024]{1,0:T(8,128)(2,1)}, bf16[512,1024]{1,0:T(8,128)(2,1)S(1)}, u32[]{:S(2)}, u32[]{:S(2)}) %collective-permute-start) | collective-permute-done | bytes 1048608 | tf_op jit(solution)/shard_map/ppermute | solution.py:412
  138.3 11.6 %all-to-all-start.2 = ((bf16[64,8,512]{2,1,0:T(8,128)(2,1)}), bf16[64,8,512]{2,1,0:T(8,128)(2,1)S(1)}, u32[]{:S(2)}, u32[]{:S(2)}) async-start(bf16[64,8,512]{2,1,0:T(8,128)(2,1)} %bitcast.29), calls=%async_computation.2 | async-start | bytes 1048576 | tf_op jit(solution)/shard_map/all_to_all | solution.py:397
  149.9 5.3 %middle0.1 = (bf16[512,512]{1,0:T(8,128)(2,1)}, bf16[512,2048]{1,0:T(8,128)(2,1)}) custom-call(s32[1,8]{1,0:T(1,128)S(1)} %copy-done.5, s32[1]{0:T(128)S(6)} %copy.9.length_ref.refs_1_, bf16[512,512]{1,0:T(8,128)(2,1)S(1)} %bitcast.24, bf16[512,1024]{1,0:T(8,128)(2,1)} %get-tuple-element.28.refs_3_, bf16[512,512]{1,0:T(8,128)(2,1)S(1)} %get-tuple-element.23.prow_ref.refs_4_, ...), custom_call_target="tpu_custom_call" | custom-call | tf_op jit(solution)/shard_map/middle0/pallas_call | solution.py:227
  155.1 9.5 %all-to-all-done.2 = bf16[64,8,512]{2,1,0:T(8,128)(2,1)S(1)} async-done(((bf16[64,8,512]{2,1,0:T(8,128)(2,1)}), bf16[64,8,512]{2,1,0:T(8,128)(2,1)S(1)}, u32[]{:S(2)}, u32[]{:S(2)}) %all-to-all-start.2) | async-done | bytes 524320 | tf_op jit(solution)/shard_map/all_to_all | solution.py:397
  164.6 5.3 %middle1.1 = (bf16[512,512]{1,0:T(8,128)(2,1)}, bf16[512,2048]{1,0:T(8,128)(2,1)}) custom-call(s32[1,8]{1,0:T(1,128)S(1)} %copy-done.5, s32[1]{0:T(128)S(6)} %copy.9.length_ref.refs_1_, bf16[512,512]{1,0:T(8,128)(2,1)S(1)} %bitcast.23, bf16[512,1024]{1,0:T(8,128)(2,1)} %get-tuple-element.28.refs_3_, ...), custom_call_target="tpu_custom_call", output_to_operand_aliasing={{1}: (8, {})} | custom-call | tf_op jit(solution)/shard_map/middle1/pallas_call | solution.py:227
  169.9 51.4 %all_to_all.41 = bf16[64,8,2048]{2,1,0:T(8,128)(2,1)S(1)} all-to-all(bf16[64,8,2048]{2,1,0:T(8,128)(2,1)} %bitcast.27), channel_id=1, replica_groups={{0,1,2,3,4,5,6,7,8,9,10,11,12,13,14,15,16,17,18,19,20,21,22,23,24,25,26..., dimensions={0} | all-to-all | bytes 4194304 | tf_op jit(solution)/shard_map/all_to_all | solution.py:397
  221.3 2.2 own_products.3
  223.7 9.5 %all-to-all-start.6 = ((bf16[64,8,512]{2,1,0:T(8,128)(2,1)}), bf16[64,8,512]{2,1,0:T(8,128)(2,1)S(1)}, u32[]{:S(2)}, u32[]{:S(2)}) async-start(bf16[64,8,512]{2,1,0:T(8,128)(2,1)} %bitcast.12), calls=%async_computation.6 | async-start | bytes 1048576 | tf_op jit(solution)/shard_map/all_to_all | solution.py:397
  233.2 9.9 %collective-permute-done.1.right_ref = bf16[512,1024]{1,0:T(8,128)(2,1)S(1)} collective-permute-done((bf16[512,1024]{1,0:T(8,128)(2,1)}, bf16[512,1024]{1,0:T(8,128)(2,1)S(1)}, u32[]{:S(2)}, u32[]{:S(2)}) %collective-permute-start.1) | collective-permute-done | bytes 1048608 | tf_op jit(solution)/shard_map/ppermute | solution.py:412
  248.0 11.9 %all-to-all-start.5 = ((bf16[64,8,512]{2,1,0:T(8,128)(2,1)}), bf16[64,8,512]{2,1,0:T(8,128)(2,1)S(1)}, u32[]{:S(2)}, u32[]{:S(2)}) async-start(bf16[64,8,512]{2,1,0:T(8,128)(2,1)} %bitcast.30), calls=%async_computation.5 | async-start | bytes 1048576 | tf_op jit(solution)/shard_map/all_to_all | solution.py:397
  259.8 3.4 %last_own.1.own_hbm = bf16[512,512]{1,0:T(8,128)(2,1)} custom-call(bf16[512,512]{1,0:T(8,128)(2,1)S(1)} %bitcast.21, bf16[512,512]{1,0:T(8,128)(2,1)} %get-tuple-element.36.cur_ref, bf16[512,512]{1,0:T(8,128)(2,1)S(1)} %get-tuple-element.23.prow_ref.refs_4_, bf16[2,64,320]{2,1,0:T(8,128)(2,1)S(1)} %copy-done, bf16[2,64,64]{2,1,0:T(8,128)(2,1)S(1)} %copy-done.3), custom_call_target="tpu_custom_call" | custom-call | tf_op jit(solution)/shard_map/last_own/pallas_call | solution.py:290
  263.2 11.4 %all-to-all-done.5 = bf16[64,8,512]{2,1,0:T(8,128)(2,1)S(1)} async-done(((bf16[64,8,512]{2,1,0:T(8,128)(2,1)}), bf16[64,8,512]{2,1,0:T(8,128)(2,1)S(1)}, u32[]{:S(2)}, u32[]{:S(2)}) %all-to-all-start.5) | async-done | bytes 524320 | tf_op jit(solution)/shard_map/all_to_all | solution.py:397
  274.6 4.3 %last_peer.1 = (bf16[1024,256]{1,0:T(8,128)(2,1)S(1)}, bf16[1024,256]{1,0:T(8,128)(2,1)S(1)}) custom-call(bf16[512,512]{1,0:T(8,128)(2,1)S(1)} %bitcast.22, bf16[512,512]{1,0:T(8,128)(2,1)} %get-tuple-element.34.cur_ref, bf16[512,512]{1,0:T(8,128)(2,1)S(1)} %get-tuple-element.23.prow_ref.refs_4_, bf16[2,64,320]{2,1,0:T(8,128)(2,1)S(1)} %copy-done, ...), custom_call_target="tpu_custom_call" | custom-call | tf_op jit(solution)/shard_map/last_peer/pallas_call | solution.py:302
  278.9 8.2 %collective-permute-start.2 = (bf16[1024,256]{1,0:T(8,128)(2,1)S(1)}, bf16[1024,256]{1,0:T(8,128)(2,1)S(1)}, u32[]{:S(2)}, u32[]{:S(2)}) collective-permute-start(bf16[1024,256]{1,0:T(8,128)(2,1)S(1)} %get-tuple-element.39), channel_id=1, source_target_pairs={{0,128},{128,0},{1,129},{129,1},{2,130},{130,2},{3,131},{131,3},{4... | collective-permute-start | bytes 1572872 | tf_op jit(solution)/shard_map/ppermute | solution.py:421
  288.8 25.8 %all_to_all.42 = bf16[128,8,256]{2,1,0:T(8,128)(2,1)S(1)} all-to-all(bf16[128,8,256]{2,1,0:T(8,128)(2,1)S(1)} %fusion), channel_id=1, replica_groups={{0,8,16,24,32,40,48,56,64,72,80,88,96,104,112,120,1,9,17,25,33,41,49,57..., dimensions={0} | all-to-all | bytes 1048576 | tf_op jit(solution)/shard_map/all_to_all | solution.py:397
  314.6 2.8 collective-permute-start.3
  319.0 3.1 final.1
  (24 shorter events, 14.0 us)
Async XLA Ops:
  0.0 0.7 copy-start.4
  5.6 8.4 %copy-start.6 = (bf16[64,128]{1,0:T(8,128)(2,1)S(1)}, bf16[64,128]{1,0:T(8,128)(2,1)}, u32[]{:S(2)}) copy-start(bf16[64,128]{1,0:T(8,128)(2,1)} %final_ref.1) | copy-start | bytes 49156
  5.6 35.6 %all-to-all-start = ((bf16[16,64,1024]{2,1,0:T(8,128)(2,1)}), bf16[16,64,1024]{2,1,0:T(8,128)(2,1)S(1)}, u32[]{:S(2)}, u32[]{:S(2)}) async-start(bf16[16,64,1024]{2,1,0:T(8,128)(2,1)} %crop.1), calls=%async_computation | async-start | bytes 4194304 | tf_op jit(solution)/shard_map/all_to_all | solution.py:405
  13.4 27.9 %copy-start = (bf16[2,64,320]{2,1,0:T(8,128)(2,1)S(1)}, bf16[2,64,320]{2,1,0:T(8,128)(2,1)}, u32[]{:S(2)}) copy-start(bf16[2,64,320]{2,1,0:T(8,128)(2,1)} %w_ref.5) | copy-start | bytes 245764
  13.4 27.9 %copy-start.5 = (s32[1,8]{1,0:T(1,128)S(1)}, s32[1,8]{1,0:T(1,128)}, u32[]{:S(2)}) copy-start(s32[1,8]{1,0:T(1,128)} %refs_0_.3) | copy-start | bytes 100
  111.1 24.5 %collective-permute-start = (bf16[512,1024]{1,0:T(8,128)(2,1)}, bf16[512,1024]{1,0:T(8,128)(2,1)S(1)}, u32[]{:S(2)}, u32[]{:S(2)}) collective-permute-start(bf16[512,1024]{1,0:T(8,128)(2,1)} %get-tuple-element.27), channel_id=1, source_target_pairs={{0,32},{1,33},{2,34},{3,35},{4,36},{5,37},{6,38},{7,39},{8,40},{9,... | collective-permute-start | bytes 3145736 | tf_op jit(solution)/shard_map/ppermute | solution.py:412
  111.2 38.7 %copy-start.3 = (bf16[2,64,64]{2,1,0:T(8,128)(2,1)S(1)}, bf16[2,64,64]{2,1,0:T(8,128)(2,1)}, u32[]{:S(2)}) copy-start(bf16[2,64,64]{2,1,0:T(8,128)(2,1)} %w_out_ref.3) | copy-start | bytes 49156
  111.2 27.1 %all-to-all-start.3 = ((bf16[64,8,512]{2,1,0:T(8,128)(2,1)}), bf16[64,8,512]{2,1,0:T(8,128)(2,1)S(1)}, u32[]{:S(2)}, u32[]{:S(2)}) async-start(bf16[64,8,512]{2,1,0:T(8,128)(2,1)} %bitcast.6), calls=%async_computation.3 | async-start | bytes 1048576 | tf_op jit(solution)/shard_map/all_to_all | solution.py:397
  135.5 1.2 copy-start.1
  138.3 26.3 %all-to-all-start.2 = ((bf16[64,8,512]{2,1,0:T(8,128)(2,1)}), bf16[64,8,512]{2,1,0:T(8,128)(2,1)S(1)}, u32[]{:S(2)}, u32[]{:S(2)}) async-start(bf16[64,8,512]{2,1,0:T(8,128)(2,1)} %bitcast.29), calls=%async_computation.2 | async-start | bytes 1048576 | tf_op jit(solution)/shard_map/all_to_all | solution.py:397
  223.6 19.5 %collective-permute-start.1 = (bf16[512,1024]{1,0:T(8,128)(2,1)}, bf16[512,1024]{1,0:T(8,128)(2,1)S(1)}, u32[]{:S(2)}, u32[]{:S(2)}) collective-permute-start(bf16[512,1024]{1,0:T(8,128)(2,1)} %get-tuple-element.33), channel_id=1, source_target_pairs={{0,32},{1,33},{2,34},{3,35},{4,36},{5,37},{6,38},{7,39},{8,40},{9,... | collective-permute-start | bytes 3145736 | tf_op jit(solution)/shard_map/ppermute | solution.py:412
  223.7 24.3 %all-to-all-start.6 = ((bf16[64,8,512]{2,1,0:T(8,128)(2,1)}), bf16[64,8,512]{2,1,0:T(8,128)(2,1)S(1)}, u32[]{:S(2)}, u32[]{:S(2)}) async-start(bf16[64,8,512]{2,1,0:T(8,128)(2,1)} %bitcast.12), calls=%async_computation.6 | async-start | bytes 1048576 | tf_op jit(solution)/shard_map/all_to_all | solution.py:397
  243.1 1.2 copy-start.2
  248.0 26.6 %all-to-all-start.5 = ((bf16[64,8,512]{2,1,0:T(8,128)(2,1)}), bf16[64,8,512]{2,1,0:T(8,128)(2,1)S(1)}, u32[]{:S(2)}, u32[]{:S(2)}) async-start(bf16[64,8,512]{2,1,0:T(8,128)(2,1)} %bitcast.30), calls=%async_computation.5 | async-start | bytes 1048576 | tf_op jit(solution)/shard_map/all_to_all | solution.py:397
  278.9 9.7 %collective-permute-start.2 = (bf16[1024,256]{1,0:T(8,128)(2,1)S(1)}, bf16[1024,256]{1,0:T(8,128)(2,1)S(1)}, u32[]{:S(2)}, u32[]{:S(2)}) collective-permute-start(bf16[1024,256]{1,0:T(8,128)(2,1)S(1)} %get-tuple-element.39), channel_id=1, source_target_pairs={{0,128},{128,0},{1,129},{129,1},{2,130},{130,2},{3,131},{131,3},{4... | collective-permute-start | bytes 1572872 | tf_op jit(solution)/shard_map/ppermute | solution.py:421
  314.6 4.3 %collective-permute-start.3 = (bf16[1024,256]{1,0:T(8,128)(2,1)S(1)}, bf16[1024,256]{1,0:T(8,128)(2,1)S(1)}, u32[]{:S(2)}, u32[]{:S(2)}) collective-permute-start(bf16[1024,256]{1,0:T(8,128)(2,1)S(1)} %bitcast.25), channel_id=1, source_target_pairs={{0,128},{128,0},{1,129},{129,1},{2,130},{130,2},{3,131},{131,3},{4... | collective-permute-start | bytes 1572872 | tf_op jit(solution)/shard_map/ppermute | solution.py:423

commit v7 on v6

--- a/solution.py
+++ b/solution.py
@@ -26,7 +26,7 @@
 BY_Z = [[s * 8 + z for z in range(8) for s in range(16)]]
 X0_PAIRS = [(r, r ^ 32) for r in range(128)]
 CORES = [(0, 1), (1, 0)]
-VMEM_LIMIT = 20 * 1024 * 1024
+VMEM_LIMIT = 24 * 1024 * 1024
 
 
 def in_vmem(*arrays):
@@ -96,10 +96,30 @@
     )(final_weight)
 
 
-def crop_kernel(crop_ref, x_ref, o_ref):
-    for a in range(8):
-        start = pl.multiple_of(crop_ref[0, a] * TILE, TILE)
-        o_ref[:, :, a * TILE : (a + 1) * TILE] = x_ref[:, :, pl.ds(start, TILE)]
+CROP_CHUNKS = 4
+
+
+def crop_kernel(crop_ref, x_hbm, o_hbm, rows_ref, in_sems, out_sems):
+    size = 16 // CROP_CHUNKS
+    loads, stores = [], []
+    for chunk in range(CROP_CHUNKS):
+        rows = pl.ds(chunk * size, size)
+        for a in range(8):
+            tile = pl.ds(pl.multiple_of(crop_ref[0, a] * TILE, TILE), TILE)
+            load = pltpu.make_async_copy(
+                x_hbm.at[rows, :, tile], rows_ref.at[rows, :, pl.ds(a * TILE, TILE)], in_sems.at[chunk * 8 + a]
+            )
+            load.start()
+            loads.append(load)
+    for chunk in range(CROP_CHUNKS):
+        rows = pl.ds(chunk * size, size)
+        for load in loads[chunk * 8 : chunk * 8 + 8]:
+            load.wait()
+        store = pltpu.make_async_copy(rows_ref.at[rows], o_hbm.at[rows], out_sems.at[chunk])
+        store.start()
+        stores.append(store)
+    for store in stores:
+        store.wait()
 
 
 def crop_columns(crop_tiles, pair):
@@ -107,9 +127,14 @@
         crop_kernel,
         grid_spec=pltpu.PrefetchScalarGridSpec(
             num_scalar_prefetch=1,
-            grid=(4,),
-            in_specs=[pl.BlockSpec((4, CH, FULL), lambda m, crop: (m, 0, 0))],
-            out_specs=pl.BlockSpec((4, CH, CROP), lambda m, crop: (m, 0, 0)),
+            grid=(1,),
+            in_specs=[pl.BlockSpec(memory_space=pl.ANY)],
+            out_specs=pl.BlockSpec(memory_space=pl.ANY),
+            scratch_shapes=[
+                pltpu.VMEM((16, CH, CROP), BF),
+                pltpu.SemaphoreType.DMA((8 * CROP_CHUNKS,)),
+                pltpu.SemaphoreType.DMA((CROP_CHUNKS,)),
+            ],
         ),
         out_shape=pltpu.HBM((16, CH, CROP), BF),
         compiler_params=pltpu.CompilerParams(vmem_limit_bytes=VMEM_LIMIT),
@@ -161,10 +186,13 @@
         both_ref[:, side * lanes : (side + 1) * lanes] = dot(prow, stacked(factor)).astype(BF)
 
 
-BLOCK = 256
+BLOCK = 512
 ANYWHERE = pl.BlockSpec(memory_space=pl.ANY)
+RESIDENT = pl.BlockSpec(memory_space=pltpu.VMEM)
 STEPS = CROP // BLOCK
 HALF_STEPS = STEPS // 2
+LAST_BLOCK = 256
+LAST_STEPS = 512 // LAST_BLOCK
 BOTH = pltpu.HBM((512, 2 * CROP), BF)
 
 
@@ -195,19 +223,21 @@
         grid_spec=pltpu.PrefetchScalarGridSpec(
             num_scalar_prefetch=2,
             grid=(STEPS,),
-            in_specs=[full((16, CH, CROP)), full((512, 512)), lanes_of(CROP), layer_weight(320, 0)],
+            in_specs=[RESIDENT, RESIDENT, lanes_of(CROP), layer_weight(320, 0)],
             out_specs=[lanes_of(512), lanes_of(512, 2 * BLOCK)],
         ),
         out_shape=[pltpu.HBM((512, CROP), BF), BOTH],
         compiler_params=pltpu.CompilerParams(vmem_limit_bytes=VMEM_LIMIT),
         name="first",
-    )(crop_tiles, full_length, got, *in_vmem(prow), *in_hbm(q), proj_weight)
+    )(crop_tiles, full_length, *in_vmem(got, prow), *in_hbm(q), proj_weight)
 
 
 def update(back_ref, cur_ref, prow, w_proj, w_out):
+    block = cur_ref.shape[1]
     current = side_by_side(cur_ref[...].astype(F32))
     gate = sigmoid(dot_tn(w_proj[:, 4 * CH :], norm_channels(current).astype(BF)))
-    products = side_by_side(dot_tn(prow, back_ref[...]))
+    lanes = pl.ds(pl.multiple_of(pl.program_id(0) * block, block), block)
+    products = side_by_side(dot_tn(prow, back_ref[:, lanes]))
     change = dot_tn(w_out, norm_channels(products).astype(BF))
     return (current + gate * change).astype(BF)
 
@@ -230,7 +260,7 @@
             num_scalar_prefetch=2,
             grid=(HALF_STEPS,),
             in_specs=[
-                lanes_of(512), lanes_of(512, offset=offset), full((512, 512)),
+                RESIDENT, lanes_of(512, offset=offset), RESIDENT,
                 layer_weight(320, layer), layer_weight(CH, layer), layer_weight(320, layer + 1),
             ]
             + [ANYWHERE] * len(aliased),
@@ -241,7 +271,7 @@
         compiler_params=pltpu.CompilerParams(vmem_limit_bytes=VMEM_LIMIT),
         name="middle" + str(half),
     )(
-        crop_tiles, full_length, back, *in_hbm(current), *in_vmem(prow), proj_weight, out_weight, proj_weight,
+        crop_tiles, full_length, *in_vmem(back), *in_hbm(current), *in_vmem(prow), proj_weight, out_weight, proj_weight,
         *aliased,
     )
 
@@ -269,10 +299,10 @@
         for load in loads:
             load.start()
 
-    lanes = pl.ds(pl.multiple_of(512 + step * BLOCK, BLOCK), BLOCK)
+    lanes = pl.ds(pl.multiple_of(512 + step * LAST_BLOCK, LAST_BLOCK), LAST_BLOCK)
     rows_ref[:, lanes] = last_rows(back_ref, cur_ref, prow_ref, w_ref, w_out_ref)
 
-    @pl.when(step == HALF_STEPS - 1)
+    @pl.when(step == LAST_STEPS - 1)
     def _():
         for load in loads:
             load.wait()
@@ -283,25 +313,25 @@
 
 
 def last_specs(layer):
-    return [lanes_of(512)] * 2 + [full((512, 512)), layer_weight(320, layer), layer_weight(CH, layer)]
+    return [RESIDENT, lanes_of(512, LAST_BLOCK), RESIDENT, layer_weight(320, layer), layer_weight(CH, layer)]
 
 
 def last_own(back, current, prow, proj_weight, out_weight, layer):
     return pl.pallas_call(
         last_own_kernel,
-        grid=(HALF_STEPS,),
+        grid=(LAST_STEPS,),
         in_specs=last_specs(layer),
-        out_specs=lanes_of(512),
+        out_specs=lanes_of(512, LAST_BLOCK),
         out_shape=pltpu.HBM((512, 512), BF),
         compiler_params=pltpu.CompilerParams(vmem_limit_bytes=VMEM_LIMIT),
         name="last_own",
-    )(back, *in_hbm(current), *in_vmem(prow), proj_weight, out_weight)
+    )(*in_vmem(back), *in_hbm(current), *in_vmem(prow), proj_weight, out_weight)
 
 
 def last_peer(back, current, prow, proj_weight, out_weight, own, pj, layer):
     return pl.pallas_call(
         last_peer_kernel,
-        grid=(HALF_STEPS,),
+        grid=(LAST_STEPS,),
         in_specs=last_specs(layer) + [ANYWHERE, ANYWHERE],
         out_specs=[full((CROP, 256))] * 2,
         out_shape=[jax.ShapeDtypeStruct((CROP, 256), BF)] * 2,
@@ -310,7 +340,7 @@
         ],
         compiler_params=pltpu.CompilerParams(vmem_limit_bytes=VMEM_LIMIT),
         name="last_peer",
-    )(back, *in_hbm(current), *in_vmem(prow), proj_weight, out_weight, *in_hbm(own, pj))
+    )(*in_vmem(back), *in_hbm(current), *in_vmem(prow), proj_weight, out_weight, *in_hbm(own, pj))
 
 
 def own_products_kernel(both_ref, out_ref, left_hbm, right_hbm, sems):

time: 323 us -> 319 us (0.988)
  Pallas kernels: 45.9 us -> 42.3 us
where the time goes in v7:
time: 319 us; the launch traced here: 318 us
  blocking collectives  136 us (43%)
  waiting for transfers between devices  74 us (23%)
  starting transfers between devices  61.8 us (19%)
  Pallas kernels  42.3 us (13%)
    all_to_all x3, blocking collectives, exchange(): lax.all_to_all(cube, 'row', 0, 0, axis_index_groups=groups, tiled=True)  136 us
    all_to_all x4, starting transfers between devices, exchange(): lax.all_to_all(cube, 'row', 0, 0, axis_index_groups=groups, tiled=True)  43 us
    ppermute x2, waiting for transfers between devices, on_device(): right_peer = lax.ppermute(right, 'row', X0_PAIRS)  24.6 us
    all_to_all x1, waiting for transfers between devices, on_device(): lax.all_to_all(cropped, 'row', 0, 0, axis_index_groups=PLANE, tiled=True)  23.8 us
    all_to_all x4, waiting for transfers between devices, exchange(): lax.all_to_all(cube, 'row', 0, 0, axis_index_groups=groups, tiled=True)  22.6 us
    pallas_call x2, Pallas kernels, middle_half(): pl.pallas_call(functools.partial(middle_kernel, half), grid_spec=pltpu.Pr...  10.6 us
    ppermute x1, starting transfers between devices, on_device(): hidden = hidden_features(mine, lax.ppermute(other, 'tmpl', CORES))  8.19 us
    all_to_all x1, starting transfers between devices, on_device(): lax.all_to_all(cropped, 'row', 0, 0, axis_index_groups=PLANE, tiled=True)  7.6 us
  transfers between devices with their start and end apart: 9, of which 8 were waited for; matrix products, arithmetic and copies ran while one was open for 0% of the time, Pallas kernels for 5%

profile of v7, /device:TPU:1, one launch (start us, length us, event | category | flops | bytes accessed | tf_op | source)
XLA Modules:
  0.0 318.2 jit_solution(6129755560261057606)
XLA Ops:
  0.7 3.3 %crop.1 = bf16[16,64,1024]{2,1,0:T(8,128)(2,1)} custom-call(s32[1,8]{1,0:T(1,128)S(1)} %copy-done.4, bf16[16,64,2048]{2,1,0:T(8,128)(2,1)} %bitcast.28), custom_call_target="tpu_custom_call" | custom-call | tf_op jit(solution)/shard_map/crop/pallas_call | solution.py:126
  3.9 7.6 %all-to-all-start = ((bf16[16,64,1024]{2,1,0:T(8,128)(2,1)}), bf16[16,64,1024]{2,1,0:T(8,128)(2,1)S(1)}, u32[]{:S(2)}, u32[]{:S(2)}) async-start(bf16[16,64,1024]{2,1,0:T(8,128)(2,1)} %crop.1), calls=%async_computation | async-start | bytes 4194304 | tf_op jit(solution)/shard_map/all_to_all | solution.py:435
  12.3 3.3 %tables.1 = (bf16[512,256]{1,0:T(8,128)(2,1)S(1)}, bf16[512,512]{1,0:T(8,128)(2,1)S(1)}, bf16[1024,1024]{1,0:T(8,128)(2,1)}, bf16[1024,1024]{1,0:T(8,128)(2,1)}) custom-call(bf16[64,128]{1,0:T(8,128)(2,1)S(1)} %copy-done.6), custom_call_target="tpu_custom_call" | custom-call | flops 1000000000 | bytes 6291456 | tf_op jit(solution)/shard_map/tables/pallas_call | solution.py:87
  15.6 23.8 %all-to-all-done.got_ref = bf16[16,64,1024]{2,1,0:T(8,128)(2,1)S(1)} async-done(((bf16[16,64,1024]{2,1,0:T(8,128)(2,1)}), bf16[16,64,1024]{2,1,0:T(8,128)(2,1)S(1)}, u32[]{:S(2)}, u32[]{:S(2)}) %all-to-all-start) | async-done | bytes 2097184 | tf_op jit(solution)/shard_map/all_to_all | solution.py:435
  39.4 7.0 %first.1 = (bf16[512,1024]{1,0:T(8,128)(2,1)}, bf16[512,2048]{1,0:T(8,128)(2,1)}) custom-call(s32[1,8]{1,0:T(1,128)S(1)} %copy-done.5, s32[1]{0:T(128)S(6)} %copy.9.length_ref.refs_1_, bf16[16,64,1024]{2,1,0:T(8,128)(2,1)S(1)} %all-to-all-done.got_ref, bf16[512,512]{1,0:T(8,128)(2,1)S(1)} %get-tuple-element.23.prow_ref.refs_4_, ...), custom_call_target="tpu_custom_call" | custom-call | tf_op jit(solution)/shard_map/first/pallas_call | solution.py:221
  46.4 58.8 %all_to_all.40 = bf16[64,8,2048]{2,1,0:T(8,128)(2,1)S(1)} all-to-all(bf16[64,8,2048]{2,1,0:T(8,128)(2,1)} %bitcast.31), channel_id=1, replica_groups={{0,1,2,3,4,5,6,7,8,9,10,11,12,13,14,15,16,17,18,19,20,21,22,23,24,25,26..., dimensions={0} | all-to-all | bytes 4194304 | tf_op jit(solution)/shard_map/all_to_all | solution.py:427
  107.6 9.6 %all-to-all-start.3 = ((bf16[64,8,512]{2,1,0:T(8,128)(2,1)}), bf16[64,8,512]{2,1,0:T(8,128)(2,1)S(1)}, u32[]{:S(2)}, u32[]{:S(2)}) async-start(bf16[64,8,512]{2,1,0:T(8,128)(2,1)} %bitcast.6), calls=%async_computation.3 | async-start | bytes 1048576 | tf_op jit(solution)/shard_map/all_to_all | solution.py:427
  117.2 14.7 %collective-permute-done.right_ref = bf16[512,1024]{1,0:T(8,128)(2,1)S(1)} collective-permute-done((bf16[512,1024]{1,0:T(8,128)(2,1)}, bf16[512,1024]{1,0:T(8,128)(2,1)S(1)}, u32[]{:S(2)}, u32[]{:S(2)}) %collective-permute-start) | collective-permute-done | bytes 1048608 | tf_op jit(solution)/shard_map/ppermute | solution.py:442
  134.7 11.7 %all-to-all-start.2 = ((bf16[64,8,512]{2,1,0:T(8,128)(2,1)}), bf16[64,8,512]{2,1,0:T(8,128)(2,1)S(1)}, u32[]{:S(2)}, u32[]{:S(2)}) async-start(bf16[64,8,512]{2,1,0:T(8,128)(2,1)} %bitcast.29), calls=%async_computation.2 | async-start | bytes 1048576 | tf_op jit(solution)/shard_map/all_to_all | solution.py:427
  146.4 5.3 %middle0.1 = (bf16[512,512]{1,0:T(8,128)(2,1)}, bf16[512,2048]{1,0:T(8,128)(2,1)}) custom-call(s32[1,8]{1,0:T(1,128)S(1)} %copy-done.5, s32[1]{0:T(128)S(6)} %copy.9.length_ref.refs_1_, bf16[512,512]{1,0:T(8,128)(2,1)S(1)} %bitcast.24, bf16[512,1024]{1,0:T(8,128)(2,1)} %get-tuple-element.28.refs_3_, bf16[512,512]{1,0:T(8,128)(2,1)S(1)} %get-tuple-element.23.prow_ref.refs_4_, ...), custom_call_target="tpu_custom_call" | custom-call | tf_op jit(solution)/shard_map/middle0/pallas_call | solution.py:257
  151.8 9.2 %all-to-all-done.2 = bf16[64,8,512]{2,1,0:T(8,128)(2,1)S(1)} async-done(((bf16[64,8,512]{2,1,0:T(8,128)(2,1)}), bf16[64,8,512]{2,1,0:T(8,128)(2,1)S(1)}, u32[]{:S(2)}, u32[]{:S(2)}) %all-to-all-start.2) | async-done | bytes 524320 | tf_op jit(solution)/shard_map/all_to_all | solution.py:427
  161.0 5.3 %middle1.1 = (bf16[512,512]{1,0:T(8,128)(2,1)}, bf16[512,2048]{1,0:T(8,128)(2,1)}) custom-call(s32[1,8]{1,0:T(1,128)S(1)} %copy-done.5, s32[1]{0:T(128)S(6)} %copy.9.length_ref.refs_1_, bf16[512,512]{1,0:T(8,128)(2,1)S(1)} %bitcast.23, bf16[512,1024]{1,0:T(8,128)(2,1)} %get-tuple-element.28.refs_3_, ...), custom_call_target="tpu_custom_call", output_to_operand_aliasing={{1}: (8, {})} | custom-call | tf_op jit(solution)/shard_map/middle1/pallas_call | solution.py:257
  166.3 51.4 %all_to_all.41 = bf16[64,8,2048]{2,1,0:T(8,128)(2,1)S(1)} all-to-all(bf16[64,8,2048]{2,1,0:T(8,128)(2,1)} %bitcast.27), channel_id=1, replica_groups={{0,1,2,3,4,5,6,7,8,9,10,11,12,13,14,15,16,17,18,19,20,21,22,23,24,25,26..., dimensions={0} | all-to-all | bytes 4194304 | tf_op jit(solution)/shard_map/all_to_all | solution.py:427
  217.7 2.2 own_products.3
  220.0 9.6 %all-to-all-start.6 = ((bf16[64,8,512]{2,1,0:T(8,128)(2,1)}), bf16[64,8,512]{2,1,0:T(8,128)(2,1)S(1)}, u32[]{:S(2)}, u32[]{:S(2)}) async-start(bf16[64,8,512]{2,1,0:T(8,128)(2,1)} %bitcast.12), calls=%async_computation.6 | async-start | bytes 1048576 | tf_op jit(solution)/shard_map/all_to_all | solution.py:427
  229.6 9.8 %collective-permute-done.1.right_ref = bf16[512,1024]{1,0:T(8,128)(2,1)S(1)} collective-permute-done((bf16[512,1024]{1,0:T(8,128)(2,1)}, bf16[512,1024]{1,0:T(8,128)(2,1)S(1)}, u32[]{:S(2)}, u32[]{:S(2)}) %collective-permute-start.1) | collective-permute-done | bytes 1048608 | tf_op jit(solution)/shard_map/ppermute | solution.py:442
  244.3 12.1 %all-to-all-start.5 = ((bf16[64,8,512]{2,1,0:T(8,128)(2,1)}), bf16[64,8,512]{2,1,0:T(8,128)(2,1)S(1)}, u32[]{:S(2)}, u32[]{:S(2)}) async-start(bf16[64,8,512]{2,1,0:T(8,128)(2,1)} %bitcast.30), calls=%async_computation.5 | async-start | bytes 1048576 | tf_op jit(solution)/shard_map/all_to_all | solution.py:427
  256.4 3.3 %last_own.1.own_hbm = bf16[512,512]{1,0:T(8,128)(2,1)} custom-call(bf16[512,512]{1,0:T(8,128)(2,1)S(1)} %bitcast.21, bf16[512,512]{1,0:T(8,128)(2,1)} %get-tuple-element.36.cur_ref, bf16[512,512]{1,0:T(8,128)(2,1)S(1)} %get-tuple-element.23.prow_ref.refs_4_, bf16[2,64,320]{2,1,0:T(8,128)(2,1)S(1)} %copy-done, bf16[2,64,64]{2,1,0:T(8,128)(2,1)S(1)} %copy-done.3), custom_call_target="tpu_custom_call" | custom-call | tf_op jit(solution)/shard_map/last_own/pallas_call | solution.py:320
  259.8 11.2 %all-to-all-done.5 = bf16[64,8,512]{2,1,0:T(8,128)(2,1)S(1)} async-done(((bf16[64,8,512]{2,1,0:T(8,128)(2,1)}), bf16[64,8,512]{2,1,0:T(8,128)(2,1)S(1)}, u32[]{:S(2)}, u32[]{:S(2)}) %all-to-all-start.5) | async-done | bytes 524320 | tf_op jit(solution)/shard_map/all_to_all | solution.py:427
  271.0 4.2 %last_peer.1 = (bf16[1024,256]{1,0:T(8,128)(2,1)S(1)}, bf16[1024,256]{1,0:T(8,128)(2,1)S(1)}) custom-call(bf16[512,512]{1,0:T(8,128)(2,1)S(1)} %bitcast.22, bf16[512,512]{1,0:T(8,128)(2,1)} %get-tuple-element.34.cur_ref, bf16[512,512]{1,0:T(8,128)(2,1)S(1)} %get-tuple-element.23.prow_ref.refs_4_, bf16[2,64,320]{2,1,0:T(8,128)(2,1)S(1)} %copy-done, ...), custom_call_target="tpu_custom_call" | custom-call | tf_op jit(solution)/shard_map/last_peer/pallas_call | solution.py:332
  275.1 8.2 %collective-permute-start.2 = (bf16[1024,256]{1,0:T(8,128)(2,1)S(1)}, bf16[1024,256]{1,0:T(8,128)(2,1)S(1)}, u32[]{:S(2)}, u32[]{:S(2)}) collective-permute-start(bf16[1024,256]{1,0:T(8,128)(2,1)S(1)} %get-tuple-element.39), channel_id=1, source_target_pairs={{0,128},{128,0},{1,129},{129,1},{2,130},{130,2},{3,131},{131,3},{4... | collective-permute-start | bytes 1572872 | tf_op jit(solution)/shard_map/ppermute | solution.py:451
  285.1 25.8 %all_to_all.42 = bf16[128,8,256]{2,1,0:T(8,128)(2,1)S(1)} all-to-all(bf16[128,8,256]{2,1,0:T(8,128)(2,1)S(1)} %fusion), channel_id=1, replica_groups={{0,8,16,24,32,40,48,56,64,72,80,88,96,104,112,120,1,9,17,25,33,41,49,57..., dimensions={0} | all-to-all | bytes 1048576 | tf_op jit(solution)/shard_map/all_to_all | solution.py:427
  310.8 2.8 collective-permute-start.3
  315.2 3.1 final.1
  (24 shorter events, 14.0 us)
Async XLA Ops:
  0.0 0.7 copy-start.4
  3.9 8.3 %copy-start.6 = (bf16[64,128]{1,0:T(8,128)(2,1)S(1)}, bf16[64,128]{1,0:T(8,128)(2,1)}, u32[]{:S(2)}) copy-start(bf16[64,128]{1,0:T(8,128)(2,1)} %final_ref.1) | copy-start | bytes 49156
  3.9 35.5 %all-to-all-start = ((bf16[16,64,1024]{2,1,0:T(8,128)(2,1)}), bf16[16,64,1024]{2,1,0:T(8,128)(2,1)S(1)}, u32[]{:S(2)}, u32[]{:S(2)}) async-start(bf16[16,64,1024]{2,1,0:T(8,128)(2,1)} %crop.1), calls=%async_computation | async-start | bytes 4194304 | tf_op jit(solution)/shard_map/all_to_all | solution.py:435
  11.6 27.9 %copy-start = (bf16[2,64,320]{2,1,0:T(8,128)(2,1)S(1)}, bf16[2,64,320]{2,1,0:T(8,128)(2,1)}, u32[]{:S(2)}) copy-start(bf16[2,64,320]{2,1,0:T(8,128)(2,1)} %w_ref.5) | copy-start | bytes 245764
  11.6 27.9 %copy-start.5 = (s32[1,8]{1,0:T(1,128)S(1)}, s32[1,8]{1,0:T(1,128)}, u32[]{:S(2)}) copy-start(s32[1,8]{1,0:T(1,128)} %refs_0_.3) | copy-start | bytes 100
  107.5 24.5 %collective-permute-start = (bf16[512,1024]{1,0:T(8,128)(2,1)}, bf16[512,1024]{1,0:T(8,128)(2,1)S(1)}, u32[]{:S(2)}, u32[]{:S(2)}) collective-permute-start(bf16[512,1024]{1,0:T(8,128)(2,1)} %get-tuple-element.27), channel_id=1, source_target_pairs={{0,32},{1,33},{2,34},{3,35},{4,36},{5,37},{6,38},{7,39},{8,40},{9,... | collective-permute-start | bytes 3145736 | tf_op jit(solution)/shard_map/ppermute | solution.py:442
  107.6 38.9 %copy-start.3 = (bf16[2,64,64]{2,1,0:T(8,128)(2,1)S(1)}, bf16[2,64,64]{2,1,0:T(8,128)(2,1)}, u32[]{:S(2)}) copy-start(bf16[2,64,64]{2,1,0:T(8,128)(2,1)} %w_out_ref.3) | copy-start | bytes 49156
  107.6 27.1 %all-to-all-start.3 = ((bf16[64,8,512]{2,1,0:T(8,128)(2,1)}), bf16[64,8,512]{2,1,0:T(8,128)(2,1)S(1)}, u32[]{:S(2)}, u32[]{:S(2)}) async-start(bf16[64,8,512]{2,1,0:T(8,128)(2,1)} %bitcast.6), calls=%async_computation.3 | async-start | bytes 1048576 | tf_op jit(solution)/shard_map/all_to_all | solution.py:427
  131.9 1.2 copy-start.1
  134.7 26.3 %all-to-all-start.2 = ((bf16[64,8,512]{2,1,0:T(8,128)(2,1)}), bf16[64,8,512]{2,1,0:T(8,128)(2,1)S(1)}, u32[]{:S(2)}, u32[]{:S(2)}) async-start(bf16[64,8,512]{2,1,0:T(8,128)(2,1)} %bitcast.29), calls=%async_computation.2 | async-start | bytes 1048576 | tf_op jit(solution)/shard_map/all_to_all | solution.py:427
  219.9 19.5 %collective-permute-start.1 = (bf16[512,1024]{1,0:T(8,128)(2,1)}, bf16[512,1024]{1,0:T(8,128)(2,1)S(1)}, u32[]{:S(2)}, u32[]{:S(2)}) collective-permute-start(bf16[512,1024]{1,0:T(8,128)(2,1)} %get-tuple-element.33), channel_id=1, source_target_pairs={{0,32},{1,33},{2,34},{3,35},{4,36},{5,37},{6,38},{7,39},{8,40},{9,... | collective-permute-start | bytes 3145736 | tf_op jit(solution)/shard_map/ppermute | solution.py:442
  220.0 24.3 %all-to-all-start.6 = ((bf16[64,8,512]{2,1,0:T(8,128)(2,1)}), bf16[64,8,512]{2,1,0:T(8,128)(2,1)S(1)}, u32[]{:S(2)}, u32[]{:S(2)}) async-start(bf16[64,8,512]{2,1,0:T(8,128)(2,1)} %bitcast.12), calls=%async_computation.6 | async-start | bytes 1048576 | tf_op jit(solution)/shard_map/all_to_all | solution.py:427
  239.4 1.2 copy-start.2
  244.3 26.6 %all-to-all-start.5 = ((bf16[64,8,512]{2,1,0:T(8,128)(2,1)}), bf16[64,8,512]{2,1,0:T(8,128)(2,1)S(1)}, u32[]{:S(2)}, u32[]{:S(2)}) async-start(bf16[64,8,512]{2,1,0:T(8,128)(2,1)} %bitcast.30), calls=%async_computation.5 | async-start | bytes 1048576 | tf_op jit(solution)/shard_map/all_to_all | solution.py:427
  275.1 9.7 %collective-permute-start.2 = (bf16[1024,256]{1,0:T(8,128)(2,1)S(1)}, bf16[1024,256]{1,0:T(8,128)(2,1)S(1)}, u32[]{:S(2)}, u32[]{:S(2)}) collective-permute-start(bf16[1024,256]{1,0:T(8,128)(2,1)S(1)} %get-tuple-element.39), channel_id=1, source_target_pairs={{0,128},{128,0},{1,129},{129,1},{2,130},{130,2},{3,131},{131,3},{4... | collective-permute-start | bytes 1572872 | tf_op jit(solution)/shard_map/ppermute | solution.py:451
  310.8 4.3 %collective-permute-start.3 = (bf16[1024,256]{1,0:T(8,128)(2,1)S(1)}, bf16[1024,256]{1,0:T(8,128)(2,1)S(1)}, u32[]{:S(2)}, u32[]{:S(2)}) collective-permute-start(bf16[1024,256]{1,0:T(8,128)(2,1)S(1)} %bitcast.25), channel_id=1, source_target_pairs={{0,128},{128,0},{1,129},{129,1},{2,130},{130,2},{3,131},{131,3},{4... | collective-permute-start | bytes 1572872 | tf_op jit(solution)/shard_map/ppermute | solution.py:453

commit v8 on v7

--- a/solution.py
+++ b/solution.py
@@ -19,12 +19,16 @@
 F32 = jnp.float32
 
 PLANE = [[s * 8 + z for s in range(16)] for z in range(8)]
-SAME_X0 = [
+BOTH_AXES = ("tmpl", "row")
+SAME_PART = [
     [(x1 * 2 + x0) * 32 + y * 8 + z for x1 in range(2) for y in range(4) for z in range(8)]
     for x0 in range(2)
+] + [
+    [128 + x * 32 + (y1 * 2 + y0) * 8 + z for x in range(4) for y1 in range(2) for z in range(8)]
+    for y0 in range(2)
 ]
+OTHER_PART = [(r, r ^ 32) for r in range(128)] + [(128 + r, 128 + (r ^ 8)) for r in range(128)]
 BY_Z = [[s * 8 + z for z in range(8) for s in range(16)]]
-X0_PAIRS = [(r, r ^ 32) for r in range(128)]
 CORES = [(0, 1), (1, 0)]
 VMEM_LIMIT = 24 * 1024 * 1024
 
@@ -58,14 +62,13 @@
 
 
 def lane_token(lane):
-    x0 = (lax.axis_index("row") // 32) % 2
-    return (
-        (lane % 8) * 128
-        + ((lane // 8) % 8) * 16
-        + ((lane // 256) % 2) * 8
-        + ((lane // 512) ^ x0) * 4
-        + ((lane // 64) % 4)
-    )
+    core, chip = lax.axis_index("tmpl"), lax.axis_index("row")
+    part = jnp.where(core == 0, (chip // 32) % 2, (chip // 8) % 2)
+    part = (lane // 512) ^ part
+    group = (lane // 64) % 8
+    by_x0 = (group // 4) * 8 + part * 4 + group % 4
+    by_y0 = (group // 2) * 4 + (group % 2) * 2 + part
+    return (lane % 8) * 128 + ((lane // 8) % 8) * 16 + jnp.where(core == 0, by_x0, by_y0)
 
 
 def tables_kernel(final_ref, wf_ref, prow_ref, q_ref, pj_ref):
@@ -422,9 +425,9 @@
     )(mine, peer, wf)
 
 
-def exchange(values, groups, count):
+def exchange(values, axes, groups, count):
     cube = values.reshape(count, -1, values.shape[-1])
-    moved = lax.all_to_all(cube, "row", 0, 0, axis_index_groups=groups, tiled=True)
+    moved = lax.all_to_all(cube, axes, 0, 0, axis_index_groups=groups, tiled=True)
     return moved.reshape(values.shape)
 
 
@@ -437,10 +440,10 @@
     currents = (current, current)
     weights = (prow, proj_weight, out_weight)
     for layer in range(NLAYER):
-        products, left, right = own_products(exchange(both, SAME_X0, CH))
-        back_own = exchange(products, SAME_X0, CH)
-        right_peer = lax.ppermute(right, "row", X0_PAIRS)
-        back_peer = exchange(peer_products(left, right_peer), SAME_X0, CH)
+        products, left, right = own_products(exchange(both, BOTH_AXES, SAME_PART, CH))
+        back_own = exchange(products, BOTH_AXES, SAME_PART, CH)
+        right_peer = lax.ppermute(right, BOTH_AXES, OTHER_PART)
+        back_peer = exchange(peer_products(left, right_peer), BOTH_AXES, SAME_PART, CH)
         if layer + 1 < NLAYER:
             scalars = (crop_tiles, full_length)
             own, both = middle_half(0, *scalars, back_own, currents[0], *weights, layer, None)
@@ -449,7 +452,7 @@
     rows = last_own(back_own, currents[0], *weights, NLAYER - 1)
     mine, other = last_peer(back_peer, currents[1], *weights, rows, pj, NLAYER - 1)
     hidden = hidden_features(mine, lax.ppermute(other, "tmpl", CORES))
-    moved = exchange(hidden, BY_Z, 128)
+    moved = exchange(hidden, "row", BY_Z, 128)
     result = final_projection(moved, lax.ppermute(moved, "tmpl", CORES), wf)
     return result.reshape(CZ, 8, CROP)
 

time: 319 us -> 314 us (0.984)
  starting transfers between devices: 61.8 us -> 52.1 us
  blocking collectives: 136 us -> 140 us
    all_to_all x4, waiting for transfers between devices: 22.6 us -> 39.7 us  [exchange(): lax.all_to_all(cube, axes, 0, 0, axis_index_groups=groups, tiled=True)]
    ppermute x2, waiting for transfers between devices: 24.6 us -> 7.65 us  [on_device(): right_peer = lax.ppermute(right, BOTH_AXES, OTHER_PART)]
    all_to_all x4, starting transfers between devices: 43 us -> 35.4 us  [exchange(): lax.all_to_all(cube, axes, 0, 0, axis_index_groups=groups, tiled=True)]
    all_to_all x3, blocking collectives: 136 us -> 140 us  [exchange(): lax.all_to_all(cube, axes, 0, 0, axis_index_groups=groups, tiled=True)]
    ppermute x1, starting transfers between devices: 8.19 us -> 4.82 us  [on_device(): hidden = hidden_features(mine, lax.ppermute(other, 'tmpl', CORES))]
  transfers between devices with their start and end apart: 9 -> 9, of which waited for: 8 -> 9; matrix products, arithmetic and copies ran while one was open for 0% -> 0% of each run, Pallas kernels for 5% -> 5%
where the time goes in v8:
time: 314 us; the launch traced here: 313 us
  blocking collectives  140 us (45%)
  waiting for transfers between devices  74.3 us (24%)
  starting transfers between devices  52.1 us (17%)
  Pallas kernels  42.3 us (13%)
    all_to_all x3, blocking collectives, exchange(): lax.all_to_all(cube, axes, 0, 0, axis_index_groups=groups, tiled=True)  140 us
    all_to_all x4, waiting for transfers between devices, exchange(): lax.all_to_all(cube, axes, 0, 0, axis_index_groups=groups, tiled=True)  39.7 us
    all_to_all x4, starting transfers between devices, exchange(): lax.all_to_all(cube, axes, 0, 0, axis_index_groups=groups, tiled=True)  35.4 us
    all_to_all x1, waiting for transfers between devices, on_device(): lax.all_to_all(cropped, 'row', 0, 0, axis_index_groups=PLANE, tiled=True)  23.8 us
    pallas_call x2, Pallas kernels, middle_half(): pl.pallas_call(functools.partial(middle_kernel, half), grid_spec=pltpu.Pr...  10.6 us
    ppermute x2, waiting for transfers between devices, on_device(): right_peer = lax.ppermute(right, BOTH_AXES, OTHER_PART)  7.65 us
    all_to_all x1, starting transfers between devices, on_device(): lax.all_to_all(cropped, 'row', 0, 0, axis_index_groups=PLANE, tiled=True)  7.6 us
    pallas_call x1, Pallas kernels, first_projection(): pl.pallas_call(first_kernel, grid_spec=pltpu.PrefetchScalarGridSpec(num_s...  6.96 us
  transfers between devices with their start and end apart: 9, of which 9 were waited for; matrix products, arithmetic and copies ran while one was open for 0% of the time, Pallas kernels for 5%

profile of v8, /device:TPU:1, one launch (start us, length us, event | category | flops | bytes accessed | tf_op | source)
XLA Modules:
  0.0 313.2 jit_solution(16868086863551870240)
XLA Ops:
  0.7 3.3 %crop.1 = bf16[16,64,1024]{2,1,0:T(8,128)(2,1)} custom-call(s32[1,8]{1,0:T(1,128)S(1)} %copy-done.4, bf16[16,64,2048]{2,1,0:T(8,128)(2,1)} %bitcast.28), custom_call_target="tpu_custom_call" | custom-call | tf_op jit(solution)/shard_map/crop/pallas_call | solution.py:129
  3.9 7.6 %all-to-all-start = ((bf16[16,64,1024]{2,1,0:T(8,128)(2,1)}), bf16[16,64,1024]{2,1,0:T(8,128)(2,1)S(1)}, u32[]{:S(2)}, u32[]{:S(2)}) async-start(bf16[16,64,1024]{2,1,0:T(8,128)(2,1)} %crop.1), calls=%async_computation | async-start | bytes 4194304 | tf_op jit(solution)/shard_map/all_to_all | solution.py:438
  12.3 3.4 %tables.1 = (bf16[512,256]{1,0:T(8,128)(2,1)S(1)}, bf16[512,512]{1,0:T(8,128)(2,1)S(1)}, bf16[1024,1024]{1,0:T(8,128)(2,1)}, bf16[1024,1024]{1,0:T(8,128)(2,1)}) custom-call(bf16[64,128]{1,0:T(8,128)(2,1)S(1)} %copy-done.6), custom_call_target="tpu_custom_call" | custom-call | flops 1000000000 | bytes 6291456 | tf_op jit(solution)/shard_map/tables/pallas_call | solution.py:90
  15.6 23.8 %all-to-all-done.got_ref = bf16[16,64,1024]{2,1,0:T(8,128)(2,1)S(1)} async-done(((bf16[16,64,1024]{2,1,0:T(8,128)(2,1)}), bf16[16,64,1024]{2,1,0:T(8,128)(2,1)S(1)}, u32[]{:S(2)}, u32[]{:S(2)}) %all-to-all-start) | async-done | bytes 2097184 | tf_op jit(solution)/shard_map/all_to_all | solution.py:438
  39.4 7.0 %first.1 = (bf16[512,1024]{1,0:T(8,128)(2,1)}, bf16[512,2048]{1,0:T(8,128)(2,1)}) custom-call(s32[1,8]{1,0:T(1,128)S(1)} %copy-done.5, s32[1]{0:T(128)S(6)} %copy.9.length_ref.refs_1_, bf16[16,64,1024]{2,1,0:T(8,128)(2,1)S(1)} %all-to-all-done.got_ref, bf16[512,512]{1,0:T(8,128)(2,1)S(1)} %get-tuple-element.23.prow_ref.refs_4_, ...), custom_call_target="tpu_custom_call" | custom-call | tf_op jit(solution)/shard_map/first/pallas_call | solution.py:224
  46.4 59.6 %all_to_all.40 = bf16[64,8,2048]{2,1,0:T(8,128)(2,1)S(1)} all-to-all(bf16[64,8,2048]{2,1,0:T(8,128)(2,1)} %bitcast.31), channel_id=1, replica_groups={{0,1,2,3,4,5,6,7,8,9,10,11,12,13,14,15,16,17,18,19,20,21,22,23,24,25,26..., dimensions={0} | all-to-all | bytes 4194304 | tf_op jit(solution)/shard_map/all_to_all | solution.py:430
  108.4 10.3 %all-to-all-start.3 = ((bf16[64,8,512]{2,1,0:T(8,128)(2,1)}), bf16[64,8,512]{2,1,0:T(8,128)(2,1)S(1)}, u32[]{:S(2)}, u32[]{:S(2)}) async-start(bf16[64,8,512]{2,1,0:T(8,128)(2,1)} %bitcast.6), calls=%async_computation.3 | async-start | bytes 1048576 | tf_op jit(solution)/shard_map/all_to_all | solution.py:430
  118.7 4.1 %collective-permute-done.right_ref = bf16[512,1024]{1,0:T(8,128)(2,1)S(1)} collective-permute-done((bf16[512,1024]{1,0:T(8,128)(2,1)}, bf16[512,1024]{1,0:T(8,128)(2,1)S(1)}, u32[]{:S(2)}, u32[]{:S(2)}) %collective-permute-start) | collective-permute-done | bytes 1048608 | tf_op jit(solution)/shard_map/ppermute | solution.py:445
  125.5 9.4 %all-to-all-done.3 = bf16[64,8,512]{2,1,0:T(8,128)(2,1)S(1)} async-done(((bf16[64,8,512]{2,1,0:T(8,128)(2,1)}), bf16[64,8,512]{2,1,0:T(8,128)(2,1)S(1)}, u32[]{:S(2)}, u32[]{:S(2)}) %all-to-all-start.3) | async-done | bytes 524320 | tf_op jit(solution)/shard_map/all_to_all | solution.py:430
  134.9 7.6 %all-to-all-start.2 = ((bf16[64,8,512]{2,1,0:T(8,128)(2,1)}), bf16[64,8,512]{2,1,0:T(8,128)(2,1)S(1)}, u32[]{:S(2)}, u32[]{:S(2)}) async-start(bf16[64,8,512]{2,1,0:T(8,128)(2,1)} %bitcast.29), calls=%async_computation.2 | async-start | bytes 1048576 | tf_op jit(solution)/shard_map/all_to_all | solution.py:430
  142.5 5.3 %middle0.1 = (bf16[512,512]{1,0:T(8,128)(2,1)}, bf16[512,2048]{1,0:T(8,128)(2,1)}) custom-call(s32[1,8]{1,0:T(1,128)S(1)} %copy-done.5, s32[1]{0:T(128)S(6)} %copy.9.length_ref.refs_1_, bf16[512,512]{1,0:T(8,128)(2,1)S(1)} %bitcast.24, bf16[512,1024]{1,0:T(8,128)(2,1)} %get-tuple-element.28.refs_3_, bf16[512,512]{1,0:T(8,128)(2,1)S(1)} %get-tuple-element.23.prow_ref.refs_4_, ...), custom_call_target="tpu_custom_call" | custom-call | tf_op jit(solution)/shard_map/middle0/pallas_call | solution.py:260
  147.8 10.3 %all-to-all-done.2 = bf16[64,8,512]{2,1,0:T(8,128)(2,1)S(1)} async-done(((bf16[64,8,512]{2,1,0:T(8,128)(2,1)}), bf16[64,8,512]{2,1,0:T(8,128)(2,1)S(1)}, u32[]{:S(2)}, u32[]{:S(2)}) %all-to-all-start.2) | async-done | bytes 524320 | tf_op jit(solution)/shard_map/all_to_all | solution.py:430
  158.1 5.3 %middle1.1 = (bf16[512,512]{1,0:T(8,128)(2,1)}, bf16[512,2048]{1,0:T(8,128)(2,1)}) custom-call(s32[1,8]{1,0:T(1,128)S(1)} %copy-done.5, s32[1]{0:T(128)S(6)} %copy.9.length_ref.refs_1_, bf16[512,512]{1,0:T(8,128)(2,1)S(1)} %bitcast.23, bf16[512,1024]{1,0:T(8,128)(2,1)} %get-tuple-element.28.refs_3_, ...), custom_call_target="tpu_custom_call", output_to_operand_aliasing={{1}: (8, {})} | custom-call | tf_op jit(solution)/shard_map/middle1/pallas_call | solution.py:260
  163.4 54.8 %all_to_all.41 = bf16[64,8,2048]{2,1,0:T(8,128)(2,1)S(1)} all-to-all(bf16[64,8,2048]{2,1,0:T(8,128)(2,1)} %bitcast.27), channel_id=1, replica_groups={{0,1,2,3,4,5,6,7,8,9,10,11,12,13,14,15,16,17,18,19,20,21,22,23,24,25,26..., dimensions={0} | all-to-all | bytes 4194304 | tf_op jit(solution)/shard_map/all_to_all | solution.py:430
  221.8 9.7 %all-to-all-start.6 = ((bf16[64,8,512]{2,1,0:T(8,128)(2,1)}), bf16[64,8,512]{2,1,0:T(8,128)(2,1)S(1)}, u32[]{:S(2)}, u32[]{:S(2)}) async-start(bf16[64,8,512]{2,1,0:T(8,128)(2,1)} %bitcast.12), calls=%async_computation.6 | async-start | bytes 1048576 | tf_op jit(solution)/shard_map/all_to_all | solution.py:430
  231.5 3.6 %collective-permute-done.1.right_ref = bf16[512,1024]{1,0:T(8,128)(2,1)S(1)} collective-permute-done((bf16[512,1024]{1,0:T(8,128)(2,1)}, bf16[512,1024]{1,0:T(8,128)(2,1)S(1)}, u32[]{:S(2)}, u32[]{:S(2)}) %collective-permute-start.1) | collective-permute-done | bytes 1048608 | tf_op jit(solution)/shard_map/ppermute | solution.py:445
  237.9 8.9 %all-to-all-done.6 = bf16[64,8,512]{2,1,0:T(8,128)(2,1)S(1)} async-done(((bf16[64,8,512]{2,1,0:T(8,128)(2,1)}), bf16[64,8,512]{2,1,0:T(8,128)(2,1)S(1)}, u32[]{:S(2)}, u32[]{:S(2)}) %all-to-all-start.6) | async-done | bytes 524320 | tf_op jit(solution)/shard_map/all_to_all | solution.py:430
  246.7 7.8 %all-to-all-start.5 = ((bf16[64,8,512]{2,1,0:T(8,128)(2,1)}), bf16[64,8,512]{2,1,0:T(8,128)(2,1)S(1)}, u32[]{:S(2)}, u32[]{:S(2)}) async-start(bf16[64,8,512]{2,1,0:T(8,128)(2,1)} %bitcast.30), calls=%async_computation.5 | async-start | bytes 1048576 | tf_op jit(solution)/shard_map/all_to_all | solution.py:430
  254.5 3.3 %last_own.1.own_hbm = bf16[512,512]{1,0:T(8,128)(2,1)} custom-call(bf16[512,512]{1,0:T(8,128)(2,1)S(1)} %bitcast.21, bf16[512,512]{1,0:T(8,128)(2,1)} %get-tuple-element.36.cur_ref, bf16[512,512]{1,0:T(8,128)(2,1)S(1)} %get-tuple-element.23.prow_ref.refs_4_, bf16[2,64,320]{2,1,0:T(8,128)(2,1)S(1)} %copy-done, bf16[2,64,64]{2,1,0:T(8,128)(2,1)S(1)} %copy-done.3), custom_call_target="tpu_custom_call" | custom-call | tf_op jit(solution)/shard_map/last_own/pallas_call | solution.py:323
  257.9 11.2 %all-to-all-done.5 = bf16[64,8,512]{2,1,0:T(8,128)(2,1)S(1)} async-done(((bf16[64,8,512]{2,1,0:T(8,128)(2,1)}), bf16[64,8,512]{2,1,0:T(8,128)(2,1)S(1)}, u32[]{:S(2)}, u32[]{:S(2)}) %all-to-all-start.5) | async-done | bytes 524320 | tf_op jit(solution)/shard_map/all_to_all | solution.py:430
  269.1 4.2 %last_peer.1 = (bf16[1024,256]{1,0:T(8,128)(2,1)S(1)}, bf16[1024,256]{1,0:T(8,128)(2,1)S(1)}) custom-call(bf16[512,512]{1,0:T(8,128)(2,1)S(1)} %bitcast.22, bf16[512,512]{1,0:T(8,128)(2,1)} %get-tuple-element.34.cur_ref, bf16[512,512]{1,0:T(8,128)(2,1)S(1)} %get-tuple-element.23.prow_ref.refs_4_, bf16[2,64,320]{2,1,0:T(8,128)(2,1)S(1)} %copy-done, ...), custom_call_target="tpu_custom_call" | custom-call | tf_op jit(solution)/shard_map/last_peer/pallas_call | solution.py:335
  273.3 4.8 %collective-permute-start.2 = (bf16[1024,256]{1,0:T(8,128)(2,1)S(1)}, bf16[1024,256]{1,0:T(8,128)(2,1)S(1)}, u32[]{:S(2)}, u32[]{:S(2)}) collective-permute-start(bf16[1024,256]{1,0:T(8,128)(2,1)S(1)} %get-tuple-element.39), channel_id=1, source_target_pairs={{0,128},{128,0},{1,129},{129,1},{2,130},{130,2},{3,131},{131,3},{4... | collective-permute-start | bytes 1572872 | tf_op jit(solution)/shard_map/ppermute | solution.py:454
  279.8 26.0 %all_to_all.42 = bf16[128,8,256]{2,1,0:T(8,128)(2,1)S(1)} all-to-all(bf16[128,8,256]{2,1,0:T(8,128)(2,1)S(1)} %fusion), channel_id=1, replica_groups={{0,8,16,24,32,40,48,56,64,72,80,88,96,104,112,120,1,9,17,25,33,41,49,57..., dimensions={0} | all-to-all | bytes 1048576 | tf_op jit(solution)/shard_map/all_to_all | solution.py:430
  310.1 3.1 final.1
  (24 shorter events, 18.2 us)
Async XLA Ops:
  0.0 0.7 copy-start.4
  3.9 8.3 %copy-start.6 = (bf16[64,128]{1,0:T(8,128)(2,1)S(1)}, bf16[64,128]{1,0:T(8,128)(2,1)}, u32[]{:S(2)}) copy-start(bf16[64,128]{1,0:T(8,128)(2,1)} %final_ref.1) | copy-start | bytes 49156
  3.9 35.5 %all-to-all-start = ((bf16[16,64,1024]{2,1,0:T(8,128)(2,1)}), bf16[16,64,1024]{2,1,0:T(8,128)(2,1)S(1)}, u32[]{:S(2)}, u32[]{:S(2)}) async-start(bf16[16,64,1024]{2,1,0:T(8,128)(2,1)} %crop.1), calls=%async_computation | async-start | bytes 4194304 | tf_op jit(solution)/shard_map/all_to_all | solution.py:438
  11.6 27.9 %copy-start = (bf16[2,64,320]{2,1,0:T(8,128)(2,1)S(1)}, bf16[2,64,320]{2,1,0:T(8,128)(2,1)}, u32[]{:S(2)}) copy-start(bf16[2,64,320]{2,1,0:T(8,128)(2,1)} %w_ref.5) | copy-start | bytes 245764
  11.6 27.9 %copy-start.5 = (s32[1,8]{1,0:T(1,128)S(1)}, s32[1,8]{1,0:T(1,128)}, u32[]{:S(2)}) copy-start(s32[1,8]{1,0:T(1,128)} %refs_0_.3) | copy-start | bytes 100
  108.3 14.5 %collective-permute-start = (bf16[512,1024]{1,0:T(8,128)(2,1)}, bf16[512,1024]{1,0:T(8,128)(2,1)S(1)}, u32[]{:S(2)}, u32[]{:S(2)}) collective-permute-start(bf16[512,1024]{1,0:T(8,128)(2,1)} %get-tuple-element.27), channel_id=1, source_target_pairs={{0,32},{1,33},{2,34},{3,35},{4,36},{5,37},{6,38},{7,39},{8,40},{9,... | collective-permute-start | bytes 3145736 | tf_op jit(solution)/shard_map/ppermute | solution.py:445
  108.4 34.2 %copy-start.3 = (bf16[2,64,64]{2,1,0:T(8,128)(2,1)S(1)}, bf16[2,64,64]{2,1,0:T(8,128)(2,1)}, u32[]{:S(2)}) copy-start(bf16[2,64,64]{2,1,0:T(8,128)(2,1)} %w_out_ref.3) | copy-start | bytes 49156
  108.4 26.5 %all-to-all-start.3 = ((bf16[64,8,512]{2,1,0:T(8,128)(2,1)}), bf16[64,8,512]{2,1,0:T(8,128)(2,1)S(1)}, u32[]{:S(2)}, u32[]{:S(2)}) async-start(bf16[64,8,512]{2,1,0:T(8,128)(2,1)} %bitcast.6), calls=%async_computation.3 | async-start | bytes 1048576 | tf_op jit(solution)/shard_map/all_to_all | solution.py:430
  122.8 1.2 copy-start.1
  134.9 23.2 %all-to-all-start.2 = ((bf16[64,8,512]{2,1,0:T(8,128)(2,1)}), bf16[64,8,512]{2,1,0:T(8,128)(2,1)S(1)}, u32[]{:S(2)}, u32[]{:S(2)}) async-start(bf16[64,8,512]{2,1,0:T(8,128)(2,1)} %bitcast.29), calls=%async_computation.2 | async-start | bytes 1048576 | tf_op jit(solution)/shard_map/all_to_all | solution.py:430
  220.4 14.7 %collective-permute-start.1 = (bf16[512,1024]{1,0:T(8,128)(2,1)}, bf16[512,1024]{1,0:T(8,128)(2,1)S(1)}, u32[]{:S(2)}, u32[]{:S(2)}) collective-permute-start(bf16[512,1024]{1,0:T(8,128)(2,1)} %get-tuple-element.33), channel_id=1, source_target_pairs={{0,32},{1,33},{2,34},{3,35},{4,36},{5,37},{6,38},{7,39},{8,40},{9,... | collective-permute-start | bytes 3145736 | tf_op jit(solution)/shard_map/ppermute | solution.py:445
  221.8 24.9 %all-to-all-start.6 = ((bf16[64,8,512]{2,1,0:T(8,128)(2,1)}), bf16[64,8,512]{2,1,0:T(8,128)(2,1)S(1)}, u32[]{:S(2)}, u32[]{:S(2)}) async-start(bf16[64,8,512]{2,1,0:T(8,128)(2,1)} %bitcast.12), calls=%async_computation.6 | async-start | bytes 1048576 | tf_op jit(solution)/shard_map/all_to_all | solution.py:430
  235.1 1.2 copy-start.2
  246.7 22.4 %all-to-all-start.5 = ((bf16[64,8,512]{2,1,0:T(8,128)(2,1)}), bf16[64,8,512]{2,1,0:T(8,128)(2,1)S(1)}, u32[]{:S(2)}, u32[]{:S(2)}) async-start(bf16[64,8,512]{2,1,0:T(8,128)(2,1)} %bitcast.30), calls=%async_computation.5 | async-start | bytes 1048576 | tf_op jit(solution)/shard_map/all_to_all | solution.py:430
  273.3 6.4 %collective-permute-start.2 = (bf16[1024,256]{1,0:T(8,128)(2,1)S(1)}, bf16[1024,256]{1,0:T(8,128)(2,1)S(1)}, u32[]{:S(2)}, u32[]{:S(2)}) collective-permute-start(bf16[1024,256]{1,0:T(8,128)(2,1)S(1)} %get-tuple-element.39), channel_id=1, source_target_pairs={{0,128},{128,0},{1,129},{129,1},{2,130},{130,2},{3,131},{131,3},{4... | collective-permute-start | bytes 1572872 | tf_op jit(solution)/shard_map/ppermute | solution.py:454
  305.8 4.3 %collective-permute-start.3 = (bf16[1024,256]{1,0:T(8,128)(2,1)S(1)}, bf16[1024,256]{1,0:T(8,128)(2,1)S(1)}, u32[]{:S(2)}, u32[]{:S(2)}) collective-permute-start(bf16[1024,256]{1,0:T(8,128)(2,1)S(1)} %bitcast.25), channel_id=1, source_target_pairs={{0,128},{128,0},{1,129},{129,1},{2,130},{130,2},{3,131},{131,3},{4... | collective-permute-start | bytes 1572872 | tf_op jit(solution)/shard_map/ppermute | solution.py:456

commit v9 on v8

--- a/solution.py
+++ b/solution.py
@@ -21,13 +21,13 @@
 PLANE = [[s * 8 + z for s in range(16)] for z in range(8)]
 BOTH_AXES = ("tmpl", "row")
 SAME_PART = [
-    [(x1 * 2 + x0) * 32 + y * 8 + z for x1 in range(2) for y in range(4) for z in range(8)]
-    for x0 in range(2)
-] + [
-    [128 + x * 32 + (y1 * 2 + y0) * 8 + z for x in range(4) for y1 in range(2) for z in range(8)]
-    for y0 in range(2)
+    [t * 128 + s * 8 + ((7 - zi if part else zi) + 2 * t) % 8 for s in range(16) for zi in range(4)]
+    for t in range(2)
+    for part in range(2)
 ]
-OTHER_PART = [(r, r ^ 32) for r in range(128)] + [(128 + r, 128 + (r ^ 8)) for r in range(128)]
+OTHER_PART = [
+    (t * 128 + s * 8 + z, t * 128 + s * 8 + (7 + 4 * t - z) % 8) for t in range(2) for s in range(16) for z in range(8)
+]
 BY_Z = [[s * 8 + z for z in range(8) for s in range(16)]]
 CORES = [(0, 1), (1, 0)]
 VMEM_LIMIT = 24 * 1024 * 1024
@@ -63,12 +63,10 @@
 
 def lane_token(lane):
     core, chip = lax.axis_index("tmpl"), lax.axis_index("row")
-    part = jnp.where(core == 0, (chip // 32) % 2, (chip // 8) % 2)
-    part = (lane // 512) ^ part
-    group = (lane // 64) % 8
-    by_x0 = (group // 4) * 8 + part * 4 + group % 4
-    by_y0 = (group // 2) * 4 + (group % 2) * 2 + part
-    return (lane % 8) * 128 + ((lane // 8) % 8) * 16 + jnp.where(core == 0, by_x0, by_y0)
+    part = (lane // 512) ^ (((chip % 8 + 8 - 2 * core) % 8) // 4)
+    place = (lane // 8) % 4
+    z = (jnp.where(part == 0, place, 7 - place) + 2 * core) % 8
+    return (lane % 8) * 128 + z * 16 + (lane // 32) % 16
 
 
 def tables_kernel(final_ref, wf_ref, prow_ref, q_ref, pj_ref):

time: 314 us -> 314 us (level)
  waiting for transfers between devices: 74.3 us -> 102 us
  blocking collectives: 140 us -> 125 us
  starting transfers between devices: 52.1 us -> 39.6 us
    ppermute x2, waiting for transfers between devices: 7.65 us -> 43.6 us  [on_device(): right_peer = lax.ppermute(right, BOTH_AXES, OTHER_PART)]
    all_to_all x3, blocking collectives: 140 us -> 125 us  [exchange(): lax.all_to_all(cube, axes, 0, 0, axis_index_groups=groups, tiled=True)]
    all_to_all x4, starting transfers between devices: 35.4 us -> 25.2 us  [exchange(): lax.all_to_all(cube, axes, 0, 0, axis_index_groups=groups, tiled=True)]
    all_to_all x4, waiting for transfers between devices: 39.7 us -> 31.1 us  [exchange(): lax.all_to_all(cube, axes, 0, 0, axis_index_groups=groups, tiled=True)]
    ppermute x1, starting transfers between devices: 4.82 us -> 0.51 us  [on_device(): hidden = hidden_features(mine, lax.ppermute(other, 'tmpl', CORES))]
where the time goes in v9:
time: 314 us; the launch traced here: 313 us
  blocking collectives  125 us (40%)
  waiting for transfers between devices  102 us (32%)
  Pallas kernels  42.3 us (13%)
  starting transfers between devices  39.6 us (13%)
    all_to_all x3, blocking collectives, exchange(): lax.all_to_all(cube, axes, 0, 0, axis_index_groups=groups, tiled=True)  125 us
    ppermute x2, waiting for transfers between devices, on_device(): right_peer = lax.ppermute(right, BOTH_AXES, OTHER_PART)  43.6 us
    all_to_all x4, waiting for transfers between devices, exchange(): lax.all_to_all(cube, axes, 0, 0, axis_index_groups=groups, tiled=True)  31.1 us
    all_to_all x4, starting transfers between devices, exchange(): lax.all_to_all(cube, axes, 0, 0, axis_index_groups=groups, tiled=True)  25.2 us
    all_to_all x1, waiting for transfers between devices, on_device(): lax.all_to_all(cropped, 'row', 0, 0, axis_index_groups=PLANE, tiled=True)  23.8 us
    pallas_call x2, Pallas kernels, middle_half(): pl.pallas_call(functools.partial(middle_kernel, half), grid_spec=pltpu.Pr...  10.6 us
    all_to_all x1, starting transfers between devices, on_device(): lax.all_to_all(cropped, 'row', 0, 0, axis_index_groups=PLANE, tiled=True)  7.6 us
    pallas_call x1, Pallas kernels, first_projection(): pl.pallas_call(first_kernel, grid_spec=pltpu.PrefetchScalarGridSpec(num_s...  6.97 us
  transfers between devices with their start and end apart: 9, of which 9 were waited for; matrix products, arithmetic and copies ran while one was open for 0% of the time, Pallas kernels for 5%

profile of v9, /device:TPU:1, one launch (start us, length us, event | category | flops | bytes accessed | tf_op | source)
XLA Modules:
  0.0 312.6 jit_solution(838427517060063190)
XLA Ops:
  0.7 3.3 %crop.1 = bf16[16,64,1024]{2,1,0:T(8,128)(2,1)} custom-call(s32[1,8]{1,0:T(1,128)S(1)} %copy-done.4, bf16[16,64,2048]{2,1,0:T(8,128)(2,1)} %bitcast.28), custom_call_target="tpu_custom_call" | custom-call | tf_op jit(solution)/shard_map/crop/pallas_call | solution.py:127
  3.9 7.6 %all-to-all-start = ((bf16[16,64,1024]{2,1,0:T(8,128)(2,1)}), bf16[16,64,1024]{2,1,0:T(8,128)(2,1)S(1)}, u32[]{:S(2)}, u32[]{:S(2)}) async-start(bf16[16,64,1024]{2,1,0:T(8,128)(2,1)} %crop.1), calls=%async_computation | async-start | bytes 4194304 | tf_op jit(solution)/shard_map/all_to_all | solution.py:436
  12.3 3.3 %tables.1 = (bf16[512,256]{1,0:T(8,128)(2,1)S(1)}, bf16[512,512]{1,0:T(8,128)(2,1)S(1)}, bf16[1024,1024]{1,0:T(8,128)(2,1)}, bf16[1024,1024]{1,0:T(8,128)(2,1)}) custom-call(bf16[64,128]{1,0:T(8,128)(2,1)S(1)} %copy-done.6), custom_call_target="tpu_custom_call" | custom-call | flops 1000000000 | bytes 6291456 | tf_op jit(solution)/shard_map/tables/pallas_call | solution.py:88
  15.6 23.8 %all-to-all-done.got_ref = bf16[16,64,1024]{2,1,0:T(8,128)(2,1)S(1)} async-done(((bf16[16,64,1024]{2,1,0:T(8,128)(2,1)}), bf16[16,64,1024]{2,1,0:T(8,128)(2,1)S(1)}, u32[]{:S(2)}, u32[]{:S(2)}) %all-to-all-start) | async-done | bytes 2097184 | tf_op jit(solution)/shard_map/all_to_all | solution.py:436
  39.4 7.0 %first.1 = (bf16[512,1024]{1,0:T(8,128)(2,1)}, bf16[512,2048]{1,0:T(8,128)(2,1)}) custom-call(s32[1,8]{1,0:T(1,128)S(1)} %copy-done.5, s32[1]{0:T(128)S(6)} %copy.9.length_ref.refs_1_, bf16[16,64,1024]{2,1,0:T(8,128)(2,1)S(1)} %all-to-all-done.got_ref, bf16[512,512]{1,0:T(8,128)(2,1)S(1)} %get-tuple-element.23.prow_ref.refs_4_, ...), custom_call_target="tpu_custom_call" | custom-call | tf_op jit(solution)/shard_map/first/pallas_call | solution.py:222
  46.4 52.9 %all_to_all.40 = bf16[64,8,2048]{2,1,0:T(8,128)(2,1)S(1)} all-to-all(bf16[64,8,2048]{2,1,0:T(8,128)(2,1)} %bitcast.31), channel_id=1, replica_groups={{0,1,2,3,8,9,10,11,16,17,18,19,24,25,26,27,32,33,34,35,40,41,42,43,48,4..., dimensions={0} | all-to-all | bytes 4194304 | tf_op jit(solution)/shard_map/all_to_all | solution.py:428
  103.1 4.3 %all-to-all-start.3 = ((bf16[64,8,512]{2,1,0:T(8,128)(2,1)}), bf16[64,8,512]{2,1,0:T(8,128)(2,1)S(1)}, u32[]{:S(2)}, u32[]{:S(2)}) async-start(bf16[64,8,512]{2,1,0:T(8,128)(2,1)} %bitcast.6), calls=%async_computation.3 | async-start | bytes 1048576 | tf_op jit(solution)/shard_map/all_to_all | solution.py:428
  107.5 21.9 %collective-permute-done.right_ref = bf16[512,1024]{1,0:T(8,128)(2,1)S(1)} collective-permute-done((bf16[512,1024]{1,0:T(8,128)(2,1)}, bf16[512,1024]{1,0:T(8,128)(2,1)S(1)}, u32[]{:S(2)}, u32[]{:S(2)}) %collective-permute-start) | collective-permute-done | bytes 1048608 | tf_op jit(solution)/shard_map/ppermute | solution.py:443
  132.1 2.7 all-to-all-done.3
  134.9 8.3 %all-to-all-start.2 = ((bf16[64,8,512]{2,1,0:T(8,128)(2,1)}), bf16[64,8,512]{2,1,0:T(8,128)(2,1)S(1)}, u32[]{:S(2)}, u32[]{:S(2)}) async-start(bf16[64,8,512]{2,1,0:T(8,128)(2,1)} %bitcast.29), calls=%async_computation.2 | async-start | bytes 1048576 | tf_op jit(solution)/shard_map/all_to_all | solution.py:428
  143.2 5.3 %middle0.1 = (bf16[512,512]{1,0:T(8,128)(2,1)}, bf16[512,2048]{1,0:T(8,128)(2,1)}) custom-call(s32[1,8]{1,0:T(1,128)S(1)} %copy-done.5, s32[1]{0:T(128)S(6)} %copy.9.length_ref.refs_1_, bf16[512,512]{1,0:T(8,128)(2,1)S(1)} %bitcast.24, bf16[512,1024]{1,0:T(8,128)(2,1)} %get-tuple-element.28.refs_3_, bf16[512,512]{1,0:T(8,128)(2,1)S(1)} %get-tuple-element.23.prow_ref.refs_4_, ...), custom_call_target="tpu_custom_call" | custom-call | tf_op jit(solution)/shard_map/middle0/pallas_call | solution.py:258
  148.6 11.7 %all-to-all-done.2 = bf16[64,8,512]{2,1,0:T(8,128)(2,1)S(1)} async-done(((bf16[64,8,512]{2,1,0:T(8,128)(2,1)}), bf16[64,8,512]{2,1,0:T(8,128)(2,1)S(1)}, u32[]{:S(2)}, u32[]{:S(2)}) %all-to-all-start.2) | async-done | bytes 524320 | tf_op jit(solution)/shard_map/all_to_all | solution.py:428
  160.2 5.3 %middle1.1 = (bf16[512,512]{1,0:T(8,128)(2,1)}, bf16[512,2048]{1,0:T(8,128)(2,1)}) custom-call(s32[1,8]{1,0:T(1,128)S(1)} %copy-done.5, s32[1]{0:T(128)S(6)} %copy.9.length_ref.refs_1_, bf16[512,512]{1,0:T(8,128)(2,1)S(1)} %bitcast.23, bf16[512,1024]{1,0:T(8,128)(2,1)} %get-tuple-element.28.refs_3_, ...), custom_call_target="tpu_custom_call", output_to_operand_aliasing={{1}: (8, {})} | custom-call | tf_op jit(solution)/shard_map/middle1/pallas_call | solution.py:258
  165.5 46.3 %all_to_all.41 = bf16[64,8,2048]{2,1,0:T(8,128)(2,1)S(1)} all-to-all(bf16[64,8,2048]{2,1,0:T(8,128)(2,1)} %bitcast.27), channel_id=1, replica_groups={{0,1,2,3,8,9,10,11,16,17,18,19,24,25,26,27,32,33,34,35,40,41,42,43,48,4..., dimensions={0} | all-to-all | bytes 4194304 | tf_op jit(solution)/shard_map/all_to_all | solution.py:428
  215.9 4.2 %all-to-all-start.6 = ((bf16[64,8,512]{2,1,0:T(8,128)(2,1)}), bf16[64,8,512]{2,1,0:T(8,128)(2,1)S(1)}, u32[]{:S(2)}, u32[]{:S(2)}) async-start(bf16[64,8,512]{2,1,0:T(8,128)(2,1)} %bitcast.12), calls=%async_computation.6 | async-start | bytes 1048576 | tf_op jit(solution)/shard_map/all_to_all | solution.py:428
  220.1 21.7 %collective-permute-done.1.right_ref = bf16[512,1024]{1,0:T(8,128)(2,1)S(1)} collective-permute-done((bf16[512,1024]{1,0:T(8,128)(2,1)}, bf16[512,1024]{1,0:T(8,128)(2,1)S(1)}, u32[]{:S(2)}, u32[]{:S(2)}) %collective-permute-start.1) | collective-permute-done | bytes 1048608 | tf_op jit(solution)/shard_map/ppermute | solution.py:443
  244.6 3.0 all-to-all-done.6
  247.6 8.3 %all-to-all-start.5 = ((bf16[64,8,512]{2,1,0:T(8,128)(2,1)}), bf16[64,8,512]{2,1,0:T(8,128)(2,1)S(1)}, u32[]{:S(2)}, u32[]{:S(2)}) async-start(bf16[64,8,512]{2,1,0:T(8,128)(2,1)} %bitcast.30), calls=%async_computation.5 | async-start | bytes 1048576 | tf_op jit(solution)/shard_map/all_to_all | solution.py:428
  256.0 3.3 %last_own.1.own_hbm = bf16[512,512]{1,0:T(8,128)(2,1)} custom-call(bf16[512,512]{1,0:T(8,128)(2,1)S(1)} %bitcast.21, bf16[512,512]{1,0:T(8,128)(2,1)} %get-tuple-element.36.cur_ref, bf16[512,512]{1,0:T(8,128)(2,1)S(1)} %get-tuple-element.23.prow_ref.refs_4_, bf16[2,64,320]{2,1,0:T(8,128)(2,1)S(1)} %copy-done, bf16[2,64,64]{2,1,0:T(8,128)(2,1)S(1)} %copy-done.3), custom_call_target="tpu_custom_call" | custom-call | tf_op jit(solution)/shard_map/last_own/pallas_call | solution.py:321
  259.3 13.7 %all-to-all-done.5 = bf16[64,8,512]{2,1,0:T(8,128)(2,1)S(1)} async-done(((bf16[64,8,512]{2,1,0:T(8,128)(2,1)}), bf16[64,8,512]{2,1,0:T(8,128)(2,1)S(1)}, u32[]{:S(2)}, u32[]{:S(2)}) %all-to-all-start.5) | async-done | bytes 524320 | tf_op jit(solution)/shard_map/all_to_all | solution.py:428
  273.0 4.2 %last_peer.1 = (bf16[1024,256]{1,0:T(8,128)(2,1)S(1)}, bf16[1024,256]{1,0:T(8,128)(2,1)S(1)}) custom-call(bf16[512,512]{1,0:T(8,128)(2,1)S(1)} %bitcast.22, bf16[512,512]{1,0:T(8,128)(2,1)} %get-tuple-element.34.cur_ref, bf16[512,512]{1,0:T(8,128)(2,1)S(1)} %get-tuple-element.23.prow_ref.refs_4_, bf16[2,64,320]{2,1,0:T(8,128)(2,1)S(1)} %copy-done, ...), custom_call_target="tpu_custom_call" | custom-call | tf_op jit(solution)/shard_map/last_peer/pallas_call | solution.py:333
  279.4 25.8 %all_to_all.42 = bf16[128,8,256]{2,1,0:T(8,128)(2,1)S(1)} all-to-all(bf16[128,8,256]{2,1,0:T(8,128)(2,1)S(1)} %fusion), channel_id=1, replica_groups={{0,8,16,24,32,40,48,56,64,72,80,88,96,104,112,120,1,9,17,25,33,41,49,57..., dimensions={0} | all-to-all | bytes 1048576 | tf_op jit(solution)/shard_map/all_to_all | solution.py:428
  305.2 2.8 collective-permute-start.3
  309.5 3.1 final.1
  (24 shorter events, 17.9 us)
Async XLA Ops:
  0.0 0.7 copy-start.4
  3.9 8.3 %copy-start.6 = (bf16[64,128]{1,0:T(8,128)(2,1)S(1)}, bf16[64,128]{1,0:T(8,128)(2,1)}, u32[]{:S(2)}) copy-start(bf16[64,128]{1,0:T(8,128)(2,1)} %final_ref.1) | copy-start | bytes 49156
  3.9 35.5 %all-to-all-start = ((bf16[16,64,1024]{2,1,0:T(8,128)(2,1)}), bf16[16,64,1024]{2,1,0:T(8,128)(2,1)S(1)}, u32[]{:S(2)}, u32[]{:S(2)}) async-start(bf16[16,64,1024]{2,1,0:T(8,128)(2,1)} %crop.1), calls=%async_computation | async-start | bytes 4194304 | tf_op jit(solution)/shard_map/all_to_all | solution.py:436
  11.6 27.9 %copy-start = (bf16[2,64,320]{2,1,0:T(8,128)(2,1)S(1)}, bf16[2,64,320]{2,1,0:T(8,128)(2,1)}, u32[]{:S(2)}) copy-start(bf16[2,64,320]{2,1,0:T(8,128)(2,1)} %w_ref.5) | copy-start | bytes 245764
  11.6 27.9 %copy-start.5 = (s32[1,8]{1,0:T(1,128)S(1)}, s32[1,8]{1,0:T(1,128)}, u32[]{:S(2)}) copy-start(s32[1,8]{1,0:T(1,128)} %refs_0_.3) | copy-start | bytes 100
  101.5 27.9 %collective-permute-start = (bf16[512,1024]{1,0:T(8,128)(2,1)}, bf16[512,1024]{1,0:T(8,128)(2,1)S(1)}, u32[]{:S(2)}, u32[]{:S(2)}) collective-permute-start(bf16[512,1024]{1,0:T(8,128)(2,1)} %get-tuple-element.27), channel_id=1, source_target_pairs={{0,7},{1,6},{2,5},{3,4},{4,3},{5,2},{6,1},{7,0},{8,15},{9,14},{10,... | collective-permute-start | bytes 3145736 | tf_op jit(solution)/shard_map/ppermute | solution.py:443
  103.1 40.1 %copy-start.3 = (bf16[2,64,64]{2,1,0:T(8,128)(2,1)S(1)}, bf16[2,64,64]{2,1,0:T(8,128)(2,1)}, u32[]{:S(2)}) copy-start(bf16[2,64,64]{2,1,0:T(8,128)(2,1)} %w_out_ref.3) | copy-start | bytes 49156
  103.1 31.7 %all-to-all-start.3 = ((bf16[64,8,512]{2,1,0:T(8,128)(2,1)}), bf16[64,8,512]{2,1,0:T(8,128)(2,1)S(1)}, u32[]{:S(2)}, u32[]{:S(2)}) async-start(bf16[64,8,512]{2,1,0:T(8,128)(2,1)} %bitcast.6), calls=%async_computation.3 | async-start | bytes 1048576 | tf_op jit(solution)/shard_map/all_to_all | solution.py:428
  129.4 1.2 copy-start.1
  134.9 25.3 %all-to-all-start.2 = ((bf16[64,8,512]{2,1,0:T(8,128)(2,1)}), bf16[64,8,512]{2,1,0:T(8,128)(2,1)S(1)}, u32[]{:S(2)}, u32[]{:S(2)}) async-start(bf16[64,8,512]{2,1,0:T(8,128)(2,1)} %bitcast.29), calls=%async_computation.2 | async-start | bytes 1048576 | tf_op jit(solution)/shard_map/all_to_all | solution.py:428
  214.0 27.8 %collective-permute-start.1 = (bf16[512,1024]{1,0:T(8,128)(2,1)}, bf16[512,1024]{1,0:T(8,128)(2,1)S(1)}, u32[]{:S(2)}, u32[]{:S(2)}) collective-permute-start(bf16[512,1024]{1,0:T(8,128)(2,1)} %get-tuple-element.33), channel_id=1, source_target_pairs={{0,7},{1,6},{2,5},{3,4},{4,3},{5,2},{6,1},{7,0},{8,15},{9,14},{10,... | collective-permute-start | bytes 3145736 | tf_op jit(solution)/shard_map/ppermute | solution.py:443
  215.9 31.7 %all-to-all-start.6 = ((bf16[64,8,512]{2,1,0:T(8,128)(2,1)}), bf16[64,8,512]{2,1,0:T(8,128)(2,1)S(1)}, u32[]{:S(2)}, u32[]{:S(2)}) async-start(bf16[64,8,512]{2,1,0:T(8,128)(2,1)} %bitcast.12), calls=%async_computation.6 | async-start | bytes 1048576 | tf_op jit(solution)/shard_map/all_to_all | solution.py:428
  241.8 1.2 copy-start.2
  247.6 25.4 %all-to-all-start.5 = ((bf16[64,8,512]{2,1,0:T(8,128)(2,1)}), bf16[64,8,512]{2,1,0:T(8,128)(2,1)S(1)}, u32[]{:S(2)}, u32[]{:S(2)}) async-start(bf16[64,8,512]{2,1,0:T(8,128)(2,1)} %bitcast.30), calls=%async_computation.5 | async-start | bytes 1048576 | tf_op jit(solution)/shard_map/all_to_all | solution.py:428
  277.2 2.0 collective-permute-start.2
  305.2 4.3 %collective-permute-start.3 = (bf16[1024,256]{1,0:T(8,128)(2,1)S(1)}, bf16[1024,256]{1,0:T(8,128)(2,1)S(1)}, u32[]{:S(2)}, u32[]{:S(2)}) collective-permute-start(bf16[1024,256]{1,0:T(8,128)(2,1)S(1)} %bitcast.25), channel_id=1, source_target_pairs={{0,128},{128,0},{1,129},{129,1},{2,130},{130,2},{3,131},{131,3},{4... | collective-permute-start | bytes 1572872 | tf_op jit(solution)/shard_map/ppermute | solution.py:454

commit v10 on v9

--- a/solution.py
+++ b/solution.py
@@ -69,7 +69,7 @@
     return (lane % 8) * 128 + z * 16 + (lane // 32) % 16
 
 
-def tables_kernel(final_ref, wf_ref, prow_ref, q_ref, pj_ref):
+def tables_kernel(final_ref, wf_ref, prow_ref, pj_ref):
     down = onehot(iota((512, CZ), 0) % CZ == iota((512, CZ), 1))
     across = onehot(iota((CH, 256), 0) == iota((CH, 256), 1) % CH)
     tall = dot_nt(down, final_ref[...]).astype(BF)
@@ -79,7 +79,6 @@
     prow_ref[...] = onehot((r0 // 8 == c0 % CH) & (r0 % 8 == c0 // CH))
     r1, c1 = iota((CROP, CROP), 0), iota((CROP, CROP), 1)
     token = lane_token(c1)
-    q_ref[...] = onehot(r1 == token)
     dest = r1 // 8
     pj_ref[...] = onehot(((dest % 16) * 8 + dest // 16) * 8 + r1 % 8 == token)
 
@@ -89,7 +88,7 @@
         tables_kernel,
         out_shape=[
             pltpu.VMEM((512, 256), BF), pltpu.VMEM((512, 512), BF),
-            pltpu.HBM((CROP, CROP), BF), pltpu.HBM((CROP, CROP), BF),
+            pltpu.HBM((CROP, CROP), BF),
         ],
         compiler_params=pltpu.CompilerParams(vmem_limit_bytes=40 * 1024 * 1024),
         cost_estimate=pl.CostEstimate(flops=10**9, bytes_accessed=6 * 2**20, transcendentals=0),
@@ -193,14 +192,15 @@
 STEPS = CROP // BLOCK
 HALF_STEPS = STEPS // 2
 LAST_BLOCK = 256
-LAST_STEPS = 512 // LAST_BLOCK
+LAST_STEPS = CROP // LAST_BLOCK
 BOTH = pltpu.HBM((512, 2 * CROP), BF)
 
 
-def first_kernel(crop_ref, length_ref, got_ref, prow_ref, q_ref, w_ref, cur_ref, both_ref):
+def first_kernel(crop_ref, length_ref, got_ref, prow_ref, w_ref, cur_ref, both_ref):
     step = pl.program_id(0)
     parts = jnp.concatenate([got_ref[crop_ref[0, a]] for a in range(ROWS)], axis=0)
-    current = dot(parts, q_ref[...])
+    order = onehot(iota((CROP, BLOCK), 0) == lane_token(iota((1, BLOCK), 1) + step * BLOCK))
+    current = dot(parts, order)
     cur_ref[...] = current.astype(BF)
     mask = pair_mask(crop_ref, length_ref, BLOCK, step * BLOCK)
     project(side_by_side(current), w_ref[0], prow_ref[...], mask, both_ref)
@@ -218,19 +218,19 @@
     return pl.BlockSpec((1, CH, columns), lambda step, *_: (layer, 0, 0), pipeline_mode=pl.Buffered(1))
 
 
-def first_projection(crop_tiles, full_length, got, prow, q, proj_weight):
+def first_projection(crop_tiles, full_length, got, prow, proj_weight):
     return pl.pallas_call(
         first_kernel,
         grid_spec=pltpu.PrefetchScalarGridSpec(
             num_scalar_prefetch=2,
             grid=(STEPS,),
-            in_specs=[RESIDENT, RESIDENT, lanes_of(CROP), layer_weight(320, 0)],
+            in_specs=[RESIDENT, RESIDENT, layer_weight(320, 0)],
             out_specs=[lanes_of(512), lanes_of(512, 2 * BLOCK)],
         ),
         out_shape=[pltpu.HBM((512, CROP), BF), BOTH],
         compiler_params=pltpu.CompilerParams(vmem_limit_bytes=VMEM_LIMIT),
         name="first",
-    )(crop_tiles, full_length, *in_vmem(got, prow), *in_hbm(q), proj_weight)
+    )(crop_tiles, full_length, *in_vmem(got, prow), proj_weight)
 
 
 def update(back_ref, cur_ref, prow, w_proj, w_out):
@@ -243,37 +243,33 @@
     return (current + gate * change).astype(BF)
 
 
-def middle_kernel(half, *refs):
-    crop_ref, length_ref, back_ref, cur_ref, prow_ref, w_ref, w_out_ref, w_next_ref = refs[:8]
-    next_ref, both_ref = refs[-2:]
+def middle_kernel(
+    crop_ref, length_ref, back_ref, cur_ref, prow_ref, w_ref, w_out_ref, w_next_ref, next_ref, both_ref
+):
     current = update(back_ref, cur_ref, prow_ref[...], w_ref[0], w_out_ref[0])
     next_ref[...] = stacked(current)
-    mask = pair_mask(crop_ref, length_ref, BLOCK, half * 512 + pl.program_id(0) * BLOCK)
+    mask = pair_mask(crop_ref, length_ref, BLOCK, pl.program_id(0) * BLOCK)
     project(current.astype(F32), w_next_ref[0], prow_ref[...], mask, both_ref)
 
 
-def middle_half(half, crop_tiles, full_length, back, current, prow, proj_weight, out_weight, layer, both):
-    offset = half * HALF_STEPS
-    aliased = [] if both is None else [both]
-    return pl.pallas_call(
-        functools.partial(middle_kernel, half),
+def middle_layer(crop_tiles, full_length, back, current, prow, proj_weight, out_weight, layer):
+    return pl.pallas_call(
+        middle_kernel,
         grid_spec=pltpu.PrefetchScalarGridSpec(
             num_scalar_prefetch=2,
-            grid=(HALF_STEPS,),
+            grid=(STEPS,),
             in_specs=[
-                RESIDENT, lanes_of(512, offset=offset), RESIDENT,
+                RESIDENT, lanes_of(512), RESIDENT,
                 layer_weight(320, layer), layer_weight(CH, layer), layer_weight(320, layer + 1),
-            ]
-            + [ANYWHERE] * len(aliased),
-            out_specs=[lanes_of(512), lanes_of(512, 2 * BLOCK, offset)],
+            ],
+            out_specs=[lanes_of(512), lanes_of(512, 2 * BLOCK)],
         ),
-        out_shape=[pltpu.HBM((512, 512), BF), BOTH],
-        input_output_aliases={8: 1} if aliased else {},
-        compiler_params=pltpu.CompilerParams(vmem_limit_bytes=VMEM_LIMIT),
-        name="middle" + str(half),
+        out_shape=[pltpu.HBM((512, CROP), BF), BOTH],
+        compiler_params=pltpu.CompilerParams(vmem_limit_bytes=VMEM_LIMIT),
+        name="middle",
     )(
-        crop_tiles, full_length, *in_vmem(back), *in_hbm(current), *in_vmem(prow), proj_weight, out_weight, proj_weight,
-        *aliased,
+        crop_tiles, full_length, *in_vmem(back), *in_hbm(current), *in_vmem(prow), proj_weight, out_weight,
+        proj_weight,
     )
 
 
@@ -282,72 +278,45 @@
     return stacked(norm_channels(current.astype(F32)).astype(BF))
 
 
-def last_own_kernel(back_ref, cur_ref, prow_ref, w_ref, w_out_ref, rows_ref):
-    rows_ref[...] = last_rows(back_ref, cur_ref, prow_ref, w_ref, w_out_ref)
-
-
-def last_peer_kernel(
-    back_ref, cur_ref, prow_ref, w_ref, w_out_ref, own_hbm, pj_hbm, mine_ref, other_ref, rows_ref, pj_ref, sems
-):
+def last_kernel(back_ref, cur_ref, prow_ref, w_ref, w_out_ref, pj_hbm, mine_ref, other_ref, rows_ref, pj_ref, sem):
     step = pl.program_id(0)
-    loads = [
-        pltpu.make_async_copy(own_hbm, rows_ref.at[:, pl.ds(0, 512)], sems.at[0]),
-        pltpu.make_async_copy(pj_hbm, pj_ref, sems.at[1]),
-    ]
+    load = pltpu.make_async_copy(pj_hbm, pj_ref, sem)
 
     @pl.when(step == 0)
     def _():
-        for load in loads:
-            load.start()
-
-    lanes = pl.ds(pl.multiple_of(512 + step * LAST_BLOCK, LAST_BLOCK), LAST_BLOCK)
+        load.start()
+
+    lanes = pl.ds(pl.multiple_of(step * LAST_BLOCK, LAST_BLOCK), LAST_BLOCK)
     rows_ref[:, lanes] = last_rows(back_ref, cur_ref, prow_ref, w_ref, w_out_ref)
 
     @pl.when(step == LAST_STEPS - 1)
     def _():
-        for load in loads:
-            load.wait()
+        load.wait()
         core = lax.axis_index("tmpl")
         pj = pj_ref[...]
         mine_ref[...] = dot_nt(pj, rows_ref[pl.ds(pl.multiple_of(core * 256, 256), 256), :]).astype(BF)
         other_ref[...] = dot_nt(pj, rows_ref[pl.ds(pl.multiple_of(256 - core * 256, 256), 256), :]).astype(BF)
 
 
-def last_specs(layer):
-    return [RESIDENT, lanes_of(512, LAST_BLOCK), RESIDENT, layer_weight(320, layer), layer_weight(CH, layer)]
-
-
-def last_own(back, current, prow, proj_weight, out_weight, layer):
-    return pl.pallas_call(
-        last_own_kernel,
+def last_layer(back, current, prow, proj_weight, out_weight, pj, layer):
+    return pl.pallas_call(
+        last_kernel,
         grid=(LAST_STEPS,),
-        in_specs=last_specs(layer),
-        out_specs=lanes_of(512, LAST_BLOCK),
-        out_shape=pltpu.HBM((512, 512), BF),
-        compiler_params=pltpu.CompilerParams(vmem_limit_bytes=VMEM_LIMIT),
-        name="last_own",
-    )(*in_vmem(back), *in_hbm(current), *in_vmem(prow), proj_weight, out_weight)
-
-
-def last_peer(back, current, prow, proj_weight, out_weight, own, pj, layer):
-    return pl.pallas_call(
-        last_peer_kernel,
-        grid=(LAST_STEPS,),
-        in_specs=last_specs(layer) + [ANYWHERE, ANYWHERE],
+        in_specs=[
+            RESIDENT, lanes_of(512, LAST_BLOCK), RESIDENT, layer_weight(320, layer), layer_weight(CH, layer), ANYWHERE
+        ],
         out_specs=[full((CROP, 256))] * 2,
         out_shape=[jax.ShapeDtypeStruct((CROP, 256), BF)] * 2,
-        scratch_shapes=[
-            pltpu.VMEM((512, CROP), BF), pltpu.VMEM((CROP, CROP), BF), pltpu.SemaphoreType.DMA((2,)),
-        ],
-        compiler_params=pltpu.CompilerParams(vmem_limit_bytes=VMEM_LIMIT),
-        name="last_peer",
-    )(*in_vmem(back), *in_hbm(current), *in_vmem(prow), proj_weight, out_weight, *in_hbm(own, pj))
-
-
-def own_products_kernel(both_ref, out_ref, left_hbm, right_hbm, sems):
+        scratch_shapes=[pltpu.VMEM((512, CROP), BF), pltpu.VMEM((CROP, CROP), BF), pltpu.SemaphoreType.DMA],
+        compiler_params=pltpu.CompilerParams(vmem_limit_bytes=VMEM_LIMIT),
+        name="last",
+    )(*in_vmem(back), *in_hbm(current), *in_vmem(prow), proj_weight, out_weight, *in_hbm(pj))
+
+
+def own_products_kernel(both_ref, out_hbm, left_hbm, right_hbm, own_ref, sems):
     copies = []
-    for block in range(STEPS):
-        for side, target in enumerate((left_hbm, right_hbm)):
+    for side, target in ((1, right_hbm), (0, left_hbm)):
+        for block in range(STEPS):
             source = both_ref.at[:, pl.ds((2 * block + side) * BLOCK, BLOCK)]
             place = target.at[:, pl.ds(block * BLOCK, BLOCK)]
             copies.append(pltpu.make_async_copy(source, place, sems.at[2 * block + side]))
@@ -356,36 +325,48 @@
     starts = [2 * block * BLOCK for block in range(STEPS)]
     left = jnp.concatenate([both_ref[:, start : start + BLOCK] for start in starts], axis=1)
     right = jnp.concatenate([both_ref[:, start + BLOCK : start + 2 * BLOCK] for start in starts], axis=1)
-    out_ref[...] = dot_nt(left, right).astype(BF)
+    own_ref[...] = dot_nt(left, right).astype(BF)
+    store = pltpu.make_async_copy(own_ref, out_hbm.at[:, pl.ds(0, 512)], sems.at[2 * STEPS])
+    store.start()
     for copy in copies:
         copy.wait()
+    store.wait()
 
 
 def own_products(both):
+    square = pltpu.HBM((512, CROP), BF)
     return pl.pallas_call(
         own_products_kernel,
-        out_specs=[pl.BlockSpec(memory_space=pltpu.VMEM), ANYWHERE, ANYWHERE],
-        out_shape=[jax.ShapeDtypeStruct((512, 512), BF), pltpu.HBM((512, CROP), BF), pltpu.HBM((512, CROP), BF)],
-        scratch_shapes=[pltpu.SemaphoreType.DMA((2 * STEPS,))],
+        out_specs=[ANYWHERE] * 3,
+        out_shape=[square] * 3,
+        scratch_shapes=[pltpu.VMEM((512, 512), BF), pltpu.SemaphoreType.DMA((2 * STEPS + 1,))],
         compiler_params=pltpu.CompilerParams(vmem_limit_bytes=VMEM_LIMIT),
         cost_estimate=pl.CostEstimate(flops=2**29, bytes_accessed=4 * 2**20, transcendentals=0),
         name="own_products",
     )(both)
 
 
-def peer_products_kernel(left_ref, right_ref, out_ref):
+def peer_products_kernel(left_ref, right_ref, products_hbm, out_hbm, peer_ref, sem):
+    del products_hbm
     left = jnp.concatenate([left_ref[:, 512:], left_ref[:, :512]], axis=1)
-    out_ref[...] = dot_nt(left, right_ref[...]).astype(BF)
-
-
-def peer_products(left, right):
+    peer_ref[...] = dot_nt(left, right_ref[...]).astype(BF)
+    store = pltpu.make_async_copy(peer_ref, out_hbm.at[:, pl.ds(512, 512)], sem)
+    store.start()
+    store.wait()
+
+
+def peer_products(left, right, products):
     return pl.pallas_call(
         peer_products_kernel,
-        out_shape=pltpu.HBM((512, 512), BF),
+        in_specs=[RESIDENT, RESIDENT, ANYWHERE],
+        out_specs=ANYWHERE,
+        out_shape=pltpu.HBM((512, CROP), BF),
+        input_output_aliases={2: 0},
+        scratch_shapes=[pltpu.VMEM((512, 512), BF), pltpu.SemaphoreType.DMA],
         compiler_params=pltpu.CompilerParams(vmem_limit_bytes=VMEM_LIMIT),
         cost_estimate=pl.CostEstimate(flops=2**29, bytes_accessed=4 * 2**20, transcendentals=0),
         name="peer_products",
-    )(left, right)
+    )(left, right, products)
 
 
 def hidden_features(mine, peer):
@@ -393,34 +374,48 @@
     return jnp.maximum(total * 0.5, 0.0).astype(BF)
 
 
-def final_kernel(mine_ref, peer_ref, wf_ref, out_ref, tall0_ref, tall1_ref, wide_ref):
+def final_kernel(source, *refs):
+    rows_ref, wf_ref = refs[:2]
+    out_hbm, tall0_ref, tall1_ref, wide_ref, stage_ref, sems = refs[-6:]
     core = lax.axis_index("tmpl")
+    half = core if source == 0 else 1 - core
     wf = wf_ref[...]
-    for source, ref in enumerate((mine_ref, peer_ref)):
-        half = core if source == 0 else 1 - core
-        tall0_ref[...] = ref[:, :128].astype(F32)
-        tall1_ref[...] = ref[:, 128:].astype(F32)
-        for j in range(8):
-            rows = jnp.concatenate(
-                [tall0_ref[pl.ds(j, 128, stride=8), :], tall1_ref[pl.ds(j, 128, stride=8), :]], axis=1
-            ).astype(BF)
-            result = dot_nt(wf, rows)
-            for a in range(4):
-                wide_ref[half * 4 + a, pl.ds(j, CZ, stride=8), :] = result[a * CZ : (a + 1) * CZ]
-    for a in range(8):
-        out_ref[:, a * TILE : (a + 1) * TILE] = wide_ref[a].astype(BF)
-
-
-def final_projection(mine, peer, wf):
-    return pl.pallas_call(
-        final_kernel,
-        out_shape=jax.ShapeDtypeStruct((CZ * 8, CROP), BF),
+    tall0_ref[...] = rows_ref[:, :128].astype(F32)
+    tall1_ref[...] = rows_ref[:, 128:].astype(F32)
+    for j in range(8):
+        rows = jnp.concatenate(
+            [tall0_ref[pl.ds(j, 128, stride=8), :], tall1_ref[pl.ds(j, 128, stride=8), :]], axis=1
+        ).astype(BF)
+        result = dot_nt(wf, rows)
+        for a in range(4):
+            wide_ref[a, pl.ds(j, CZ, stride=8), :] = result[a * CZ : (a + 1) * CZ]
+    stores = []
+    for a in range(4):
+        lanes = pl.ds(a * TILE, TILE)
+        stage_ref[:, lanes] = wide_ref[a].astype(BF)
+        place = pl.ds(pl.multiple_of(half * 512 + a * TILE, TILE), TILE)
+        store = pltpu.make_async_copy(stage_ref.at[:, lanes], out_hbm.at[:, place], sems.at[a])
+        store.start()
+        stores.append(store)
+    for store in stores:
+        store.wait()
+
+
+def final_projection(source, rows, wf, earlier=()):
+    return pl.pallas_call(
+        functools.partial(final_kernel, source),
+        in_specs=[RESIDENT, RESIDENT] + [ANYWHERE] * len(earlier),
+        out_specs=ANYWHERE,
+        out_shape=pltpu.HBM((CZ * 8, CROP), BF),
+        input_output_aliases={2 + k: 0 for k in range(len(earlier))},
         scratch_shapes=[
-            pltpu.VMEM((CROP, 128), F32), pltpu.VMEM((CROP, 128), F32), pltpu.VMEM((8, CZ * 8, TILE), F32)
+            pltpu.VMEM((CROP, 128), F32), pltpu.VMEM((CROP, 128), F32), pltpu.VMEM((4, CZ * 8, TILE), F32),
+            pltpu.VMEM((CZ * 8, 512), BF), pltpu.SemaphoreType.DMA((4,)),
         ],
         compiler_params=pltpu.CompilerParams(vmem_limit_bytes=VMEM_LIMIT),
-        name="final",
-    )(mine, peer, wf)
+        cost_estimate=pl.CostEstimate(flops=2**28, bytes_accessed=2 * 2**20, transcendentals=0),
+        name="final" + str(source),
+    )(rows, wf, *earlier)
 
 
 def exchange(values, axes, groups, count):
@@ -430,28 +425,24 @@
 
 
 def on_device(pair_maps, crop_tiles, full_length, proj_weight, out_weight, final_weight):
-    wf, prow, q, pj = make_tables(final_weight)
+    wf, prow, pj = make_tables(final_weight)
     pair = jnp.transpose(pair_maps[0], (0, 2, 1))
     cropped = crop_columns(crop_tiles, pair)
     got = lax.all_to_all(cropped, "row", 0, 0, axis_index_groups=PLANE, tiled=True)
-    current, both = first_projection(crop_tiles, full_length, got, prow, q, proj_weight)
-    currents = (current, current)
+    current, both = first_projection(crop_tiles, full_length, got, prow, proj_weight)
     weights = (prow, proj_weight, out_weight)
     for layer in range(NLAYER):
         products, left, right = own_products(exchange(both, BOTH_AXES, SAME_PART, CH))
-        back_own = exchange(products, BOTH_AXES, SAME_PART, CH)
         right_peer = lax.ppermute(right, BOTH_AXES, OTHER_PART)
-        back_peer = exchange(peer_products(left, right_peer), BOTH_AXES, SAME_PART, CH)
+        products = peer_products(left, right_peer, products)
+        back = exchange(products, BOTH_AXES, SAME_PART, CH)
         if layer + 1 < NLAYER:
-            scalars = (crop_tiles, full_length)
-            own, both = middle_half(0, *scalars, back_own, currents[0], *weights, layer, None)
-            peer, both = middle_half(1, *scalars, back_peer, currents[1], *weights, layer, both)
-            currents = (own, peer)
-    rows = last_own(back_own, currents[0], *weights, NLAYER - 1)
-    mine, other = last_peer(back_peer, currents[1], *weights, rows, pj, NLAYER - 1)
+            current, both = middle_layer(crop_tiles, full_length, back, current, *weights, layer)
+    mine, other = last_layer(back, current, *weights, pj, NLAYER - 1)
     hidden = hidden_features(mine, lax.ppermute(other, "tmpl", CORES))
     moved = exchange(hidden, "row", BY_Z, 128)
-    result = final_projection(moved, lax.ppermute(moved, "tmpl", CORES), wf)
+    result = final_projection(0, moved, wf)
+    result = final_projection(1, lax.ppermute(moved, "tmpl", CORES), wf, (result,))
     return result.reshape(CZ, 8, CROP)
 
 

time: 314 us -> 314 us (level)
  blocking collectives: 125 us -> 196 us
  waiting for transfers between devices: 102 us -> 64.3 us
  starting transfers between devices: 39.6 us -> 13.4 us
  Pallas kernels: 42.3 us -> 34.8 us
    all_to_all x3 -> x5, blocking collectives: 125 us -> 196 us  [exchange(): lax.all_to_all(cube, axes, 0, 0, axis_index_groups=groups, tiled=True)]
    all_to_all x4 -> x0, waiting for transfers between devices: 31.1 us -> none  [exchange(): lax.all_to_all(cube, axes, 0, 0, axis_index_groups=groups, tiled=True)]
    all_to_all x4 -> x0, starting transfers between devices: 25.2 us -> none  [exchange(): lax.all_to_all(cube, axes, 0, 0, axis_index_groups=groups, tiled=True)]
    ppermute x2, waiting for transfers between devices: 43.6 us -> 37.6 us  [on_device(): right_peer = lax.ppermute(right, BOTH_AXES, OTHER_PART)]
    pallas_call x9 -> x8, Pallas kernels: 28.7 us -> 23.7 us  [the longest x1 8.09 us: middle_layer(): pl.pallas_call(middle_kernel, grid_spec=pltpu.PrefetchScalarGridSpec(num_...]
  transfers between devices with their start and end apart: 9 -> 5, of which waited for: 9 -> 4; matrix products, arithmetic and copies ran while one was open for 0% -> 0% of each run, Pallas kernels for 5% -> 1%
where the time goes in v10:
time: 314 us; the launch traced here: 313 us
  blocking collectives  196 us (62%)
  waiting for transfers between devices  64.3 us (20%)
  Pallas kernels  34.8 us (11%)
  starting transfers between devices  13.4 us (4%)
    all_to_all x5, blocking collectives, exchange(): lax.all_to_all(cube, axes, 0, 0, axis_index_groups=groups, tiled=True)  196 us
    ppermute x2, waiting for transfers between devices, on_device(): right_peer = lax.ppermute(right, BOTH_AXES, OTHER_PART)  37.6 us
    all_to_all x1, waiting for transfers between devices, on_device(): lax.all_to_all(cropped, 'row', 0, 0, axis_index_groups=PLANE, tiled=True)  24.8 us
    pallas_call x1, Pallas kernels, middle_layer(): pl.pallas_call(middle_kernel, grid_spec=pltpu.PrefetchScalarGridSpec(num_...  8.09 us
    all_to_all x1, starting transfers between devices, on_device(): lax.all_to_all(cropped, 'row', 0, 0, axis_index_groups=PLANE, tiled=True)  7.6 us
  transfers between devices with their start and end apart: 5, of which 4 were waited for; matrix products, arithmetic and copies ran while one was open for 0% of the time, Pallas kernels for 1%

profile of v10, /device:TPU:1, one launch (start us, length us, event | category | flops | bytes accessed | tf_op | source)
XLA Modules:
  0.0 312.7 jit_solution(2687396403400723036)
XLA Ops:
  0.7 3.3 %crop.1 = bf16[16,64,1024]{2,1,0:T(8,128)(2,1)} custom-call(s32[1,8]{1,0:T(1,128)S(1)} %copy-done.4, bf16[16,64,2048]{2,1,0:T(8,128)(2,1)} %bitcast.21), custom_call_target="tpu_custom_call" | custom-call | tf_op jit(solution)/shard_map/crop/pallas_call | solution.py:126
  3.9 7.6 %all-to-all-start = ((bf16[16,64,1024]{2,1,0:T(8,128)(2,1)}), bf16[16,64,1024]{2,1,0:T(8,128)(2,1)S(1)}, u32[]{:S(2)}, u32[]{:S(2)}) async-start(bf16[16,64,1024]{2,1,0:T(8,128)(2,1)} %crop.1), calls=%async_computation | async-start | bytes 4194304 | tf_op jit(solution)/shard_map/all_to_all | solution.py:431
  12.3 2.4 tables.1
  14.6 24.8 %all-to-all-done.got_ref = bf16[16,64,1024]{2,1,0:T(8,128)(2,1)S(1)} async-done(((bf16[16,64,1024]{2,1,0:T(8,128)(2,1)}), bf16[16,64,1024]{2,1,0:T(8,128)(2,1)S(1)}, u32[]{:S(2)}, u32[]{:S(2)}) %all-to-all-start) | async-done | bytes 2097184 | tf_op jit(solution)/shard_map/all_to_all | solution.py:431
  39.4 5.5 %first.1 = (bf16[512,1024]{1,0:T(8,128)(2,1)}, bf16[512,2048]{1,0:T(8,128)(2,1)}) custom-call(s32[1,8]{1,0:T(1,128)S(1)} %copy-done.5, s32[1]{0:T(128)S(6)} %copy.13.length_ref, bf16[16,64,1024]{2,1,0:T(8,128)(2,1)S(1)} %all-to-all-done.got_ref, bf16[512,512]{1,0:T(8,128)(2,1)S(1)} %get-tuple-element.20.prow_ref, bf16[2,64,320]{2,1,0:T(8,128)(2,1)S(1)} %copy-done), custom_call_target="tpu_custom_call" | custom-call | tf_op jit(solution)/shard_map/first/pallas_call | solution.py:222
  44.9 52.8 %all_to_all.30 = bf16[64,8,2048]{2,1,0:T(8,128)(2,1)S(1)} all-to-all(bf16[64,8,2048]{2,1,0:T(8,128)(2,1)} %bitcast.25), channel_id=1, replica_groups={{0,1,2,3,8,9,10,11,16,17,18,19,24,25,26,27,32,33,34,35,40,41,42,43,48,4..., dimensions={0} | all-to-all | bytes 4194304 | tf_op jit(solution)/shard_map/all_to_all | solution.py:423
  97.8 1.6 own_products.2
  99.4 1.6 collective-permute-start
  101.0 17.0 %collective-permute-done.right_ref = bf16[512,1024]{1,0:T(8,128)(2,1)S(1)} collective-permute-done((bf16[512,1024]{1,0:T(8,128)(2,1)}, bf16[512,1024]{1,0:T(8,128)(2,1)S(1)}, u32[]{:S(2)}, u32[]{:S(2)}) %collective-permute-start) | collective-permute-done | bytes 1048608 | tf_op jit(solution)/shard_map/ppermute | solution.py:436
  119.2 1.5 peer_products.2
  120.7 36.8 %all_to_all.31 = bf16[64,8,1024]{2,1,0:T(8,128)(2,1)S(1)} all-to-all(bf16[64,8,1024]{2,1,0:T(8,128)(2,1)} %bitcast.22), channel_id=1, replica_groups={{0,1,2,3,8,9,10,11,16,17,18,19,24,25,26,27,32,33,34,35,40,41,42,43,48,4..., dimensions={0} | all-to-all | bytes 2097152 | tf_op jit(solution)/shard_map/all_to_all | solution.py:423
  157.5 8.1 %middle.1 = (bf16[512,1024]{1,0:T(8,128)(2,1)}, bf16[512,2048]{1,0:T(8,128)(2,1)}) custom-call(s32[1,8]{1,0:T(1,128)S(1)} %copy-done.5, s32[1]{0:T(128)S(6)} %copy.13.length_ref, bf16[512,1024]{1,0:T(8,128)(2,1)S(1)} %bitcast.18, bf16[512,1024]{1,0:T(8,128)(2,1)} %get-tuple-element.25.cur_ref, bf16[512,512]{1,0:T(8,128)(2,1)S(1)} %get-tuple-element.20.prow_ref, ...), custom_call_target="tpu_custom_call" | custom-call | tf_op jit(solution)/shard_map/middle/pallas_call | solution.py:256
  165.6 46.1 %all_to_all.32 = bf16[64,8,2048]{2,1,0:T(8,128)(2,1)S(1)} all-to-all(bf16[64,8,2048]{2,1,0:T(8,128)(2,1)} %bitcast.24), channel_id=1, replica_groups={{0,1,2,3,8,9,10,11,16,17,18,19,24,25,26,27,32,33,34,35,40,41,42,43,48,4..., dimensions={0} | all-to-all | bytes 4194304 | tf_op jit(solution)/shard_map/all_to_all | solution.py:423
  211.7 1.6 own_products.3
  213.3 1.2 collective-permute-start.1
  214.6 20.7 %collective-permute-done.1.right_ref = bf16[512,1024]{1,0:T(8,128)(2,1)S(1)} collective-permute-done((bf16[512,1024]{1,0:T(8,128)(2,1)}, bf16[512,1024]{1,0:T(8,128)(2,1)S(1)}, u32[]{:S(2)}, u32[]{:S(2)}) %collective-permute-start.1) | collective-permute-done | bytes 1048608 | tf_op jit(solution)/shard_map/ppermute | solution.py:436
  236.5 1.5 peer_products.3
  238.0 34.6 %all_to_all.33 = bf16[64,8,1024]{2,1,0:T(8,128)(2,1)S(1)} all-to-all(bf16[64,8,1024]{2,1,0:T(8,128)(2,1)} %bitcast.23), channel_id=1, replica_groups={{0,1,2,3,8,9,10,11,16,17,18,19,24,25,26,27,32,33,34,35,40,41,42,43,48,4..., dimensions={0} | all-to-all | bytes 2097152 | tf_op jit(solution)/shard_map/all_to_all | solution.py:423
  272.6 5.8 %last.1 = (bf16[1024,256]{1,0:T(8,128)(2,1)S(1)}, bf16[1024,256]{1,0:T(8,128)(2,1)S(1)}) custom-call(bf16[512,1024]{1,0:T(8,128)(2,1)S(1)} %bitcast.17, bf16[512,1024]{1,0:T(8,128)(2,1)} %get-tuple-element.30.cur_ref, bf16[512,512]{1,0:T(8,128)(2,1)S(1)} %get-tuple-element.20.prow_ref, bf16[2,64,320]{2,1,0:T(8,128)(2,1)S(1)} %copy-done, ...), custom_call_target="tpu_custom_call" | custom-call | tf_op jit(solution)/shard_map/last/pallas_call | solution.py:302
  278.6 1.9 collective-permute-done.2
  280.7 25.5 %all_to_all.34 = bf16[128,8,256]{2,1,0:T(8,128)(2,1)S(1)} all-to-all(bf16[128,8,256]{2,1,0:T(8,128)(2,1)S(1)} %fusion), channel_id=1, replica_groups={{0,8,16,24,32,40,48,56,64,72,80,88,96,104,112,120,1,9,17,25,33,41,49,57..., dimensions={0} | all-to-all | bytes 1048576 | tf_op jit(solution)/shard_map/all_to_all | solution.py:423
  306.2 2.8 collective-permute-start.3
  309.0 1.7 final0.1.refs_2_
  310.8 1.7 final1.1
  (17 shorter events, 3.4 us)
Async XLA Ops:
  0.0 0.7 copy-start.4
  3.9 8.3 %copy-start.6 = (bf16[64,128]{1,0:T(8,128)(2,1)S(1)}, bf16[64,128]{1,0:T(8,128)(2,1)}, u32[]{:S(2)}) copy-start(bf16[64,128]{1,0:T(8,128)(2,1)} %final_ref.1) | copy-start | bytes 49156
  3.9 35.5 %all-to-all-start = ((bf16[16,64,1024]{2,1,0:T(8,128)(2,1)}), bf16[16,64,1024]{2,1,0:T(8,128)(2,1)S(1)}, u32[]{:S(2)}, u32[]{:S(2)}) async-start(bf16[16,64,1024]{2,1,0:T(8,128)(2,1)} %crop.1), calls=%async_computation | async-start | bytes 4194304 | tf_op jit(solution)/shard_map/all_to_all | solution.py:431
  11.6 27.9 %copy-start = (bf16[2,64,320]{2,1,0:T(8,128)(2,1)S(1)}, bf16[2,64,320]{2,1,0:T(8,128)(2,1)}, u32[]{:S(2)}) copy-start(bf16[2,64,320]{2,1,0:T(8,128)(2,1)} %w_ref.5) | copy-start | bytes 245764
  11.6 27.9 %copy-start.5 = (s32[1,8]{1,0:T(1,128)S(1)}, s32[1,8]{1,0:T(1,128)}, u32[]{:S(2)}) copy-start(s32[1,8]{1,0:T(1,128)} %crop_ref.5) | copy-start | bytes 100
  99.4 18.6 %collective-permute-start = (bf16[512,1024]{1,0:T(8,128)(2,1)}, bf16[512,1024]{1,0:T(8,128)(2,1)S(1)}, u32[]{:S(2)}, u32[]{:S(2)}) collective-permute-start(bf16[512,1024]{1,0:T(8,128)(2,1)} %get-tuple-element.23), channel_id=1, source_target_pairs={{0,7},{1,6},{2,5},{3,4},{4,3},{5,2},{6,1},{7,0},{8,15},{9,14},{10,... | collective-permute-start | bytes 3145736 | tf_op jit(solution)/shard_map/ppermute | solution.py:436
  118.0 1.2 copy-start.1
  120.7 36.8 %copy-start.3 = (bf16[2,64,64]{2,1,0:T(8,128)(2,1)S(1)}, bf16[2,64,64]{2,1,0:T(8,128)(2,1)}, u32[]{:S(2)}) copy-start(bf16[2,64,64]{2,1,0:T(8,128)(2,1)} %w_out_ref.3) | copy-start | bytes 49156
  213.3 21.9 %collective-permute-start.1 = (bf16[512,1024]{1,0:T(8,128)(2,1)}, bf16[512,1024]{1,0:T(8,128)(2,1)S(1)}, u32[]{:S(2)}, u32[]{:S(2)}) collective-permute-start(bf16[512,1024]{1,0:T(8,128)(2,1)} %get-tuple-element.28), channel_id=1, source_target_pairs={{0,7},{1,6},{2,5},{3,4},{4,3},{5,2},{6,1},{7,0},{8,15},{9,14},{10,... | collective-permute-start | bytes 3145736 | tf_op jit(solution)/shard_map/ppermute | solution.py:436
  235.2 1.2 copy-start.2
  278.5 2.0 collective-permute-start.2
  306.2 4.5 %collective-permute-start.3 = (bf16[1024,256]{1,0:T(8,128)(2,1)S(1)}, bf16[1024,256]{1,0:T(8,128)(2,1)S(1)}, u32[]{:S(2)}, u32[]{:S(2)}) collective-permute-start(bf16[1024,256]{1,0:T(8,128)(2,1)S(1)} %bitcast.19), channel_id=1, source_target_pairs={{0,128},{128,0},{1,129},{129,1},{2,130},{130,2},{3,131},{131,3},{4... | collective-permute-start | bytes 1572872 | tf_op jit(solution)/shard_map/ppermute | solution.py:445

commit v11 on v10

--- a/solution.py
+++ b/solution.py
@@ -148,8 +148,8 @@
     return center * lax.rsqrt(spread + EPSILON)
 
 
-def sigmoid(values):
-    return 0.5 * jnp.tanh(0.5 * values) + 0.5
+def halved(weights):
+    return (weights.astype(F32) * 0.5).astype(BF)
 
 
 def side_by_side(values):
@@ -177,12 +177,12 @@
 
 
 def project(current, w, prow, mask, both_ref):
-    values = dot_tn(w[:, : 4 * CH], norm_channels(current).astype(BF))
+    values = dot_tn(halved(w[:, : 4 * CH]), norm_channels(current).astype(BF))
     lanes = both_ref.shape[1] // 2
     for side in range(2):
         gate = values[side * 128 : side * 128 + CH]
         value = values[side * 128 + CH : side * 128 + 2 * CH]
-        factor = (sigmoid(gate) * value * mask).astype(BF)
+        factor = ((jnp.tanh(gate) + 1.0) * (value * mask)).astype(BF)
         both_ref[:, side * lanes : (side + 1) * lanes] = dot(prow, stacked(factor)).astype(BF)
 
 
@@ -236,10 +236,10 @@
 def update(back_ref, cur_ref, prow, w_proj, w_out):
     block = cur_ref.shape[1]
     current = side_by_side(cur_ref[...].astype(F32))
-    gate = sigmoid(dot_tn(w_proj[:, 4 * CH :], norm_channels(current).astype(BF)))
+    gate = jnp.tanh(dot_tn(halved(w_proj[:, 4 * CH :]), norm_channels(current).astype(BF))) + 1.0
     lanes = pl.ds(pl.multiple_of(pl.program_id(0) * block, block), block)
     products = side_by_side(dot_tn(prow, back_ref[:, lanes]))
-    change = dot_tn(w_out, norm_channels(products).astype(BF))
+    change = dot_tn(halved(w_out), norm_channels(products).astype(BF))
     return (current + gate * change).astype(BF)
 
 
@@ -313,60 +313,62 @@
     )(*in_vmem(back), *in_hbm(current), *in_vmem(prow), proj_weight, out_weight, *in_hbm(pj))
 
 
-def own_products_kernel(both_ref, out_hbm, left_hbm, right_hbm, own_ref, sems):
+def right_kernel(both_ref, right_hbm, sems):
     copies = []
-    for side, target in ((1, right_hbm), (0, left_hbm)):
-        for block in range(STEPS):
-            source = both_ref.at[:, pl.ds((2 * block + side) * BLOCK, BLOCK)]
-            place = target.at[:, pl.ds(block * BLOCK, BLOCK)]
-            copies.append(pltpu.make_async_copy(source, place, sems.at[2 * block + side]))
+    for block in range(STEPS):
+        source = both_ref.at[:, pl.ds((2 * block + 1) * BLOCK, BLOCK)]
+        place = right_hbm.at[:, pl.ds(block * BLOCK, BLOCK)]
+        copies.append(pltpu.make_async_copy(source, place, sems.at[block]))
     for copy in copies:
         copy.start()
-    starts = [2 * block * BLOCK for block in range(STEPS)]
-    left = jnp.concatenate([both_ref[:, start : start + BLOCK] for start in starts], axis=1)
-    right = jnp.concatenate([both_ref[:, start + BLOCK : start + 2 * BLOCK] for start in starts], axis=1)
-    own_ref[...] = dot_nt(left, right).astype(BF)
-    store = pltpu.make_async_copy(own_ref, out_hbm.at[:, pl.ds(0, 512)], sems.at[2 * STEPS])
-    store.start()
     for copy in copies:
         copy.wait()
-    store.wait()
-
-
-def own_products(both):
-    square = pltpu.HBM((512, CROP), BF)
-    return pl.pallas_call(
-        own_products_kernel,
-        out_specs=[ANYWHERE] * 3,
-        out_shape=[square] * 3,
-        scratch_shapes=[pltpu.VMEM((512, 512), BF), pltpu.SemaphoreType.DMA((2 * STEPS + 1,))],
-        compiler_params=pltpu.CompilerParams(vmem_limit_bytes=VMEM_LIMIT),
-        cost_estimate=pl.CostEstimate(flops=2**29, bytes_accessed=4 * 2**20, transcendentals=0),
-        name="own_products",
+
+
+def right_alone(both):
+    return pl.pallas_call(
+        right_kernel,
+        in_specs=[RESIDENT],
+        out_specs=ANYWHERE,
+        out_shape=pltpu.HBM((512, CROP), BF),
+        scratch_shapes=[pltpu.SemaphoreType.DMA((STEPS,))],
+        compiler_params=pltpu.CompilerParams(vmem_limit_bytes=VMEM_LIMIT),
+        cost_estimate=pl.CostEstimate(flops=0, bytes_accessed=2 * 2**20, transcendentals=0),
+        name="right",
     )(both)
 
 
-def peer_products_kernel(left_ref, right_ref, products_hbm, out_hbm, peer_ref, sem):
-    del products_hbm
-    left = jnp.concatenate([left_ref[:, 512:], left_ref[:, :512]], axis=1)
-    peer_ref[...] = dot_nt(left, right_ref[...]).astype(BF)
-    store = pltpu.make_async_copy(peer_ref, out_hbm.at[:, pl.ds(512, 512)], sem)
+def lane_blocks(both_ref, side, order):
+    starts = [(2 * block + side) * BLOCK for block in order]
+    return jnp.concatenate([both_ref[:, start : start + BLOCK] for start in starts], axis=1)
+
+
+def products_kernel(peer, *refs):
+    both_ref, right_ref = refs[0], refs[1]
+    out_hbm, square_ref, sem = refs[-3:]
+    if peer:
+        left, right = lane_blocks(both_ref, 0, [1, 0]), right_ref[...]
+    else:
+        left, right = lane_blocks(both_ref, 0, [0, 1]), lane_blocks(both_ref, 1, [0, 1])
+    square_ref[...] = dot_nt(left, right).astype(BF)
+    store = pltpu.make_async_copy(square_ref, out_hbm.at[:, pl.ds(512 * peer, 512)], sem)
     store.start()
     store.wait()
 
 
-def peer_products(left, right, products):
-    return pl.pallas_call(
-        peer_products_kernel,
-        in_specs=[RESIDENT, RESIDENT, ANYWHERE],
+def half_products(both, *others):
+    peer = len(others) // 2
+    return pl.pallas_call(
+        functools.partial(products_kernel, peer),
+        in_specs=[RESIDENT, RESIDENT, ANYWHERE][: 1 + len(others)],
         out_specs=ANYWHERE,
         out_shape=pltpu.HBM((512, CROP), BF),
-        input_output_aliases={2: 0},
+        input_output_aliases={2: 0} if peer else {},
         scratch_shapes=[pltpu.VMEM((512, 512), BF), pltpu.SemaphoreType.DMA],
         compiler_params=pltpu.CompilerParams(vmem_limit_bytes=VMEM_LIMIT),
         cost_estimate=pl.CostEstimate(flops=2**29, bytes_accessed=4 * 2**20, transcendentals=0),
-        name="peer_products",
-    )(left, right, products)
+        name="products" + str(peer),
+    )(both, *others)
 
 
 def hidden_features(mine, peer):
@@ -432,9 +434,9 @@
     current, both = first_projection(crop_tiles, full_length, got, prow, proj_weight)
     weights = (prow, proj_weight, out_weight)
     for layer in range(NLAYER):
-        products, left, right = own_products(exchange(both, BOTH_AXES, SAME_PART, CH))
-        right_peer = lax.ppermute(right, BOTH_AXES, OTHER_PART)
-        products = peer_products(left, right_peer, products)
+        gathered = exchange(both, BOTH_AXES, SAME_PART, CH)
+        right_peer = lax.ppermute(right_alone(gathered), BOTH_AXES, OTHER_PART)
+        products = half_products(gathered, right_peer, half_products(gathered))
         back = exchange(products, BOTH_AXES, SAME_PART, CH)
         if layer + 1 < NLAYER:
             current, both = middle_layer(crop_tiles, full_length, back, current, *weights, layer)

time: 314 us -> 310 us (0.987)
    pallas_call x4 -> x6, Pallas kernels: 6.25 us -> 8.29 us  [the longest x4 6.33 us: half_products(): pl.pallas_call(functools.partial(products_kernel, peer), in_specs=[RESIDE...]
  transfers between devices with their start and end apart: 5 -> 5, of which waited for: 4 -> 4; matrix products, arithmetic and copies ran while one was open for 0% -> 0% of each run, Pallas kernels for 1% -> 2%
where the time goes in v11:
time: 310 us; the launch traced here: 309 us
  blocking collectives  196 us (63%)
  waiting for transfers between devices  61.4 us (20%)
  Pallas kernels  36.7 us (12%)
  starting transfers between devices  13.2 us (4%)
    all_to_all x5, blocking collectives, exchange(): lax.all_to_all(cube, axes, 0, 0, axis_index_groups=groups, tiled=True)  196 us
    ppermute x2, waiting for transfers between devices, on_device(): right_peer = lax.ppermute(right_alone(gathered), BOTH_AXES, OTHER_PART)  34.7 us
    all_to_all x1, waiting for transfers between devices, on_device(): lax.all_to_all(cropped, 'row', 0, 0, axis_index_groups=PLANE, tiled=True)  24.8 us
    pallas_call x1, Pallas kernels, middle_layer(): pl.pallas_call(middle_kernel, grid_spec=pltpu.PrefetchScalarGridSpec(num_...  7.89 us
    all_to_all x1, starting transfers between devices, on_device(): lax.all_to_all(cropped, 'row', 0, 0, axis_index_groups=PLANE, tiled=True)  7.6 us
    pallas_call x4, Pallas kernels, half_products(): pl.pallas_call(functools.partial(products_kernel, peer), in_specs=[RESIDE...  6.33 us
  transfers between devices with their start and end apart: 5, of which 4 were waited for; matrix products, arithmetic and copies ran while one was open for 0% of the time, Pallas kernels for 2%

profile of v11, /device:TPU:1, one launch (start us, length us, event | category | flops | bytes accessed | tf_op | source)
XLA Modules:
  0.0 308.9 jit_solution(13778414861842498955)
XLA Ops:
  0.7 3.3 %crop.1 = bf16[16,64,1024]{2,1,0:T(8,128)(2,1)} custom-call(s32[1,8]{1,0:T(1,128)S(1)} %copy-done.2, bf16[16,64,2048]{2,1,0:T(8,128)(2,1)} %bitcast.27), custom_call_target="tpu_custom_call" | custom-call | tf_op jit(solution)/shard_map/crop/pallas_call | solution.py:126
  3.9 7.6 %all-to-all-start = ((bf16[16,64,1024]{2,1,0:T(8,128)(2,1)}), bf16[16,64,1024]{2,1,0:T(8,128)(2,1)S(1)}, u32[]{:S(2)}, u32[]{:S(2)}) async-start(bf16[16,64,1024]{2,1,0:T(8,128)(2,1)} %crop.1), calls=%async_computation | async-start | bytes 4194304 | tf_op jit(solution)/shard_map/all_to_all | solution.py:433
  12.3 2.4 tables.1
  14.6 24.8 %all-to-all-done.got_ref = bf16[16,64,1024]{2,1,0:T(8,128)(2,1)S(1)} async-done(((bf16[16,64,1024]{2,1,0:T(8,128)(2,1)}), bf16[16,64,1024]{2,1,0:T(8,128)(2,1)S(1)}, u32[]{:S(2)}, u32[]{:S(2)}) %all-to-all-start) | async-done | bytes 2097184 | tf_op jit(solution)/shard_map/all_to_all | solution.py:433
  39.4 5.5 %first.1 = (bf16[512,1024]{1,0:T(8,128)(2,1)}, bf16[512,2048]{1,0:T(8,128)(2,1)}) custom-call(s32[1,8]{1,0:T(1,128)S(1)} %copy-done.3, s32[1]{0:T(128)S(6)} %copy.13.length_ref, bf16[16,64,1024]{2,1,0:T(8,128)(2,1)S(1)} %all-to-all-done.got_ref, bf16[512,512]{1,0:T(8,128)(2,1)S(1)} %get-tuple-element.14.prow_ref, bf16[2,64,320]{2,1,0:T(8,128)(2,1)S(1)} %copy-done), custom_call_target="tpu_custom_call" | custom-call | tf_op jit(solution)/shard_map/first/pallas_call | solution.py:222
  44.9 52.9 %all_to_all.30 = bf16[64,8,2048]{2,1,0:T(8,128)(2,1)S(1)} all-to-all(bf16[64,8,2048]{2,1,0:T(8,128)(2,1)} %bitcast.29), channel_id=1, replica_groups={{0,1,2,3,8,9,10,11,16,17,18,19,24,25,26,27,32,33,34,35,40,41,42,43,48,4..., dimensions={0} | all-to-all | bytes 4194304 | tf_op jit(solution)/shard_map/all_to_all | solution.py:425
  98.8 1.6 collective-permute-start
  100.4 1.6 products0.2.refs_2_
  102.0 15.3 %collective-permute-done.refs_1_ = bf16[512,1024]{1,0:T(8,128)(2,1)S(1)} collective-permute-done((bf16[512,1024]{1,0:T(8,128)(2,1)}, bf16[512,1024]{1,0:T(8,128)(2,1)S(1)}, u32[]{:S(2)}, u32[]{:S(2)}) %collective-permute-start) | collective-permute-done | bytes 1048608 | tf_op jit(solution)/shard_map/ppermute | solution.py:438
  117.3 1.6 products1.2
  119.0 36.8 %all_to_all.31 = bf16[64,8,1024]{2,1,0:T(8,128)(2,1)S(1)} all-to-all(bf16[64,8,1024]{2,1,0:T(8,128)(2,1)} %bitcast.25), channel_id=1, replica_groups={{0,1,2,3,8,9,10,11,16,17,18,19,24,25,26,27,32,33,34,35,40,41,42,43,48,4..., dimensions={0} | all-to-all | bytes 2097152 | tf_op jit(solution)/shard_map/all_to_all | solution.py:425
  155.7 7.9 %middle.1 = (bf16[512,1024]{1,0:T(8,128)(2,1)}, bf16[512,2048]{1,0:T(8,128)(2,1)}) custom-call(s32[1,8]{1,0:T(1,128)S(1)} %copy-done.3, s32[1]{0:T(128)S(6)} %copy.13.length_ref, bf16[512,1024]{1,0:T(8,128)(2,1)S(1)} %bitcast.22, bf16[512,1024]{1,0:T(8,128)(2,1)} %get-tuple-element.16.cur_ref, bf16[512,512]{1,0:T(8,128)(2,1)S(1)} %get-tuple-element.14.prow_ref, ...), custom_call_target="tpu_custom_call" | custom-call | tf_op jit(solution)/shard_map/middle/pallas_call | solution.py:256
  163.6 46.1 %all_to_all.32 = bf16[64,8,2048]{2,1,0:T(8,128)(2,1)S(1)} all-to-all(bf16[64,8,2048]{2,1,0:T(8,128)(2,1)} %bitcast.28), channel_id=1, replica_groups={{0,1,2,3,8,9,10,11,16,17,18,19,24,25,26,27,32,33,34,35,40,41,42,43,48,4..., dimensions={0} | all-to-all | bytes 4194304 | tf_op jit(solution)/shard_map/all_to_all | solution.py:425
  210.7 1.1 collective-permute-start.1
  211.8 1.6 products0.3.refs_2_
  213.4 19.4 %collective-permute-done.1.refs_1_ = bf16[512,1024]{1,0:T(8,128)(2,1)S(1)} collective-permute-done((bf16[512,1024]{1,0:T(8,128)(2,1)}, bf16[512,1024]{1,0:T(8,128)(2,1)S(1)}, u32[]{:S(2)}, u32[]{:S(2)}) %collective-permute-start.1) | collective-permute-done | bytes 1048608 | tf_op jit(solution)/shard_map/ppermute | solution.py:438
  232.8 1.6 products1.3
  234.3 34.5 %all_to_all.33 = bf16[64,8,1024]{2,1,0:T(8,128)(2,1)S(1)} all-to-all(bf16[64,8,1024]{2,1,0:T(8,128)(2,1)} %bitcast.26), channel_id=1, replica_groups={{0,1,2,3,8,9,10,11,16,17,18,19,24,25,26,27,32,33,34,35,40,41,42,43,48,4..., dimensions={0} | all-to-all | bytes 2097152 | tf_op jit(solution)/shard_map/all_to_all | solution.py:425
  268.9 5.9 %last.1 = (bf16[1024,256]{1,0:T(8,128)(2,1)S(1)}, bf16[1024,256]{1,0:T(8,128)(2,1)S(1)}) custom-call(bf16[512,1024]{1,0:T(8,128)(2,1)S(1)} %bitcast.21, bf16[512,1024]{1,0:T(8,128)(2,1)} %get-tuple-element.18.cur_ref, bf16[512,512]{1,0:T(8,128)(2,1)S(1)} %get-tuple-element.14.prow_ref, bf16[2,64,320]{2,1,0:T(8,128)(2,1)S(1)} %copy-done, ...), custom_call_target="tpu_custom_call" | custom-call | tf_op jit(solution)/shard_map/last/pallas_call | solution.py:302
  274.9 1.9 collective-permute-done.2
  277.0 25.5 %all_to_all.34 = bf16[128,8,256]{2,1,0:T(8,128)(2,1)S(1)} all-to-all(bf16[128,8,256]{2,1,0:T(8,128)(2,1)S(1)} %fusion), channel_id=1, replica_groups={{0,8,16,24,32,40,48,56,64,72,80,88,96,104,112,120,1,9,17,25,33,41,49,57..., dimensions={0} | all-to-all | bytes 1048576 | tf_op jit(solution)/shard_map/all_to_all | solution.py:425
  302.5 2.8 collective-permute-start.3
  305.3 1.7 final0.1.refs_2_
  307.0 1.7 final1.1
  (15 shorter events, 2.9 us)
Async XLA Ops:
  0.0 0.7 copy-start.2
  3.9 8.3 %copy-start.4 = (bf16[64,128]{1,0:T(8,128)(2,1)S(1)}, bf16[64,128]{1,0:T(8,128)(2,1)}, u32[]{:S(2)}) copy-start(bf16[64,128]{1,0:T(8,128)(2,1)} %final_ref.1) | copy-start | bytes 49156
  3.9 35.5 %all-to-all-start = ((bf16[16,64,1024]{2,1,0:T(8,128)(2,1)}), bf16[16,64,1024]{2,1,0:T(8,128)(2,1)S(1)}, u32[]{:S(2)}, u32[]{:S(2)}) async-start(bf16[16,64,1024]{2,1,0:T(8,128)(2,1)} %crop.1), calls=%async_computation | async-start | bytes 4194304 | tf_op jit(solution)/shard_map/all_to_all | solution.py:433
  11.6 27.9 %copy-start = (bf16[2,64,320]{2,1,0:T(8,128)(2,1)S(1)}, bf16[2,64,320]{2,1,0:T(8,128)(2,1)}, u32[]{:S(2)}) copy-start(bf16[2,64,320]{2,1,0:T(8,128)(2,1)} %w_ref.5) | copy-start | bytes 245764
  11.6 27.9 %copy-start.3 = (s32[1,8]{1,0:T(1,128)S(1)}, s32[1,8]{1,0:T(1,128)}, u32[]{:S(2)}) copy-start(s32[1,8]{1,0:T(1,128)} %crop_ref.5) | copy-start | bytes 100
  98.8 18.6 %collective-permute-start = (bf16[512,1024]{1,0:T(8,128)(2,1)}, bf16[512,1024]{1,0:T(8,128)(2,1)S(1)}, u32[]{:S(2)}, u32[]{:S(2)}) collective-permute-start(bf16[512,1024]{1,0:T(8,128)(2,1)} %right.2), channel_id=1, source_target_pairs={{0,7},{1,6},{2,5},{3,4},{4,3},{5,2},{6,1},{7,0},{8,15},{9,14},{10,... | collective-permute-start | bytes 3145736 | tf_op jit(solution)/shard_map/ppermute | solution.py:438
  118.9 36.8 %copy-start.1 = (bf16[2,64,64]{2,1,0:T(8,128)(2,1)S(1)}, bf16[2,64,64]{2,1,0:T(8,128)(2,1)}, u32[]{:S(2)}) copy-start(bf16[2,64,64]{2,1,0:T(8,128)(2,1)} %w_out_ref.3) | copy-start | bytes 49156
  210.7 22.0 %collective-permute-start.1 = (bf16[512,1024]{1,0:T(8,128)(2,1)}, bf16[512,1024]{1,0:T(8,128)(2,1)S(1)}, u32[]{:S(2)}, u32[]{:S(2)}) collective-permute-start(bf16[512,1024]{1,0:T(8,128)(2,1)} %right.3), channel_id=1, source_target_pairs={{0,7},{1,6},{2,5},{3,4},{4,3},{5,2},{6,1},{7,0},{8,15},{9,14},{10,... | collective-permute-start | bytes 3145736 | tf_op jit(solution)/shard_map/ppermute | solution.py:438
  274.8 2.0 collective-permute-start.2
  302.5 4.5 %collective-permute-start.3 = (bf16[1024,256]{1,0:T(8,128)(2,1)S(1)}, bf16[1024,256]{1,0:T(8,128)(2,1)S(1)}, u32[]{:S(2)}, u32[]{:S(2)}) collective-permute-start(bf16[1024,256]{1,0:T(8,128)(2,1)S(1)} %bitcast.23), channel_id=1, source_target_pairs={{0,128},{128,0},{1,129},{129,1},{2,130},{130,2},{3,131},{131,3},{4... | collective-permute-start | bytes 1572872 | tf_op jit(solution)/shard_map/ppermute | solution.py:447

commit v12 on v11

--- a/solution.py
+++ b/solution.py
@@ -191,9 +191,9 @@
 RESIDENT = pl.BlockSpec(memory_space=pltpu.VMEM)
 STEPS = CROP // BLOCK
 HALF_STEPS = STEPS // 2
-LAST_BLOCK = 256
+LAST_BLOCK = 512
 LAST_STEPS = CROP // LAST_BLOCK
-BOTH = pltpu.HBM((512, 2 * CROP), BF)
+BOTH = pltpu.VMEM((512, 2 * CROP), BF)
 
 
 def first_kernel(crop_ref, length_ref, got_ref, prow_ref, w_ref, cur_ref, both_ref):

time: 310 us -> 306 us (0.987)
  no operation moved by 1% of the time
where the time goes in v12:
time: 306 us; the launch traced here: 305 us
  blocking collectives  197 us (64%)
  waiting for transfers between devices  58.5 us (19%)
  Pallas kernels  34.7 us (11%)
  starting transfers between devices  13.9 us (5%)
    all_to_all x5, blocking collectives, exchange(): lax.all_to_all(cube, axes, 0, 0, axis_index_groups=groups, tiled=True)  197 us
    ppermute x2, waiting for transfers between devices, on_device(): right_peer = lax.ppermute(right_alone(gathered), BOTH_AXES, OTHER_PART)  31.8 us
    all_to_all x1, waiting for transfers between devices, on_device(): lax.all_to_all(cropped, 'row', 0, 0, axis_index_groups=PLANE, tiled=True)  24.8 us
    all_to_all x1, starting transfers between devices, on_device(): lax.all_to_all(cropped, 'row', 0, 0, axis_index_groups=PLANE, tiled=True)  7.6 us
    pallas_call x1, Pallas kernels, middle_layer(): pl.pallas_call(middle_kernel, grid_spec=pltpu.PrefetchScalarGridSpec(num_...  7.19 us
    pallas_call x4, Pallas kernels, half_products(): pl.pallas_call(functools.partial(products_kernel, peer), in_specs=[RESIDE...  6.33 us
  transfers between devices with their start and end apart: 5, of which 4 were waited for; matrix products, arithmetic and copies ran while one was open for 0% of the time, Pallas kernels for 2%

profile of v12, /device:TPU:1, one launch (start us, length us, event | category | flops | bytes accessed | tf_op | source)
XLA Modules:
  0.0 305.5 jit_solution(6585911919458723673)
XLA Ops:
  0.7 3.3 %crop.1 = bf16[16,64,1024]{2,1,0:T(8,128)(2,1)} custom-call(s32[1,8]{1,0:T(1,128)S(1)} %copy-done.2, bf16[16,64,2048]{2,1,0:T(8,128)(2,1)} %bitcast.29), custom_call_target="tpu_custom_call" | custom-call | tf_op jit(solution)/shard_map/crop/pallas_call | solution.py:126
  3.9 7.6 %all-to-all-start = ((bf16[16,64,1024]{2,1,0:T(8,128)(2,1)}), bf16[16,64,1024]{2,1,0:T(8,128)(2,1)S(1)}, u32[]{:S(2)}, u32[]{:S(2)}) async-start(bf16[16,64,1024]{2,1,0:T(8,128)(2,1)} %crop.1), calls=%async_computation | async-start | bytes 4194304 | tf_op jit(solution)/shard_map/all_to_all | solution.py:433
  12.3 2.4 tables.1
  14.6 24.8 %all-to-all-done.got_ref = bf16[16,64,1024]{2,1,0:T(8,128)(2,1)S(1)} async-done(((bf16[16,64,1024]{2,1,0:T(8,128)(2,1)}), bf16[16,64,1024]{2,1,0:T(8,128)(2,1)S(1)}, u32[]{:S(2)}, u32[]{:S(2)}) %all-to-all-start) | async-done | bytes 2097184 | tf_op jit(solution)/shard_map/all_to_all | solution.py:433
  39.4 4.7 %first.1 = (bf16[512,1024]{1,0:T(8,128)(2,1)}, bf16[512,2048]{1,0:T(8,128)(2,1)S(1)}) custom-call(s32[1,8]{1,0:T(1,128)S(1)} %copy-done.3, s32[1]{0:T(128)S(6)} %copy.13.length_ref, bf16[16,64,1024]{2,1,0:T(8,128)(2,1)S(1)} %all-to-all-done.got_ref, bf16[512,512]{1,0:T(8,128)(2,1)S(1)} %get-tuple-element.14.prow_ref, bf16[2,64,320]{2,1,0:T(8,128)(2,1)S(1)} %copy-done), custom_call_target="tpu_custom_call" | custom-call | tf_op jit(solution)/shard_map/first/pallas_call | solution.py:222
  44.1 52.7 %all_to_all.30 = bf16[64,8,2048]{2,1,0:T(8,128)(2,1)S(1)} all-to-all(bf16[64,8,2048]{2,1,0:T(8,128)(2,1)S(1)} %bitcast.24), channel_id=1, replica_groups={{0,1,2,3,8,9,10,11,16,17,18,19,24,25,26,27,32,33,34,35,40,41,42,43,48,4..., dimensions={0} | all-to-all | bytes 4194304 | tf_op jit(solution)/shard_map/all_to_all | solution.py:425
  97.8 1.6 collective-permute-start
  99.5 1.6 products0.2.refs_2_
  101.1 15.3 %collective-permute-done.refs_1_ = bf16[512,1024]{1,0:T(8,128)(2,1)S(1)} collective-permute-done((bf16[512,1024]{1,0:T(8,128)(2,1)}, bf16[512,1024]{1,0:T(8,128)(2,1)S(1)}, u32[]{:S(2)}, u32[]{:S(2)}) %collective-permute-start) | collective-permute-done | bytes 1048608 | tf_op jit(solution)/shard_map/ppermute | solution.py:438
  116.3 1.6 products1.2
  118.0 36.8 %all_to_all.31 = bf16[64,8,1024]{2,1,0:T(8,128)(2,1)S(1)} all-to-all(bf16[64,8,1024]{2,1,0:T(8,128)(2,1)} %bitcast.27), channel_id=1, replica_groups={{0,1,2,3,8,9,10,11,16,17,18,19,24,25,26,27,32,33,34,35,40,41,42,43,48,4..., dimensions={0} | all-to-all | bytes 2097152 | tf_op jit(solution)/shard_map/all_to_all | solution.py:425
  154.8 7.2 %middle.1 = (bf16[512,1024]{1,0:T(8,128)(2,1)}, bf16[512,2048]{1,0:T(8,128)(2,1)S(1)}) custom-call(s32[1,8]{1,0:T(1,128)S(1)} %copy-done.3, s32[1]{0:T(128)S(6)} %copy.13.length_ref, bf16[512,1024]{1,0:T(8,128)(2,1)S(1)} %bitcast.22, bf16[512,1024]{1,0:T(8,128)(2,1)} %get-tuple-element.16.cur_ref, bf16[512,512]{1,0:T(8,128)(2,1)S(1)} %get-tuple-element.14.prow_ref, ...), custom_call_target="tpu_custom_call" | custom-call | tf_op jit(solution)/shard_map/middle/pallas_call | solution.py:256
  162.0 45.8 %all_to_all.32 = bf16[64,8,2048]{2,1,0:T(8,128)(2,1)S(1)} all-to-all(bf16[64,8,2048]{2,1,0:T(8,128)(2,1)S(1)} %bitcast.23), channel_id=1, replica_groups={{0,1,2,3,8,9,10,11,16,17,18,19,24,25,26,27,32,33,34,35,40,41,42,43,48,4..., dimensions={0} | all-to-all | bytes 4194304 | tf_op jit(solution)/shard_map/all_to_all | solution.py:425
  208.8 1.8 collective-permute-start.1
  210.5 1.6 products0.3.refs_2_
  212.1 16.5 %collective-permute-done.1.refs_1_ = bf16[512,1024]{1,0:T(8,128)(2,1)S(1)} collective-permute-done((bf16[512,1024]{1,0:T(8,128)(2,1)}, bf16[512,1024]{1,0:T(8,128)(2,1)S(1)}, u32[]{:S(2)}, u32[]{:S(2)}) %collective-permute-start.1) | collective-permute-done | bytes 1048608 | tf_op jit(solution)/shard_map/ppermute | solution.py:438
  228.7 1.6 products1.3
  230.2 35.5 %all_to_all.33 = bf16[64,8,1024]{2,1,0:T(8,128)(2,1)S(1)} all-to-all(bf16[64,8,1024]{2,1,0:T(8,128)(2,1)} %bitcast.28), channel_id=1, replica_groups={{0,1,2,3,8,9,10,11,16,17,18,19,24,25,26,27,32,33,34,35,40,41,42,43,48,4..., dimensions={0} | all-to-all | bytes 2097152 | tf_op jit(solution)/shard_map/all_to_all | solution.py:425
  265.8 5.4 %last.1 = (bf16[1024,256]{1,0:T(8,128)(2,1)S(1)}, bf16[1024,256]{1,0:T(8,128)(2,1)S(1)}) custom-call(bf16[512,1024]{1,0:T(8,128)(2,1)S(1)} %bitcast.21, bf16[512,1024]{1,0:T(8,128)(2,1)} %get-tuple-element.18.cur_ref, bf16[512,512]{1,0:T(8,128)(2,1)S(1)} %get-tuple-element.14.prow_ref, bf16[2,64,320]{2,1,0:T(8,128)(2,1)S(1)} %copy-done, ...), custom_call_target="tpu_custom_call" | custom-call | tf_op jit(solution)/shard_map/last/pallas_call | solution.py:302
  271.3 1.9 collective-permute-done.2
  273.3 25.7 %all_to_all.34 = bf16[128,8,256]{2,1,0:T(8,128)(2,1)S(1)} all-to-all(bf16[128,8,256]{2,1,0:T(8,128)(2,1)S(1)} %fusion), channel_id=1, replica_groups={{0,8,16,24,32,40,48,56,64,72,80,88,96,104,112,120,1,9,17,25,33,41,49,57..., dimensions={0} | all-to-all | bytes 1048576 | tf_op jit(solution)/shard_map/all_to_all | solution.py:425
  299.0 2.8 collective-permute-start.3
  301.8 1.7 final0.1.refs_2_
  303.6 1.7 final1.1
  (15 shorter events, 3.0 us)
Async XLA Ops:
  0.0 0.7 copy-start.2
  3.9 8.3 %copy-start.4 = (bf16[64,128]{1,0:T(8,128)(2,1)S(1)}, bf16[64,128]{1,0:T(8,128)(2,1)}, u32[]{:S(2)}) copy-start(bf16[64,128]{1,0:T(8,128)(2,1)} %final_ref.1) | copy-start | bytes 49156
  3.9 35.5 %all-to-all-start = ((bf16[16,64,1024]{2,1,0:T(8,128)(2,1)}), bf16[16,64,1024]{2,1,0:T(8,128)(2,1)S(1)}, u32[]{:S(2)}, u32[]{:S(2)}) async-start(bf16[16,64,1024]{2,1,0:T(8,128)(2,1)} %crop.1), calls=%async_computation | async-start | bytes 4194304 | tf_op jit(solution)/shard_map/all_to_all | solution.py:433
  11.6 27.9 %copy-start = (bf16[2,64,320]{2,1,0:T(8,128)(2,1)S(1)}, bf16[2,64,320]{2,1,0:T(8,128)(2,1)}, u32[]{:S(2)}) copy-start(bf16[2,64,320]{2,1,0:T(8,128)(2,1)} %w_ref.5) | copy-start | bytes 245764
  11.6 27.9 %copy-start.3 = (s32[1,8]{1,0:T(1,128)S(1)}, s32[1,8]{1,0:T(1,128)}, u32[]{:S(2)}) copy-start(s32[1,8]{1,0:T(1,128)} %crop_ref.5) | copy-start | bytes 100
  97.8 18.5 %collective-permute-start = (bf16[512,1024]{1,0:T(8,128)(2,1)}, bf16[512,1024]{1,0:T(8,128)(2,1)S(1)}, u32[]{:S(2)}, u32[]{:S(2)}) collective-permute-start(bf16[512,1024]{1,0:T(8,128)(2,1)} %right.2), channel_id=1, source_target_pairs={{0,7},{1,6},{2,5},{3,4},{4,3},{5,2},{6,1},{7,0},{8,15},{9,14},{10,... | collective-permute-start | bytes 3145736 | tf_op jit(solution)/shard_map/ppermute | solution.py:438
  117.9 36.9 %copy-start.1 = (bf16[2,64,64]{2,1,0:T(8,128)(2,1)S(1)}, bf16[2,64,64]{2,1,0:T(8,128)(2,1)}, u32[]{:S(2)}) copy-start(bf16[2,64,64]{2,1,0:T(8,128)(2,1)} %w_out_ref.3) | copy-start | bytes 49156
  208.8 19.9 %collective-permute-start.1 = (bf16[512,1024]{1,0:T(8,128)(2,1)}, bf16[512,1024]{1,0:T(8,128)(2,1)S(1)}, u32[]{:S(2)}, u32[]{:S(2)}) collective-permute-start(bf16[512,1024]{1,0:T(8,128)(2,1)} %right.3), channel_id=1, source_target_pairs={{0,7},{1,6},{2,5},{3,4},{4,3},{5,2},{6,1},{7,0},{8,15},{9,14},{10,... | collective-permute-start | bytes 3145736 | tf_op jit(solution)/shard_map/ppermute | solution.py:438
  271.2 2.0 collective-permute-start.2
  299.0 4.5 %collective-permute-start.3 = (bf16[1024,256]{1,0:T(8,128)(2,1)S(1)}, bf16[1024,256]{1,0:T(8,128)(2,1)S(1)}, u32[]{:S(2)}, u32[]{:S(2)}) collective-permute-start(bf16[1024,256]{1,0:T(8,128)(2,1)S(1)} %bitcast.25), channel_id=1, source_target_pairs={{0,128},{128,0},{1,129},{129,1},{2,130},{130,2},{3,131},{131,3},{4... | collective-permute-start | bytes 1572872 | tf_op jit(solution)/shard_map/ppermute | solution.py:447

commit v13 on v12

--- a/solution.py
+++ b/solution.py
@@ -227,7 +227,7 @@
             in_specs=[RESIDENT, RESIDENT, layer_weight(320, 0)],
             out_specs=[lanes_of(512), lanes_of(512, 2 * BLOCK)],
         ),
-        out_shape=[pltpu.HBM((512, CROP), BF), BOTH],
+        out_shape=[pltpu.VMEM((512, CROP), BF), BOTH],
         compiler_params=pltpu.CompilerParams(vmem_limit_bytes=VMEM_LIMIT),
         name="first",
     )(crop_tiles, full_length, *in_vmem(got, prow), proj_weight)
@@ -264,11 +264,11 @@
             ],
             out_specs=[lanes_of(512), lanes_of(512, 2 * BLOCK)],
         ),
-        out_shape=[pltpu.HBM((512, CROP), BF), BOTH],
+        out_shape=[pltpu.VMEM((512, CROP), BF), BOTH],
         compiler_params=pltpu.CompilerParams(vmem_limit_bytes=VMEM_LIMIT),
         name="middle",
     )(
-        crop_tiles, full_length, *in_vmem(back), *in_hbm(current), *in_vmem(prow), proj_weight, out_weight,
+        crop_tiles, full_length, *in_vmem(back, current, prow), proj_weight, out_weight,
         proj_weight,
     )
 
@@ -310,7 +310,7 @@
         scratch_shapes=[pltpu.VMEM((512, CROP), BF), pltpu.VMEM((CROP, CROP), BF), pltpu.SemaphoreType.DMA],
         compiler_params=pltpu.CompilerParams(vmem_limit_bytes=VMEM_LIMIT),
         name="last",
-    )(*in_vmem(back), *in_hbm(current), *in_vmem(prow), proj_weight, out_weight, *in_hbm(pj))
+    )(*in_vmem(back, current, prow), proj_weight, out_weight, *in_hbm(pj))
 
 
 def right_kernel(both_ref, right_hbm, sems):
@@ -343,32 +343,25 @@
     return jnp.concatenate([both_ref[:, start : start + BLOCK] for start in starts], axis=1)
 
 
-def products_kernel(peer, *refs):
-    both_ref, right_ref = refs[0], refs[1]
-    out_hbm, square_ref, sem = refs[-3:]
-    if peer:
-        left, right = lane_blocks(both_ref, 0, [1, 0]), right_ref[...]
-    else:
-        left, right = lane_blocks(both_ref, 0, [0, 1]), lane_blocks(both_ref, 1, [0, 1])
-    square_ref[...] = dot_nt(left, right).astype(BF)
-    store = pltpu.make_async_copy(square_ref, out_hbm.at[:, pl.ds(512 * peer, 512)], sem)
-    store.start()
-    store.wait()
-
-
-def half_products(both, *others):
-    peer = len(others) // 2
-    return pl.pallas_call(
-        functools.partial(products_kernel, peer),
-        in_specs=[RESIDENT, RESIDENT, ANYWHERE][: 1 + len(others)],
-        out_specs=ANYWHERE,
-        out_shape=pltpu.HBM((512, CROP), BF),
-        input_output_aliases={2: 0} if peer else {},
-        scratch_shapes=[pltpu.VMEM((512, 512), BF), pltpu.SemaphoreType.DMA],
+def own_products_kernel(both_ref, out_ref):
+    out_ref[...] = dot_nt(lane_blocks(both_ref, 0, [0, 1]), lane_blocks(both_ref, 1, [0, 1])).astype(BF)
+
+
+def all_products_kernel(both_ref, right_ref, own_ref, out_ref):
+    out_ref[:, :512] = own_ref[...]
+    out_ref[:, 512:] = dot_nt(lane_blocks(both_ref, 0, [1, 0]), right_ref[...]).astype(BF)
+
+
+def products_call(kernel, lanes, *operands):
+    return pl.pallas_call(
+        kernel,
+        in_specs=[RESIDENT] * len(operands),
+        out_specs=RESIDENT,
+        out_shape=pltpu.VMEM((512, lanes), BF),
         compiler_params=pltpu.CompilerParams(vmem_limit_bytes=VMEM_LIMIT),
         cost_estimate=pl.CostEstimate(flops=2**29, bytes_accessed=4 * 2**20, transcendentals=0),
-        name="products" + str(peer),
-    )(both, *others)
+        name="products" + str(lanes),
+    )(*operands)
 
 
 def hidden_features(mine, peer):
@@ -436,7 +429,8 @@
     for layer in range(NLAYER):
         gathered = exchange(both, BOTH_AXES, SAME_PART, CH)
         right_peer = lax.ppermute(right_alone(gathered), BOTH_AXES, OTHER_PART)
-        products = half_products(gathered, right_peer, half_products(gathered))
+        own = products_call(own_products_kernel, 512, gathered)
+        products = products_call(all_products_kernel, CROP, gathered, right_peer, own)
         back = exchange(products, BOTH_AXES, SAME_PART, CH)
         if layer + 1 < NLAYER:
             current, both = middle_layer(crop_tiles, full_length, back, current, *weights, layer)

time: 306 us -> 303 us (level)
  Pallas kernels: 34.7 us -> 29.3 us
  waiting for transfers between devices: 58.5 us -> 62 us
    ppermute x2, waiting for transfers between devices: 31.8 us -> 35.3 us  [on_device(): right_peer = lax.ppermute(right_alone(gathered), BOTH_AXES, OTHER_PART)]
    pallas_call x4, Pallas kernels: 6.33 us -> 2.98 us  [products_call(): pl.pallas_call(kernel, in_specs=[RESIDENT] * len(operands), out_specs=RES...]
where the time goes in v13:
time: 303 us; the launch traced here: 302 us
  blocking collectives  196 us (65%)
  waiting for transfers between devices  62 us (20%)
  Pallas kernels  29.3 us (10%)
  starting transfers between devices  13.5 us (4%)
    all_to_all x5, blocking collectives, exchange(): lax.all_to_all(cube, axes, 0, 0, axis_index_groups=groups, tiled=True)  196 us
    ppermute x2, waiting for transfers between devices, on_device(): right_peer = lax.ppermute(right_alone(gathered), BOTH_AXES, OTHER_PART)  35.3 us
    all_to_all x1, waiting for transfers between devices, on_device(): lax.all_to_all(cropped, 'row', 0, 0, axis_index_groups=PLANE, tiled=True)  24.8 us
    all_to_all x1, starting transfers between devices, on_device(): lax.all_to_all(cropped, 'row', 0, 0, axis_index_groups=PLANE, tiled=True)  7.6 us
    pallas_call x1, Pallas kernels, middle_layer(): pl.pallas_call(middle_kernel, grid_spec=pltpu.PrefetchScalarGridSpec(num_...  6.14 us
  transfers between devices with their start and end apart: 5, of which 4 were waited for; matrix products, arithmetic and copies ran while one was open for 0% of the time, Pallas kernels for 2%

profile of v13, /device:TPU:1, one launch (start us, length us, event | category | flops | bytes accessed | tf_op | source)
XLA Modules:
  0.0 302.4 jit_solution(16126952310076267225)
XLA Ops:
  0.7 3.3 %crop.1 = bf16[16,64,1024]{2,1,0:T(8,128)(2,1)} custom-call(s32[1,8]{1,0:T(1,128)S(1)} %copy-done.2, bf16[16,64,2048]{2,1,0:T(8,128)(2,1)} %bitcast.29), custom_call_target="tpu_custom_call" | custom-call | tf_op jit(solution)/shard_map/crop/pallas_call | solution.py:126
  3.9 7.6 %all-to-all-start = ((bf16[16,64,1024]{2,1,0:T(8,128)(2,1)}), bf16[16,64,1024]{2,1,0:T(8,128)(2,1)S(1)}, u32[]{:S(2)}, u32[]{:S(2)}) async-start(bf16[16,64,1024]{2,1,0:T(8,128)(2,1)} %crop.1), calls=%async_computation | async-start | bytes 4194304 | tf_op jit(solution)/shard_map/all_to_all | solution.py:426
  12.3 2.4 tables.1
  14.6 24.8 %all-to-all-done.got_ref = bf16[16,64,1024]{2,1,0:T(8,128)(2,1)S(1)} async-done(((bf16[16,64,1024]{2,1,0:T(8,128)(2,1)}), bf16[16,64,1024]{2,1,0:T(8,128)(2,1)S(1)}, u32[]{:S(2)}, u32[]{:S(2)}) %all-to-all-start) | async-done | bytes 2097184 | tf_op jit(solution)/shard_map/all_to_all | solution.py:426
  39.4 4.7 %first.1 = (bf16[512,1024]{1,0:T(8,128)(2,1)S(1)}, bf16[512,2048]{1,0:T(8,128)(2,1)S(1)}) custom-call(s32[1,8]{1,0:T(1,128)S(1)} %copy-done.3, s32[1]{0:T(128)S(6)} %copy.9.length_ref, bf16[16,64,1024]{2,1,0:T(8,128)(2,1)S(1)} %all-to-all-done.got_ref, bf16[512,512]{1,0:T(8,128)(2,1)S(1)} %get-tuple-element.14.prow_ref, bf16[2,64,320]{2,1,0:T(8,128)(2,1)S(1)} %copy-done), custom_call_target="tpu_custom_call" | custom-call | tf_op jit(solution)/shard_map/first/pallas_call | solution.py:222
  44.1 52.7 %all_to_all.30 = bf16[64,8,2048]{2,1,0:T(8,128)(2,1)S(1)} all-to-all(bf16[64,8,2048]{2,1,0:T(8,128)(2,1)S(1)} %bitcast.26), channel_id=1, replica_groups={{0,1,2,3,8,9,10,11,16,17,18,19,24,25,26,27,32,33,34,35,40,41,42,43,48,4..., dimensions={0} | all-to-all | bytes 4194304 | tf_op jit(solution)/shard_map/all_to_all | solution.py:418
  96.8 1.0 right.2
  97.8 1.6 collective-permute-start
  100.2 16.1 %collective-permute-done.right_ref = bf16[512,1024]{1,0:T(8,128)(2,1)S(1)} collective-permute-done((bf16[512,1024]{1,0:T(8,128)(2,1)}, bf16[512,1024]{1,0:T(8,128)(2,1)S(1)}, u32[]{:S(2)}, u32[]{:S(2)}) %collective-permute-start) | collective-permute-done | bytes 1048608 | tf_op jit(solution)/shard_map/ppermute | solution.py:431
  116.3 0.8 products1024.2
  117.1 36.6 %all_to_all.31 = bf16[64,8,1024]{2,1,0:T(8,128)(2,1)S(1)} all-to-all(bf16[64,8,1024]{2,1,0:T(8,128)(2,1)S(1)} %bitcast.23), channel_id=1, replica_groups={{0,1,2,3,8,9,10,11,16,17,18,19,24,25,26,27,32,33,34,35,40,41,42,43,48,4..., dimensions={0} | all-to-all | bytes 2097152 | tf_op jit(solution)/shard_map/all_to_all | solution.py:418
  153.7 6.1 %middle.1 = (bf16[512,1024]{1,0:T(8,128)(2,1)S(1)}, bf16[512,2048]{1,0:T(8,128)(2,1)S(1)}) custom-call(s32[1,8]{1,0:T(1,128)S(1)} %copy-done.3, s32[1]{0:T(128)S(6)} %copy.9.length_ref, bf16[512,1024]{1,0:T(8,128)(2,1)S(1)} %bitcast.22, bf16[512,1024]{1,0:T(8,128)(2,1)S(1)} %get-tuple-element.16.cur_ref, bf16[512,512]{1,0:T(8,128)(2,1)S(1)} %get-tuple-element.14.prow_ref, ...), custom_call_target="tpu_custom_call" | custom-call | tf_op jit(solution)/shard_map/middle/pallas_call | solution.py:256
  159.8 45.8 %all_to_all.32 = bf16[64,8,2048]{2,1,0:T(8,128)(2,1)S(1)} all-to-all(bf16[64,8,2048]{2,1,0:T(8,128)(2,1)S(1)} %bitcast.25), channel_id=1, replica_groups={{0,1,2,3,8,9,10,11,16,17,18,19,24,25,26,27,32,33,34,35,40,41,42,43,48,4..., dimensions={0} | all-to-all | bytes 4194304 | tf_op jit(solution)/shard_map/all_to_all | solution.py:418
  205.6 1.0 right.3
  206.6 1.4 collective-permute-start.1
  208.7 19.1 %collective-permute-done.1.right_ref = bf16[512,1024]{1,0:T(8,128)(2,1)S(1)} collective-permute-done((bf16[512,1024]{1,0:T(8,128)(2,1)}, bf16[512,1024]{1,0:T(8,128)(2,1)S(1)}, u32[]{:S(2)}, u32[]{:S(2)}) %collective-permute-start.1) | collective-permute-done | bytes 1048608 | tf_op jit(solution)/shard_map/ppermute | solution.py:431
  227.9 0.8 products1024.3
  228.6 35.2 %all_to_all.33 = bf16[64,8,1024]{2,1,0:T(8,128)(2,1)S(1)} all-to-all(bf16[64,8,1024]{2,1,0:T(8,128)(2,1)S(1)} %bitcast.24), channel_id=1, replica_groups={{0,1,2,3,8,9,10,11,16,17,18,19,24,25,26,27,32,33,34,35,40,41,42,43,48,4..., dimensions={0} | all-to-all | bytes 2097152 | tf_op jit(solution)/shard_map/all_to_all | solution.py:418
  263.8 4.4 %last.1 = (bf16[1024,256]{1,0:T(8,128)(2,1)S(1)}, bf16[1024,256]{1,0:T(8,128)(2,1)S(1)}) custom-call(bf16[512,1024]{1,0:T(8,128)(2,1)S(1)} %bitcast.21, bf16[512,1024]{1,0:T(8,128)(2,1)S(1)} %get-tuple-element.18.cur_ref, bf16[512,512]{1,0:T(8,128)(2,1)S(1)} %get-tuple-element.14.prow_ref, bf16[2,64,320]{2,1,0:T(8,128)(2,1)S(1)} %copy-done, ...), custom_call_target="tpu_custom_call" | custom-call | tf_op jit(solution)/shard_map/last/pallas_call | solution.py:302
  268.4 1.9 collective-permute-done.2
  270.5 25.5 %all_to_all.34 = bf16[128,8,256]{2,1,0:T(8,128)(2,1)S(1)} all-to-all(bf16[128,8,256]{2,1,0:T(8,128)(2,1)S(1)} %fusion), channel_id=1, replica_groups={{0,8,16,24,32,40,48,56,64,72,80,88,96,104,112,120,1,9,17,25,33,41,49,57..., dimensions={0} | all-to-all | bytes 1048576 | tf_op jit(solution)/shard_map/all_to_all | solution.py:418
  296.0 2.8 collective-permute-start.3
  298.8 1.7 final0.1.refs_2_
  300.5 1.7 final1.1
  (15 shorter events, 2.4 us)
Async XLA Ops:
  0.0 0.7 copy-start.2
  3.9 8.3 %copy-start.4 = (bf16[64,128]{1,0:T(8,128)(2,1)S(1)}, bf16[64,128]{1,0:T(8,128)(2,1)}, u32[]{:S(2)}) copy-start(bf16[64,128]{1,0:T(8,128)(2,1)} %final_ref.1) | copy-start | bytes 49156
  3.9 35.5 %all-to-all-start = ((bf16[16,64,1024]{2,1,0:T(8,128)(2,1)}), bf16[16,64,1024]{2,1,0:T(8,128)(2,1)S(1)}, u32[]{:S(2)}, u32[]{:S(2)}) async-start(bf16[16,64,1024]{2,1,0:T(8,128)(2,1)} %crop.1), calls=%async_computation | async-start | bytes 4194304 | tf_op jit(solution)/shard_map/all_to_all | solution.py:426
  11.6 27.9 %copy-start = (bf16[2,64,320]{2,1,0:T(8,128)(2,1)S(1)}, bf16[2,64,320]{2,1,0:T(8,128)(2,1)}, u32[]{:S(2)}) copy-start(bf16[2,64,320]{2,1,0:T(8,128)(2,1)} %w_ref.5) | copy-start | bytes 245764
  11.6 27.9 %copy-start.3 = (s32[1,8]{1,0:T(1,128)S(1)}, s32[1,8]{1,0:T(1,128)}, u32[]{:S(2)}) copy-start(s32[1,8]{1,0:T(1,128)} %crop_ref.5) | copy-start | bytes 100
  97.8 18.5 %collective-permute-start = (bf16[512,1024]{1,0:T(8,128)(2,1)}, bf16[512,1024]{1,0:T(8,128)(2,1)S(1)}, u32[]{:S(2)}, u32[]{:S(2)}) collective-permute-start(bf16[512,1024]{1,0:T(8,128)(2,1)} %right.2), channel_id=1, source_target_pairs={{0,7},{1,6},{2,5},{3,4},{4,3},{5,2},{6,1},{7,0},{8,15},{9,14},{10,... | collective-permute-start | bytes 3145736 | tf_op jit(solution)/shard_map/ppermute | solution.py:431
  117.1 36.6 %copy-start.1 = (bf16[2,64,64]{2,1,0:T(8,128)(2,1)S(1)}, bf16[2,64,64]{2,1,0:T(8,128)(2,1)}, u32[]{:S(2)}) copy-start(bf16[2,64,64]{2,1,0:T(8,128)(2,1)} %w_out_ref.3) | copy-start | bytes 49156
  206.6 21.2 %collective-permute-start.1 = (bf16[512,1024]{1,0:T(8,128)(2,1)}, bf16[512,1024]{1,0:T(8,128)(2,1)S(1)}, u32[]{:S(2)}, u32[]{:S(2)}) collective-permute-start(bf16[512,1024]{1,0:T(8,128)(2,1)} %right.3), channel_id=1, source_target_pairs={{0,7},{1,6},{2,5},{3,4},{4,3},{5,2},{6,1},{7,0},{8,15},{9,14},{10,... | collective-permute-start | bytes 3145736 | tf_op jit(solution)/shard_map/ppermute | solution.py:431
  268.3 2.0 collective-permute-start.2
  296.0 4.5 %collective-permute-start.3 = (bf16[1024,256]{1,0:T(8,128)(2,1)S(1)}, bf16[1024,256]{1,0:T(8,128)(2,1)S(1)}, u32[]{:S(2)}, u32[]{:S(2)}) collective-permute-start(bf16[1024,256]{1,0:T(8,128)(2,1)S(1)} %bitcast.27), channel_id=1, source_target_pairs={{0,128},{128,0},{1,129},{129,1},{2,130},{130,2},{3,131},{131,3},{4... | collective-permute-start | bytes 1572872 | tf_op jit(solution)/shard_map/ppermute | solution.py:441

commit v14 on v13

--- a/solution.py
+++ b/solution.py
@@ -21,12 +21,12 @@
 PLANE = [[s * 8 + z for s in range(16)] for z in range(8)]
 BOTH_AXES = ("tmpl", "row")
 SAME_PART = [
-    [t * 128 + s * 8 + ((7 - zi if part else zi) + 2 * t) % 8 for s in range(16) for zi in range(4)]
+    [t * 128 + s * 8 + ((zi ^ 6 if part else zi) + 2 * t) % 8 for s in range(16) for zi in range(4)]
     for t in range(2)
     for part in range(2)
 ]
 OTHER_PART = [
-    (t * 128 + s * 8 + z, t * 128 + s * 8 + (7 + 4 * t - z) % 8) for t in range(2) for s in range(16) for z in range(8)
+    (t * 128 + s * 8 + z, t * 128 + s * 8 + (((z - 2 * t) % 8 ^ 6) + 2 * t) % 8) for t in range(2) for s in range(16) for z in range(8)
 ]
 BY_Z = [[s * 8 + z for z in range(8) for s in range(16)]]
 CORES = [(0, 1), (1, 0)]
@@ -65,7 +65,7 @@
     core, chip = lax.axis_index("tmpl"), lax.axis_index("row")
     part = (lane // 512) ^ (((chip % 8 + 8 - 2 * core) % 8) // 4)
     place = (lane // 8) % 4
-    z = (jnp.where(part == 0, place, 7 - place) + 2 * core) % 8
+    z = (jnp.where(part == 0, place, place ^ 6) + 2 * core) % 8
     return (lane % 8) * 128 + z * 16 + (lane // 32) % 16
 
 

time: 303 us -> 304 us (level)
  waiting for transfers between devices: 62 us -> 74.4 us
  blocking collectives: 196 us -> 184 us
    ppermute x2, waiting for transfers between devices: 35.3 us -> 47.7 us  [on_device(): right_peer = lax.ppermute(right_alone(gathered), BOTH_AXES, OTHER_PART)]
    all_to_all x5, blocking collectives: 196 us -> 184 us  [exchange(): lax.all_to_all(cube, axes, 0, 0, axis_index_groups=groups, tiled=True)]
where the time goes in v14:
time: 304 us; the launch traced here: 303 us
  blocking collectives  184 us (61%)
  waiting for transfers between devices  74.4 us (24%)
  Pallas kernels  29.3 us (10%)
  starting transfers between devices  13.3 us (4%)
    all_to_all x5, blocking collectives, exchange(): lax.all_to_all(cube, axes, 0, 0, axis_index_groups=groups, tiled=True)  184 us
    ppermute x2, waiting for transfers between devices, on_device(): right_peer = lax.ppermute(right_alone(gathered), BOTH_AXES, OTHER_PART)  47.7 us
    all_to_all x1, waiting for transfers between devices, on_device(): lax.all_to_all(cropped, 'row', 0, 0, axis_index_groups=PLANE, tiled=True)  24.8 us
    all_to_all x1, starting transfers between devices, on_device(): lax.all_to_all(cropped, 'row', 0, 0, axis_index_groups=PLANE, tiled=True)  7.6 us
    pallas_call x1, Pallas kernels, middle_layer(): pl.pallas_call(middle_kernel, grid_spec=pltpu.PrefetchScalarGridSpec(num_...  6.15 us
  transfers between devices with their start and end apart: 5, of which 4 were waited for; matrix products, arithmetic and copies ran while one was open for 0% of the time, Pallas kernels for 2%

profile of v14, /device:TPU:1, one launch (start us, length us, event | category | flops | bytes accessed | tf_op | source)
XLA Modules:
  0.0 303.1 jit_solution(6374124794640499665)
XLA Ops:
  0.7 3.3 %crop.1 = bf16[16,64,1024]{2,1,0:T(8,128)(2,1)} custom-call(s32[1,8]{1,0:T(1,128)S(1)} %copy-done.2, bf16[16,64,2048]{2,1,0:T(8,128)(2,1)} %bitcast.29), custom_call_target="tpu_custom_call" | custom-call | tf_op jit(solution)/shard_map/crop/pallas_call | solution.py:126
  3.9 7.6 %all-to-all-start = ((bf16[16,64,1024]{2,1,0:T(8,128)(2,1)}), bf16[16,64,1024]{2,1,0:T(8,128)(2,1)S(1)}, u32[]{:S(2)}, u32[]{:S(2)}) async-start(bf16[16,64,1024]{2,1,0:T(8,128)(2,1)} %crop.1), calls=%async_computation | async-start | bytes 4194304 | tf_op jit(solution)/shard_map/all_to_all | solution.py:426
  12.3 2.4 tables.1
  14.6 24.8 %all-to-all-done.got_ref = bf16[16,64,1024]{2,1,0:T(8,128)(2,1)S(1)} async-done(((bf16[16,64,1024]{2,1,0:T(8,128)(2,1)}), bf16[16,64,1024]{2,1,0:T(8,128)(2,1)S(1)}, u32[]{:S(2)}, u32[]{:S(2)}) %all-to-all-start) | async-done | bytes 2097184 | tf_op jit(solution)/shard_map/all_to_all | solution.py:426
  39.4 4.7 %first.1 = (bf16[512,1024]{1,0:T(8,128)(2,1)S(1)}, bf16[512,2048]{1,0:T(8,128)(2,1)S(1)}) custom-call(s32[1,8]{1,0:T(1,128)S(1)} %copy-done.3, s32[1]{0:T(128)S(6)} %copy.9.length_ref, bf16[16,64,1024]{2,1,0:T(8,128)(2,1)S(1)} %all-to-all-done.got_ref, bf16[512,512]{1,0:T(8,128)(2,1)S(1)} %get-tuple-element.14.prow_ref, bf16[2,64,320]{2,1,0:T(8,128)(2,1)S(1)} %copy-done), custom_call_target="tpu_custom_call" | custom-call | tf_op jit(solution)/shard_map/first/pallas_call | solution.py:222
  44.1 51.0 %all_to_all.30 = bf16[64,8,2048]{2,1,0:T(8,128)(2,1)S(1)} all-to-all(bf16[64,8,2048]{2,1,0:T(8,128)(2,1)S(1)} %bitcast.26), channel_id=1, replica_groups={{0,1,2,3,8,9,10,11,16,17,18,19,24,25,26,27,32,33,34,35,40,41,42,43,48,4..., dimensions={0} | all-to-all | bytes 4194304 | tf_op jit(solution)/shard_map/all_to_all | solution.py:418
  95.1 1.0 right.2
  96.1 1.9 collective-permute-start
  98.8 23.0 %collective-permute-done.right_ref = bf16[512,1024]{1,0:T(8,128)(2,1)S(1)} collective-permute-done((bf16[512,1024]{1,0:T(8,128)(2,1)}, bf16[512,1024]{1,0:T(8,128)(2,1)S(1)}, u32[]{:S(2)}, u32[]{:S(2)}) %collective-permute-start) | collective-permute-done | bytes 1048608 | tf_op jit(solution)/shard_map/ppermute | solution.py:431
  121.8 0.8 products1024.2
  122.6 30.7 %all_to_all.31 = bf16[64,8,1024]{2,1,0:T(8,128)(2,1)S(1)} all-to-all(bf16[64,8,1024]{2,1,0:T(8,128)(2,1)S(1)} %bitcast.23), channel_id=1, replica_groups={{0,1,2,3,8,9,10,11,16,17,18,19,24,25,26,27,32,33,34,35,40,41,42,43,48,4..., dimensions={0} | all-to-all | bytes 2097152 | tf_op jit(solution)/shard_map/all_to_all | solution.py:418
  153.3 6.1 %middle.1 = (bf16[512,1024]{1,0:T(8,128)(2,1)S(1)}, bf16[512,2048]{1,0:T(8,128)(2,1)S(1)}) custom-call(s32[1,8]{1,0:T(1,128)S(1)} %copy-done.3, s32[1]{0:T(128)S(6)} %copy.9.length_ref, bf16[512,1024]{1,0:T(8,128)(2,1)S(1)} %bitcast.22, bf16[512,1024]{1,0:T(8,128)(2,1)S(1)} %get-tuple-element.16.cur_ref, bf16[512,512]{1,0:T(8,128)(2,1)S(1)} %get-tuple-element.14.prow_ref, ...), custom_call_target="tpu_custom_call" | custom-call | tf_op jit(solution)/shard_map/middle/pallas_call | solution.py:256
  159.4 45.9 %all_to_all.32 = bf16[64,8,2048]{2,1,0:T(8,128)(2,1)S(1)} all-to-all(bf16[64,8,2048]{2,1,0:T(8,128)(2,1)S(1)} %bitcast.25), channel_id=1, replica_groups={{0,1,2,3,8,9,10,11,16,17,18,19,24,25,26,27,32,33,34,35,40,41,42,43,48,4..., dimensions={0} | all-to-all | bytes 4194304 | tf_op jit(solution)/shard_map/all_to_all | solution.py:418
  205.3 1.0 right.3
  206.3 1.0 collective-permute-start.1
  208.0 24.7 %collective-permute-done.1.right_ref = bf16[512,1024]{1,0:T(8,128)(2,1)S(1)} collective-permute-done((bf16[512,1024]{1,0:T(8,128)(2,1)}, bf16[512,1024]{1,0:T(8,128)(2,1)S(1)}, u32[]{:S(2)}, u32[]{:S(2)}) %collective-permute-start.1) | collective-permute-done | bytes 1048608 | tf_op jit(solution)/shard_map/ppermute | solution.py:431
  232.7 0.8 products1024.3
  233.4 29.9 %all_to_all.33 = bf16[64,8,1024]{2,1,0:T(8,128)(2,1)S(1)} all-to-all(bf16[64,8,1024]{2,1,0:T(8,128)(2,1)S(1)} %bitcast.24), channel_id=1, replica_groups={{0,1,2,3,8,9,10,11,16,17,18,19,24,25,26,27,32,33,34,35,40,41,42,43,48,4..., dimensions={0} | all-to-all | bytes 2097152 | tf_op jit(solution)/shard_map/all_to_all | solution.py:418
  263.3 4.4 %last.1 = (bf16[1024,256]{1,0:T(8,128)(2,1)S(1)}, bf16[1024,256]{1,0:T(8,128)(2,1)S(1)}) custom-call(bf16[512,1024]{1,0:T(8,128)(2,1)S(1)} %bitcast.21, bf16[512,1024]{1,0:T(8,128)(2,1)S(1)} %get-tuple-element.18.cur_ref, bf16[512,512]{1,0:T(8,128)(2,1)S(1)} %get-tuple-element.14.prow_ref, bf16[2,64,320]{2,1,0:T(8,128)(2,1)S(1)} %copy-done, ...), custom_call_target="tpu_custom_call" | custom-call | tf_op jit(solution)/shard_map/last/pallas_call | solution.py:302
  267.8 1.9 collective-permute-done.2
  269.9 26.7 %all_to_all.34 = bf16[128,8,256]{2,1,0:T(8,128)(2,1)S(1)} all-to-all(bf16[128,8,256]{2,1,0:T(8,128)(2,1)S(1)} %fusion), channel_id=1, replica_groups={{0,8,16,24,32,40,48,56,64,72,80,88,96,104,112,120,1,9,17,25,33,41,49,57..., dimensions={0} | all-to-all | bytes 1048576 | tf_op jit(solution)/shard_map/all_to_all | solution.py:418
  296.6 2.8 collective-permute-start.3
  299.4 1.7 final0.1.refs_2_
  301.2 1.7 final1.1
  (15 shorter events, 2.4 us)
Async XLA Ops:
  0.0 0.7 copy-start.2
  3.9 8.3 %copy-start.4 = (bf16[64,128]{1,0:T(8,128)(2,1)S(1)}, bf16[64,128]{1,0:T(8,128)(2,1)}, u32[]{:S(2)}) copy-start(bf16[64,128]{1,0:T(8,128)(2,1)} %final_ref.1) | copy-start | bytes 49156
  3.9 35.5 %all-to-all-start = ((bf16[16,64,1024]{2,1,0:T(8,128)(2,1)}), bf16[16,64,1024]{2,1,0:T(8,128)(2,1)S(1)}, u32[]{:S(2)}, u32[]{:S(2)}) async-start(bf16[16,64,1024]{2,1,0:T(8,128)(2,1)} %crop.1), calls=%async_computation | async-start | bytes 4194304 | tf_op jit(solution)/shard_map/all_to_all | solution.py:426
  11.6 27.9 %copy-start = (bf16[2,64,320]{2,1,0:T(8,128)(2,1)S(1)}, bf16[2,64,320]{2,1,0:T(8,128)(2,1)}, u32[]{:S(2)}) copy-start(bf16[2,64,320]{2,1,0:T(8,128)(2,1)} %w_ref.5) | copy-start | bytes 245764
  11.6 27.9 %copy-start.3 = (s32[1,8]{1,0:T(1,128)S(1)}, s32[1,8]{1,0:T(1,128)}, u32[]{:S(2)}) copy-start(s32[1,8]{1,0:T(1,128)} %crop_ref.5) | copy-start | bytes 100
  96.1 25.7 %collective-permute-start = (bf16[512,1024]{1,0:T(8,128)(2,1)}, bf16[512,1024]{1,0:T(8,128)(2,1)S(1)}, u32[]{:S(2)}, u32[]{:S(2)}) collective-permute-start(bf16[512,1024]{1,0:T(8,128)(2,1)} %right.2), channel_id=1, source_target_pairs={{0,6},{1,7},{2,4},{3,5},{4,2},{5,3},{6,0},{7,1},{8,14},{9,15},{10,... | collective-permute-start | bytes 3145736 | tf_op jit(solution)/shard_map/ppermute | solution.py:431
  122.6 30.7 %copy-start.1 = (bf16[2,64,64]{2,1,0:T(8,128)(2,1)S(1)}, bf16[2,64,64]{2,1,0:T(8,128)(2,1)}, u32[]{:S(2)}) copy-start(bf16[2,64,64]{2,1,0:T(8,128)(2,1)} %w_out_ref.3) | copy-start | bytes 49156
  206.3 26.4 %collective-permute-start.1 = (bf16[512,1024]{1,0:T(8,128)(2,1)}, bf16[512,1024]{1,0:T(8,128)(2,1)S(1)}, u32[]{:S(2)}, u32[]{:S(2)}) collective-permute-start(bf16[512,1024]{1,0:T(8,128)(2,1)} %right.3), channel_id=1, source_target_pairs={{0,6},{1,7},{2,4},{3,5},{4,2},{5,3},{6,0},{7,1},{8,14},{9,15},{10,... | collective-permute-start | bytes 3145736 | tf_op jit(solution)/shard_map/ppermute | solution.py:431
  267.7 2.0 collective-permute-start.2
  296.6 4.5 %collective-permute-start.3 = (bf16[1024,256]{1,0:T(8,128)(2,1)S(1)}, bf16[1024,256]{1,0:T(8,128)(2,1)S(1)}, u32[]{:S(2)}, u32[]{:S(2)}) collective-permute-start(bf16[1024,256]{1,0:T(8,128)(2,1)S(1)} %bitcast.27), channel_id=1, source_target_pairs={{0,128},{128,0},{1,129},{129,1},{2,130},{130,2},{3,131},{131,3},{4... | collective-permute-start | bytes 1572872 | tf_op jit(solution)/shard_map/ppermute | solution.py:441

commit v15 on v13

--- a/solution.py
+++ b/solution.py
@@ -313,25 +313,16 @@
     )(*in_vmem(back, current, prow), proj_weight, out_weight, *in_hbm(pj))
 
 
-def right_kernel(both_ref, right_hbm, sems):
-    copies = []
-    for block in range(STEPS):
-        source = both_ref.at[:, pl.ds((2 * block + 1) * BLOCK, BLOCK)]
-        place = right_hbm.at[:, pl.ds(block * BLOCK, BLOCK)]
-        copies.append(pltpu.make_async_copy(source, place, sems.at[block]))
-    for copy in copies:
-        copy.start()
-    for copy in copies:
-        copy.wait()
+def right_kernel(both_ref, right_ref):
+    right_ref[...] = lane_blocks(both_ref, 1, [0, 1])
 
 
 def right_alone(both):
     return pl.pallas_call(
         right_kernel,
         in_specs=[RESIDENT],
-        out_specs=ANYWHERE,
-        out_shape=pltpu.HBM((512, CROP), BF),
-        scratch_shapes=[pltpu.SemaphoreType.DMA((STEPS,))],
+        out_specs=RESIDENT,
+        out_shape=pltpu.VMEM((512, CROP), BF),
         compiler_params=pltpu.CompilerParams(vmem_limit_bytes=VMEM_LIMIT),
         cost_estimate=pl.CostEstimate(flops=0, bytes_accessed=2 * 2**20, transcendentals=0),
         name="right",

time: 303 us -> 301 us (level)
  no operation moved by 1% of the time
where the time goes in v15:
time: 301 us; the launch traced here: 300 us
  blocking collectives  196 us (65%)
  waiting for transfers between devices  61.7 us (20%)
  Pallas kernels  27.5 us (9%)
  starting transfers between devices  13.5 us (4%)
    all_to_all x5, blocking collectives, exchange(): lax.all_to_all(cube, axes, 0, 0, axis_index_groups=groups, tiled=True)  196 us
    ppermute x2, waiting for transfers between devices, on_device(): right_peer = lax.ppermute(right_alone(gathered), BOTH_AXES, OTHER_PART)  35 us
    all_to_all x1, waiting for transfers between devices, on_device(): lax.all_to_all(cropped, 'row', 0, 0, axis_index_groups=PLANE, tiled=True)  24.8 us
    all_to_all x1, starting transfers between devices, on_device(): lax.all_to_all(cropped, 'row', 0, 0, axis_index_groups=PLANE, tiled=True)  7.6 us
    pallas_call x1, Pallas kernels, middle_layer(): pl.pallas_call(middle_kernel, grid_spec=pltpu.PrefetchScalarGridSpec(num_...  6.14 us
  transfers between devices with their start and end apart: 5, of which 4 were waited for; matrix products, arithmetic and copies ran while one was open for 0% of the time, Pallas kernels for 2%

profile of v15, /device:TPU:1, one launch (start us, length us, event | category | flops | bytes accessed | tf_op | source)
XLA Modules:
  0.0 300.2 jit_solution(14421702349290511538)
XLA Ops:
  0.7 3.3 %crop.1 = bf16[16,64,1024]{2,1,0:T(8,128)(2,1)} custom-call(s32[1,8]{1,0:T(1,128)S(1)} %copy-done.2, bf16[16,64,2048]{2,1,0:T(8,128)(2,1)} %bitcast.29), custom_call_target="tpu_custom_call" | custom-call | tf_op jit(solution)/shard_map/crop/pallas_call | solution.py:126
  3.9 7.6 %all-to-all-start = ((bf16[16,64,1024]{2,1,0:T(8,128)(2,1)}), bf16[16,64,1024]{2,1,0:T(8,128)(2,1)S(1)}, u32[]{:S(2)}, u32[]{:S(2)}) async-start(bf16[16,64,1024]{2,1,0:T(8,128)(2,1)} %crop.1), calls=%async_computation | async-start | bytes 4194304 | tf_op jit(solution)/shard_map/all_to_all | solution.py:417
  12.3 2.4 tables.1
  14.6 24.8 %all-to-all-done.got_ref = bf16[16,64,1024]{2,1,0:T(8,128)(2,1)S(1)} async-done(((bf16[16,64,1024]{2,1,0:T(8,128)(2,1)}), bf16[16,64,1024]{2,1,0:T(8,128)(2,1)S(1)}, u32[]{:S(2)}, u32[]{:S(2)}) %all-to-all-start) | async-done | bytes 2097184 | tf_op jit(solution)/shard_map/all_to_all | solution.py:417
  39.4 4.7 %first.1 = (bf16[512,1024]{1,0:T(8,128)(2,1)S(1)}, bf16[512,2048]{1,0:T(8,128)(2,1)S(1)}) custom-call(s32[1,8]{1,0:T(1,128)S(1)} %copy-done.3, s32[1]{0:T(128)S(6)} %copy.9.length_ref, bf16[16,64,1024]{2,1,0:T(8,128)(2,1)S(1)} %all-to-all-done.got_ref, bf16[512,512]{1,0:T(8,128)(2,1)S(1)} %get-tuple-element.14.prow_ref, bf16[2,64,320]{2,1,0:T(8,128)(2,1)S(1)} %copy-done), custom_call_target="tpu_custom_call" | custom-call | tf_op jit(solution)/shard_map/first/pallas_call | solution.py:222
  44.1 52.7 %all_to_all.30 = bf16[64,8,2048]{2,1,0:T(8,128)(2,1)S(1)} all-to-all(bf16[64,8,2048]{2,1,0:T(8,128)(2,1)S(1)} %bitcast.26), channel_id=1, replica_groups={{0,1,2,3,8,9,10,11,16,17,18,19,24,25,26,27,32,33,34,35,40,41,42,43,48,4..., dimensions={0} | all-to-all | bytes 4194304 | tf_op jit(solution)/shard_map/all_to_all | solution.py:409
  96.9 1.6 collective-permute-start
  98.5 0.7 products512.2.own_ref
  99.2 15.9 %collective-permute-done.right_ref = bf16[512,1024]{1,0:T(8,128)(2,1)S(1)} collective-permute-done((bf16[512,1024]{1,0:T(8,128)(2,1)S(1)}, bf16[512,1024]{1,0:T(8,128)(2,1)S(1)}, u32[]{:S(2)}, u32[]{:S(2)}) %collective-permute-start) | collective-permute-done | bytes 1048608 | tf_op jit(solution)/shard_map/ppermute | solution.py:422
  115.2 0.8 products1024.2
  116.0 36.6 %all_to_all.31 = bf16[64,8,1024]{2,1,0:T(8,128)(2,1)S(1)} all-to-all(bf16[64,8,1024]{2,1,0:T(8,128)(2,1)S(1)} %bitcast.23), channel_id=1, replica_groups={{0,1,2,3,8,9,10,11,16,17,18,19,24,25,26,27,32,33,34,35,40,41,42,43,48,4..., dimensions={0} | all-to-all | bytes 2097152 | tf_op jit(solution)/shard_map/all_to_all | solution.py:409
  152.6 6.1 %middle.1 = (bf16[512,1024]{1,0:T(8,128)(2,1)S(1)}, bf16[512,2048]{1,0:T(8,128)(2,1)S(1)}) custom-call(s32[1,8]{1,0:T(1,128)S(1)} %copy-done.3, s32[1]{0:T(128)S(6)} %copy.9.length_ref, bf16[512,1024]{1,0:T(8,128)(2,1)S(1)} %bitcast.22, bf16[512,1024]{1,0:T(8,128)(2,1)S(1)} %get-tuple-element.16.cur_ref, bf16[512,512]{1,0:T(8,128)(2,1)S(1)} %get-tuple-element.14.prow_ref, ...), custom_call_target="tpu_custom_call" | custom-call | tf_op jit(solution)/shard_map/middle/pallas_call | solution.py:256
  158.7 45.8 %all_to_all.32 = bf16[64,8,2048]{2,1,0:T(8,128)(2,1)S(1)} all-to-all(bf16[64,8,2048]{2,1,0:T(8,128)(2,1)S(1)} %bitcast.25), channel_id=1, replica_groups={{0,1,2,3,8,9,10,11,16,17,18,19,24,25,26,27,32,33,34,35,40,41,42,43,48,4..., dimensions={0} | all-to-all | bytes 4194304 | tf_op jit(solution)/shard_map/all_to_all | solution.py:409
  204.6 1.4 collective-permute-start.1
  205.9 0.7 products512.3.own_ref
  206.7 19.1 %collective-permute-done.1.right_ref = bf16[512,1024]{1,0:T(8,128)(2,1)S(1)} collective-permute-done((bf16[512,1024]{1,0:T(8,128)(2,1)S(1)}, bf16[512,1024]{1,0:T(8,128)(2,1)S(1)}, u32[]{:S(2)}, u32[]{:S(2)}) %collective-permute-start.1) | collective-permute-done | bytes 1048608 | tf_op jit(solution)/shard_map/ppermute | solution.py:422
  225.8 0.8 products1024.3
  226.5 35.1 %all_to_all.33 = bf16[64,8,1024]{2,1,0:T(8,128)(2,1)S(1)} all-to-all(bf16[64,8,1024]{2,1,0:T(8,128)(2,1)S(1)} %bitcast.24), channel_id=1, replica_groups={{0,1,2,3,8,9,10,11,16,17,18,19,24,25,26,27,32,33,34,35,40,41,42,43,48,4..., dimensions={0} | all-to-all | bytes 2097152 | tf_op jit(solution)/shard_map/all_to_all | solution.py:409
  261.6 4.4 %last.1 = (bf16[1024,256]{1,0:T(8,128)(2,1)S(1)}, bf16[1024,256]{1,0:T(8,128)(2,1)S(1)}) custom-call(bf16[512,1024]{1,0:T(8,128)(2,1)S(1)} %bitcast.21, bf16[512,1024]{1,0:T(8,128)(2,1)S(1)} %get-tuple-element.18.cur_ref, bf16[512,512]{1,0:T(8,128)(2,1)S(1)} %get-tuple-element.14.prow_ref, bf16[2,64,320]{2,1,0:T(8,128)(2,1)S(1)} %copy-done, ...), custom_call_target="tpu_custom_call" | custom-call | tf_op jit(solution)/shard_map/last/pallas_call | solution.py:302
  266.1 1.9 collective-permute-done.2
  268.2 25.5 %all_to_all.34 = bf16[128,8,256]{2,1,0:T(8,128)(2,1)S(1)} all-to-all(bf16[128,8,256]{2,1,0:T(8,128)(2,1)S(1)} %fusion), channel_id=1, replica_groups={{0,8,16,24,32,40,48,56,64,72,80,88,96,104,112,120,1,9,17,25,33,41,49,57..., dimensions={0} | all-to-all | bytes 1048576 | tf_op jit(solution)/shard_map/all_to_all | solution.py:409
  293.7 2.8 collective-permute-start.3
  296.5 1.7 final0.1.refs_2_
  298.3 1.7 final1.1
  (15 shorter events, 1.1 us)
Async XLA Ops:
  0.0 0.7 copy-start.2
  3.9 8.3 %copy-start.4 = (bf16[64,128]{1,0:T(8,128)(2,1)S(1)}, bf16[64,128]{1,0:T(8,128)(2,1)}, u32[]{:S(2)}) copy-start(bf16[64,128]{1,0:T(8,128)(2,1)} %final_ref.1) | copy-start | bytes 49156
  3.9 35.5 %all-to-all-start = ((bf16[16,64,1024]{2,1,0:T(8,128)(2,1)}), bf16[16,64,1024]{2,1,0:T(8,128)(2,1)S(1)}, u32[]{:S(2)}, u32[]{:S(2)}) async-start(bf16[16,64,1024]{2,1,0:T(8,128)(2,1)} %crop.1), calls=%async_computation | async-start | bytes 4194304 | tf_op jit(solution)/shard_map/all_to_all | solution.py:417
  11.6 27.9 %copy-start = (bf16[2,64,320]{2,1,0:T(8,128)(2,1)S(1)}, bf16[2,64,320]{2,1,0:T(8,128)(2,1)}, u32[]{:S(2)}) copy-start(bf16[2,64,320]{2,1,0:T(8,128)(2,1)} %w_ref.5) | copy-start | bytes 245764
  11.6 27.9 %copy-start.3 = (s32[1,8]{1,0:T(1,128)S(1)}, s32[1,8]{1,0:T(1,128)}, u32[]{:S(2)}) copy-start(s32[1,8]{1,0:T(1,128)} %crop_ref.5) | copy-start | bytes 100
  96.9 18.3 %collective-permute-start = (bf16[512,1024]{1,0:T(8,128)(2,1)S(1)}, bf16[512,1024]{1,0:T(8,128)(2,1)S(1)}, u32[]{:S(2)}, u32[]{:S(2)}) collective-permute-start(bf16[512,1024]{1,0:T(8,128)(2,1)S(1)} %right.2), channel_id=1, source_target_pairs={{0,7},{1,6},{2,5},{3,4},{4,3},{5,2},{6,1},{7,0},{8,15},{9,14},{10,... | collective-permute-start | bytes 3145736 | tf_op jit(solution)/shard_map/ppermute | solution.py:422
  115.9 36.6 %copy-start.1 = (bf16[2,64,64]{2,1,0:T(8,128)(2,1)S(1)}, bf16[2,64,64]{2,1,0:T(8,128)(2,1)}, u32[]{:S(2)}) copy-start(bf16[2,64,64]{2,1,0:T(8,128)(2,1)} %w_out_ref.3) | copy-start | bytes 49156
  204.6 21.2 %collective-permute-start.1 = (bf16[512,1024]{1,0:T(8,128)(2,1)S(1)}, bf16[512,1024]{1,0:T(8,128)(2,1)S(1)}, u32[]{:S(2)}, u32[]{:S(2)}) collective-permute-start(bf16[512,1024]{1,0:T(8,128)(2,1)S(1)} %right.3), channel_id=1, source_target_pairs={{0,7},{1,6},{2,5},{3,4},{4,3},{5,2},{6,1},{7,0},{8,15},{9,14},{10,... | collective-permute-start | bytes 3145736 | tf_op jit(solution)/shard_map/ppermute | solution.py:422
  266.0 2.0 collective-permute-start.2
  293.7 4.5 %collective-permute-start.3 = (bf16[1024,256]{1,0:T(8,128)(2,1)S(1)}, bf16[1024,256]{1,0:T(8,128)(2,1)S(1)}, u32[]{:S(2)}, u32[]{:S(2)}) collective-permute-start(bf16[1024,256]{1,0:T(8,128)(2,1)S(1)} %bitcast.27), channel_id=1, source_target_pairs={{0,128},{128,0},{1,129},{129,1},{2,130},{130,2},{3,131},{131,3},{4... | collective-permute-start | bytes 1572872 | tf_op jit(solution)/shard_map/ppermute | solution.py:432
